TPU v7x, 32 devices: a whole 2x2x4 slice. The times are simulated.
32 devices in a mesh: dp: 8 (over z, x), head: 4 (over y, core).
Axes of the slice: x: 2, y: 2, z: 4, core: 2. Of those that a mesh axis runs over, the one named last changes fastest.
Arguments:
- tokens: bfloat16 [32, 196, 216], P('dp'), may hold values from -6 to 6
- cotangent: float32 [32, 196, 216], P('dp'), may hold values from -6 to 6
- image_count: int32 [8], P('dp'), may hold values from 1 to 4, as said below
- subnet_heads: int32 [1], replicated, may hold values from 6 to 12
- subnet_width: int32 [1], replicated, may hold values from 432 to 864
- block_slot: int32 [12], replicated, may hold values from 0 to 15, as said below
- master: float32 [16, 54, 864], P('dp', None, 'head'), may hold values from -0.8164966 to 0.8164966
- master_m1: float32 [16, 54, 864], P('dp', None, 'head'), may hold values from -187.82971 to 187.82971
- master_m2: float32 [16, 54, 864], P('dp', None, 'head'), may hold values from 78 to 15680
- norm_params: float32 [4, 216], replicated, may hold values from -0.9 to 1.45
- norm_m1: float32 [4, 216], replicated, may hold values from -265.63132 to 265.63132
- norm_m2: float32 [4, 216], replicated, may hold values from 3920 to 35280
- talk: float32 [2, 12, 12], replicated, may hold values from -0.45 to 1.45
- talk_m1: float32 [2, 12, 12], replicated, may hold values from -831.55756 to 831.55756
- talk_m2: float32 [2, 12, 12], replicated, may hold values from 38416 to 307328
- conv: float32 [9, 864], P(None, 'head'), may hold values from -1 to 1
- conv_m1: float32 [9, 864], P(None, 'head'), may hold values from -108.41586 to 108.41586
- conv_m2: float32 [9, 864], P(None, 'head'), may hold values from 653 to 5226
Outputs:
- output: float32 [32, 196, 216], P('dp')
- token_grad: float32 [32, 196, 216], P('dp')
- new_master: float32 [16, 54, 864], P('dp', None, 'head')
- new_master_m1: float32 [16, 54, 864], P('dp', None, 'head')
- new_master_m2: float32 [16, 54, 864], P('dp', None, 'head')
- master_copy: bfloat16 [16, 54, 864], P('dp', None, 'head')
- new_norm: float32 [4, 216], replicated
- new_norm_m1: float32 [4, 216], replicated
- new_norm_m2: float32 [4, 216], replicated
- new_talk: float32 [2, 12, 12], replicated
- new_talk_m1: float32 [2, 12, 12], replicated
- new_talk_m2: float32 [2, 12, 12], replicated
- new_conv: float32 [9, 864], P(None, 'head')
- new_conv_m1: float32 [9, 864], P(None, 'head')
- new_conv_m2: float32 [9, 864], P(None, 'head')
Inputs may be any that keep to these rules, and one draw needn't show every extreme that they name: `image_count`: image slots at or beyond a dp index's count are padding; some dp index holds exactly 4 images and some exactly 1. `block_slot`: the twelve slots are distinct.
All inputs are finite; a program needn't handle non-finite values.
Results may differ from a plain program's by a relative error of at most 0.012.
The roundings to bfloat16 on the way count: a program that leaves them out, or rounds other values in their place, can miss the bound.
Values may be sent and summed in bfloat16 or wider, within the bound.
No kernel may reach another device: no remote copies, remote signals or barrier semaphores. Data moves between devices by JAX's collectives and lax.ppermute only.
A program may use at most 64 MiB of HBM per device.

v0:
```python
import jax
import jax.numpy as jnp
from jax import lax
from jax.sharding import PartitionSpec as P

HD = 18
SIDE = 14


norm_eps = 1e-05
beta_first = 0.5
beta_second = 0.5
adam_eps = 1e-08
rate_matrix = 0.06
rate_small = 0.2
decay_matrix = 0.05
adam_steps = 3
highest = lax.Precision.HIGHEST


def normalize(values, gain_row, bias_row):
    centred = values - jnp.mean(values, axis=-1, keepdims=True)
    inverse = lax.rsqrt(jnp.mean(centred * centred, axis=-1, keepdims=True) + norm_eps)
    scaled = centred * inverse
    return (scaled, inverse, scaled * gain_row + bias_row)


def normalize_back(grad_normed, scaled, inverse, gain_row):
    grad_scaled = grad_normed * gain_row
    centred_grad = grad_scaled - jnp.mean(grad_scaled, axis=-1, keepdims=True)
    return inverse * (
        centred_grad - scaled * jnp.mean(grad_scaled * scaled, axis=-1, keepdims=True)
    )


def pad_grid(values):
    images, length, channels = values.shape
    return jnp.pad(values.reshape(images, SIDE, SIDE, channels), ((0, 0), (1, 1), (1, 1), (0, 0)))


def shifted(padded, row_off, col_off):
    return padded[:, 1 + row_off : 1 + row_off + SIDE, 1 + col_off : 1 + col_off + SIDE, :]


def conv_grid(hidden, kernel):
    padded = pad_grid(hidden)
    summed = jnp.zeros_like(shifted(padded, 0, 0))
    for tap_index in range(9):
        summed = summed + kernel[tap_index] * shifted(padded, tap_index // 3 - 1, tap_index % 3 - 1)
    return summed.reshape(hidden.shape)


def conv_back(grad_act, hidden, kernel):
    padded_grad = pad_grid(grad_act)
    padded_hidden = pad_grid(hidden)
    grad_grid = shifted(padded_grad, 0, 0)
    grad_hidden = jnp.zeros_like(grad_grid)
    kernel_rows = []
    for tap_index in range(9):
        row_off = tap_index // 3 - 1
        col_off = tap_index % 3 - 1
        grad_hidden = grad_hidden + kernel[tap_index] * shifted(padded_grad, -row_off, -col_off)
        kernel_rows.append(
            jnp.sum(grad_grid * shifted(padded_hidden, row_off, col_off), axis=(0, 1, 2))
        )
    return (grad_hidden.reshape(hidden.shape), jnp.stack(kernel_rows))


def mix_scores(received, talk):
    pre_mixed = jnp.einsum(
        "mn,gnqk->gmqk", talk[0], received.astype(jnp.float32), precision=highest
    )
    softmaxed = jax.nn.softmax(pre_mixed, axis=-1)
    post_mixed = jnp.einsum("jm,gmqk->gjqk", talk[1], softmaxed, precision=highest).astype(
        jnp.bfloat16
    )
    return (softmaxed, post_mixed)


def mix_back(grad_post_all, softmaxed, received, talk):
    grad_soft = jnp.einsum("jm,gjqk->gmqk", talk[1], grad_post_all, precision=highest)
    talk_post = jnp.einsum("gjqk,gmqk->jm", grad_post_all, softmaxed, precision=highest)
    grad_mixed = softmaxed * (grad_soft - jnp.sum(grad_soft * softmaxed, axis=-1, keepdims=True))
    talk_pre = jnp.einsum(
        "gmqk,gnqk->mn", grad_mixed, received.astype(jnp.float32), precision=highest
    )
    grad_scores = jnp.einsum("mn,gmqk->gnqk", talk[0], grad_mixed, precision=highest).astype(
        jnp.bfloat16
    )
    return (grad_scores, talk_pre, talk_post)


def adamw(weights_old, gradient, moment_one, moment_two, step_rate, decay_rate):
    one_new = beta_first * moment_one + (1.0 - beta_first) * gradient
    two_new = beta_second * moment_two + (1.0 - beta_second) * gradient * gradient
    hat_one = one_new / (1.0 - beta_first**adam_steps)
    hat_two = two_new / (1.0 - beta_second**adam_steps)
    weights_new = weights_old - step_rate * (
        hat_one / (jnp.sqrt(hat_two) + adam_eps) + decay_rate * weights_old
    )
    return (weights_new, one_new, two_new)


def local(
    tokens,
    cotangent,
    image_count,
    subnet_heads,
    subnet_width,
    block_slot,
    master,
    master_m1,
    master_m2,
    norm_params,
    norm_m1,
    norm_m2,
    talk,
    talk_m1,
    talk_m2,
    conv,
    conv_m1,
    conv_m2,
):
    slot_count = master.shape[0]
    block_rows = master.shape[1]
    model_width = master.shape[2]
    capacity = tokens.shape[0]
    seq_len = tokens.shape[1]
    head_devices = lax.axis_size("head")
    head_place = lax.axis_index("head")
    per_head = block_rows // HD
    hidden_local = 4 * block_rows
    scale_factor = HD ** (-0.5)
    every_slot = lax.all_gather(master.astype(jnp.bfloat16), "dp", axis=0, tiled=True)
    blocks = jnp.take(every_slot, block_slot, axis=0)
    w_qkv = blocks[0:3].reshape(3 * block_rows, model_width)
    w_out = blocks[3]
    w_in = blocks[4:8].reshape(hidden_local, model_width)
    w_down = blocks[8:12].reshape(hidden_local, model_width)
    image_valid = (jnp.arange(capacity) < image_count[0]).astype(jnp.float32)
    head_keep = (head_place * per_head + jnp.arange(per_head) < subnet_heads[0]).astype(jnp.float32)
    unit_keep = (head_place * hidden_local + jnp.arange(hidden_local) < subnet_width[0]).astype(
        jnp.float32
    )
    token_values = tokens.astype(jnp.float32)
    scaled_one, inverse_one, normed_full = normalize(token_values, norm_params[0], norm_params[1])
    normed_one = normed_full.astype(jnp.bfloat16)
    projected = jnp.einsum(
        "gsd,fd->gsf", normed_one, w_qkv, preferred_element_type=jnp.float32
    ).astype(jnp.bfloat16)
    qkv_heads = projected.reshape(capacity, seq_len, 3, per_head, HD)
    queries = qkv_heads[:, :, 0]
    key_vecs = qkv_heads[:, :, 1]
    value_vecs = qkv_heads[:, :, 2]
    scores = (
        jnp.einsum("gqhe,gkhe->ghqk", queries, key_vecs, preferred_element_type=jnp.float32)
        * scale_factor
    ).astype(jnp.bfloat16)
    received = lax.all_to_all(scores, "head", split_axis=2, concat_axis=1, tiled=True)
    softmaxed, post_mixed = mix_scores(received, talk)
    post_local = lax.all_to_all(post_mixed, "head", split_axis=1, concat_axis=2, tiled=True)
    post_local, softmaxed, received = (post_local, softmaxed, received)
    attended = (
        jnp.einsum("ghqk,gkhe->gqhe", post_local, value_vecs, preferred_element_type=jnp.float32)
        * head_keep[None, None, :, None]
    )
    attended = attended.astype(jnp.bfloat16).reshape(capacity, seq_len, per_head * HD)
    saved = (
        scaled_one,
        inverse_one,
        normed_one,
        queries,
        key_vecs,
        value_vecs,
        received,
        softmaxed,
        post_local,
        attended,
    )
    attended = saved[9]
    attn_part = jnp.einsum("gsf,fd->gsd", attended, w_out, preferred_element_type=jnp.float32)
    middle = token_values + lax.psum(attn_part, "head")
    scaled_two, inverse_two, normed_full_two = normalize(middle, norm_params[2], norm_params[3])
    normed_two = normed_full_two.astype(jnp.bfloat16)
    hidden = jnp.einsum("gsd,ud->gsu", normed_two, w_in, preferred_element_type=jnp.float32)
    activated = conv_grid(hidden, conv)
    sigmoid_act = jax.nn.sigmoid(activated)
    gated = (activated * sigmoid_act * unit_keep).astype(jnp.bfloat16)
    down_part = jnp.einsum("gsu,ud->gsd", gated, w_down, preferred_element_type=jnp.float32)
    output = (
        middle + lax.psum(down_part.astype(jnp.bfloat16), "head").astype(jnp.float32)
    ) * image_valid[:, None, None]
    grad_output = cotangent * image_valid[:, None, None]
    grad_low = grad_output.astype(jnp.bfloat16)
    grad_down = jnp.einsum("gsu,gsd->ud", gated, grad_low, preferred_element_type=jnp.float32)
    grad_gated = (
        jnp.einsum("gsd,ud->gsu", grad_low, w_down, preferred_element_type=jnp.float32) * unit_keep
    )
    grad_act = grad_gated * sigmoid_act * (1.0 + activated * (1.0 - sigmoid_act))
    grad_hidden, grad_kernel = conv_back(grad_act, hidden, conv)
    grad_hidden_low = grad_hidden.astype(jnp.bfloat16)
    grad_in = jnp.einsum(
        "gsu,gsd->ud", grad_hidden_low, normed_two, preferred_element_type=jnp.float32
    )
    grad_two_part = jnp.einsum(
        "gsu,ud->gsd", grad_hidden_low, w_in, preferred_element_type=jnp.float32
    )
    grad_normed_two = lax.psum(grad_two_part, "head")
    grad_middle = grad_output + normalize_back(
        grad_normed_two, scaled_two, inverse_two, norm_params[2]
    )
    (
        scaled_one,
        inverse_one,
        normed_one,
        queries,
        key_vecs,
        value_vecs,
        received,
        softmaxed,
        post_local,
        attended,
    ) = saved
    grad_branch = grad_middle.astype(jnp.bfloat16)
    grad_out_proj = jnp.einsum(
        "gsf,gsd->fd", attended, grad_branch, preferred_element_type=jnp.float32
    )
    grad_attended = jnp.einsum(
        "gsd,fd->gsf", grad_branch, w_out, preferred_element_type=jnp.float32
    ).reshape(capacity, seq_len, per_head, HD)
    grad_att_low = (grad_attended * head_keep[None, None, :, None]).astype(jnp.bfloat16)
    grad_values = jnp.einsum(
        "ghqk,gqhe->gkhe", post_local, grad_att_low, preferred_element_type=jnp.float32
    ).astype(jnp.bfloat16)
    grad_post = jnp.einsum(
        "gqhe,gkhe->ghqk", grad_att_low, value_vecs, preferred_element_type=jnp.float32
    ).astype(jnp.bfloat16)
    grad_post_all = lax.all_to_all(
        grad_post, "head", split_axis=2, concat_axis=1, tiled=True
    ).astype(jnp.float32)
    grad_scores, talk_pre, talk_post = mix_back(grad_post_all, softmaxed, received, talk)
    grad_scores_local = lax.all_to_all(grad_scores, "head", split_axis=1, concat_axis=2, tiled=True)
    grad_queries = (
        jnp.einsum(
            "ghqk,gkhe->gqhe", grad_scores_local, key_vecs, preferred_element_type=jnp.float32
        )
        * scale_factor
    ).astype(jnp.bfloat16)
    grad_keys = (
        jnp.einsum(
            "ghqk,gqhe->gkhe", grad_scores_local, queries, preferred_element_type=jnp.float32
        )
        * scale_factor
    ).astype(jnp.bfloat16)
    grad_proj = jnp.stack([grad_queries, grad_keys, grad_values], axis=2).reshape(
        capacity, seq_len, 3 * block_rows
    )
    grad_qkv_w = jnp.einsum(
        "gsf,gsd->fd", grad_proj, normed_one, preferred_element_type=jnp.float32
    )
    grad_one_part = jnp.einsum("gsf,fd->gsd", grad_proj, w_qkv, preferred_element_type=jnp.float32)
    grad_normed_one = lax.psum(grad_one_part, "head")
    token_grad = grad_middle + normalize_back(
        grad_normed_one, scaled_one, inverse_one, norm_params[0]
    )
    share = (jnp.arange(capacity) % head_devices == head_place).astype(jnp.float32)[:, None, None]
    norm_part = jnp.stack(
        [
            jnp.sum(share * grad_normed_one * scaled_one, axis=(0, 1)),
            jnp.sum(share * grad_normed_one, axis=(0, 1)),
            jnp.sum(share * grad_normed_two * scaled_two, axis=(0, 1)),
            jnp.sum(share * grad_normed_two, axis=(0, 1)),
        ]
    )
    talk_part = jnp.stack([talk_pre, talk_post])
    conv_wide = lax.dynamic_update_slice(
        jnp.zeros((9, hidden_local * head_devices), jnp.float32),
        grad_kernel,
        (0, head_place * hidden_local),
    )
    norm_grad, talk_grad, conv_grad_wide = lax.psum(
        (norm_part, talk_part, conv_wide), ("dp", "head")
    )
    conv_grad = lax.dynamic_slice(conv_grad_wide, (0, head_place * hidden_local), (9, hidden_local))
    block_grads = jnp.concatenate(
        [
            grad_qkv_w.reshape(3, block_rows, model_width),
            grad_out_proj[None],
            grad_in.reshape(4, block_rows, model_width),
            grad_down.reshape(4, block_rows, model_width),
        ],
        axis=0,
    )
    all_slots = slot_count * lax.axis_size("dp")
    spread_grads = (
        jnp.zeros((all_slots, block_rows, model_width), jnp.float32).at[block_slot].set(block_grads)
    )
    slot_grads = lax.psum_scatter(spread_grads, "dp", scatter_dimension=0, tiled=True)
    new_master, new_master_m1, new_master_m2 = adamw(
        master, slot_grads, master_m1, master_m2, rate_matrix, decay_matrix
    )
    new_norm, new_norm_m1, new_norm_m2 = adamw(
        norm_params, norm_grad, norm_m1, norm_m2, rate_small, 0.0
    )
    new_talk, new_talk_m1, new_talk_m2 = adamw(talk, talk_grad, talk_m1, talk_m2, rate_small, 0.0)
    new_conv, new_conv_m1, new_conv_m2 = adamw(
        conv, conv_grad, conv_m1, conv_m2, rate_small, decay_matrix
    )
    return (
        output,
        token_grad,
        new_master,
        new_master_m1,
        new_master_m2,
        new_master.astype(jnp.bfloat16),
        new_norm,
        new_norm_m1,
        new_norm_m2,
        new_talk,
        new_talk_m1,
        new_talk_m2,
        new_conv,
        new_conv_m1,
        new_conv_m2,
    )


def solution(mesh):
    in_specs = (
        P("dp", None, None),
        P("dp", None, None),
        P("dp"),
        P(),
        P(),
        P(),
        P("dp", None, "head"),
        P("dp", None, "head"),
        P("dp", None, "head"),
        P(),
        P(),
        P(),
        P(),
        P(),
        P(),
        P(None, "head"),
        P(None, "head"),
        P(None, "head"),
    )
    out_specs = (
        P("dp", None, None),
        P("dp", None, None),
        P("dp", None, "head"),
        P("dp", None, "head"),
        P("dp", None, "head"),
        P("dp", None, "head"),
        P(),
        P(),
        P(),
        P(),
        P(),
        P(),
        P(None, "head"),
        P(None, "head"),
        P(None, "head"),
    )
    return jax.shard_map(local, mesh=mesh, in_specs=in_specs, out_specs=out_specs, check_vma=False)
```

profile of v0, /device:TPU:0, one launch (start us, length us, event | category | flops | bytes accessed | tf_op | source)
XLA Modules:
  0.0 392.8 jit_solution(17498265783803520196)
XLA Ops:
  8.6 1.2 convert_reduce_fusion
  9.8 1.4 fusion.69
  11.2 1.4 fusion.115
  13.6 32.9 %all_gather.3 = bf16[16,54,216]{2,1,0:T(8,128)(2,1)S(1)} all-gather(bf16[2,54,216]{2,1,0:T(8,128)(2,1)S(1)} %copy.210), channel_id=1, replica_groups=mesh['dp'=8,'head'=4] {'dp'}, dimensions={0}, use_global_device_ids=true | all-gather | bytes 419904 | tf_op jit(solution)/shard_map/all_gather | solution.py:134
  49.2 1.5 copy.215
  50.7 3.5 all-to-all-start
  54.3 16.1 %all-to-all-done = bf16[4,3,196,196]{3,0,1,2:T(4,128)(2,1)S(1)} async-done(((bf16[4,3,196,196]{3,0,1,2:T(4,128)(2,1)}), bf16[4,3,196,196]{3,0,1,2:T(4,128)(2,1)S(1)}, u32[]{:S(2)}, u32[]{:S(2)}) %all-to-all-start) | async-done | bytes 922016 | tf_op jit(solution)/shard_map/all_to_all | solution.py:159
  70.7 2.0 bitcast_reduce_fusion
  72.7 1.2 fusion.4
  73.9 3.7 fusion.13
  77.7 1.6 copy.221
  79.3 3.5 all-to-all-start.1
  85.4 13.5 %all-to-all-done.1 = bf16[4,12,49,196]{3,0,2,1:T(4,128)(2,1)S(1)} async-done(((bf16[4,12,49,196]{3,0,2,1:T(4,128)(2,1)}), bf16[4,12,49,196]{3,0,2,1:T(4,128)(2,1)S(1)}, u32[]{:S(2)}, u32[]{:S(2)}) %all-to-all-start.1) | async-done | bytes 922016 | tf_op jit(solution)/shard_map/all_to_all | solution.py:161
  100.9 1.2 fusion.91
  104.0 33.3 %all-reduce.8.cloned.1.call-done = f32[4,196,216]{2,1,0:T(8,128)} async-done(((f32[4,196,216]{2,1,0:T(8,128)}), f32[4,196,216]{2,1,0:T(8,128)}) %all-reduce.8.cloned.1.call-update) | async-done | bytes 677392 | tf_op jit(solution)/shard_map/psum | solution.py:182
  137.3 1.4 fusion.111
  142.9 1.7 multiply_reduce_fusion
  145.7 1.2 fusion.77
  146.9 2.1 fusion.80
  150.2 1.3 copy.257
  153.6 2.0 convolution_convert_fusion.3
  156.8 25.2 %all-reduce.12.cloned.1.call-done = f32[4,196,216]{2,1,0:T(8,128)} async-done(((f32[4,196,216]{2,1,0:T(8,128)}), f32[4,196,216]{2,1,0:T(8,128)}) %all-reduce.12.cloned.1.call-update) | async-done | bytes 677392 | tf_op jit(solution)/shard_map/psum | solution.py:208
  182.0 2.4 multiply_reduce_fusion.9
  184.4 32.6 %all-reduce.10.cloned.1.call-done = bf16[4,196,216]{2,1,0:T(8,128)(2,1)} async-done(((bf16[4,196,216]{2,1,0:T(8,128)(2,1)}), bf16[4,196,216]{2,1,0:T(8,128)(2,1)}) %all-reduce.10.cloned.1.call-update) | async-done | bytes 338704 | tf_op jit(solution)/shard_map/psum | solution.py:191
  217.0 2.8 multiply_add_fusion.1
  220.1 1.5 convolution_convert_fusion.2
  221.6 1.5 copy.239
  223.1 4.5 %all-to-all-start.2 = ((bf16[4,3,196,196]{3,0,1,2:T(4,128)(2,1)}), bf16[4,3,196,196]{3,0,1,2:T(4,128)(2,1)}, u32[]{:S(2)}, u32[]{:S(2)}) async-start(bf16[4,3,196,196]{3,0,1,2:T(4,128)(2,1)} %copy.239), calls=%async_computation.2 | async-start | bytes 2408448 | tf_op jit(solution)/shard_map/all_to_all | solution.py:238
  227.6 2.2 convolution_bitcast_fusion.1
  229.8 2.4 convolution_bitcast_fusion
  232.2 2.4 copy.276
  235.7 7.8 %all-to-all-done.2 = bf16[4,3,196,196]{3,0,1,2:T(4,128)(2,1)} async-done(((bf16[4,3,196,196]{3,0,1,2:T(4,128)(2,1)}), bf16[4,3,196,196]{3,0,1,2:T(4,128)(2,1)}, u32[]{:S(2)}, u32[]{:S(2)}) %all-to-all-start.2) | async-done | bytes 922016 | tf_op jit(solution)/shard_map/all_to_all | solution.py:238
  243.6 1.7 copy.241
  245.3 4.7 %fusion = (f32[4,12,49]{1,2,0:T(8,128)S(1)}, f32[4,49,196,12]{2,3,1,0:T(8,128)S(1)}) fusion(f32[4,12,49]{1,2,0:T(8,128)S(1)} %copy-done.30, f32[4,12,49]{1,2,0:T(8,128)S(1)} %copy-done.20, f32[4,49,196,12]{2,3,1,0:T(8,128)} %copy-done, f32[2,12,12]{2,1,0:T(8,128)S(1)} %copy-done.40, bf16[4,12,49,196]{3,0,2,1:T(4,128)(2,1)S(1)} %bitcast.228), kind=kOutput, calls=%fused_computation.4 | convolution fusion | flops 68224464 | bytes 5139136 | tf_op jit(solution)/shard_map/jm,gjqk->gmqk/dot_general | solution.py:81
  250.1 4.7 %fusion.14 = bf16[4,12,49,196]{3,1,2,0:T(8,128)(2,1)S(1)} fusion(f32[4,49,196,12]{2,3,1,0:T(8,128)S(1)} %get-tuple-element.136, f32[4,12,49]{1,2,0:T(8,128)S(1)} %get-tuple-element.135, f32[2,12,12]{2,1,0:T(8,128)S(1)} %copy-done.40, f32[4,49,196,12]{2,3,1,0:T(8,128)S(1)} %copy-done.1, f32[4,12,49]{1,2,0:T(8,128)S(1)} %copy-done.30, ...), kind=kOutput, calls=%fused_computation.24 | convolution fusion | flops 68687808 | bytes 7696768 | tf_op jit(solution)/shard_map/mn,gmqk->gnqk/dot_general | solution.py:87
  254.8 1.6 copy.245
  256.4 4.3 %all-to-all-start.3 = ((bf16[4,12,49,196]{3,0,2,1:T(4,128)(2,1)}), bf16[4,12,49,196]{3,0,2,1:T(4,128)(2,1)}, u32[]{:S(2)}, u32[]{:S(2)}) async-start(bf16[4,12,49,196]{3,0,2,1:T(4,128)(2,1)} %copy.245), calls=%async_computation.3 | async-start | bytes 2408448 | tf_op jit(solution)/shard_map/all_to_all | solution.py:242
  260.7 5.6 %fusion.27 = f32[1,12,12]{2,1,0:T(8,128)S(1)} fusion(bf16[4,12,49,196]{3,0,2,1:T(4,128)(2,1)S(1)} %bitcast.211, f32[4,49,196,12]{2,3,1,0:T(8,128)} %copy-done.68, f32[4,12,49]{1,2,0:T(8,128)S(1)} %get-tuple-element.135, f32[4,49,196,12]{2,3,1,0:T(8,128)} %copy-done, f32[4,12,49]{1,2,0:T(8,128)S(1)} %copy-done.30, f32[4,12,49]{1,2,0:T(8,128)S(1)} %copy-done.20), kind=kOutput, calls=%fused_computation.50 | convolution fusion | flops 68226816 | bytes 4638720 | tf_op jit(solution)/shard_map/gmqk,gnqk->mn/dot_general | solution.py:84
  266.4 2.8 fusion.32
  269.2 7.7 %all-to-all-done.3 = bf16[4,12,49,196]{3,0,2,1:T(4,128)(2,1)} async-done(((bf16[4,12,49,196]{3,0,2,1:T(4,128)(2,1)}), bf16[4,12,49,196]{3,0,2,1:T(4,128)(2,1)}, u32[]{:S(2)}, u32[]{:S(2)}) %all-to-all-start.3) | async-done | bytes 922016 | tf_op jit(solution)/shard_map/all_to_all | solution.py:242
  276.9 1.7 copy.246
  279.7 1.2 fusion.82
  284.2 31.7 %all-reduce.14.cloned.1.call-done = f32[4,196,216]{2,1,0:T(8,128)} async-done(((f32[4,196,216]{2,1,0:T(8,128)}), f32[4,196,216]{2,1,0:T(8,128)}) %all-reduce.14.cloned.1.call-update) | async-done | bytes 677392 | tf_op jit(solution)/shard_map/psum | solution.py:262
  315.9 1.8 fusion.68
  317.8 1.6 fusion.67
  319.4 1.2 copy.277
  320.7 41.0 %all-reduce.2 = (f32[4,216]{1,0:T(4,128)S(1)}, f32[2,12,12]{2,1,0:T(8,128)S(1)}, f32[9,864]{1,0:T(8,128)S(1)}) all-reduce(f32[4,216]{1,0:T(4,128)S(1)} %pad_maximum_fusion.3, f32[2,12,12]{2,1,0:T(8,128)S(1)} %pad_maximum_fusion.2, f32[9,864]{1,0:T(8,128)S(1)} %copy-done.27), channel_id=1, replica_groups=mesh['dp'=8,'head'=4] {'dp','head'}, use_global_device_ids=true, to_apply=%region_21.22 | all-reduce | flops 8928 | bytes 71424 | tf_op jit(solution)/shard_map/psum | solution.py:281
  364.9 17.6 %reduce-scatter.2.cloned.1.call-done = f32[2,54,216]{2,1,0:T(8,128)} async-done(((f32[16,54,216]{2,1,0:T(8,128)}), f32[2,54,216]{2,1,0:T(8,128)}) %reduce-scatter.2.cloned.1.call-update) | async-done | bytes 93328 | tf_op jit(solution)/shard_map/reduce_scatter | solution.py:298
  (225 shorter events, 31.8 us)
Async XLA Ops:
  7.2 40.6 %copy-start.3 = (bf16[4,196,216]{2,0,1:T(4,128)(2,1)S(1)}, bf16[4,196,216]{2,0,1:T(4,128)(2,1)}, u32[]{:S(2)}) copy-start(bf16[4,196,216]{2,0,1:T(4,128)(2,1)} %param.18) | copy-start | bytes 1016068
  11.2 37.2 %copy-start.37 = (f32[4,196]{1,0:T(4,128)}, f32[4,196]{1,0:T(4,128)S(1)}, u32[]{:S(2)}) copy-start(f32[4,196]{1,0:T(4,128)S(1)} %add_rsqrt_fusion.1) | copy-start | bytes 9412
  12.6 35.8 %copy-start.49 = (f32[1,216]{1,0:T(1,128)}, f32[1,216]{1,0:T(1,128)S(1)}, u32[]{:S(2)}) copy-start(f32[1,216]{1,0:T(1,128)S(1)} %get-tuple-element.131) | copy-start | bytes 2596
  12.6 35.8 %copy-start.64 = (f32[1,216]{1,0:T(1,128)}, f32[1,216]{1,0:T(1,128)S(1)}, u32[]{:S(2)}) copy-start(f32[1,216]{1,0:T(1,128)S(1)} %get-tuple-element.130) | copy-start | bytes 2596
  48.6 22.2 %copy-start.15 = (bf16[4,196,1,3,18]{1,0,4,3,2:T(4,128)(2,1)}, bf16[4,196,1,3,18]{1,0,4,3,2:T(4,128)(2,1)S(1)}, u32[]{:S(2)}) copy-start(bf16[4,196,1,3,18]{1,0,4,3,2:T(4,128)(2,1)S(1)} %get-tuple-element.118) | copy-start | bytes 254020
  48.6 50.8 %copy-start.17 = (bf16[4,196,1,3,18]{1,0,4,3,2:T(4,128)(2,1)}, bf16[4,196,1,3,18]{1,0,4,3,2:T(4,128)(2,1)S(1)}, u32[]{:S(2)}) copy-start(bf16[4,196,1,3,18]{1,0,4,3,2:T(4,128)(2,1)S(1)} %get-tuple-element.117) | copy-start | bytes 254020
  50.7 19.6 %all-to-all-start = ((bf16[4,3,196,196]{3,0,1,2:T(4,128)(2,1)}), bf16[4,3,196,196]{3,0,1,2:T(4,128)(2,1)S(1)}, u32[]{:S(2)}, u32[]{:S(2)}) async-start(bf16[4,3,196,196]{3,0,1,2:T(4,128)(2,1)} %copy.215), calls=%async_computation | async-start | bytes 2408448 | tf_op jit(solution)/shard_map/all_to_all | solution.py:159
  54.2 19.7 %copy-start.39 = (f32[2,12,12]{2,1,0:T(8,128)}, f32[2,12,12]{2,1,0:T(8,128)S(1)}, u32[]{:S(2)}) copy-start(f32[2,12,12]{2,1,0:T(8,128)S(1)} %copy.218) | copy-start | bytes 3460
  79.3 19.6 %all-to-all-start.1 = ((bf16[4,12,49,196]{3,0,2,1:T(4,128)(2,1)}), bf16[4,12,49,196]{3,0,2,1:T(4,128)(2,1)S(1)}, u32[]{:S(2)}, u32[]{:S(2)}) async-start(bf16[4,12,49,196]{3,0,2,1:T(4,128)(2,1)} %copy.221), calls=%async_computation.1 | async-start | bytes 2408448 | tf_op jit(solution)/shard_map/all_to_all | solution.py:161
  82.9 54.4 %all-reduce.8.cloned.1.call-start = ((), (), s32[]{:S(2)}) async-start(), calls=%async_computation.5 | async-start | bytes 1638400 | tf_op jit(solution)/shard_map/psum | solution.py:182
  84.8 17.4 %copy-start.66 = (f32[3]{0:T(128)}, f32[3]{0:T(128)S(1)}, u32[]{:S(2)}) copy-start(f32[3]{0:T(128)S(1)} %compare_convert_fusion.3) | copy-start | bytes 40
  100.9 38.2 %copy-start.44 = (f32[1,216]{1,0:T(1,128)S(1)}, f32[1,216]{1,0:T(1,128)}, u32[]{:S(2)}) copy-start(f32[1,216]{1,0:T(1,128)} %get-tuple-element.129) | copy-start | bytes 2596
  100.9 38.2 %copy-start.54 = (f32[1,216]{1,0:T(1,128)S(1)}, f32[1,216]{1,0:T(1,128)}, u32[]{:S(2)}) copy-start(f32[1,216]{1,0:T(1,128)} %get-tuple-element.132) | copy-start | bytes 2596
  102.2 79.8 %all-reduce.12.cloned.1.call-start = ((), (), s32[]{:S(2)}) async-start(), calls=%async_computation.7 | async-start | bytes 1638400 | tf_op jit(solution)/shard_map/psum | solution.py:208
  102.4 39.5 %copy-start.62 = (f32[4]{0:T(128)}, f32[4]{0:T(128)S(1)}, u32[]{:S(2)}) copy-start(f32[4]{0:T(128)S(1)} %compare_convert_fusion.1) | copy-start | bytes 52
  103.9 38.0 %copy-start.21 = (bf16[216,216,1]{1,0,2:T(8,128)(2,1)}, bf16[216,216,1]{1,0,2:T(8,128)(2,1)S(1)}, u32[]{:S(2)}) copy-start(bf16[216,216,1]{1,0,2:T(8,128)(2,1)S(1)} %reshape.190) | copy-start | bytes 279940
  104.0 38.0 %copy-start.48 = (f32[216]{0:T(256)}, f32[216]{0:T(256)S(1)}, u32[]{:S(2)}) copy-start(f32[216]{0:T(256)S(1)} %compare_convert_fusion.2) | copy-start | bytes 2596
  146.9 70.1 %all-reduce.10.cloned.1.call-start = ((), (), s32[]{:S(2)}) async-start(), calls=%async_computation.6 | async-start | bytes 819200 | tf_op jit(solution)/shard_map/psum | solution.py:191
  150.2 66.8 %copy-start.45 = (f32[1,216]{1,0:T(1,128)S(1)}, f32[1,216]{1,0:T(1,128)}, u32[]{:S(2)}) copy-start(f32[1,216]{1,0:T(1,128)} %get-tuple-element.129) | copy-start | bytes 2596
  155.6 64.2 %copy-start.67 = (f32[3]{0:T(128)S(1)}, f32[3]{0:T(128)}, u32[]{:S(2)}) copy-start(f32[3]{0:T(128)} %copy-done.66) | copy-start | bytes 40
  156.8 60.2 %copy-start.26 = (f32[9,864]{1,0:T(8,128)}, f32[9,864]{1,0:T(8,128)S(1)}, u32[]{:S(2)}) copy-start(f32[9,864]{1,0:T(8,128)S(1)} %dynamic_update_slice.3) | copy-start | bytes 93316
  220.1 7.5 %copy-start.8 = (bf16[4,196,216]{2,1,0:T(8,128)(2,1)S(1)}, bf16[4,196,216]{2,1,0:T(8,128)(2,1)}, u32[]{:S(2)}) copy-start(bf16[4,196,216]{2,1,0:T(8,128)(2,1)} %copy-done.7) | copy-start | bytes 1016068
  221.6 8.2 %copy-start.63 = (f32[4]{0:T(128)S(1)}, f32[4]{0:T(128)}, u32[]{:S(2)}) copy-start(f32[4]{0:T(128)} %copy-done.62) | copy-start | bytes 52
  223.1 20.5 %all-to-all-start.2 = ((bf16[4,3,196,196]{3,0,1,2:T(4,128)(2,1)}), bf16[4,3,196,196]{3,0,1,2:T(4,128)(2,1)}, u32[]{:S(2)}, u32[]{:S(2)}) async-start(bf16[4,3,196,196]{3,0,1,2:T(4,128)(2,1)} %copy.239), calls=%async_computation.2 | async-start | bytes 2408448 | tf_op jit(solution)/shard_map/all_to_all | solution.py:238
  227.6 6.9 %copy-start.6 = (bf16[4,3,4,49,196]{4,0,3,2,1:T(4,128)(2,1)S(1)}, bf16[4,3,4,49,196]{4,0,3,2,1:T(4,128)(2,1)}, u32[]{:S(2)}) copy-start(bf16[4,3,4,49,196]{4,0,3,2,1:T(4,128)(2,1)} %copy-done.5) | copy-start | bytes 2765956
  232.1 13.1 %copy-start.20 = (f32[4,12,49]{1,2,0:T(8,128)S(1)}, f32[4,12,49]{1,2,0:T(8,128)}, u32[]{:S(2)}) copy-start(f32[4,12,49]{1,2,0:T(8,128)} %copy-done.19) | copy-start | bytes 28228
  232.1 13.1 %copy-start.30 = (f32[4,12,49]{1,2,0:T(8,128)S(1)}, f32[4,12,49]{1,2,0:T(8,128)}, u32[]{:S(2)}) copy-start(f32[4,12,49]{1,2,0:T(8,128)} %copy-done.29) | copy-start | bytes 28228
  232.2 13.1 %copy-start.40 = (f32[2,12,12]{2,1,0:T(8,128)S(1)}, f32[2,12,12]{2,1,0:T(8,128)}, u32[]{:S(2)}) copy-start(f32[2,12,12]{2,1,0:T(8,128)} %copy-done.39) | copy-start | bytes 3460
  256.4 20.5 %all-to-all-start.3 = ((bf16[4,12,49,196]{3,0,2,1:T(4,128)(2,1)}), bf16[4,12,49,196]{3,0,2,1:T(4,128)(2,1)}, u32[]{:S(2)}, u32[]{:S(2)}) async-start(bf16[4,12,49,196]{3,0,2,1:T(4,128)(2,1)} %copy.245), calls=%async_computation.3 | async-start | bytes 2408448 | tf_op jit(solution)/shard_map/all_to_all | solution.py:242
  260.7 55.2 %all-reduce.14.cloned.1.call-start = ((), (), s32[]{:S(2)}) async-start(), calls=%async_computation.8 | async-start | bytes 1638400 | tf_op jit(solution)/shard_map/psum | solution.py:262
  266.4 12.2 %copy-start.16 = (bf16[4,196,1,3,18]{1,0,4,3,2:T(4,128)(2,1)S(1)}, bf16[4,196,1,3,18]{1,0,4,3,2:T(4,128)(2,1)}, u32[]{:S(2)}) copy-start(bf16[4,196,1,3,18]{1,0,4,3,2:T(4,128)(2,1)} %copy-done.15) | copy-start | bytes 254020
  281.0 101.6 %reduce-scatter.2.cloned.1.call-start = ((), (), s32[]{:S(2)}) async-start(), calls=%async_computation.9 | async-start | bytes 1032192 | tf_op jit(solution)/shard_map/reduce_scatter | solution.py:298
  281.3 34.6 %copy-start.59 = (f32[4]{0:T(128)S(1)}, f32[4]{0:T(128)}, u32[]{:S(2)}) copy-start(f32[4]{0:T(128)} %compare_convert_fusion) | copy-start | bytes 52
  283.2 37.5 %copy-start.57 = (f32[216]{0:T(256)S(1)}, f32[216]{0:T(256)}, u32[]{:S(2)}) copy-start(f32[216]{0:T(256)} %get-tuple-element.84) | copy-start | bytes 2596
  283.2 37.5 %copy-start.58 = (f32[216]{0:T(256)S(1)}, f32[216]{0:T(256)}, u32[]{:S(2)}) copy-start(f32[216]{0:T(256)} %get-tuple-element.91) | copy-start | bytes 2596
  283.2 37.5 %copy-start.27 = (f32[9,864]{1,0:T(8,128)S(1)}, f32[9,864]{1,0:T(8,128)}, u32[]{:S(2)}) copy-start(f32[9,864]{1,0:T(8,128)} %copy-done.26) | copy-start | bytes 93316
  283.2 78.5 %copy-start.34 = (f32[2,12,12]{2,0,1:T(2,128)S(1)}, f32[2,12,12]{2,0,1:T(2,128)}, u32[]{:S(2)}) copy-start(f32[2,12,12]{2,0,1:T(2,128)} %param.30) | copy-start | bytes 3460
  283.2 78.5 %copy-start.46 = (f32[2,12,12]{2,0,1:T(2,128)S(1)}, f32[2,12,12]{2,0,1:T(2,128)}, u32[]{:S(2)}) copy-start(f32[2,12,12]{2,0,1:T(2,128)} %param.31) | copy-start | bytes 3460
  283.2 78.5 %copy-start.47 = (f32[2,12,12]{2,0,1:T(2,128)S(1)}, f32[2,12,12]{2,0,1:T(2,128)}, u32[]{:S(2)}) copy-start(f32[2,12,12]{2,0,1:T(2,128)} %param.32) | copy-start | bytes 3460
  284.1 79.4 %copy-start.43 = (f32[4,216]{1,0:T(4,128)S(1)}, f32[4,216]{1,0:T(4,128)}, u32[]{:S(2)}) copy-start(f32[4,216]{1,0:T(4,128)} %param.27) | copy-start | bytes 10372
  284.1 79.4 %copy-start.55 = (f32[4,216]{1,0:T(4,128)S(1)}, f32[4,216]{1,0:T(4,128)}, u32[]{:S(2)}) copy-start(f32[4,216]{1,0:T(4,128)} %param.28) | copy-start | bytes 10372
  284.1 79.4 %copy-start.56 = (f32[4,216]{1,0:T(4,128)S(1)}, f32[4,216]{1,0:T(4,128)}, u32[]{:S(2)}) copy-start(f32[4,216]{1,0:T(4,128)} %param.29) | copy-start | bytes 10372
  284.1 80.0 %copy-start.36 = (f32[9,216]{1,0:T(8,128)S(1)}, f32[9,216]{1,0:T(8,128)}, u32[]{:S(2)}) copy-start(f32[9,216]{1,0:T(8,128)} %param.33) | copy-start | bytes 23332
  284.1 80.0 %copy-start.41 = (f32[9,216]{1,0:T(8,128)S(1)}, f32[9,216]{1,0:T(8,128)}, u32[]{:S(2)}) copy-start(f32[9,216]{1,0:T(8,128)} %param.34) | copy-start | bytes 23332
  284.2 80.0 %copy-start.42 = (f32[9,216]{1,0:T(8,128)S(1)}, f32[9,216]{1,0:T(8,128)}, u32[]{:S(2)}) copy-start(f32[9,216]{1,0:T(8,128)} %param.35) | copy-start | bytes 23332
  284.2 98.4 %copy-start.22 = (f32[2,54,216]{2,0,1:T(2,128)S(1)}, f32[2,54,216]{2,0,1:T(2,128)}, u32[]{:S(2)}) copy-start(f32[2,54,216]{2,0,1:T(2,128)} %param.24) | copy-start | bytes 279940
  284.2 98.4 %copy-start.31 = (f32[2,54,216]{2,0,1:T(2,128)S(1)}, f32[2,54,216]{2,0,1:T(2,128)}, u32[]{:S(2)}) copy-start(f32[2,54,216]{2,0,1:T(2,128)} %param.25) | copy-start | bytes 279940
  284.2 98.3 %copy-start.32 = (f32[2,54,216]{2,0,1:T(2,128)S(1)}, f32[2,54,216]{2,0,1:T(2,128)}, u32[]{:S(2)}) copy-start(f32[2,54,216]{2,0,1:T(2,128)} %param.26) | copy-start | bytes 279940
  (30 other events, 101.9 us)
Sparse Core Ops, SparseCore 0:
  102.3 34.9 all-reduce.7
  147.0 34.9 all-reduce.11
  184.4 32.5 all-reduce.9
  281.1 34.8 all-reduce.13
  319.5 63.0 reduce-scatter.1
where the time goes:
time: 394 us; the launch traced here: 393 us
  waiting for transfers between devices  186 us (47%)
  blocking collectives  73.8 us (19%)
  matrix products  40.3 us (10%)
  local copies, waits for them, and re-layouts  34.1 us (9%)
  other arithmetic  25.5 us (6%)
  between operations  17 us (4%)
  starting transfers between devices  16.5 us (4%)
    psum x1, blocking collectives, local(): lax.psum((norm_part, talk_part, conv_wide), ('dp', 'head'))  41 us
    psum x1, waiting for transfers between devices, local(): middle = token_values + lax.psum(attn_part, 'head')  33.3 us
    all_gather x1, blocking collectives, local(): lax.all_gather(master.astype(jnp.bfloat16), 'dp', axis=0, tiled=True)  32.9 us
    psum x1, waiting for transfers between devices, local(): lax.psum(down_part.astype(jnp.bfloat16), 'head').astype(jnp.float32)  32.6 us
    psum x1, waiting for transfers between devices, local(): grad_normed_one = lax.psum(grad_one_part, 'head')  31.7 us
    psum x1, waiting for transfers between devices, local(): grad_normed_two = lax.psum(grad_two_part, 'head')  25.2 us
    reduce_scatter x1, waiting for transfers between devices, local(): lax.psum_scatter(spread_grads, 'dp', scatter_dimension=0, tiled=True)  17.6 us
    all_to_all x1, waiting for transfers between devices, local(): lax.all_to_all(scores, 'head', split_axis=2, concat_axis=1, tiled=True)  16.1 us
  transfers between devices with their start and end apart: 9, of which 9 were waited for; matrix products, arithmetic and copies ran while one was open for 10% of the time, Pallas kernels for 0%

commit v1 on v0

v1 whole, which is shorter than its diff:
```python
import jax
import jax.numpy as jnp
from jax import lax
from jax.sharding import PartitionSpec as P

HD = 18
SIDE = 14


norm_eps = 1e-05
beta_first = 0.5
beta_second = 0.5
adam_eps = 1e-08
rate_matrix = 0.06
rate_small = 0.2
decay_matrix = 0.05
adam_steps = 3
highest = lax.Precision.HIGHEST


def normalize(values, gain_row, bias_row):
    centred = values - jnp.mean(values, axis=-1, keepdims=True)
    inverse = lax.rsqrt(jnp.mean(centred * centred, axis=-1, keepdims=True) + norm_eps)
    scaled = centred * inverse
    return (scaled, inverse, scaled * gain_row + bias_row)


def normalize_back(grad_normed, scaled, inverse, gain_row):
    grad_scaled = grad_normed * gain_row
    centred_grad = grad_scaled - jnp.mean(grad_scaled, axis=-1, keepdims=True)
    return inverse * (
        centred_grad - scaled * jnp.mean(grad_scaled * scaled, axis=-1, keepdims=True)
    )


def pad_grid(values):
    images, length, channels = values.shape
    return jnp.pad(values.reshape(images, SIDE, SIDE, channels), ((0, 0), (1, 1), (1, 1), (0, 0)))


def shifted(padded, row_off, col_off):
    return padded[:, 1 + row_off : 1 + row_off + SIDE, 1 + col_off : 1 + col_off + SIDE, :]


def conv_grid(hidden, kernel):
    padded = pad_grid(hidden)
    summed = jnp.zeros_like(shifted(padded, 0, 0))
    for tap_index in range(9):
        summed = summed + kernel[tap_index] * shifted(padded, tap_index // 3 - 1, tap_index % 3 - 1)
    return summed.reshape(hidden.shape)


def conv_back(grad_act, hidden, kernel):
    padded_grad = pad_grid(grad_act)
    padded_hidden = pad_grid(hidden)
    grad_grid = shifted(padded_grad, 0, 0)
    grad_hidden = jnp.zeros_like(grad_grid)
    kernel_rows = []
    for tap_index in range(9):
        row_off = tap_index // 3 - 1
        col_off = tap_index % 3 - 1
        grad_hidden = grad_hidden + kernel[tap_index] * shifted(padded_grad, -row_off, -col_off)
        kernel_rows.append(
            jnp.sum(grad_grid * shifted(padded_hidden, row_off, col_off), axis=(0, 1, 2))
        )
    return (grad_hidden.reshape(hidden.shape), jnp.stack(kernel_rows))


def mix_scores(received, talk):
    pre_mixed = jnp.einsum(
        "mn,gnqk->gmqk", talk[0], received.astype(jnp.float32), precision=highest
    )
    softmaxed = jax.nn.softmax(pre_mixed, axis=-1)
    post_mixed = jnp.einsum("jm,gmqk->gjqk", talk[1], softmaxed, precision=highest).astype(
        jnp.bfloat16
    )
    return (softmaxed, post_mixed)


def mix_back(grad_post_all, softmaxed, received, talk):
    grad_soft = jnp.einsum("jm,gjqk->gmqk", talk[1], grad_post_all, precision=highest)
    talk_post = jnp.einsum("gjqk,gmqk->jm", grad_post_all, softmaxed, precision=highest)
    grad_mixed = softmaxed * (grad_soft - jnp.sum(grad_soft * softmaxed, axis=-1, keepdims=True))
    talk_pre = jnp.einsum(
        "gmqk,gnqk->mn", grad_mixed, received.astype(jnp.float32), precision=highest
    )
    grad_scores = jnp.einsum("mn,gmqk->gnqk", talk[0], grad_mixed, precision=highest).astype(
        jnp.bfloat16
    )
    return (grad_scores, talk_pre, talk_post)


def adamw(weights_old, gradient, moment_one, moment_two, step_rate, decay_rate):
    one_new = beta_first * moment_one + (1.0 - beta_first) * gradient
    two_new = beta_second * moment_two + (1.0 - beta_second) * gradient * gradient
    hat_one = one_new / (1.0 - beta_first**adam_steps)
    hat_two = two_new / (1.0 - beta_second**adam_steps)
    weights_new = weights_old - step_rate * (
        hat_one / (jnp.sqrt(hat_two) + adam_eps) + decay_rate * weights_old
    )
    return (weights_new, one_new, two_new)


def gather_blocks(master, block_slot):
    mine = master.astype(jnp.bfloat16)
    data_devices = lax.axis_size("dp")
    every = lax.all_to_all(
        jnp.broadcast_to(mine[None], (data_devices,) + mine.shape), "dp", split_axis=0, concat_axis=0, tiled=True
    )
    every = every.reshape((data_devices * mine.shape[0],) + mine.shape[1:])
    return jnp.take(every, block_slot, axis=0)


def split_pair(values):
    high = lax.reduce_precision(values, exponent_bits=8, mantissa_bits=7)
    low = values - high
    return jnp.concatenate([high.astype(jnp.bfloat16), low.astype(jnp.bfloat16)], axis=-2)


def join_pair(values):
    rows = values.shape[-2] // 2
    return values[..., :rows, :].astype(jnp.float32) + values[..., rows:, :].astype(jnp.float32)


def local(
    tokens,
    cotangent,
    image_count,
    subnet_heads,
    subnet_width,
    block_slot,
    master,
    master_m1,
    master_m2,
    norm_params,
    norm_m1,
    norm_m2,
    talk,
    talk_m1,
    talk_m2,
    conv,
    conv_m1,
    conv_m2,
):
    slot_count = master.shape[0]
    block_rows = master.shape[1]
    model_width = master.shape[2]
    capacity = tokens.shape[0]
    seq_len = tokens.shape[1]
    head_devices = lax.axis_size("head")
    data_devices = lax.axis_size("dp")
    head_place = lax.axis_index("head")
    images = capacity // head_devices
    heads = head_devices * (block_rows // HD)
    hidden_all = head_devices * 4 * block_rows
    scale_factor = HD ** (-0.5)
    first_image = head_place * images
    blocks = gather_blocks(master, block_slot)
    attn_blocks = lax.all_gather(blocks[0:4], "head", axis=0)
    ffn_blocks = lax.all_gather(blocks[4:12], "head", axis=0)
    conv_full = lax.all_gather(conv, "head", axis=1, tiled=True)
    w_query, w_key, w_value, w_out = [
        attn_blocks[:, i].reshape(head_devices * block_rows, model_width) for i in range(4)
    ]
    w_in = ffn_blocks[:, 0:4].reshape(hidden_all, model_width)
    w_down = ffn_blocks[:, 4:8].reshape(hidden_all, model_width)
    image_valid = (first_image + jnp.arange(images) < image_count[0]).astype(jnp.float32)
    head_keep = (jnp.arange(heads) < subnet_heads[0]).astype(jnp.float32)
    unit_keep = (jnp.arange(hidden_all) < subnet_width[0]).astype(jnp.float32)
    token_values = lax.dynamic_slice_in_dim(tokens, first_image, images, 0).astype(jnp.float32)
    my_cotangent = lax.dynamic_slice_in_dim(cotangent, first_image, images, 0)
    scaled_one, inverse_one, normed_full = normalize(token_values, norm_params[0], norm_params[1])
    normed_one = normed_full.astype(jnp.bfloat16)

    def project(weight):
        return (
            jnp.einsum("gsd,fd->gsf", normed_one, weight, preferred_element_type=jnp.float32)
            .astype(jnp.bfloat16)
            .reshape(images, seq_len, heads, HD)
        )

    queries, key_vecs, value_vecs = project(w_query), project(w_key), project(w_value)
    scores = (
        jnp.einsum("gqhe,gkhe->ghqk", queries, key_vecs, preferred_element_type=jnp.float32)
        * scale_factor
    ).astype(jnp.bfloat16)
    softmaxed, post_mixed = mix_scores(scores, talk)
    attended = (
        jnp.einsum("ghqk,gkhe->gqhe", post_mixed, value_vecs, preferred_element_type=jnp.float32)
        * head_keep[None, None, :, None]
    )
    attended = attended.astype(jnp.bfloat16).reshape(images, seq_len, heads * HD)
    middle = token_values + jnp.einsum(
        "gsf,fd->gsd", attended, w_out, preferred_element_type=jnp.float32
    )
    scaled_two, inverse_two, normed_full_two = normalize(middle, norm_params[2], norm_params[3])
    normed_two = normed_full_two.astype(jnp.bfloat16)
    hidden = jnp.einsum("gsd,ud->gsu", normed_two, w_in, preferred_element_type=jnp.float32)
    activated = conv_grid(hidden, conv_full)
    sigmoid_act = jax.nn.sigmoid(activated)
    gated = (activated * sigmoid_act * unit_keep).astype(jnp.bfloat16)
    down = jnp.einsum("gsu,ud->gsd", gated, w_down, preferred_element_type=jnp.float32)
    my_output = (middle + down) * image_valid[:, None, None]
    output = lax.all_gather(my_output.astype(jnp.bfloat16), "head", axis=0, tiled=True).astype(
        jnp.float32
    )
    grad_output = my_cotangent * image_valid[:, None, None]
    grad_low = grad_output.astype(jnp.bfloat16)
    grad_down = jnp.einsum("gsu,gsd->ud", gated, grad_low, preferred_element_type=jnp.float32)
    grad_gated = (
        jnp.einsum("gsd,ud->gsu", grad_low, w_down, preferred_element_type=jnp.float32) * unit_keep
    )
    grad_act = grad_gated * sigmoid_act * (1.0 + activated * (1.0 - sigmoid_act))
    grad_hidden, grad_kernel = conv_back(grad_act, hidden, conv_full)
    grad_hidden_low = grad_hidden.astype(jnp.bfloat16)
    grad_in = jnp.einsum(
        "gsu,gsd->ud", grad_hidden_low, normed_two, preferred_element_type=jnp.float32
    )
    grad_normed_two = jnp.einsum(
        "gsu,ud->gsd", grad_hidden_low, w_in, preferred_element_type=jnp.float32
    )
    grad_middle = grad_output + normalize_back(
        grad_normed_two, scaled_two, inverse_two, norm_params[2]
    )
    grad_branch = grad_middle.astype(jnp.bfloat16)
    grad_out_proj = jnp.einsum(
        "gsf,gsd->fd", attended, grad_branch, preferred_element_type=jnp.float32
    )
    grad_attended = jnp.einsum(
        "gsd,fd->gsf", grad_branch, w_out, preferred_element_type=jnp.float32
    ).reshape(images, seq_len, heads, HD)
    grad_att_low = (grad_attended * head_keep[None, None, :, None]).astype(jnp.bfloat16)
    grad_values = jnp.einsum(
        "ghqk,gqhe->gkhe", post_mixed, grad_att_low, preferred_element_type=jnp.float32
    ).astype(jnp.bfloat16)
    grad_post = jnp.einsum(
        "gqhe,gkhe->ghqk", grad_att_low, value_vecs, preferred_element_type=jnp.float32
    ).astype(jnp.bfloat16)
    grad_scores, talk_pre, talk_post = mix_back(
        grad_post.astype(jnp.float32), softmaxed, scores, talk
    )
    grad_queries = (
        jnp.einsum("ghqk,gkhe->gqhe", grad_scores, key_vecs, preferred_element_type=jnp.float32)
        * scale_factor
    ).astype(jnp.bfloat16)
    grad_keys = (
        jnp.einsum("ghqk,gqhe->gkhe", grad_scores, queries, preferred_element_type=jnp.float32)
        * scale_factor
    ).astype(jnp.bfloat16)
    grad_parts = [
        part.reshape(images, seq_len, heads * HD) for part in (grad_queries, grad_keys, grad_values)
    ]
    grad_projs = [
        jnp.einsum("gsf,gsd->fd", part, normed_one, preferred_element_type=jnp.float32)
        for part in grad_parts
    ]
    grad_normed_one = sum(
        jnp.einsum("gsf,fd->gsd", part, weight, preferred_element_type=jnp.float32)
        for part, weight in zip(grad_parts, (w_query, w_key, w_value))
    )
    my_token_grad = grad_middle + normalize_back(
        grad_normed_one, scaled_one, inverse_one, norm_params[0]
    )
    token_grad = lax.all_gather(
        my_token_grad.astype(jnp.bfloat16), "head", axis=0, tiled=True
    ).astype(jnp.float32)
    norm_part = jnp.stack(
        [
            jnp.sum(grad_normed_one * scaled_one, axis=(0, 1)),
            jnp.sum(grad_normed_one, axis=(0, 1)),
            jnp.sum(grad_normed_two * scaled_two, axis=(0, 1)),
            jnp.sum(grad_normed_two, axis=(0, 1)),
        ]
    )
    talk_part = jnp.stack([talk_pre, talk_post]).reshape(2, heads * heads)
    talk_part = jnp.pad(talk_part, ((0, 0), (0, model_width - heads * heads)))
    every_head = jnp.broadcast_to(
        jnp.concatenate([norm_part, talk_part])[None], (head_devices, 6, model_width)
    )
    conv_part = grad_kernel.reshape(9, head_devices, model_width).transpose(1, 0, 2)
    small = split_pair(jnp.concatenate([every_head, conv_part], axis=1))

    def by_head(matrix):
        return matrix.reshape(head_devices, -1, model_width)

    message = jnp.concatenate(
        [by_head(m).astype(jnp.bfloat16) for m in (*grad_projs, grad_out_proj, grad_in, grad_down)]
        + [small],
        axis=1,
    )
    received = lax.all_to_all(message, "head", split_axis=0, concat_axis=0, tiled=True)
    matrix_rows = 12 * block_rows
    block_grads = jnp.sum(received[:, :matrix_rows].astype(jnp.float32), axis=0).reshape(
        12, block_rows, model_width
    )
    small_sum = jnp.sum(join_pair(received[:, matrix_rows:]), axis=0)
    all_slots = slot_count * data_devices
    spread_grads = (
        jnp.zeros((all_slots, block_rows, model_width), jnp.bfloat16)
        .at[block_slot]
        .set(block_grads.astype(jnp.bfloat16))
        .reshape(data_devices, slot_count * block_rows, model_width)
    )
    small_pair = split_pair(small_sum)
    message_two = jnp.concatenate(
        [spread_grads, jnp.broadcast_to(small_pair[None], (data_devices,) + small_pair.shape)],
        axis=1,
    )
    received_two = lax.all_to_all(message_two, "dp", split_axis=0, concat_axis=0, tiled=True)
    slot_rows = slot_count * block_rows
    slot_grads = jnp.sum(received_two[:, :slot_rows].astype(jnp.float32), axis=0).reshape(
        slot_count, block_rows, model_width
    )
    small_total = jnp.sum(join_pair(received_two[:, slot_rows:]), axis=0)
    norm_grad = small_total[0:4]
    talk_grad = small_total[4:6, : heads * heads].reshape(2, heads, heads)
    conv_grad = small_total[6:15]
    new_master, new_master_m1, new_master_m2 = adamw(
        master, slot_grads, master_m1, master_m2, rate_matrix, decay_matrix
    )
    new_norm, new_norm_m1, new_norm_m2 = adamw(
        norm_params, norm_grad, norm_m1, norm_m2, rate_small, 0.0
    )
    new_talk, new_talk_m1, new_talk_m2 = adamw(talk, talk_grad, talk_m1, talk_m2, rate_small, 0.0)
    new_conv, new_conv_m1, new_conv_m2 = adamw(
        conv, conv_grad, conv_m1, conv_m2, rate_small, decay_matrix
    )
    return (
        output,
        token_grad,
        new_master,
        new_master_m1,
        new_master_m2,
        new_master.astype(jnp.bfloat16),
        new_norm,
        new_norm_m1,
        new_norm_m2,
        new_talk,
        new_talk_m1,
        new_talk_m2,
        new_conv,
        new_conv_m1,
        new_conv_m2,
    )


def solution(mesh):
    in_specs = (
        P("dp", None, None),
        P("dp", None, None),
        P("dp"),
        P(),
        P(),
        P(),
        P("dp", None, "head"),
        P("dp", None, "head"),
        P("dp", None, "head"),
        P(),
        P(),
        P(),
        P(),
        P(),
        P(),
        P(None, "head"),
        P(None, "head"),
        P(None, "head"),
    )
    out_specs = (
        P("dp", None, None),
        P("dp", None, None),
        P("dp", None, "head"),
        P("dp", None, "head"),
        P("dp", None, "head"),
        P("dp", None, "head"),
        P(),
        P(),
        P(),
        P(),
        P(),
        P(),
        P(None, "head"),
        P(None, "head"),
        P(None, "head"),
    )
    return jax.shard_map(local, mesh=mesh, in_specs=in_specs, out_specs=out_specs, check_vma=False)
```

time: 394 us -> 177 us (0.45)
  waiting for transfers between devices: 186 us -> 14.8 us
  blocking collectives: 73.8 us -> 34.5 us
  between operations: 17 us -> 3.87 us
  local copies, waits for them, and re-layouts: 34.1 us -> 39.8 us
  other arithmetic: 25.5 us -> 20.8 us
  matrix products: 40.3 us -> 44.6 us
    psum x4 -> x0, waiting for transfers between devices: 123 us -> none  [the longest x1 33.3 us: local(): middle = token_values + lax.psum(attn_part, 'head')]
    psum x1 -> x0, blocking collectives: 41 us -> none  [local(): lax.psum((norm_part, talk_part, conv_wide), ('dp', 'head'))]
    all_to_all x4 -> x3, waiting for transfers between devices: 45.1 us -> 14.8 us  [the longest x1 14.2 us: local(): lax.all_to_all(message, 'head', split_axis=0, concat_axis=0, tiled=True)]
    reduce_scatter x1 -> x0, waiting for transfers between devices: 17.6 us -> none  [local(): lax.psum_scatter(spread_grads, 'dp', scatter_dimension=0, tiled=True)]
    dot_general x7 -> x13, matrix products: 3.73 us -> 10.9 us  [the longest x3 3.44 us: local(): jnp.einsum('gsf,fd->gsd', part, weight, preferred_element_type=jnp.float32)]
    reshape x4 -> x8, local copies, waits for them, and re-layouts: 0.81 us -> 6.8 us  [the longest x2 3.27 us: pad_grid(): values.reshape(images, SIDE, SIDE, channels)]
    reduce_sum x1, other arithmetic: 1.71 us -> 7.31 us  [conv_back(): jnp.sum(grad_grid * shifted(padded_hidden, row_off, col_off), axis=(0, 1,...]
    all_to_all x4 -> x1, local copies, waits for them, and re-layouts: 4.25 us -> 0.07 us  [gather_blocks(): lax.all_to_all(jnp.broadcast_to(mine[None], (data_devices,) + mine.shape)...]
  transfers between devices with their start and end apart: 9 -> 3, of which waited for: 9 -> 2; matrix products, arithmetic and copies ran while one was open for 10% -> 6% of each run, Pallas kernels for 0% -> 0%
where the time goes in v1:
time: 177 us; the launch traced here: 175 us
  matrix products  44.6 us (25%)
  local copies, waits for them, and re-layouts  39.8 us (22%)
  blocking collectives  34.5 us (19%)
  other arithmetic  20.8 us (12%)
  starting transfers between devices  16.9 us (10%)
  waiting for transfers between devices  14.8 us (8%)
  between operations  3.87 us (2%)
    all_to_all x1, waiting for transfers between devices, local(): lax.all_to_all(message, 'head', split_axis=0, concat_axis=0, tiled=True)  14.2 us
    unnamed x159, local copies, waits for them, and re-layouts  10.6 us
    all_gather x1, blocking collectives, local(): ffn_blocks = lax.all_gather(blocks[4:12], 'head', axis=0)  9.25 us
    reduce_sum x1, other arithmetic, conv_back(): jnp.sum(grad_grid * shifted(padded_hidden, row_off, col_off), axis=(0, 1,...  7.31 us
    all_to_all x1, starting transfers between devices, gather_blocks(): lax.all_to_all(jnp.broadcast_to(mine[None], (data_devices,) + mine.shape)...  7.25 us
    all_gather x1, blocking collectives, local(): attn_blocks = lax.all_gather(blocks[0:4], 'head', axis=0)  6.93 us
    all_gather x1, blocking collectives, local(): lax.all_gather(my_token_grad.astype(jnp.bfloat16), 'head', axis=0, tiled=...  6.68 us
    all_gather x1, blocking collectives, local(): lax.all_gather(my_output.astype(jnp.bfloat16), 'head', axis=0, tiled=True)  6.18 us
  transfers between devices with their start and end apart: 3, of which 2 were waited for; matrix products, arithmetic and copies ran while one was open for 6% of the time, Pallas kernels for 0%

profile of v1, /device:TPU:0, one launch (start us, length us, event | category | flops | bytes accessed | tf_op | source)
XLA Modules:
  0.0 175.3 jit_solution(16513780593674227736)
XLA Ops:
  0.7 1.0 convert_element_type.208
  1.7 1.0 broadcast_in_dim.21
  2.7 7.3 %all-to-all-start = ((bf16[8,2,54,216]{3,1,2,0:T(2,128)(2,1)}), bf16[8,2,54,216]{3,1,2,0:T(2,128)(2,1)S(1)}, u32[]{:S(2)}, u32[]{:S(2)}) async-start(bf16[8,2,54,216]{3,1,2,0:T(2,128)(2,1)} %broadcast_in_dim.21), calls=%async_computation | async-start | bytes 884736 | tf_op jit(solution)/shard_map/all_to_all | solution.py:107
  13.3 5.4 %all-gather.2 = f32[4,216,9]{1,2,0:T(8,128)S(1)} all-gather(f32[1,216,9]{1,2,0:T(8,128)} %bitcast.275), channel_id=1, replica_groups=mesh['dp'=8,'head'=4] {'head'}, dimensions={0}, use_global_device_ids=true | all-gather | bytes 38880 | tf_op jit(solution)/shard_map/all_gather | solution.py:161
  19.8 1.2 constant_dynamic-slice_fusion.1
  23.7 6.9 %all-gather = bf16[16,54,216]{2,1,0:T(8,128)(2,1)S(1)} all-gather(bf16[4,54,216]{2,1,0:T(8,128)(2,1)S(1)} %slice.225), channel_id=2, replica_groups=mesh['dp'=8,'head'=4] {'head'}, dimensions={0}, use_global_device_ids=true | all-gather | bytes 466560 | tf_op jit(solution)/shard_map/all_gather | solution.py:159
  33.6 9.3 %all-gather.1 = bf16[32,54,216]{2,0,1:T(8,128)(2,1)S(1)} all-gather(bf16[8,54,216]{2,0,1:T(8,128)(2,1)S(1)} %copy.283), channel_id=3, replica_groups=mesh['dp'=8,'head'=4] {'head'}, dimensions={0}, use_global_device_ids=true | all-gather | bytes 933120 | tf_op jit(solution)/shard_map/all_gather | solution.py:160
  43.3 1.0 reshape.508
  45.2 2.0 %bitcast_reduce_fusion = (f32[12,196]{0,1:T(8,128)S(1)}, f32[196,196,12]{1,2,0:T(8,128)S(1)}) fusion(f32[2,12,12]{2,1,0:T(8,128)S(1)} %copy.278, bf16[12,196,196]{2,1,0:T(8,128)(2,1)S(1)} %multiply_convert_fusion), kind=kOutput, calls=%fused_computation.15 | convolution fusion | flops 66841488 | bytes 3090368 | tf_op jit(solution)/shard_map/mn,gnqk->gmqk/dot_general | solution.py:70
  47.2 1.1 fusion.12
  48.9 3.9 %fusion.28 = bf16[12,196,196]{2,0,1:T(8,128)(2,1)S(1)} fusion(f32[2,12,12]{2,1,0:T(8,128)S(1)} %copy.278, f32[196,196,12]{1,2,0:T(8,128)S(1)} %get-tuple-element.163, f32[12,196]{0,1:T(8,128)S(1)} %fusion.12, f32[12,196]{0,1:T(8,128)S(1)} %get-tuple-element.162), kind=kOutput, calls=%fused_computation.30 | convolution fusion | flops 67765824 | bytes 4346240 | tf_op jit(solution)/shard_map/jm,gmqk->gjqk/dot_general | solution.py:74
  52.9 1.2 copy-done.3
  55.2 1.2 fusion.111
  56.4 1.2 reshape.507
  57.6 1.8 %multiply_convert_fusion.1 = (bf16[1,14,14,864]{3,2,1,0:T(8,128)(2,1)}, f32[1,14,14,864]{3,2,1,0:T(8,128)}) fusion(f32[864]{0:T(1024)S(1)} %fusion.125, f32[864]{0:T(1024)S(1)} %get-tuple-element.122, f32[864]{0:T(1024)S(1)} %get-tuple-element.123, f32[864]{0:T(1024)S(1)} %get-tuple-element.124, f32[864]{0:T(1024)S(1)} %get-tuple-element.125, ...), kind=kLoop, calls=%fused_computation.114 | loop fusion | flops 3894912 | bytes 1728000 | tf_op jit(solution)/shard_map/convert_element_type | solution.py:201
  59.4 2.1 %reshape.510 = f32[196,864]{1,0:T(8,128)} reshape(f32[1,14,14,864]{3,2,1,0:T(8,128)} %get-tuple-element.144) | data formatting | bytes 1354752 | tf_op jit(solution)/shard_map/reshape | solution.py:50
  61.5 2.0 %fusion.81 = bf16[864,196]{0,1:T(8,128)(2,1)} fusion(f32[864]{0:T(1024)S(1)} %fusion.125, f32[196,864]{1,0:T(8,128)} %reshape.510), kind=kLoop, calls=%fused_computation.123 | loop fusion | flops 1016064 | bytes 1019520 | tf_op jit(solution)/shard_map/gsu,gsd->ud/dot_general | solution.py:209
  63.5 3.5 %multiply_reduce_fusion.8 = (f32[864]{0:T(1024)}, f32[196,864]{1,0:T(8,128)}) fusion(f32[196,864]{1,0:T(8,128)} %fusion.111, f32[196,864]{1,0:T(8,128)} %reshape.510, f32[864]{0:T(1024)S(1)} %fusion.125, bf16[864,216]{1,0:T(8,128)(2,1)} %reshape.508, f32[]{:T(128)} %bitcast.30, f32[1,196,216]{2,0,1:T(1,128)} %constant_dynamic-slice_fusion), kind=kOutput, calls=%fused_computation.116 | convolution fusion | flops 75103200 | bytes 2581636 | tf_op jit(solution)/shard_map/gsd,ud->gsu/dot_general | solution.py:211
  67.0 2.1 %reshape.511 = f32[1,14,14,864]{3,2,1,0:T(8,128)} reshape(f32[196,864]{1,0:T(8,128)} %get-tuple-element.171) | data formatting | bytes 1354752 | tf_op jit(solution)/shard_map/reshape | solution.py:38
  69.1 7.3 %multiply_reduce_fusion = (f32[864]{0:T(1024)}, f32[864]{0:T(1024)}, f32[864]{0:T(1024)}, f32[864]{0:T(1024)}, f32[864]{0:T(1024)}, /*index=5*/f32[864]{0:T(1024...) fusion(f32[1,14,14,864]{3,2,1,0:T(8,128)} %reshape.511, f32[1,14,14,864]{3,2,1,0:T(8,128)S(1)} %reshape.507, ...), kind=kLoop, calls=%fused_computation.106 | loop fusion | flops 5750784 | bytes 1752192 | tf_op jit(solution)/shard_map/reduce_sum | solution.py:64
  76.4 1.2 convert_element_type.227
  77.6 1.8 %fusion.97 = (f32[216]{0:T(256)}, f32[196]{0:T(256)S(1)}, f32[196,216]{1,0:T(8,128)S(1)}) fusion(f32[1,196,216]{2,1,0:T(8,128)S(1)} %get-tuple-element.165, f32[196]{0:T(256)} %copy-done.34, f32[196]{0:T(256)} %copy-done.30, f32[216]{0:T(256)} %bitcast.278, bf16[196,864]{1,0:T(8,128)(2,1)S(1)} %convert_element_type.227, bf16[864,216]{1,0:T(8,128)(2,1)S(1)} %reshape.506), kind=kOutput, calls=%fused_computation.144 | convolution fusion | flops 73452544 | bytes 1054704 | tf_op jit(solution)/shard_map/gsu,ud->gsd/dot_general | solution.py:219
  79.4 1.3 fusion.136
  80.7 1.1 fusion.100
  81.8 1.1 fusion.36
  82.9 1.9 %fusion.44 = bf16[1,196,12,18]{1,3,2,0:T(8,128)(2,1)S(1)} fusion(bf16[196,12,18]{0,2,1:T(8,128)(2,1)S(1)} %fusion.36, bf16[12,196,196]{2,0,1:T(8,128)(2,1)} %copy-done.3), kind=kOutput, calls=%fused_computation.62 | convolution fusion | flops 16638048 | bytes 1091328 | tf_op jit(solution)/shard_map/ghqk,gqhe->gkhe/dot_general | solution.py:233
  85.4 3.4 %fusion.48 = f32[12,12]{1,0:T(8,128)} fusion(bf16[12,196,196]{2,1,0:T(8,128)(2,1)S(1)} %convolution_convert_fusion, f32[196,196,12]{1,2,0:T(8,128)S(1)} %copy-done.2, f32[12,196]{0,1:T(8,128)S(1)} %copy-done.27, f32[12,196]{0,1:T(8,128)S(1)} %copy-done.23), kind=kOutput, calls=%fused_computation.66 | convolution fusion | flops 67304832 | bytes 2785344 | tf_op jit(solution)/shard_map/gjqk,gmqk->jm/dot_general | solution.py:82
  88.8 4.1 %fusion.4 = (f32[12,196]{0,1:T(8,128)S(1)}, f32[196,196,12]{1,2,0:T(8,128)S(1)}) fusion(f32[12,196]{0,1:T(8,128)S(1)} %copy-done.27, f32[12,196]{0,1:T(8,128)S(1)} %copy-done.23, f32[196,196,12]{1,2,0:T(8,128)S(1)} %copy-done.2, f32[2,12,12]{2,1,0:T(8,128)S(1)} %copy.278, bf16[12,196,196]{2,1,0:T(8,128)(2,1)S(1)} %convolution_convert_fusion), kind=kOutput, calls=%fused_computation.8 | convolution fusion | flops 68224464 | bytes 6506432 | tf_op jit(solution)/shard_map/jm,gjqk->gmqk/dot_general | solution.py:81
  92.9 3.8 %fusion.53 = f32[12,12]{1,0:T(8,128)} fusion(bf16[12,196,196]{2,1,0:T(8,128)(2,1)S(1)} %multiply_convert_fusion, f32[12,196]{0,1:T(8,128)S(1)} %get-tuple-element.167, f32[196,196,12]{1,2,0:T(8,128)S(1)} %get-tuple-element.168, f32[196,196,12]{1,2,0:T(8,128)S(1)} %copy-done.2, f32[12,196]{0,1:T(8,128)S(1)} %copy-done.27, f32[12,196]{0,1:T(8,128)S(1)} %copy-done.23), kind=kOutput, calls=%fused_computation.67 | convolution fusion | flops 68226816 | bytes 4638720 | tf_op jit(solution)/shard_map/gmqk,gnqk->mn/dot_general | solution.py:84
  96.7 4.7 %fusion.25 = bf16[12,196,196]{2,0,1:T(8,128)(2,1)S(1)} fusion(f32[196,196,12]{1,2,0:T(8,128)S(1)} %get-tuple-element.168, f32[12,196]{0,1:T(8,128)S(1)} %get-tuple-element.167, f32[2,12,12]{2,1,0:T(8,128)S(1)} %copy.278, f32[196,196,12]{1,2,0:T(8,128)S(1)} %copy-done.2, f32[12,196]{0,1:T(8,128)S(1)} %copy-done.27, f32[12,196]{0,1:T(8,128)S(1)} %copy-done.23), kind=kOutput, calls=%fused_computation.29 | convolution fusion | flops 68687808 | bytes 7659904 | tf_op jit(solution)/shard_map/mn,gmqk->gnqk/dot_general | solution.py:87
  101.6 1.1 fusion.45
  102.8 1.1 fusion.46
  107.2 1.1 copy.301
  110.4 1.0 reshape.516
  111.4 1.1 fusion.147
  112.5 1.1 convolution_add_fusion.1
  113.6 1.2 fusion.95
  119.3 3.8 %concatenate.19 = bf16[4,678,216]{1,2,0:T(8,128)(2,1)} concatenate(bf16[4,54,216]{1,2,0:T(8,128)(2,1)S(1)} %copy.298, bf16[4,54,216]{1,2,0:T(8,128)(2,1)} %copy.299, bf16[4,54,216]{1,2,0:T(8,128)(2,1)} %copy.300, bf16[4,54,216]{1,2,0:T(8,128)(2,1)S(1)} %copy.301, bf16[4,216,216]{1,2,0:T(8,128)(2,1)S(1)} %convolution_convert_fusion.2, ...), dimensions={1} | concatenate | bytes 2343168 | tf_op jit(solution)/shard_map/concatenate | solution.py:286
  123.1 3.5 %all-to-all-start.1 = ((bf16[4,678,216]{1,2,0:T(8,128)(2,1)}), bf16[4,678,216]{1,2,0:T(8,128)(2,1)S(1)}, u32[]{:S(2)}, u32[]{:S(2)}) async-start(bf16[4,678,216]{1,2,0:T(8,128)(2,1)} %concatenate.19), calls=%async_computation.1 | async-start | bytes 2654208 | tf_op jit(solution)/shard_map/all_to_all | solution.py:291
  126.6 1.9 %convert_element_type.222 = bf16[196,864]{1,0:T(8,128)(2,1)} reshape(bf16[1,14,14,864]{3,2,1,0:T(8,128)(2,1)} %get-tuple-element.143) | data formatting | bytes 677376 | tf_op jit(solution)/shard_map/convert_element_type | solution.py:201
  128.5 1.3 fusion.43
  129.8 14.2 %all-to-all-done.1 = bf16[4,678,216]{1,2,0:T(8,128)(2,1)S(1)} async-done(((bf16[4,678,216]{1,2,0:T(8,128)(2,1)}), bf16[4,678,216]{1,2,0:T(8,128)(2,1)S(1)}, u32[]{:S(2)}, u32[]{:S(2)}) %all-to-all-start.1) | async-done | bytes 1171616 | tf_op jit(solution)/shard_map/all_to_all | solution.py:291
  144.9 1.1 scatter_fusion
  147.2 6.1 %all-to-all-start.2 = ((bf16[8,138,216]{2,1,0:T(8,128)(2,1)}), bf16[8,138,216]{2,1,0:T(8,128)(2,1)S(1)}, u32[]{:S(2)}, u32[]{:S(2)}) async-start(bf16[8,138,216]{2,1,0:T(8,128)(2,1)} %pad_maximum_fusion), calls=%async_computation.2 | async-start | bytes 1179648 | tf_op jit(solution)/shard_map/all_to_all | solution.py:309
  153.3 6.2 %all_gather.26 = bf16[4,196,216]{2,1,0:T(8,128)(2,1)S(1)} all-gather(bf16[1,196,216]{2,1,0:T(8,128)(2,1)S(1)} %fusion.43), channel_id=1, replica_groups=mesh['dp'=8,'head'=4] {'head'}, dimensions={0}, use_global_device_ids=true | all-gather | bytes 423360 | tf_op jit(solution)/shard_map/all_gather | solution.py:204
  159.5 1.0 copy.314
  160.7 6.7 %all_gather.27 = bf16[4,196,216]{2,1,0:T(8,128)(2,1)S(1)} all-gather(bf16[1,196,216]{2,1,0:T(8,128)(2,1)S(1)} %fusion.94), channel_id=1, replica_groups=mesh['dp'=8,'head'=4] {'head'}, dimensions={0}, use_global_device_ids=true | all-gather | bytes 423360 | tf_op jit(solution)/shard_map/all_gather | solution.py:264
  167.4 1.0 copy.315
  (262 shorter events, 29.9 us)
Async XLA Ops:
  0.6 18.3 %copy-start = (f32[4,196,216]{2,0,1:T(4,128)S(1)}, f32[4,196,216]{2,0,1:T(4,128)}, u32[]{:S(2)}) copy-start(f32[4,196,216]{2,0,1:T(4,128)} %param.19) | copy-start | bytes 2032132
  2.7 20.2 %all-to-all-start = ((bf16[8,2,54,216]{3,1,2,0:T(2,128)(2,1)}), bf16[8,2,54,216]{3,1,2,0:T(2,128)(2,1)S(1)}, u32[]{:S(2)}, u32[]{:S(2)}) async-start(bf16[8,2,54,216]{3,1,2,0:T(2,128)(2,1)} %broadcast_in_dim.21), calls=%async_computation | async-start | bytes 884736 | tf_op jit(solution)/shard_map/all_to_all | solution.py:107
  11.9 41.0 %copy-start.66 = (f32[12]{0:T(128)}, f32[12]{0:T(128)S(1)}, u32[]{:S(2)}) copy-start(f32[12]{0:T(128)S(1)} %compare_convert_fusion) | copy-start | bytes 148
  12.6 18.9 %copy-start.64 = (s32[12]{0:T(128)}, s32[12]{0:T(128)S(1)}, u32[]{:S(2)}) copy-start(s32[12]{0:T(128)S(1)} %compare_select_fusion) | copy-start | bytes 148
  21.1 33.5 %copy-start.4 = (bf16[1,196,216]{2,1,0:T(8,128)(2,1)}, bf16[1,196,216]{2,1,0:T(8,128)(2,1)S(1)}, u32[]{:S(2)}) copy-start(bf16[1,196,216]{2,1,0:T(8,128)(2,1)S(1)} %get-tuple-element.146) | copy-start | bytes 254020
  21.2 11.3 %copy-start.36 = (f32[196]{0:T(256)}, f32[196]{0:T(256)S(1)}, u32[]{:S(2)}) copy-start(f32[196]{0:T(256)S(1)} %broadcast_multiply_fusion.5) | copy-start | bytes 2356
  22.0 10.5 %copy-start.53 = (f32[196]{0:T(256)}, f32[196]{0:T(256)S(1)}, u32[]{:S(2)}) copy-start(f32[196]{0:T(256)S(1)} %add_rsqrt_fusion.1) | copy-start | bytes 2356
  22.9 9.6 %copy-start.38 = (f32[1,216]{1,0:T(1,128)}, f32[1,216]{1,0:T(1,128)S(1)}, u32[]{:S(2)}) copy-start(f32[1,216]{1,0:T(1,128)S(1)} %get-tuple-element.160) | copy-start | bytes 2596
  22.9 9.6 %copy-start.67 = (f32[1,216]{1,0:T(1,128)}, f32[1,216]{1,0:T(1,128)S(1)}, u32[]{:S(2)}) copy-start(f32[1,216]{1,0:T(1,128)S(1)} %get-tuple-element.159) | copy-start | bytes 2596
  22.9 32.3 %copy-start.32 = (f32[1,216]{1,0:T(1,128)}, f32[1,216]{1,0:T(1,128)S(1)}, u32[]{:S(2)}) copy-start(f32[1,216]{1,0:T(1,128)S(1)} %get-tuple-element.158) | copy-start | bytes 2596
  22.9 32.3 %copy-start.55 = (f32[1,216]{1,0:T(1,128)}, f32[1,216]{1,0:T(1,128)S(1)}, u32[]{:S(2)}) copy-start(f32[1,216]{1,0:T(1,128)S(1)} %get-tuple-element.161) | copy-start | bytes 2596
  31.5 11.6 %copy-start.18 = (bf16[216,216]{1,0:T(8,128)(2,1)}, bf16[216,216]{1,0:T(8,128)(2,1)S(1)}, u32[]{:S(2)}) copy-start(bf16[216,216]{1,0:T(8,128)(2,1)S(1)} %reshape_squeeze.14) | copy-start | bytes 279940
  31.9 12.7 %copy-start.9 = (bf16[196,12,18]{0,2,1:T(8,128)(2,1)}, bf16[196,12,18]{0,2,1:T(8,128)(2,1)S(1)}, u32[]{:S(2)}) copy-start(bf16[196,12,18]{0,2,1:T(8,128)(2,1)S(1)} %reshape.501) | copy-start | bytes 254020
  32.0 11.1 %copy-start.20 = (bf16[216,216]{1,0:T(8,128)(2,1)}, bf16[216,216]{1,0:T(8,128)(2,1)S(1)}, u32[]{:S(2)}) copy-start(bf16[216,216]{1,0:T(8,128)(2,1)S(1)} %reshape_squeeze.13) | copy-start | bytes 279940
  32.4 12.2 %copy-start.11 = (bf16[196,12,18]{0,2,1:T(8,128)(2,1)}, bf16[196,12,18]{0,2,1:T(8,128)(2,1)S(1)}, u32[]{:S(2)}) copy-start(bf16[196,12,18]{0,2,1:T(8,128)(2,1)S(1)} %reshape.500) | copy-start | bytes 254020
  33.6 19.3 %copy-start.13 = (bf16[196,12,18]{0,2,1:T(8,128)(2,1)}, bf16[196,12,18]{0,2,1:T(8,128)(2,1)S(1)}, u32[]{:S(2)}) copy-start(bf16[196,12,18]{0,2,1:T(8,128)(2,1)S(1)} %reshape.499) | copy-start | bytes 254020
  47.1 5.7 %copy-start.1 = (f32[196,196,12]{1,2,0:T(8,128)}, f32[196,196,12]{1,2,0:T(8,128)S(1)}, u32[]{:S(2)}) copy-start(f32[196,196,12]{1,2,0:T(8,128)S(1)} %get-tuple-element.163) | copy-start | bytes 5531908
  47.1 5.7 %copy-start.22 = (f32[12,196]{0,1:T(8,128)}, f32[12,196]{0,1:T(8,128)S(1)}, u32[]{:S(2)}) copy-start(f32[12,196]{0,1:T(8,128)S(1)} %get-tuple-element.162) | copy-start | bytes 28228
  54.9 6.5 %copy-start.30 = (f32[196]{0:T(256)}, f32[196]{0:T(256)S(1)}, u32[]{:S(2)}) copy-start(f32[196]{0:T(256)S(1)} %broadcast_multiply_fusion.4) | copy-start | bytes 2356
  55.1 6.3 %copy-start.34 = (f32[196]{0:T(256)}, f32[196]{0:T(256)S(1)}, u32[]{:S(2)}) copy-start(f32[196]{0:T(256)S(1)} %add_rsqrt_fusion) | copy-start | bytes 2356
  76.4 8.5 %copy-start.14 = (bf16[196,12,18]{0,2,1:T(8,128)(2,1)S(1)}, bf16[196,12,18]{0,2,1:T(8,128)(2,1)}, u32[]{:S(2)}) copy-start(bf16[196,12,18]{0,2,1:T(8,128)(2,1)} %copy-done.13) | copy-start | bytes 254020
  76.4 9.0 %copy-start.23 = (f32[12,196]{0,1:T(8,128)S(1)}, f32[12,196]{0,1:T(8,128)}, u32[]{:S(2)}) copy-start(f32[12,196]{0,1:T(8,128)} %copy-done.22) | copy-start | bytes 28228
  76.4 9.0 %copy-start.27 = (f32[12,196]{0,1:T(8,128)S(1)}, f32[12,196]{0,1:T(8,128)}, u32[]{:S(2)}) copy-start(f32[12,196]{0,1:T(8,128)} %copy-done.26) | copy-start | bytes 28228
  77.6 7.8 %copy-start.2 = (f32[196,196,12]{1,2,0:T(8,128)S(1)}, f32[196,196,12]{1,2,0:T(8,128)}, u32[]{:S(2)}) copy-start(f32[196,196,12]{1,2,0:T(8,128)} %copy-done.1) | copy-start | bytes 5531908
  96.7 6.1 %copy-start.10 = (bf16[196,12,18]{0,2,1:T(8,128)(2,1)S(1)}, bf16[196,12,18]{0,2,1:T(8,128)(2,1)}, u32[]{:S(2)}) copy-start(bf16[196,12,18]{0,2,1:T(8,128)(2,1)} %copy-done.9) | copy-start | bytes 254020
  96.7 7.2 %copy-start.16 = (bf16[196,216]{0,1:T(8,128)(2,1)S(1)}, bf16[196,216]{0,1:T(8,128)(2,1)}, u32[]{:S(2)}) copy-start(bf16[196,216]{0,1:T(8,128)(2,1)} %copy-done.15) | copy-start | bytes 254020
  103.9 6.3 %copy-start.57 = (f32[12,12]{1,0:T(8,128)S(1)}, f32[12,12]{1,0:T(8,128)}, u32[]{:S(2)}) copy-start(f32[12,12]{1,0:T(8,128)} %fusion.48) | copy-start | bytes 1732
  103.9 6.3 %copy-start.58 = (f32[12,12]{1,0:T(8,128)S(1)}, f32[12,12]{1,0:T(8,128)}, u32[]{:S(2)}) copy-start(f32[12,12]{1,0:T(8,128)} %fusion.53) | copy-start | bytes 1732
  104.8 5.6 %copy-start.17 = (bf16[1,196,12,18]{1,3,2,0:T(8,128)(2,1)S(1)}, bf16[1,196,12,18]{1,3,2,0:T(8,128)(2,1)}, u32[]{:S(2)}) copy-start(bf16[1,196,12,18]{1,3,2,0:T(8,128)(2,1)} %fusion.46) | copy-start | bytes 254020
  107.2 9.0 %copy-start.68 = (f32[1,216]{1,0:T(1,128)S(1)}, f32[1,216]{1,0:T(1,128)}, u32[]{:S(2)}) copy-start(f32[1,216]{1,0:T(1,128)} %copy-done.67) | copy-start | bytes 2596
  107.2 10.3 %copy-start.59 = (f32[216]{0:T(256)S(1)}, f32[216]{0:T(256)}, u32[]{:S(2)}) copy-start(f32[216]{0:T(256)} %get-tuple-element.117) | copy-start | bytes 2596
  107.2 10.3 %copy-start.63 = (f32[216]{0:T(256)S(1)}, f32[216]{0:T(256)}, u32[]{:S(2)}) copy-start(f32[216]{0:T(256)} %get-tuple-element.113) | copy-start | bytes 2596
  119.3 9.2 %copy-start.7 = (bf16[864,216]{1,0:T(8,128)(2,1)S(1)}, bf16[864,216]{1,0:T(8,128)(2,1)}, u32[]{:S(2)}) copy-start(bf16[864,216]{1,0:T(8,128)(2,1)} %reshape.508) | copy-start | bytes 1119748
  123.1 21.0 %all-to-all-start.1 = ((bf16[4,678,216]{1,2,0:T(8,128)(2,1)}), bf16[4,678,216]{1,2,0:T(8,128)(2,1)S(1)}, u32[]{:S(2)}, u32[]{:S(2)}) async-start(bf16[4,678,216]{1,2,0:T(8,128)(2,1)} %concatenate.19), calls=%async_computation.1 | async-start | bytes 2654208 | tf_op jit(solution)/shard_map/all_to_all | solution.py:291
  126.6 18.2 %copy-start.65 = (s32[12]{0:T(128)S(1)}, s32[12]{0:T(128)}, u32[]{:S(2)}) copy-start(s32[12]{0:T(128)} %copy-done.64) | copy-start | bytes 148
  147.1 22.1 %copy-start.29 = (f32[2,12,12]{2,0,1:T(2,128)S(1)}, f32[2,12,12]{2,0,1:T(2,128)}, u32[]{:S(2)}) copy-start(f32[2,12,12]{2,0,1:T(2,128)} %param.30) | copy-start | bytes 3460
  147.1 22.1 %copy-start.51 = (f32[2,12,12]{2,0,1:T(2,128)S(1)}, f32[2,12,12]{2,0,1:T(2,128)}, u32[]{:S(2)}) copy-start(f32[2,12,12]{2,0,1:T(2,128)} %param.31) | copy-start | bytes 3460
  147.1 22.1 %copy-start.52 = (f32[2,12,12]{2,0,1:T(2,128)S(1)}, f32[2,12,12]{2,0,1:T(2,128)}, u32[]{:S(2)}) copy-start(f32[2,12,12]{2,0,1:T(2,128)} %param.32) | copy-start | bytes 3460
  147.1 24.0 %copy-start.19 = (f32[2,54,216]{2,0,1:T(2,128)S(1)}, f32[2,54,216]{2,0,1:T(2,128)}, u32[]{:S(2)}) copy-start(f32[2,54,216]{2,0,1:T(2,128)} %param.24) | copy-start | bytes 279940
  147.1 24.0 %copy-start.24 = (f32[2,54,216]{2,0,1:T(2,128)S(1)}, f32[2,54,216]{2,0,1:T(2,128)}, u32[]{:S(2)}) copy-start(f32[2,54,216]{2,0,1:T(2,128)} %param.25) | copy-start | bytes 279940
  147.1 24.0 %copy-start.25 = (f32[2,54,216]{2,0,1:T(2,128)S(1)}, f32[2,54,216]{2,0,1:T(2,128)}, u32[]{:S(2)}) copy-start(f32[2,54,216]{2,0,1:T(2,128)} %param.26) | copy-start | bytes 279940
  147.2 21.8 %all-to-all-start.2 = ((bf16[8,138,216]{2,1,0:T(8,128)(2,1)}), bf16[8,138,216]{2,1,0:T(8,128)(2,1)S(1)}, u32[]{:S(2)}, u32[]{:S(2)}) async-start(bf16[8,138,216]{2,1,0:T(8,128)(2,1)} %pad_maximum_fusion), calls=%async_computation.2 | async-start | bytes 1179648 | tf_op jit(solution)/shard_map/all_to_all | solution.py:309
  159.5 14.5 %copy-start.50 = (f32[4,216]{1,0:T(4,128)S(1)}, f32[4,216]{1,0:T(4,128)}, u32[]{:S(2)}) copy-start(f32[4,216]{1,0:T(4,128)} %param.27) | copy-start | bytes 10372
  159.5 14.5 %copy-start.60 = (f32[4,216]{1,0:T(4,128)S(1)}, f32[4,216]{1,0:T(4,128)}, u32[]{:S(2)}) copy-start(f32[4,216]{1,0:T(4,128)} %param.28) | copy-start | bytes 10372
  159.5 14.5 %copy-start.61 = (f32[4,216]{1,0:T(4,128)S(1)}, f32[4,216]{1,0:T(4,128)}, u32[]{:S(2)}) copy-start(f32[4,216]{1,0:T(4,128)} %param.29) | copy-start | bytes 10372
  159.5 15.1 %copy-start.28 = (f32[9,216]{1,0:T(8,128)S(1)}, f32[9,216]{1,0:T(8,128)}, u32[]{:S(2)}) copy-start(f32[9,216]{1,0:T(8,128)} %param.33) | copy-start | bytes 23332
  159.5 15.1 %copy-start.48 = (f32[9,216]{1,0:T(8,128)S(1)}, f32[9,216]{1,0:T(8,128)}, u32[]{:S(2)}) copy-start(f32[9,216]{1,0:T(8,128)} %param.34) | copy-start | bytes 23332
  159.5 15.1 %copy-start.49 = (f32[9,216]{1,0:T(8,128)S(1)}, f32[9,216]{1,0:T(8,128)}, u32[]{:S(2)}) copy-start(f32[9,216]{1,0:T(8,128)} %param.35) | copy-start | bytes 23332
  (24 other events, 86.9 us)

commit v2 on v0

v2 whole, which is shorter than its diff:
```python
import functools
import jax
import jax.numpy as jnp
from jax import lax
from jax.experimental import pallas as pl
from jax.experimental.pallas import tpu as pltpu
from jax.sharding import PartitionSpec as P

HD = 18
SIDE = 14
PITCH = 16
MARGIN = 24
norm_eps = 1e-05
bf16 = jnp.bfloat16
f32 = jnp.float32


def nn(a, b):
    return lax.dot_general(a, b, (((1,), (0,)), ((), ())), preferred_element_type=f32)


def nt(a, b):
    return lax.dot_general(a, b, (((1,), (1,)), ((), ())), preferred_element_type=f32)


def tn(a, b):
    return lax.dot_general(a, b, (((0,), (0,)), ((), ())), preferred_element_type=f32)


def iota(shape, dim):
    return lax.broadcasted_iota(jnp.int32, shape, dim)


def split2(v):
    hi = v.astype(bf16)
    return hi, (v - hi.astype(f32)).astype(bf16)


def real_rows(shape):
    return (iota(shape, 0) & (PITCH - 1)) < SIDE


def head_mask(rows_heads, keep_heads=None):
    shape = (rows_heads * PITCH, 256)
    row_head = iota(shape, 0) >> 4
    lane = iota(shape, 1)
    rest = lane & 63
    lane_head = (lane >> 6) * 3 + (rest >= 18).astype(jnp.int32) + (rest >= 36).astype(jnp.int32)
    on = (row_head == lane_head) & (rest < 54)
    if keep_heads is not None:
        on = on & (row_head < keep_heads)
    return on


def true_head(rows, place):
    return ((rows // (3 * PITCH)) ^ place) * 3 + (rows // PITCH) % 3


def prep_kernel(scal, tok_ref, cot_ref, norm_ref, talk_ref, x_ref, a_ref, dy_ref, kron_ref, mask_ref, bias_ref, tmp_ref):
    x_ref[...] = jnp.zeros_like(x_ref)
    dy_ref[...] = jnp.zeros_like(dy_ref)
    valid = (scal[0] < scal[1]).astype(f32)
    tmp_ref[...] = tok_ref[0].astype(f32)
    for y in range(SIDE):
        x_ref[PITCH * y : PITCH * y + SIDE, :] = tmp_ref[SIDE * y : SIDE * (y + 1), :]
        dy_ref[PITCH * y : PITCH * y + SIDE, :] = cot_ref[0, SIDE * y : SIDE * (y + 1), :] * valid
    x = x_ref[...]
    centred = x - jnp.mean(x, axis=-1, keepdims=True)
    inv = lax.rsqrt(jnp.mean(centred * centred, axis=-1, keepdims=True) + norm_eps)
    a = centred * inv * norm_ref[0:1, :] + norm_ref[1:2, :]
    a_ref[...] = jnp.where(real_rows(a.shape), a, 0.0).astype(bf16)
    heads = talk_ref.shape[1]
    n = heads * PITCH
    ex = (true_head(iota((n, heads), 0), scal[0]) == iota((n, heads), 1)).astype(bf16)
    same = ((iota((n, n), 0) & (PITCH - 1)) == (iota((n, n), 1) & (PITCH - 1)))
    for i in range(2):
        for j, part in enumerate(split2(talk_ref[i])):
            if i == 0:
                half = nt(ex, part).astype(bf16)
            else:
                half = nn(ex, part).astype(bf16)
            kron_ref[2 * i + j] = jnp.where(same, nt(half, ex), 0.0).astype(bf16)
    mask_ref[...] = head_mask(heads).astype(bf16)
    bias_ref[...] = jnp.where(real_rows(bias_ref.shape), 0.0, -1e30)


def load_weight(dst_ref, w_refs, b):
    for k, w_ref in enumerate(w_refs):
        dst_ref[64 * k : 64 * k + 54, :] = w_ref[b]


def attn_fwd_kernel(
    scal, x_ref, a_ref, kron_ref, mask_ref, bias_ref, *refs, parts, unroll
):
    w_refs, refs = refs[:parts], refs[parts:]
    mid_ref, q_ref, k_ref, v_ref, o_ref, s_ref, p_ref, ws_ref, keep_ref = refs
    heads = kron_ref.shape[1] // PITCH
    n = heads * PITCH
    a = a_ref[...]
    ws_ref[...] = jnp.zeros_like(ws_ref)
    for b, dst in enumerate((q_ref, k_ref, v_ref)):
        load_weight(ws_ref.at[b], w_refs, b)
        dst[...] = nt(a, ws_ref[b]).astype(bf16)
    load_weight(ws_ref.at[3], w_refs, 3)
    scale = HD ** (-0.5)
    keep_rows = (true_head(iota((n, 1), 0), scal[0]) < scal[2]).astype(f32)
    keep_ref[...] = mask_ref[...].astype(f32) * keep_rows

    def group(y, _):
        rows = pl.ds(pl.multiple_of(y * PITCH, PITCH), PITCH)
        mask = mask_ref[...]
        qx = jnp.concatenate([q_ref[rows, :]] * heads, axis=0) * mask
        s = (nt(k_ref[...], qx) * scale).astype(bf16)
        s_ref[y] = s
        t = nn(s, kron_ref[0]) + nn(s, kron_ref[1])
        t = t + bias_ref[...]
        e = jnp.exp(t - jnp.max(t, axis=0, keepdims=True))
        p = e * (1.0 / jnp.sum(e, axis=0, keepdims=True))
        p_ref[y] = p
        ph, plo = split2(p)
        r = nt(kron_ref[2], ph).astype(bf16)
        o = nn(r, v_ref[...]) * keep_ref[...]
        o_ref[rows, :] = jnp.sum(o.reshape(heads, PITCH, 256), axis=0).astype(bf16)
        return 0

    lax.fori_loop(0, SIDE, group, 0, unroll=unroll)
    mid_ref[...] = x_ref[...] + nn(o_ref[...], ws_ref[3])


def ln_stats(v):
    centred = v - jnp.mean(v, axis=-1, keepdims=True)
    inv = lax.rsqrt(jnp.mean(centred * centred, axis=-1, keepdims=True) + norm_eps)
    return centred * inv, inv


def ln_back(grad, scaled, inv, gain):
    gs = grad * gain
    return inv * (
        gs - jnp.mean(gs, axis=-1, keepdims=True) - scaled * jnp.mean(gs * scaled, axis=-1, keepdims=True)
    )


def place(rows=216):
    shape = (rows, 256)
    lane = iota(shape, 1)
    rest = lane & 63
    return ((iota(shape, 0) == (lane >> 6) * 54 + rest) & (rest < 54)).astype(bf16)


def ffn_kernel(
    scal, mid_ref, dy_ref, norm_ref, *refs, parts
):
    w_refs, refs = refs[:parts], refs[parts:]
    out_ref, dmid_ref, gn_ref = refs[:3]
    gw_refs, refs = refs[3 : 3 + parts], refs[3 + parts :]
    win_ref, wdn_ref, h_ref, d_ref, gate_ref, dh_ref, cv_ref, gcv_ref, tmp_ref = refs
    hd = parts
    lanes = hd * 256
    win_ref[...] = jnp.zeros_like(win_ref)
    wdn_ref[...] = jnp.zeros_like(wdn_ref)
    pm = place()
    for h in range(hd):
        for j in range(4):
            at = 256 * h + 64 * j
            win_ref[at : at + 54, :] = w_refs[h][j]
            wdn_ref[at : at + 54, :] = w_refs[h][4 + j]
        both = nn(w_refs[h][8], pm)
        cv_ref[:, 256 * h : 256 * (h + 1)] = both[0:9] + both[16:25]
    mid = mid_ref[...]
    z, inv = ln_stats(mid)
    rows = real_rows(mid.shape)
    w = jnp.where(rows, z * norm_ref[2:3, :] + norm_ref[3:4, :], 0.0).astype(bf16)
    dy = dy_ref[...]
    e = dy.astype(bf16)
    tokens = mid.shape[0]
    pad = MARGIN
    zero = jnp.zeros((pad, lanes), f32)
    h_ref[0:pad, :] = zero
    h_ref[pad + tokens :, :] = zero
    d_ref[0:pad, :] = zero
    d_ref[pad + tokens :, :] = zero
    h_ref[pad : pad + tokens, :] = nt(w, win_ref[...])
    d_ref[pad : pad + tokens, :] = nt(e, wdn_ref[...])
    lane = iota((1, 128), 1)
    rmask = real_rows((tokens, 128))
    for c in range(lanes // 128):
        cols = slice(128 * c, 128 * (c + 1))
        glane = lane + 128 * c
        rest = glane & 63
        unit = (((glane >> 8) ^ scal[0]) * 4 + ((glane >> 6) & 3)) * 54 + rest
        keep = ((rest < 54) & (unit < scal[3])).astype(f32)
        act = jnp.zeros((tokens, 128), f32)
        for t in range(9):
            off = PITCH * (t // 3 - 1) + t % 3 - 1
            act = act + cv_ref[t : t + 1, cols] * h_ref[pad + off : pad + off + tokens, cols]
        sig = 1.0 / (1.0 + jnp.exp(-act))
        gate_ref[:, cols] = (act * sig * keep).astype(bf16)
        dact = d_ref[pad : pad + tokens, cols] * keep * sig * (1.0 + act * (1.0 - sig))
        d_ref[pad : pad + tokens, cols] = dact
        dh = jnp.zeros((tokens, 128), f32)
        for t in range(9):
            off = PITCH * (t // 3 - 1) + t % 3 - 1
            gcv_ref[t : t + 1, cols] = jnp.sum(
                dact * h_ref[pad + off : pad + off + tokens, cols], axis=0, keepdims=True
            )
            dh = dh + cv_ref[t : t + 1, cols] * d_ref[pad - off : pad - off + tokens, cols]
        dh_ref[:, cols] = jnp.where(rmask, dh, 0.0).astype(bf16)
    valid = (scal[0] < scal[1]).astype(f32)
    down = nn(gate_ref[...], wdn_ref[...])
    tmp_ref[...] = (mid + down) * valid
    for y in range(SIDE):
        out_ref[SIDE * y : SIDE * (y + 1), :] = tmp_ref[PITCH * y : PITCH * y + SIDE, :].astype(bf16)
    dw = nn(dh_ref[...], win_ref[...])
    gn_ref[...] = jnp.zeros_like(gn_ref)
    gn_ref[0:1, :] = jnp.sum(dw * z, axis=0, keepdims=True)
    gn_ref[1:2, :] = jnp.sum(dw, axis=0, keepdims=True)
    dmid_ref[...] = dy + ln_back(dw, z, inv, norm_ref[2:3, :])
    for h in range(hd):
        cols = slice(256 * h, 256 * (h + 1))
        gi = tn(dh_ref[:, cols], w).astype(bf16)
        gd = tn(gate_ref[:, cols], e).astype(bf16)
        for j in range(4):
            gw_refs[h][j] = gi[64 * j : 64 * j + 54]
            gw_refs[h][4 + j] = gd[64 * j : 64 * j + 54]
        hi, lo = split2(gcv_ref[:, cols])
        gw_refs[h][8] = jnp.zeros_like(gw_refs[h][8])
        gw_refs[h][8, 0:9] = nt(hi, pm).astype(bf16)
        gw_refs[h][8, 16:25] = nt(lo, pm).astype(bf16)


def attn_bwd_kernel(
    scal, x_ref, a_ref, dmid_ref, norm_ref, gn2_ref, kron_ref, mask_ref, q_ref, k_ref, v_ref, o_ref, s_ref, p_ref,
    *refs, parts, unroll
):
    w_refs, refs = refs[:parts], refs[parts:]
    tg_ref, gw_refs, refs = refs[0], refs[1 : 1 + parts], refs[1 + parts :]
    ws_ref, do_ref, gq_ref, gk_ref, gv_ref, g0_ref, g1_ref, tmp_ref, fm_ref, small_ref = refs
    heads = kron_ref.shape[1] // PITCH
    n = heads * PITCH
    hd = parts
    scale = HD ** (-0.5)
    ws_ref[...] = jnp.zeros_like(ws_ref)
    for b in range(4):
        load_weight(ws_ref.at[b], w_refs, b)
    f = dmid_ref[...].astype(bf16)
    lane = iota((1, 256), 1)
    rest = lane & 63
    lane_head = ((lane >> 6) ^ scal[0]) * 3 + (rest >= 18).astype(jnp.int32) + (rest >= 36).astype(jnp.int32)
    lane_keep = ((lane_head < scal[2]) & (rest < 54)).astype(f32)
    do_ref[...] = (nt(f, ws_ref[3]) * lane_keep).astype(bf16)
    g0_ref[...] = jnp.zeros_like(g0_ref)
    g1_ref[...] = jnp.zeros_like(g1_ref)
    gk_ref[...] = jnp.zeros_like(gk_ref)
    gv_ref[...] = jnp.zeros_like(gv_ref)
    fm_ref[...] = mask_ref[...].astype(f32)

    def group(y, _):
        rows = pl.ds(pl.multiple_of(y * PITCH, PITCH), PITCH)
        mask = mask_ref[...]
        qx = jnp.concatenate([q_ref[rows, :]] * heads, axis=0) * mask
        dx = jnp.concatenate([do_ref[rows, :]] * heads, axis=0) * mask
        v = v_ref[...]
        k = k_ref[...]
        p = p_ref[y]
        ph, plo = split2(p)
        dr = nt(dx, v).astype(bf16)
        drt = nt(v, dx).astype(bf16)
        dp = nn(drt, kron_ref[2])
        dt = p * (dp - jnp.sum(dp * p, axis=0, keepdims=True))
        dth, dtl = split2(dt)
        g1_ref[...] += nn(dr, ph)
        srow = (nt(qx, k) * scale).astype(bf16)
        g0_ref[...] += nn(srow, dth)
        dst = nt(dth, kron_ref[0]).astype(bf16)
        dsr = nt(kron_ref[0], dth).astype(bf16)
        gk_ref[...] += nn(dst, qx)
        gq = nn(dsr, k) * fm_ref[...]
        gq_ref[rows, :] = (jnp.sum(gq.reshape(heads, PITCH, 256), axis=0) * scale).astype(bf16)
        rt = nt(ph, kron_ref[2]).astype(bf16)
        gv_ref[...] += nn(rt, dx)
        return 0

    lax.fori_loop(0, SIDE, group, 0, unroll=unroll)
    gq = gq_ref[...]
    gk = (gk_ref[...] * scale).astype(bf16)
    gv = gv_ref[...].astype(bf16)
    a = a_ref[...]
    da = nn(gq, ws_ref[0]) + nn(gk, ws_ref[1]) + nn(gv, ws_ref[2])
    for b, (g, t) in enumerate(((gq, a), (gk, a), (gv, a), (o_ref[...], f))):
        gw = tn(g, t).astype(bf16)
        for h in range(hd):
            gw_refs[h][b] = gw[64 * h : 64 * h + 54]
    z, inv = ln_stats(x_ref[...])
    small_ref[...] = jnp.zeros_like(small_ref)
    small_ref[0:1, :] = jnp.sum(da * z, axis=0, keepdims=True)
    small_ref[1:2, :] = jnp.sum(da, axis=0, keepdims=True)
    small_ref[2:4, :] = gn2_ref[0:2, :]
    tmp_ref[...] = dmid_ref[...] + ln_back(da, z, inv, norm_ref[0:1, :])
    for y in range(SIDE):
        tg_ref[SIDE * y : SIDE * (y + 1), :] = tmp_ref[PITCH * y : PITCH * y + SIDE, :].astype(bf16)
    same = (iota((n, n), 0) & (PITCH - 1)) == (iota((n, n), 1) & (PITCH - 1))
    ex = (true_head(iota((n, heads), 0), scal[0]) == iota((n, heads), 1)).astype(bf16)
    for i, ref in enumerate((g0_ref, g1_ref)):
        g = jnp.where(same, ref[...], 0.0)
        hi, lo = split2(g)
        cols = nn(hi, ex) + nn(lo, ex)
        hi, lo = split2(cols)
        if i == 0:
            small_ref[8:20, 0:heads] = tn(hi, ex) + tn(lo, ex)
        else:
            small_ref[8:20, 128 : 128 + heads] = tn(ex, hi) + tn(ex, lo)
    hi, lo = split2(small_ref[...])
    for h in range(hd):
        gw_refs[h][4, 0:24] = hi
        gw_refs[h][4, 24:48] = lo
        gw_refs[h][4, 48:54] = jnp.zeros((6, hi.shape[1]), bf16)


def cast_kernel(m_ref, out_ref):
    low = m_ref[...].astype(bf16)
    for i in range(out_ref.shape[0]):
        out_ref[i] = low


def select_kernel(slot_ref, every_ref, conv_ref, attn_ref, ffn_ref):
    per = every_ref.shape[1]
    for b in range(12):
        slot = slot_ref[b]
        block = every_ref[slot // per, slot % per]
        if b < 4:
            attn_ref[b] = block
        else:
            ffn_ref[b - 4] = block
    hi, lo = split2(conv_ref[...])
    ffn_ref[8] = jnp.zeros_like(ffn_ref[8])
    ffn_ref[8, 0:9] = hi
    ffn_ref[8, 16:25] = lo


def total(refs, at):
    acc = refs[0][at].astype(f32)
    for ref in refs[1:]:
        acc = acc + ref[at].astype(f32)
    return acc


def spread_kernel(slot_ref, *refs, parts):
    attn, ffn_refs, out_ref = refs[:parts], refs[parts : 2 * parts], refs[2 * parts]
    ranks, per = out_ref.shape[0], out_ref.shape[1] - 1
    out_ref[...] = jnp.zeros_like(out_ref)
    for b in range(12):
        slot = slot_ref[b]
        block = total(attn, b) if b < 4 else total(ffn_refs, b - 4)
        out_ref[slot // per, slot % per] = block.astype(bf16)
    norm = total(attn, 4)
    norm_hi, norm_lo = split2(norm[0:24] + norm[24:48])
    conv = total(ffn_refs, 8)
    conv_hi, conv_lo = split2(conv[0:9] + conv[16:25])
    for i in range(ranks):
        out_ref[i, per, 0:20] = norm_hi[0:20]
        out_ref[i, per, 20:29] = conv_hi
        out_ref[i, per, 29:38] = conv_lo
        out_ref[i, per, 38:42] = norm_lo[0:4]
        out_ref[i, per, 42:54] = norm_lo[8:20]


def adam(w, g, one, two, rate, decay):
    one_new = 0.5 * one + 0.5 * g
    two_new = 0.5 * two + 0.5 * g * g
    hat_one = one_new / (1.0 - 0.5**3)
    hat_two = two_new / (1.0 - 0.5**3)
    return w - rate * (hat_one / (jnp.sqrt(hat_two) + 1e-08) + decay * w), one_new, two_new


def update_kernel(*refs):
    got_ref, ins, outs = refs[0], refs[1:13], refs[13:]
    ranks, per = got_ref.shape[0], got_ref.shape[1] - 1
    for i in range(per):
        g = got_ref[0, i].astype(f32)
        for r in range(1, ranks):
            g = g + got_ref[r, i].astype(f32)
        w, one, two = adam(ins[0][i], g, ins[1][i], ins[2][i], 0.06, 0.05)
        outs[0][i], outs[1][i], outs[2][i], outs[3][i] = w, one, two, w.astype(bf16)
    g = got_ref[0, per].astype(f32)
    for r in range(1, ranks):
        g = g + got_ref[r, per].astype(f32)
    heads = ins[6].shape[1]
    norm = g[0:4] + g[38:42]
    mix = g[8:20] + g[42:54]
    conv = g[20:29] + g[29:38]
    outs[4][...], outs[5][...], outs[6][...] = adam(ins[3][...], norm, ins[4][...], ins[5][...], 0.2, 0.0)
    for i in range(2):
        w, one, two = adam(ins[6][i], mix[:, 128 * i : 128 * i + heads], ins[7][i], ins[8][i], 0.2, 0.0)
        outs[7][i], outs[8][i], outs[9][i] = w, one, two
    outs[10][...], outs[11][...], outs[12][...] = adam(ins[9][...], conv, ins[10][...], ins[11][...], 0.2, 0.05)


def assemble_kernel(scal, *refs, parts):
    for i, out_ref in enumerate(refs[2 * parts :]):
        for k in range(parts):
            out_ref[scal[0] ^ k] = refs[parts * i + k][...].astype(f32)


VM = pl.BlockSpec(memory_space=pltpu.VMEM)
SM = pl.BlockSpec(memory_space=pltpu.SMEM)
SDS = jax.ShapeDtypeStruct


def call(body, name, n_scalar, n_in, out_shape, scratch=(), mb=16, micros=1, **kw):
    return pl.pallas_call(
        functools.partial(body, **kw) if kw else body,
        in_specs=[SM] * n_scalar + [VM] * n_in,
        out_specs=[VM] * len(out_shape),
        out_shape=out_shape,
        scratch_shapes=scratch,
        compiler_params=pltpu.CompilerParams(vmem_limit_bytes=mb << 20),
        cost_estimate=pl.CostEstimate(flops=micros * 1000000000, transcendentals=0, bytes_accessed=micros * 3000000),
        name=name,
    )


def prep(scal, tokens, cotangent, norm_params, talk):
    tok, dim = tokens.shape[1], tokens.shape[2]
    pad = SIDE * PITCH
    heads = talk.shape[1]
    n = heads * PITCH
    full = lambda *s: pl.BlockSpec(s, lambda i, sc: (0,) * len(s))
    return pl.pallas_call(
        prep_kernel,
        grid_spec=pltpu.PrefetchScalarGridSpec(
            num_scalar_prefetch=1,
            grid=(1,),
            in_specs=[
                pl.BlockSpec((1, tok, dim), lambda i, sc: (sc[0], 0, 0)),
                pl.BlockSpec((1, tok, dim), lambda i, sc: (sc[0], 0, 0)),
                full(*norm_params.shape),
                full(*talk.shape),
            ],
            out_specs=[full(pad, dim), full(pad, dim), full(pad, dim), full(4, n, n), full(n, 256), full(pad, n)],
            scratch_shapes=[pltpu.VMEM((tok, dim), f32)],
        ),
        out_shape=[SDS((pad, dim), f32), SDS((pad, dim), bf16), SDS((pad, dim), f32), SDS((4, n, n), bf16),
                   SDS((n, 256), bf16), SDS((pad, n), f32)],
        compiler_params=pltpu.CompilerParams(vmem_limit_bytes=16 << 20),
        cost_estimate=pl.CostEstimate(flops=1000000000, transcendentals=0, bytes_accessed=3000000),
        name="prep",
    )(scal, tokens, cotangent, norm_params, talk)


def attn_fwd(scal, x, a, kron, mask, bias, w, unroll=7):
    pad, dim = x.shape
    n = kron.shape[1]
    return call(
        attn_fwd_kernel, "attn_fwd", 1, 5 + len(w),
        [SDS((pad, dim), f32)] + [SDS((pad, 256), bf16)] * 4 + [SDS((SIDE, pad, n), bf16), SDS((SIDE, pad, n), f32)],
        [pltpu.VMEM((4, 256, dim), bf16), pltpu.VMEM((n, 256), f32)],
        mb=24, micros=10, parts=len(w), unroll=unroll,
    )(scal, x, a, kron, mask, bias, *w)


def ffn(scal, mid, dy, norm_params, w):
    pad, dim = mid.shape
    lanes = len(w) * 256
    return call(
        ffn_kernel, "ffn", 1, 3 + len(w),
        [SDS((SIDE * SIDE, dim), bf16), SDS((pad, dim), f32), SDS((8, dim), f32)] + [SDS((9, 54, dim), bf16)] * len(w),
        [
            pltpu.VMEM((lanes, dim), bf16), pltpu.VMEM((lanes, dim), bf16),
            pltpu.VMEM((pad + 2 * MARGIN, lanes), f32), pltpu.VMEM((pad + 2 * MARGIN, lanes), f32),
            pltpu.VMEM((pad, lanes), bf16), pltpu.VMEM((pad, lanes), bf16),
            pltpu.VMEM((9, lanes), f32), pltpu.VMEM((9, lanes), f32), pltpu.VMEM((pad, dim), f32),
        ],
        mb=24, micros=6, parts=len(w),
    )(scal, mid, dy, norm_params, *w)


def attn_bwd(scal, x, a, dmid, norm_params, gn2, kron, mask, q, k, v, o, s, p, w, unroll=7):
    pad, dim = x.shape
    n = kron.shape[1]
    return call(
        attn_bwd_kernel, "attn_bwd", 1, 13 + len(w),
        [SDS((SIDE * SIDE, dim), bf16)] + [SDS((5, 54, dim), bf16)] * len(w),
        [
            pltpu.VMEM((4, 256, dim), bf16), pltpu.VMEM((pad, 256), bf16), pltpu.VMEM((pad, 256), bf16),
            pltpu.VMEM((pad, 256), f32), pltpu.VMEM((pad, 256), f32),
            pltpu.VMEM((n, n), f32), pltpu.VMEM((n, n), f32), pltpu.VMEM((pad, dim), f32), pltpu.VMEM((n, 256), f32),
            pltpu.VMEM((24, dim), f32),
        ],
        mb=24, micros=14, parts=len(w), unroll=unroll,
    )(scal, x, a, dmid, norm_params, gn2, kron, mask, q, k, v, o, s, p, *w)


def from_peers(x, axis):
    n = lax.axis_size(axis)
    return [lax.ppermute(x, axis, [(i, i ^ k) for i in range(n)]) for k in range(1, n)]


def exchange(messages, axis):
    n = lax.axis_size(axis)
    return [messages[0]] + [
        lax.ppermute(messages[k], axis, [(i, i ^ k) for i in range(n)]) for k in range(1, n)
    ]


def local(
    tokens, cotangent, image_count, subnet_heads, subnet_width, block_slot,
    master, master_m1, master_m2, norm_params, norm_m1, norm_m2, talk, talk_m1, talk_m2, conv, conv_m1, conv_m2,
):
    slots, rows, dim = master.shape
    parts = lax.axis_size("head")
    ranks = lax.axis_size("dp")
    place_id = lax.axis_index("head").astype(jnp.int32)
    scal = jnp.concatenate([place_id[None], image_count, subnet_heads, subnet_width])
    (mine,) = call(cast_kernel, "cast", 0, 1, [SDS((ranks, slots, rows, dim), bf16)])(master)
    every = lax.all_to_all(mine, "dp", split_axis=0, concat_axis=0, tiled=True)
    x, a, dy, kron, mask, bias = prep(scal, tokens, cotangent, norm_params, talk)
    attn_w, ffn_w = call(
        select_kernel, "select", 1, 2, [SDS((4, rows, dim), bf16), SDS((9, rows, dim), bf16)]
    )(block_slot, every, conv)
    attn_w = [attn_w] + from_peers(attn_w, "head")
    ffn_w, attn_w[1:] = lax.optimization_barrier((ffn_w, attn_w[1:]))
    ffn_w = [ffn_w] + from_peers(ffn_w, "head")
    mid, q, k, v, o, s, p = attn_fwd(scal, x, a, kron, mask, bias, attn_w)
    out, dmid, gn2, *ffn_g = ffn(scal, mid, dy, norm_params, ffn_w)
    tg, *attn_g = attn_bwd(scal, x, a, dmid, norm_params, gn2, kron, mask, q, k, v, o, s, p, attn_w)
    ffn_g = exchange(ffn_g, "head")
    outs = [out] + from_peers(out, "head")
    attn_g = exchange(attn_g, "head")
    tg, attn_g[1:] = lax.optimization_barrier((tg, attn_g[1:]))
    tgs = [tg] + from_peers(tg, "head")
    (message,) = call(
        spread_kernel, "spread", 1, 2 * parts, [SDS((ranks, slots + 1, rows, dim), bf16)], parts=parts
    )(block_slot, *attn_g, *ffn_g)
    got = lax.all_to_all(message, "dp", split_axis=0, concat_axis=0, tiled=True)
    images = SDS((parts,) + tokens.shape[1:], f32)
    output, token_grad = call(assemble_kernel, "assemble", 1, 2 * parts, [images, images], parts=parts)(
        scal, *outs, *tgs
    )
    state = (master, master_m1, master_m2, norm_params, norm_m1, norm_m2, talk, talk_m1, talk_m2, conv, conv_m1, conv_m2)
    shapes = [SDS(t.shape, f32) for t in state]
    shapes.insert(3, SDS(master.shape, bf16))
    new = call(update_kernel, "update", 0, 13, shapes)(got, *state)
    return (output, token_grad, *new)


def solution(mesh):
    in_specs = (
        P("dp", None, None),
        P("dp", None, None),
        P("dp"),
        P(),
        P(),
        P(),
        P("dp", None, "head"),
        P("dp", None, "head"),
        P("dp", None, "head"),
        P(),
        P(),
        P(),
        P(),
        P(),
        P(),
        P(None, "head"),
        P(None, "head"),
        P(None, "head"),
    )
    out_specs = (
        P("dp", None, None),
        P("dp", None, None),
        P("dp", None, "head"),
        P("dp", None, "head"),
        P("dp", None, "head"),
        P("dp", None, "head"),
        P(),
        P(),
        P(),
        P(),
        P(),
        P(),
        P(None, "head"),
        P(None, "head"),
        P(None, "head"),
    )
    return jax.shard_map(local, mesh=mesh, in_specs=in_specs, out_specs=out_specs, check_vma=False)
```

time: 394 us -> 113 us (0.29)
  waiting for transfers between devices: 186 us -> 44.5 us
  blocking collectives: 73.8 us -> 0 us
  matrix products: 40.3 us -> 0 us
  Pallas kernels: 0 us -> 33 us
  other arithmetic: 25.5 us -> 0.08 us
  local copies, waits for them, and re-layouts: 34.1 us -> 9.45 us
  between operations: 17 us -> 2.96 us
  starting transfers between devices: 16.5 us -> 22.6 us
    psum x4 -> x0, waiting for transfers between devices: 123 us -> none  [the longest x1 33.3 us: local(): middle = token_values + lax.psum(attn_part, 'head')]
    psum x1 -> x0, blocking collectives: 41 us -> none  [local(): lax.psum((norm_part, talk_part, conv_wide), ('dp', 'head'))]
    dot_general x24 -> x0, matrix products: 40.3 us -> none  [the longest x1 5.65 us: mix_back(): jnp.einsum('gmqk,gnqk->mn', grad_mixed, received.astype(jnp.float32), pre...]
    pallas_call x0 -> x9, Pallas kernels: none -> 33 us  [the longest x1 12.9 us: attn_bwd(): call(attn_bwd_kernel, 'attn_bwd', 1, 13 + len(w), [SDS((SIDE * SIDE, dim)...]
    all_gather x1 -> x0, blocking collectives: 32.9 us -> none  [local(): lax.all_gather(master.astype(jnp.bfloat16), 'dp', axis=0, tiled=True)]
    all_to_all x4 -> x2, waiting for transfers between devices: 45.1 us -> 14.5 us  [the longest x1 10.4 us: local(): every = lax.all_to_all(mine, 'dp', split_axis=0, concat_axis=0, tiled=True)]
    ppermute x0 -> x18, waiting for transfers between devices: none -> 30 us  [the longest x6 15.9 us: exchange(): lax.ppermute(messages[k], axis, [(i, i ^ k) for i in range(n)])]
    reduce_scatter x1 -> x0, waiting for transfers between devices: 17.6 us -> none  [local(): lax.psum_scatter(spread_grads, 'dp', scatter_dimension=0, tiled=True)]
  transfers between devices with their start and end apart: 9 -> 20, of which waited for: 9 -> 11; matrix products, arithmetic and copies ran while one was open for 10% -> 2% of each run, Pallas kernels for 0% -> 10%
where the time goes in v2:
time: 113 us
  waiting for transfers between devices  44.5 us (39%)
  Pallas kernels  33 us (29%)
  starting transfers between devices  22.6 us (20%)
  local copies, waits for them, and re-layouts  9.45 us (8%)
  between operations  2.96 us (3%)
    ppermute x6, waiting for transfers between devices, exchange(): lax.ppermute(messages[k], axis, [(i, i ^ k) for i in range(n)])  15.9 us
    ppermute x12, waiting for transfers between devices, from_peers(): lax.ppermute(x, axis, [(i, i ^ k) for i in range(n)])  14.1 us
    pallas_call x1, Pallas kernels, attn_bwd(): call(attn_bwd_kernel, 'attn_bwd', 1, 13 + len(w), [SDS((SIDE * SIDE, dim)...  12.9 us
    all_to_all x1, waiting for transfers between devices, local(): every = lax.all_to_all(mine, 'dp', split_axis=0, concat_axis=0, tiled=True)  10.4 us
    pallas_call x1, Pallas kernels, attn_fwd(): call(attn_fwd_kernel, 'attn_fwd', 1, 5 + len(w), [SDS((pad, dim), f32)] +...  9.28 us
    unnamed x45, local copies, waits for them, and re-layouts  8.27 us
    ppermute x12, starting transfers between devices, from_peers(): lax.ppermute(x, axis, [(i, i ^ k) for i in range(n)])  7.64 us
    all_to_all x1, starting transfers between devices, local(): every = lax.all_to_all(mine, 'dp', split_axis=0, concat_axis=0, tiled=True)  7.25 us
  transfers between devices with their start and end apart: 20, of which 11 were waited for; matrix products, arithmetic and copies ran while one was open for 2% of the time, Pallas kernels for 10%

profile of v2, /device:TPU:0, one launch (start us, length us, event | category | flops | bytes accessed | tf_op | source)
XLA Modules:
  0.0 112.6 jit_solution(9185136948742346713)
XLA Ops:
  0.7 1.0 copy.55.m_ref.refs_1_
  1.7 1.1 copy.56
  2.8 7.3 %all-to-all-start = ((bf16[8,2,54,216]{3,1,2,0:T(2,128)(2,1)}), bf16[8,2,54,216]{3,1,2,0:T(2,128)(2,1)S(1)}, u32[]{:S(2)}, u32[]{:S(2)}) async-start(bf16[8,2,54,216]{3,1,2,0:T(2,128)(2,1)} %copy.56), calls=%async_computation | async-start | bytes 884736 | tf_op jit(solution)/shard_map/all_to_all | solution.py:515
  12.1 0.2 copy.53.cot_ref
  12.3 0.1 pad_add_fusion.scal
  12.4 10.4 %all-to-all-done = bf16[8,2,54,216]{3,1,2,0:T(2,128)(2,1)S(1)} async-done(((bf16[8,2,54,216]{3,1,2,0:T(2,128)(2,1)}), bf16[8,2,54,216]{3,1,2,0:T(2,128)(2,1)S(1)}, u32[]{:S(2)}, u32[]{:S(2)}) %all-to-all-start) | async-done | bytes 373280 | tf_op jit(solution)/shard_map/all_to_all | solution.py:515
  22.9 0.6 select.1
  23.6 1.6 %collective-permute-start.1 = (bf16[4,54,216]{2,1,0:T(8,128)(2,1)S(1)}, bf16[4,54,216]{2,1,0:T(8,128)(2,1)S(1)}, u32[]{:S(2)}, u32[]{:S(2)}) collective-permute-start(bf16[4,54,216]{2,1,0:T(8,128)(2,1)S(1)} %get-tuple-element.70.refs_0_), channel_id=1, source_target_pairs={{0,2},{1,3},{2,0},{3,1},{4,6},{5,7},{6,4},{7,5},{8,10},{9,11},{10,... | collective-permute-start | bytes 279944 | tf_op jit(solution)/shard_map/ppermute | solution.py:495
  25.2 0.3 collective-permute-start.2
  25.5 1.2 %prep.1 = (f32[224,216]{1,0:T(8,128)S(1)}, bf16[224,216]{1,0:T(8,128)(2,1)S(1)}, f32[224,216]{1,0:T(8,128)S(1)}, bf16[4,192,192]{2,1,0:T(8,128)(2,1)S(1)}, bf16[...) custom-call(s32[4]{0:T(128)S(1)} %pad_add_fusion.scal, bf16[4,196,216]{2,1,0:T(8,128)(2,1)S(1)} %copy.52.tok_ref, ...), custom_call_target="tpu_custom_call" | custom-call | flops 1000000000 | bytes 3000000 | tf_op jit(solution)/shard_map/prep/pallas_call | solution.py:428
  26.7 2.9 %collective-permute-done.1.refs_2_ = bf16[4,54,216]{2,1,0:T(8,128)(2,1)S(1)} collective-permute-done((bf16[4,54,216]{2,1,0:T(8,128)(2,1)S(1)}, bf16[4,54,216]{2,1,0:T(8,128)(2,1)S(1)}, u32[]{:S(2)}, u32[]{:S(2)}) %collective-permute-start.1) | collective-permute-done | bytes 93344 | tf_op jit(solution)/shard_map/ppermute | solution.py:495
  29.6 1.6 %collective-permute-done.2.refs_3_ = bf16[4,54,216]{2,1,0:T(8,128)(2,1)S(1)} collective-permute-done((bf16[4,54,216]{2,1,0:T(8,128)(2,1)S(1)}, bf16[4,54,216]{2,1,0:T(8,128)(2,1)S(1)}, u32[]{:S(2)}, u32[]{:S(2)}) %collective-permute-start.2) | collective-permute-done | bytes 93344 | tf_op jit(solution)/shard_map/ppermute | solution.py:495
  31.2 0.3 collective-permute-start.3
  31.5 1.5 %collective-permute-start.4 = (bf16[9,54,216]{2,1,0:T(8,128)(2,1)S(1)}, bf16[9,54,216]{2,1,0:T(8,128)(2,1)S(1)}, u32[]{:S(2)}, u32[]{:S(2)}) collective-permute-start(bf16[9,54,216]{2,1,0:T(8,128)(2,1)S(1)} %get-tuple-element.77.refs_0_), channel_id=1, source_target_pairs={{0,2},{1,3},{2,0},{3,1},{4,6},{5,7},{6,4},{7,5},{8,10},{9,11},{10,... | collective-permute-start | bytes 629864 | tf_op jit(solution)/shard_map/ppermute | solution.py:495
  33.0 9.3 %attn_fwd.1 = (f32[224,216]{1,0:T(8,128)S(1)}, bf16[224,256]{1,0:T(8,128)(2,1)S(1)}, bf16[224,256]{1,0:T(8,128)(2,1)S(1)}, bf16[224,256]{1,0:T(8,128)(2,1)S(1)},...) custom-call(s32[4]{0:T(128)S(1)} %pad_add_fusion.scal, ...), custom_call_target="tpu_custom_call" | custom-call | flops 10000000000 | bytes 30000000 | tf_op jit(solution)/shard_map/attn_fwd/pallas_call | solution.py:453
  42.4 2.3 %collective-permute-done.5.refs_3_ = bf16[9,54,216]{2,1,0:T(8,128)(2,1)S(1)} collective-permute-done((bf16[9,54,216]{2,1,0:T(8,128)(2,1)S(1)}, bf16[9,54,216]{2,1,0:T(8,128)(2,1)S(1)}, u32[]{:S(2)}, u32[]{:S(2)}) %collective-permute-start.5) | collective-permute-done | bytes 209984 | tf_op jit(solution)/shard_map/ppermute | solution.py:495
  44.6 5.9 %ffn.1 = (bf16[196,216]{1,0:T(8,128)(2,1)S(1)}, f32[224,216]{1,0:T(8,128)S(1)}, f32[8,216]{1,0:T(8,128)S(1)}, bf16[9,54,216]{2,1,0:T(8,128)(2,1)S(1)}, bf16[9,54...) custom-call(s32[4]{0:T(128)S(1)} %pad_add_fusion.scal, ...), custom_call_target="tpu_custom_call" | custom-call | flops 6000000000 | bytes 18000000 | tf_op jit(solution)/shard_map/ffn/pallas_call | solution.py:464
  50.6 12.9 %attn_bwd.1 = (bf16[196,216]{1,0:T(8,128)(2,1)S(1)}, bf16[5,54,216]{2,1,0:T(8,128)(2,1)S(1)}, bf16[5,54,216]{2,1,0:T(8,128)(2,1)S(1)}, bf16[5,54,216]{2,1,0:T(8,128)(2,1)S(1)}, bf16[5,54,216]{2,1,0:T(8,128)(2,1)S(1)}) custom-call(s32[4]{0:T(128)S(1)} %pad_add_fusion.scal, f32[224,216]{1,0:T(8,128)S(1)} %get-tuple-element.65.x_ref, ...), custom_call_target="tpu_custom_call" | custom-call | flops 14000000000 | bytes 42000000 | tf_op jit(solution)/shard_map/attn_bwd/pallas_call | solution.py:480
  63.6 1.6 %collective-permute-start.10 = (bf16[5,54,216]{2,1,0:T(8,128)(2,1)S(1)}, bf16[5,54,216]{2,1,0:T(8,128)(2,1)S(1)}, u32[]{:S(2)}, u32[]{:S(2)}) collective-permute-start(bf16[5,54,216]{2,1,0:T(8,128)(2,1)S(1)} %get-tuple-element.89), channel_id=1, source_target_pairs={{0,2},{1,3},{2,0},{3,1},{4,6},{5,7},{6,4},{7,5},{8,10},{9,11},{10,... | collective-permute-start | bytes 349928 | tf_op jit(solution)/shard_map/ppermute | solution.py:501
  65.1 0.2 collective-permute-start.15
  65.4 0.5 collective-permute-start.16
  65.9 1.1 collective-permute-start.17
  67.0 0.6 collective-permute-start.11
  67.6 2.5 %collective-permute-done.10.refs_2_ = bf16[5,54,216]{2,1,0:T(8,128)(2,1)S(1)} collective-permute-done((bf16[5,54,216]{2,1,0:T(8,128)(2,1)S(1)}, bf16[5,54,216]{2,1,0:T(8,128)(2,1)S(1)}, u32[]{:S(2)}, u32[]{:S(2)}) %collective-permute-start.10) | collective-permute-done | bytes 116672 | tf_op jit(solution)/shard_map/ppermute | solution.py:501
  70.2 13.4 %collective-permute-done.11.refs_3_ = bf16[5,54,216]{2,1,0:T(8,128)(2,1)S(1)} collective-permute-done((bf16[5,54,216]{2,1,0:T(8,128)(2,1)S(1)}, bf16[5,54,216]{2,1,0:T(8,128)(2,1)S(1)}, u32[]{:S(2)}, u32[]{:S(2)}) %collective-permute-start.11) | collective-permute-done | bytes 116672 | tf_op jit(solution)/shard_map/ppermute | solution.py:501
  83.6 1.6 %spread.1 = bf16[8,3,54,216]{3,2,1,0:T(8,128)(2,1)} custom-call(s32[12]{0:T(128)S(1)} %copy-done.6, bf16[5,54,216]{2,1,0:T(8,128)(2,1)S(1)} %get-tuple-element.94.refs_0_, bf16[5,54,216]{2,1,0:T(8,128)(2,1)S(1)} %collective-permute-done.9.refs_1_, bf16[5,54,216]{2,1,0:T(8,128)(2,1)S(1)} %collective-permute-done.10.refs_2_, ...), custom_call_target="tpu_custom_call" | custom-call | flops 1000000000 | bytes 3000000 | tf_op jit(solution)/shard_map/spread/pallas_call | solution.py:531
  85.2 3.6 %all-to-all-start.1 = ((bf16[8,3,54,216]{3,2,1,0:T(8,128)(2,1)}), bf16[8,3,54,216]{3,2,1,0:T(8,128)(2,1)S(1)}, u32[]{:S(2)}, u32[]{:S(2)}) async-start(bf16[8,3,54,216]{3,2,1,0:T(8,128)(2,1)} %spread.1), calls=%async_computation.1 | async-start | bytes 1376256 | tf_op jit(solution)/shard_map/all_to_all | solution.py:534
  88.9 0.2 collective-permute-start.6
  89.0 1.5 %collective-permute-start.7 = (bf16[196,216]{1,0:T(8,128)(2,1)S(1)}, bf16[196,216]{1,0:T(8,128)(2,1)S(1)}, u32[]{:S(2)}, u32[]{:S(2)}) collective-permute-start(bf16[196,216]{1,0:T(8,128)(2,1)S(1)} %get-tuple-element.78.refs_0_), channel_id=1, source_target_pairs={{0,2},{1,3},{2,0},{3,1},{4,6},{5,7},{6,4},{7,5},{8,10},{9,11},{10,... | collective-permute-start | bytes 254024 | tf_op jit(solution)/shard_map/ppermute | solution.py:495
  90.6 0.2 collective-permute-start.8
  90.8 0.4 collective-permute-start.12
  91.2 1.5 %collective-permute-start.13 = (bf16[196,216]{1,0:T(8,128)(2,1)S(1)}, bf16[196,216]{1,0:T(8,128)(2,1)S(1)}, u32[]{:S(2)}, u32[]{:S(2)}) collective-permute-start(bf16[196,216]{1,0:T(8,128)(2,1)S(1)} %get-tuple-element.91.refs_4_), channel_id=1, source_target_pairs={{0,2},{1,3},{2,0},{3,1},{4,6},{5,7},{6,4},{7,5},{8,10},{9,11},{10,... | collective-permute-start | bytes 254024 | tf_op jit(solution)/shard_map/ppermute | solution.py:495
  92.9 1.9 %collective-permute-done.7.refs_2_ = bf16[196,216]{1,0:T(8,128)(2,1)S(1)} collective-permute-done((bf16[196,216]{1,0:T(8,128)(2,1)S(1)}, bf16[196,216]{1,0:T(8,128)(2,1)S(1)}, u32[]{:S(2)}, u32[]{:S(2)}) %collective-permute-start.7) | collective-permute-done | bytes 84704 | tf_op jit(solution)/shard_map/ppermute | solution.py:495
  94.8 1.2 %collective-permute-done.8.refs_3_ = bf16[196,216]{1,0:T(8,128)(2,1)S(1)} collective-permute-done((bf16[196,216]{1,0:T(8,128)(2,1)S(1)}, bf16[196,216]{1,0:T(8,128)(2,1)S(1)}, u32[]{:S(2)}, u32[]{:S(2)}) %collective-permute-start.8) | collective-permute-done | bytes 84704 | tf_op jit(solution)/shard_map/ppermute | solution.py:495
  96.0 3.1 %collective-permute-done.13.refs_6_ = bf16[196,216]{1,0:T(8,128)(2,1)S(1)} collective-permute-done((bf16[196,216]{1,0:T(8,128)(2,1)S(1)}, bf16[196,216]{1,0:T(8,128)(2,1)S(1)}, u32[]{:S(2)}, u32[]{:S(2)}) %collective-permute-start.13) | collective-permute-done | bytes 84704 | tf_op jit(solution)/shard_map/ppermute | solution.py:495
  99.1 1.1 collective-permute-done.14.refs_7_
  100.2 0.7 assemble.1
  100.9 1.2 %copy.64 = f32[4,196,216]{2,0,1:T(4,128)} copy(f32[4,196,216]{2,1,0:T(8,128)S(1)} %get-tuple-element.130) | data formatting | bytes 1354752
  102.1 1.2 %copy.65 = f32[4,196,216]{2,0,1:T(4,128)} copy(f32[4,196,216]{2,1,0:T(8,128)S(1)} %get-tuple-element.131) | data formatting | bytes 1354752
  103.3 4.1 %all-to-all-done.1.refs_0_ = bf16[8,3,54,216]{3,2,1,0:T(8,128)(2,1)S(1)} async-done(((bf16[8,3,54,216]{3,2,1,0:T(8,128)(2,1)}), bf16[8,3,54,216]{3,2,1,0:T(8,128)(2,1)S(1)}, u32[]{:S(2)}, u32[]{:S(2)}) %all-to-all-start.1) | async-done | bytes 559904 | tf_op jit(solution)/shard_map/all_to_all | solution.py:534
  107.4 0.7 update.1
  108.0 0.7 copy.66
  108.7 0.7 copy.67
  109.4 0.7 copy.68
  110.2 0.7 copy.69
  110.8 0.6 copy.70
  111.4 0.6 copy.71
  112.0 0.6 copy.72
  (49 shorter events, 0.4 us)
Async XLA Ops:
  0.6 11.4 %copy-start.11 = (f32[2,12,12]{2,0,1:T(2,128)S(1)}, f32[2,12,12]{2,0,1:T(2,128)}, u32[]{:S(2)}) copy-start(f32[2,12,12]{2,0,1:T(2,128)} %param.30) | copy-start | bytes 3460
  0.7 11.4 %copy-start.7 = (f32[4,196,216]{2,0,1:T(4,128)S(1)}, f32[4,196,216]{2,0,1:T(4,128)}, u32[]{:S(2)}) copy-start(f32[4,196,216]{2,0,1:T(4,128)} %param.19) | copy-start | bytes 2032132
  1.6 10.6 %copy-start.8 = (bf16[4,196,216]{2,0,1:T(4,128)(2,1)S(1)}, bf16[4,196,216]{2,0,1:T(4,128)(2,1)}, u32[]{:S(2)}) copy-start(bf16[4,196,216]{2,0,1:T(4,128)(2,1)} %param.18) | copy-start | bytes 1016068
  1.7 21.2 %copy-start = (f32[9,216]{1,0:T(8,128)S(1)}, f32[9,216]{1,0:T(8,128)}, u32[]{:S(2)}) copy-start(f32[9,216]{1,0:T(8,128)} %refs_10_.1) | copy-start | bytes 23332
  1.7 21.2 %copy-start.6 = (s32[12]{0:T(128)S(1)}, s32[12]{0:T(128)}, u32[]{:S(2)}) copy-start(s32[12]{0:T(128)} %slot_ref.3) | copy-start | bytes 148
  2.8 20.0 %all-to-all-start = ((bf16[8,2,54,216]{3,1,2,0:T(2,128)(2,1)}), bf16[8,2,54,216]{3,1,2,0:T(2,128)(2,1)S(1)}, u32[]{:S(2)}, u32[]{:S(2)}) async-start(bf16[8,2,54,216]{3,1,2,0:T(2,128)(2,1)} %copy.56), calls=%async_computation | async-start | bytes 884736 | tf_op jit(solution)/shard_map/all_to_all | solution.py:515
  12.1 13.4 %copy-start.3 = (f32[4,216]{1,0:T(4,128)S(1)}, f32[4,216]{1,0:T(4,128)}, u32[]{:S(2)}) copy-start(f32[4,216]{1,0:T(4,128)} %refs_4_.1) | copy-start | bytes 10372
  23.5 3.2 %collective-permute-start = (bf16[4,54,216]{2,1,0:T(8,128)(2,1)S(1)}, bf16[4,54,216]{2,1,0:T(8,128)(2,1)S(1)}, u32[]{:S(2)}, u32[]{:S(2)}) collective-permute-start(bf16[4,54,216]{2,1,0:T(8,128)(2,1)S(1)} %get-tuple-element.70.refs_0_), channel_id=1, source_target_pairs={{0,1},{1,0},{2,3},{3,2},{4,5},{5,4},{6,7},{7,6},{8,9},{9,8},{10,11... | collective-permute-start | bytes 279944 | tf_op jit(solution)/shard_map/ppermute | solution.py:495
  23.6 6.0 %collective-permute-start.1 = (bf16[4,54,216]{2,1,0:T(8,128)(2,1)S(1)}, bf16[4,54,216]{2,1,0:T(8,128)(2,1)S(1)}, u32[]{:S(2)}, u32[]{:S(2)}) collective-permute-start(bf16[4,54,216]{2,1,0:T(8,128)(2,1)S(1)} %get-tuple-element.70.refs_0_), channel_id=1, source_target_pairs={{0,2},{1,3},{2,0},{3,1},{4,6},{5,7},{6,4},{7,5},{8,10},{9,11},{10,... | collective-permute-start | bytes 279944 | tf_op jit(solution)/shard_map/ppermute | solution.py:495
  25.2 6.0 %collective-permute-start.2 = (bf16[4,54,216]{2,1,0:T(8,128)(2,1)S(1)}, bf16[4,54,216]{2,1,0:T(8,128)(2,1)S(1)}, u32[]{:S(2)}, u32[]{:S(2)}) collective-permute-start(bf16[4,54,216]{2,1,0:T(8,128)(2,1)S(1)} %get-tuple-element.70.refs_0_), channel_id=1, source_target_pairs={{0,3},{1,2},{2,1},{3,0},{4,7},{5,6},{6,5},{7,4},{8,11},{9,10},{10,... | collective-permute-start | bytes 279944 | tf_op jit(solution)/shard_map/ppermute | solution.py:495
  31.2 11.1 %collective-permute-start.3 = (bf16[9,54,216]{2,1,0:T(8,128)(2,1)S(1)}, bf16[9,54,216]{2,1,0:T(8,128)(2,1)S(1)}, u32[]{:S(2)}, u32[]{:S(2)}) collective-permute-start(bf16[9,54,216]{2,1,0:T(8,128)(2,1)S(1)} %get-tuple-element.77.refs_0_), channel_id=1, source_target_pairs={{0,1},{1,0},{2,3},{3,2},{4,5},{5,4},{6,7},{7,6},{8,9},{9,8},{10,11... | collective-permute-start | bytes 629864 | tf_op jit(solution)/shard_map/ppermute | solution.py:495
  31.5 10.9 %collective-permute-start.4 = (bf16[9,54,216]{2,1,0:T(8,128)(2,1)S(1)}, bf16[9,54,216]{2,1,0:T(8,128)(2,1)S(1)}, u32[]{:S(2)}, u32[]{:S(2)}) collective-permute-start(bf16[9,54,216]{2,1,0:T(8,128)(2,1)S(1)} %get-tuple-element.77.refs_0_), channel_id=1, source_target_pairs={{0,2},{1,3},{2,0},{3,1},{4,6},{5,7},{6,4},{7,5},{8,10},{9,11},{10,... | collective-permute-start | bytes 629864 | tf_op jit(solution)/shard_map/ppermute | solution.py:495
  33.0 11.7 %collective-permute-start.5 = (bf16[9,54,216]{2,1,0:T(8,128)(2,1)S(1)}, bf16[9,54,216]{2,1,0:T(8,128)(2,1)S(1)}, u32[]{:S(2)}, u32[]{:S(2)}) collective-permute-start(bf16[9,54,216]{2,1,0:T(8,128)(2,1)S(1)} %get-tuple-element.77.refs_0_), channel_id=1, source_target_pairs={{0,3},{1,2},{2,1},{3,0},{4,7},{5,6},{6,5},{7,4},{8,11},{9,10},{10,... | collective-permute-start | bytes 629864 | tf_op jit(solution)/shard_map/ppermute | solution.py:495
  63.5 29.2 %copy-start.9 = (f32[2,54,216]{2,0,1:T(2,128)S(1)}, f32[2,54,216]{2,0,1:T(2,128)}, u32[]{:S(2)}) copy-start(f32[2,54,216]{2,0,1:T(2,128)} %param.25) | copy-start | bytes 279940
  63.5 29.2 %copy-start.10 = (f32[2,54,216]{2,0,1:T(2,128)S(1)}, f32[2,54,216]{2,0,1:T(2,128)}, u32[]{:S(2)}) copy-start(f32[2,54,216]{2,0,1:T(2,128)} %param.26) | copy-start | bytes 279940
  63.5 29.2 %copy-start.12 = (f32[2,12,12]{2,0,1:T(2,128)S(1)}, f32[2,12,12]{2,0,1:T(2,128)}, u32[]{:S(2)}) copy-start(f32[2,12,12]{2,0,1:T(2,128)} %param.31) | copy-start | bytes 3460
  63.5 29.3 %copy-start.13 = (f32[2,12,12]{2,0,1:T(2,128)S(1)}, f32[2,12,12]{2,0,1:T(2,128)}, u32[]{:S(2)}) copy-start(f32[2,12,12]{2,0,1:T(2,128)} %param.32) | copy-start | bytes 3460
  63.6 6.6 %collective-permute-start.10 = (bf16[5,54,216]{2,1,0:T(8,128)(2,1)S(1)}, bf16[5,54,216]{2,1,0:T(8,128)(2,1)S(1)}, u32[]{:S(2)}, u32[]{:S(2)}) collective-permute-start(bf16[5,54,216]{2,1,0:T(8,128)(2,1)S(1)} %get-tuple-element.89), channel_id=1, source_target_pairs={{0,2},{1,3},{2,0},{3,1},{4,6},{5,7},{6,4},{7,5},{8,10},{9,11},{10,... | collective-permute-start | bytes 349928 | tf_op jit(solution)/shard_map/ppermute | solution.py:501
  65.1 18.4 %collective-permute-start.15 = (bf16[9,54,216]{2,1,0:T(8,128)(2,1)S(1)}, bf16[9,54,216]{2,1,0:T(8,128)(2,1)S(1)}, u32[]{:S(2)}, u32[]{:S(2)}) collective-permute-start(bf16[9,54,216]{2,1,0:T(8,128)(2,1)S(1)} %get-tuple-element.99), channel_id=1, source_target_pairs={{0,1},{1,0},{2,3},{3,2},{4,5},{5,4},{6,7},{7,6},{8,9},{9,8},{10,11... | collective-permute-start | bytes 629864 | tf_op jit(solution)/shard_map/ppermute | solution.py:501
  65.4 18.2 %collective-permute-start.16 = (bf16[9,54,216]{2,1,0:T(8,128)(2,1)S(1)}, bf16[9,54,216]{2,1,0:T(8,128)(2,1)S(1)}, u32[]{:S(2)}, u32[]{:S(2)}) collective-permute-start(bf16[9,54,216]{2,1,0:T(8,128)(2,1)S(1)} %get-tuple-element.100), channel_id=1, source_target_pairs={{0,2},{1,3},{2,0},{3,1},{4,6},{5,7},{6,4},{7,5},{8,10},{9,11},{10,... | collective-permute-start | bytes 629864 | tf_op jit(solution)/shard_map/ppermute | solution.py:501
  65.9 17.7 %collective-permute-start.17 = (bf16[9,54,216]{2,1,0:T(8,128)(2,1)S(1)}, bf16[9,54,216]{2,1,0:T(8,128)(2,1)S(1)}, u32[]{:S(2)}, u32[]{:S(2)}) collective-permute-start(bf16[9,54,216]{2,1,0:T(8,128)(2,1)S(1)} %get-tuple-element.101), channel_id=1, source_target_pairs={{0,3},{1,2},{2,1},{3,0},{4,7},{5,6},{6,5},{7,4},{8,11},{9,10},{10,... | collective-permute-start | bytes 629864 | tf_op jit(solution)/shard_map/ppermute | solution.py:501
  67.0 16.6 %collective-permute-start.11 = (bf16[5,54,216]{2,1,0:T(8,128)(2,1)S(1)}, bf16[5,54,216]{2,1,0:T(8,128)(2,1)S(1)}, u32[]{:S(2)}, u32[]{:S(2)}) collective-permute-start(bf16[5,54,216]{2,1,0:T(8,128)(2,1)S(1)} %get-tuple-element.90), channel_id=1, source_target_pairs={{0,3},{1,2},{2,1},{3,0},{4,7},{5,6},{6,5},{7,4},{8,11},{9,10},{10,... | collective-permute-start | bytes 349928 | tf_op jit(solution)/shard_map/ppermute | solution.py:501
  70.2 13.4 %collective-permute-start.9 = (bf16[5,54,216]{2,1,0:T(8,128)(2,1)S(1)}, bf16[5,54,216]{2,1,0:T(8,128)(2,1)S(1)}, u32[]{:S(2)}, u32[]{:S(2)}) collective-permute-start(bf16[5,54,216]{2,1,0:T(8,128)(2,1)S(1)} %get-tuple-element.88), channel_id=1, source_target_pairs={{0,1},{1,0},{2,3},{3,2},{4,5},{5,4},{6,7},{7,6},{8,9},{9,8},{10,11... | collective-permute-start | bytes 349928 | tf_op jit(solution)/shard_map/ppermute | solution.py:501
  85.2 22.1 %all-to-all-start.1 = ((bf16[8,3,54,216]{3,2,1,0:T(8,128)(2,1)}), bf16[8,3,54,216]{3,2,1,0:T(8,128)(2,1)S(1)}, u32[]{:S(2)}, u32[]{:S(2)}) async-start(bf16[8,3,54,216]{3,2,1,0:T(8,128)(2,1)} %spread.1), calls=%async_computation.1 | async-start | bytes 1376256 | tf_op jit(solution)/shard_map/all_to_all | solution.py:534
  88.9 3.9 %collective-permute-start.6 = (bf16[196,216]{1,0:T(8,128)(2,1)S(1)}, bf16[196,216]{1,0:T(8,128)(2,1)S(1)}, u32[]{:S(2)}, u32[]{:S(2)}) collective-permute-start(bf16[196,216]{1,0:T(8,128)(2,1)S(1)} %get-tuple-element.78.refs_0_), channel_id=1, source_target_pairs={{0,1},{1,0},{2,3},{3,2},{4,5},{5,4},{6,7},{7,6},{8,9},{9,8},{10,11... | collective-permute-start | bytes 254024 | tf_op jit(solution)/shard_map/ppermute | solution.py:495
  89.0 5.7 %collective-permute-start.7 = (bf16[196,216]{1,0:T(8,128)(2,1)S(1)}, bf16[196,216]{1,0:T(8,128)(2,1)S(1)}, u32[]{:S(2)}, u32[]{:S(2)}) collective-permute-start(bf16[196,216]{1,0:T(8,128)(2,1)S(1)} %get-tuple-element.78.refs_0_), channel_id=1, source_target_pairs={{0,2},{1,3},{2,0},{3,1},{4,6},{5,7},{6,4},{7,5},{8,10},{9,11},{10,... | collective-permute-start | bytes 254024 | tf_op jit(solution)/shard_map/ppermute | solution.py:495
  90.6 5.4 %collective-permute-start.8 = (bf16[196,216]{1,0:T(8,128)(2,1)S(1)}, bf16[196,216]{1,0:T(8,128)(2,1)S(1)}, u32[]{:S(2)}, u32[]{:S(2)}) collective-permute-start(bf16[196,216]{1,0:T(8,128)(2,1)S(1)} %get-tuple-element.78.refs_0_), channel_id=1, source_target_pairs={{0,3},{1,2},{2,1},{3,0},{4,7},{5,6},{6,5},{7,4},{8,11},{9,10},{10,... | collective-permute-start | bytes 254024 | tf_op jit(solution)/shard_map/ppermute | solution.py:495
  90.8 5.2 %collective-permute-start.12 = (bf16[196,216]{1,0:T(8,128)(2,1)S(1)}, bf16[196,216]{1,0:T(8,128)(2,1)S(1)}, u32[]{:S(2)}, u32[]{:S(2)}) collective-permute-start(bf16[196,216]{1,0:T(8,128)(2,1)S(1)} %get-tuple-element.91.refs_4_), channel_id=1, source_target_pairs={{0,1},{1,0},{2,3},{3,2},{4,5},{5,4},{6,7},{7,6},{8,9},{9,8},{10,11... | collective-permute-start | bytes 254024 | tf_op jit(solution)/shard_map/ppermute | solution.py:495
  91.2 7.9 %collective-permute-start.13 = (bf16[196,216]{1,0:T(8,128)(2,1)S(1)}, bf16[196,216]{1,0:T(8,128)(2,1)S(1)}, u32[]{:S(2)}, u32[]{:S(2)}) collective-permute-start(bf16[196,216]{1,0:T(8,128)(2,1)S(1)} %get-tuple-element.91.refs_4_), channel_id=1, source_target_pairs={{0,2},{1,3},{2,0},{3,1},{4,6},{5,7},{6,4},{7,5},{8,10},{9,11},{10,... | collective-permute-start | bytes 254024 | tf_op jit(solution)/shard_map/ppermute | solution.py:495
  92.7 7.5 %collective-permute-start.14 = (bf16[196,216]{1,0:T(8,128)(2,1)S(1)}, bf16[196,216]{1,0:T(8,128)(2,1)S(1)}, u32[]{:S(2)}, u32[]{:S(2)}) collective-permute-start(bf16[196,216]{1,0:T(8,128)(2,1)S(1)} %get-tuple-element.91.refs_4_), channel_id=1, source_target_pairs={{0,3},{1,2},{2,1},{3,0},{4,7},{5,6},{6,5},{7,4},{8,11},{9,10},{10,... | collective-permute-start | bytes 254024 | tf_op jit(solution)/shard_map/ppermute | solution.py:495
  92.8 14.5 %copy-start.1 = (f32[9,216]{1,0:T(8,128)S(1)}, f32[9,216]{1,0:T(8,128)}, u32[]{:S(2)}) copy-start(f32[9,216]{1,0:T(8,128)} %refs_11_.1) | copy-start | bytes 23332
  92.8 14.5 %copy-start.2 = (f32[9,216]{1,0:T(8,128)S(1)}, f32[9,216]{1,0:T(8,128)}, u32[]{:S(2)}) copy-start(f32[9,216]{1,0:T(8,128)} %refs_12_.1) | copy-start | bytes 23332
  92.8 14.5 %copy-start.4 = (f32[4,216]{1,0:T(4,128)S(1)}, f32[4,216]{1,0:T(4,128)}, u32[]{:S(2)}) copy-start(f32[4,216]{1,0:T(4,128)} %refs_5_.1) | copy-start | bytes 10372
  92.9 14.5 %copy-start.5 = (f32[4,216]{1,0:T(4,128)S(1)}, f32[4,216]{1,0:T(4,128)}, u32[]{:S(2)}) copy-start(f32[4,216]{1,0:T(4,128)} %refs_6_.1) | copy-start | bytes 10372

commit v3 on v2

--- a/solution.py
+++ b/solution.py
@@ -228,26 +228,22 @@
         gw_refs[h][8, 16:25] = nt(lo, pm).astype(bf16)
 
 
-def attn_bwd_kernel(
-    scal, x_ref, a_ref, dmid_ref, norm_ref, gn2_ref, kron_ref, mask_ref, q_ref, k_ref, v_ref, o_ref, s_ref, p_ref,
-    *refs, parts, unroll
+def scores_back_kernel(
+    scal, dmid_ref, kron_ref, mask_ref, q_ref, k_ref, v_ref, s_ref, p_ref, *refs, parts, unroll
 ):
     w_refs, refs = refs[:parts], refs[parts:]
-    tg_ref, gw_refs, refs = refs[0], refs[1 : 1 + parts], refs[1 + parts :]
-    ws_ref, do_ref, gq_ref, gk_ref, gv_ref, g0_ref, g1_ref, tmp_ref, fm_ref, small_ref = refs
+    gq_ref, gkb_ref, gvb_ref, mix_ref, wo_ref, do_ref, gk_ref, gv_ref, g0_ref, g1_ref, fm_ref = refs
     heads = kron_ref.shape[1] // PITCH
     n = heads * PITCH
-    hd = parts
     scale = HD ** (-0.5)
-    ws_ref[...] = jnp.zeros_like(ws_ref)
-    for b in range(4):
-        load_weight(ws_ref.at[b], w_refs, b)
+    wo_ref[...] = jnp.zeros_like(wo_ref)
+    load_weight(wo_ref, w_refs, 3)
     f = dmid_ref[...].astype(bf16)
     lane = iota((1, 256), 1)
     rest = lane & 63
     lane_head = ((lane >> 6) ^ scal[0]) * 3 + (rest >= 18).astype(jnp.int32) + (rest >= 36).astype(jnp.int32)
     lane_keep = ((lane_head < scal[2]) & (rest < 54)).astype(f32)
-    do_ref[...] = (nt(f, ws_ref[3]) * lane_keep).astype(bf16)
+    do_ref[...] = (nt(f, wo_ref[...]) * lane_keep).astype(bf16)
     g0_ref[...] = jnp.zeros_like(g0_ref)
     g1_ref[...] = jnp.zeros_like(g1_ref)
     gk_ref[...] = jnp.zeros_like(gk_ref)
@@ -262,12 +258,12 @@
         v = v_ref[...]
         k = k_ref[...]
         p = p_ref[y]
-        ph, plo = split2(p)
+        ph = p.astype(bf16)
         dr = nt(dx, v).astype(bf16)
         drt = nt(v, dx).astype(bf16)
         dp = nn(drt, kron_ref[2])
         dt = p * (dp - jnp.sum(dp * p, axis=0, keepdims=True))
-        dth, dtl = split2(dt)
+        dth = dt.astype(bf16)
         g1_ref[...] += nn(dr, ph)
         srow = (nt(qx, k) * scale).astype(bf16)
         g0_ref[...] += nn(srow, dth)
@@ -281,23 +277,8 @@
         return 0
 
     lax.fori_loop(0, SIDE, group, 0, unroll=unroll)
-    gq = gq_ref[...]
-    gk = (gk_ref[...] * scale).astype(bf16)
-    gv = gv_ref[...].astype(bf16)
-    a = a_ref[...]
-    da = nn(gq, ws_ref[0]) + nn(gk, ws_ref[1]) + nn(gv, ws_ref[2])
-    for b, (g, t) in enumerate(((gq, a), (gk, a), (gv, a), (o_ref[...], f))):
-        gw = tn(g, t).astype(bf16)
-        for h in range(hd):
-            gw_refs[h][b] = gw[64 * h : 64 * h + 54]
-    z, inv = ln_stats(x_ref[...])
-    small_ref[...] = jnp.zeros_like(small_ref)
-    small_ref[0:1, :] = jnp.sum(da * z, axis=0, keepdims=True)
-    small_ref[1:2, :] = jnp.sum(da, axis=0, keepdims=True)
-    small_ref[2:4, :] = gn2_ref[0:2, :]
-    tmp_ref[...] = dmid_ref[...] + ln_back(da, z, inv, norm_ref[0:1, :])
-    for y in range(SIDE):
-        tg_ref[SIDE * y : SIDE * (y + 1), :] = tmp_ref[PITCH * y : PITCH * y + SIDE, :].astype(bf16)
+    gkb_ref[...] = (gk_ref[...] * scale).astype(bf16)
+    gvb_ref[...] = gv_ref[...].astype(bf16)
     same = (iota((n, n), 0) & (PITCH - 1)) == (iota((n, n), 1) & (PITCH - 1))
     ex = (true_head(iota((n, heads), 0), scal[0]) == iota((n, heads), 1)).astype(bf16)
     for i, ref in enumerate((g0_ref, g1_ref)):
@@ -306,11 +287,41 @@
         cols = nn(hi, ex) + nn(lo, ex)
         hi, lo = split2(cols)
         if i == 0:
-            small_ref[8:20, 0:heads] = tn(hi, ex) + tn(lo, ex)
+            mix_ref[i] = tn(hi, ex) + tn(lo, ex)
         else:
-            small_ref[8:20, 128 : 128 + heads] = tn(ex, hi) + tn(ex, lo)
+            mix_ref[i] = tn(ex, hi) + tn(ex, lo)
+
+
+def weights_back_kernel(
+    scal, x_ref, a_ref, dmid_ref, norm_ref, gn2_ref, o_ref, gq_ref, gk_ref, gv_ref, mix_ref, *refs, parts
+):
+    w_refs, refs = refs[:parts], refs[parts:]
+    tg_ref, gw_refs, refs = refs[0], refs[1 : 1 + parts], refs[1 + parts :]
+    ws_ref, tmp_ref, small_ref = refs
+    heads = mix_ref.shape[1]
+    ws_ref[...] = jnp.zeros_like(ws_ref)
+    for b in range(3):
+        load_weight(ws_ref.at[b], w_refs, b)
+    gq, gk, gv = gq_ref[...], gk_ref[...], gv_ref[...]
+    a = a_ref[...]
+    f = dmid_ref[...].astype(bf16)
+    for b, (g, t) in enumerate(((gq, a), (gk, a), (gv, a), (o_ref[...], f))):
+        gw = tn(g, t).astype(bf16)
+        for h in range(parts):
+            gw_refs[h][b] = gw[64 * h : 64 * h + 54]
+    da = nn(gq, ws_ref[0]) + nn(gk, ws_ref[1]) + nn(gv, ws_ref[2])
+    z, inv = ln_stats(x_ref[...])
+    small_ref[...] = jnp.zeros_like(small_ref)
+    small_ref[0:1, :] = jnp.sum(da * z, axis=0, keepdims=True)
+    small_ref[1:2, :] = jnp.sum(da, axis=0, keepdims=True)
+    small_ref[2:4, :] = gn2_ref[0:2, :]
+    for i in range(2):
+        small_ref[8 : 8 + heads, 128 * i : 128 * i + heads] = mix_ref[i]
+    tmp_ref[...] = dmid_ref[...] + ln_back(da, z, inv, norm_ref[0:1, :])
+    for y in range(SIDE):
+        tg_ref[SIDE * y : SIDE * (y + 1), :] = tmp_ref[PITCH * y : PITCH * y + SIDE, :].astype(bf16)
     hi, lo = split2(small_ref[...])
-    for h in range(hd):
+    for h in range(parts):
         gw_refs[h][4, 0:24] = hi
         gw_refs[h][4, 24:48] = lo
         gw_refs[h][4, 48:54] = jnp.zeros((6, hi.shape[1]), bf16)
@@ -344,24 +355,45 @@
     return acc
 
 
+WIDE = 40
+SMALL = 13
+
+
 def spread_kernel(slot_ref, *refs, parts):
-    attn, ffn_refs, out_ref = refs[:parts], refs[parts : 2 * parts], refs[2 * parts]
-    ranks, per = out_ref.shape[0], out_ref.shape[1] - 1
-    out_ref[...] = jnp.zeros_like(out_ref)
+    attn, ffn_refs, out_ref, acc_ref, sm_ref = refs[:parts], refs[parts : 2 * parts], *refs[2 * parts :]
+    ranks, per = out_ref.shape[:2]
+    dim = attn[0].shape[2]
+    for i in range(ranks * per):
+        acc_ref[i] = jnp.zeros_like(acc_ref[i])
     for b in range(12):
-        slot = slot_ref[b]
         block = total(attn, b) if b < 4 else total(ffn_refs, b - 4)
-        out_ref[slot // per, slot % per] = block.astype(bf16)
+        acc_ref[slot_ref[b], :, 0:dim] = block.astype(bf16)
     norm = total(attn, 4)
-    norm_hi, norm_lo = split2(norm[0:24] + norm[24:48])
+    norm = norm[0:24] + norm[24:48]
     conv = total(ffn_refs, 8)
-    conv_hi, conv_lo = split2(conv[0:9] + conv[16:25])
-    for i in range(ranks):
-        out_ref[i, per, 0:20] = norm_hi[0:20]
-        out_ref[i, per, 20:29] = conv_hi
-        out_ref[i, per, 29:38] = conv_lo
-        out_ref[i, per, 38:42] = norm_lo[0:4]
-        out_ref[i, per, 42:54] = norm_lo[8:20]
+    conv = conv[0:9] + conv[16:25]
+    sm_ref[...] = jnp.zeros_like(sm_ref)
+    flat_ref = sm_ref.at[per]
+    flat_ref[0:4, 0:dim] = norm[0:4]
+    flat_ref[4:SMALL, 0:dim] = conv
+    flat = flat_ref[0:16, :]
+    for j in range(6):
+        at = SMALL * (j if j < 4 else j - 4)
+        moved = pltpu.roll(flat, (dim - WIDE * j) % 256, 1)
+        sm_ref[j // 4, at : at + SMALL, :] = moved[0:SMALL]
+    mix = norm[8:20]
+    heads = mix.shape[0]
+    flat_ref[16:28, 0:128] = mix[:, 0:128]
+    flat_ref[16:28, 128:dim] = mix[:, 128:dim]
+    mix = flat_ref[16:28, :]
+    lane = iota(mix.shape, 1)
+    mix = jnp.where(lane < heads, mix, 0.0) + pltpu.roll(jnp.where(lane >= 128, mix, 0.0), 128 + heads, 1)
+    sm_ref[1, 2 * SMALL : 2 * SMALL + heads, :] = pltpu.roll(mix, dim, 1)
+    free = iota((acc_ref.shape[1], 256), 1) >= dim
+    small = [jnp.where(free, sm_ref[i, 0 : acc_ref.shape[1], :], 0.0).astype(bf16) for i in range(per)]
+    for r in range(ranks):
+        for i in range(per):
+            out_ref[r, i] = acc_ref[r * per + i] + small[i]
 
 
 def adam(w, g, one, two, rate, decay):
@@ -372,27 +404,42 @@
     return w - rate * (hat_one / (jnp.sqrt(hat_two) + 1e-08) + decay * w), one_new, two_new
 
 
-def update_kernel(*refs):
-    got_ref, ins, outs = refs[0], refs[1:13], refs[13:]
-    ranks, per = got_ref.shape[0], got_ref.shape[1] - 1
+def update_kernel(got_ref, *refs):
+    ins, outs, (g_ref, sm_ref, flat_ref) = refs[0:12], refs[12:25], refs[25:]
+    ranks, per = got_ref.shape[:2]
+    dim = ins[0].shape[2]
+    rows = got_ref.shape[2]
     for i in range(per):
         g = got_ref[0, i].astype(f32)
         for r in range(1, ranks):
             g = g + got_ref[r, i].astype(f32)
-        w, one, two = adam(ins[0][i], g, ins[1][i], ins[2][i], 0.06, 0.05)
-        outs[0][i], outs[1][i], outs[2][i], outs[3][i] = w, one, two, w.astype(bf16)
-    g = got_ref[0, per].astype(f32)
-    for r in range(1, ranks):
-        g = g + got_ref[r, per].astype(f32)
-    heads = ins[6].shape[1]
-    norm = g[0:4] + g[38:42]
-    mix = g[8:20] + g[42:54]
-    conv = g[20:29] + g[29:38]
-    outs[4][...], outs[5][...], outs[6][...] = adam(ins[3][...], norm, ins[4][...], ins[5][...], 0.2, 0.0)
+        g_ref[:, i, :] = g[:, 0:dim]
+        sm_ref[i, 0:rows, :] = g
+    w, one, two = adam(ins[0][...], g_ref[...], ins[1][...], ins[2][...], 0.06, 0.05)
+    outs[0][...], outs[1][...], outs[2][...], outs[3][...] = w, one, two, w.astype(bf16)
+    flat = jnp.zeros((SMALL, 256), f32)
+    lane = iota(flat.shape, 1)
+    for j in range(6):
+        at = SMALL * (j if j < 4 else j - 4)
+        moved = pltpu.roll(sm_ref[j // 4, at : at + SMALL, :], (WIDE * j - dim) % 256, 1)
+        flat = flat + jnp.where((lane >= WIDE * j) & (lane < WIDE * (j + 1)), moved, 0.0)
+    flat_ref[0:SMALL, :] = flat
+    heads = ins[6].shape[0]
+    mix = pltpu.roll(sm_ref[1, 2 * SMALL : 2 * SMALL + heads, :], 256 - dim, 1)
+    flat_ref[16 : 16 + heads, :] = mix
+    flat_ref[32 : 32 + heads, :] = pltpu.roll(mix, 256 - heads, 1)
+    outs[4][...], outs[5][...], outs[6][...] = adam(
+        ins[3][...], flat_ref[0:4, 0:dim], ins[4][...], ins[5][...], 0.2, 0.0
+    )
     for i in range(2):
-        w, one, two = adam(ins[6][i], mix[:, 128 * i : 128 * i + heads], ins[7][i], ins[8][i], 0.2, 0.0)
-        outs[7][i], outs[8][i], outs[9][i] = w, one, two
-    outs[10][...], outs[11][...], outs[12][...] = adam(ins[9][...], conv, ins[10][...], ins[11][...], 0.2, 0.05)
+        w, one, two = adam(
+            ins[6][:, i, :], flat_ref[16 * (i + 1) : 16 * (i + 1) + heads, 0:heads], ins[7][:, i, :], ins[8][:, i, :],
+            0.2, 0.0,
+        )
+        outs[7][:, i, :], outs[8][:, i, :], outs[9][:, i, :] = w, one, two
+    outs[10][...], outs[11][...], outs[12][...] = adam(
+        ins[9][...], flat_ref[4:SMALL, 0:dim], ins[10][...], ins[11][...], 0.2, 0.05
+    )
 
 
 def assemble_kernel(scal, *refs, parts):
@@ -474,20 +521,30 @@
     )(scal, mid, dy, norm_params, *w)
 
 
-def attn_bwd(scal, x, a, dmid, norm_params, gn2, kron, mask, q, k, v, o, s, p, w, unroll=7):
+def scores_back(scal, dmid, kron, mask, q, k, v, s, p, w, unroll=7):
+    pad, dim = dmid.shape
+    n = kron.shape[1]
+    heads = n // PITCH
+    return call(
+        scores_back_kernel, "scores_back", 1, 8 + len(w),
+        [SDS((pad, 256), bf16)] * 3 + [SDS((2, heads, heads), f32)],
+        [
+            pltpu.VMEM((256, dim), bf16), pltpu.VMEM((pad, 256), bf16),
+            pltpu.VMEM((pad, 256), f32), pltpu.VMEM((pad, 256), f32),
+            pltpu.VMEM((n, n), f32), pltpu.VMEM((n, n), f32), pltpu.VMEM((n, 256), f32),
+        ],
+        mb=24, micros=12, parts=len(w), unroll=unroll,
+    )(scal, dmid, kron, mask, q, k, v, s, p, *w)
+
+
+def weights_back(scal, x, a, dmid, norm_params, gn2, o, gq, gk, gv, mix, w):
     pad, dim = x.shape
-    n = kron.shape[1]
     return call(
-        attn_bwd_kernel, "attn_bwd", 1, 13 + len(w),
+        weights_back_kernel, "weights_back", 1, 10 + len(w),
         [SDS((SIDE * SIDE, dim), bf16)] + [SDS((5, 54, dim), bf16)] * len(w),
-        [
-            pltpu.VMEM((4, 256, dim), bf16), pltpu.VMEM((pad, 256), bf16), pltpu.VMEM((pad, 256), bf16),
-            pltpu.VMEM((pad, 256), f32), pltpu.VMEM((pad, 256), f32),
-            pltpu.VMEM((n, n), f32), pltpu.VMEM((n, n), f32), pltpu.VMEM((pad, dim), f32), pltpu.VMEM((n, 256), f32),
-            pltpu.VMEM((24, dim), f32),
-        ],
-        mb=24, micros=14, parts=len(w), unroll=unroll,
-    )(scal, x, a, dmid, norm_params, gn2, kron, mask, q, k, v, o, s, p, *w)
+        [pltpu.VMEM((3, 256, dim), bf16), pltpu.VMEM((pad, dim), f32), pltpu.VMEM((24, dim), f32)],
+        mb=24, micros=3, parts=len(w),
+    )(scal, x, a, dmid, norm_params, gn2, o, gq, gk, gv, mix, *w)
 
 
 def from_peers(x, axis):
@@ -500,6 +557,28 @@
     return [messages[0]] + [
         lax.ppermute(messages[k], axis, [(i, i ^ k) for i in range(n)]) for k in range(1, n)
     ]
+
+
+def swap(t):
+    return jnp.swapaxes(t, 0, 1)
+
+
+def whole(*shape):
+    return pl.BlockSpec(shape, lambda i: (0,) * len(shape))
+
+
+def staged(body, name, ins, outs, scratch=(), micros=1):
+    return pl.pallas_call(
+        body,
+        grid=(1,),
+        in_specs=[whole(*t.shape) for t in ins],
+        out_specs=[whole(*t.shape) for t in outs],
+        out_shape=outs,
+        scratch_shapes=scratch,
+        compiler_params=pltpu.CompilerParams(vmem_limit_bytes=16 << 20),
+        cost_estimate=pl.CostEstimate(flops=micros * 1000000000, transcendentals=0, bytes_accessed=micros * 3000000),
+        name=name,
+    )(*ins)
 
 
 def local(
@@ -511,8 +590,8 @@
     ranks = lax.axis_size("dp")
     place_id = lax.axis_index("head").astype(jnp.int32)
     scal = jnp.concatenate([place_id[None], image_count, subnet_heads, subnet_width])
-    (mine,) = call(cast_kernel, "cast", 0, 1, [SDS((ranks, slots, rows, dim), bf16)])(master)
-    every = lax.all_to_all(mine, "dp", split_axis=0, concat_axis=0, tiled=True)
+    (mine,) = staged(cast_kernel, "cast", [swap(master)], [SDS((ranks, rows, slots, dim), bf16)])
+    every = lax.all_to_all(jnp.swapaxes(mine, 1, 2), "dp", split_axis=0, concat_axis=0, tiled=True)
     x, a, dy, kron, mask, bias = prep(scal, tokens, cotangent, norm_params, talk)
     attn_w, ffn_w = call(
         select_kernel, "select", 1, 2, [SDS((4, rows, dim), bf16), SDS((9, rows, dim), bf16)]
@@ -522,24 +601,34 @@
     ffn_w = [ffn_w] + from_peers(ffn_w, "head")
     mid, q, k, v, o, s, p = attn_fwd(scal, x, a, kron, mask, bias, attn_w)
     out, dmid, gn2, *ffn_g = ffn(scal, mid, dy, norm_params, ffn_w)
-    tg, *attn_g = attn_bwd(scal, x, a, dmid, norm_params, gn2, kron, mask, q, k, v, o, s, p, attn_w)
+    gq, gk, gv, mix = scores_back(scal, dmid, kron, mask, q, k, v, s, p, attn_w)
     ffn_g = exchange(ffn_g, "head")
     outs = [out] + from_peers(out, "head")
+    gq, ffn_g[1:], outs[1:] = lax.optimization_barrier((gq, ffn_g[1:], outs[1:]))
+    tg, *attn_g = weights_back(scal, x, a, dmid, norm_params, gn2, o, gq, gk, gv, mix, attn_w)
     attn_g = exchange(attn_g, "head")
     tg, attn_g[1:] = lax.optimization_barrier((tg, attn_g[1:]))
     tgs = [tg] + from_peers(tg, "head")
     (message,) = call(
-        spread_kernel, "spread", 1, 2 * parts, [SDS((ranks, slots + 1, rows, dim), bf16)], parts=parts
+        spread_kernel, "spread", 1, 2 * parts, [SDS((ranks, slots, rows, 256), bf16)],
+        [pltpu.VMEM((ranks * slots, rows, 256), bf16), pltpu.VMEM((slots + 1, 64, 256), f32)], parts=parts,
     )(block_slot, *attn_g, *ffn_g)
     got = lax.all_to_all(message, "dp", split_axis=0, concat_axis=0, tiled=True)
     images = SDS((parts,) + tokens.shape[1:], f32)
     output, token_grad = call(assemble_kernel, "assemble", 1, 2 * parts, [images, images], parts=parts)(
         scal, *outs, *tgs
     )
-    state = (master, master_m1, master_m2, norm_params, norm_m1, norm_m2, talk, talk_m1, talk_m2, conv, conv_m1, conv_m2)
+    state = [
+        swap(master), swap(master_m1), swap(master_m2), norm_params, norm_m1, norm_m2,
+        swap(talk), swap(talk_m1), swap(talk_m2), conv, conv_m1, conv_m2,
+    ]
     shapes = [SDS(t.shape, f32) for t in state]
-    shapes.insert(3, SDS(master.shape, bf16))
-    new = call(update_kernel, "update", 0, 13, shapes)(got, *state)
+    shapes.insert(3, SDS(state[0].shape, bf16))
+    new = staged(
+        update_kernel, "update", [got, *state], shapes,
+        [pltpu.VMEM((rows, slots, dim), f32), pltpu.VMEM((slots, 64, 256), f32), pltpu.VMEM((48, 256), f32)],
+    )
+    new = [swap(t) if t.ndim == 3 else t for t in new]
     return (output, token_grad, *new)
 
 

time: 113 us -> 101 us (0.89)
  waiting for transfers between devices: 44.5 us -> 36.5 us
  local copies, waits for them, and re-layouts: 9.45 us -> 4.8 us
  Pallas kernels: 33 us -> 34.3 us
    ppermute x6, waiting for transfers between devices: 15.9 us -> 7.56 us  [exchange(): lax.ppermute(messages[k], axis, [(i, i ^ k) for i in range(n)])]
    unnamed x45 -> x37, local copies, waits for them, and re-layouts: 8.27 us -> 3.57 us
    ppermute x12, waiting for transfers between devices: 14.1 us -> 15.6 us  [from_peers(): lax.ppermute(x, axis, [(i, i ^ k) for i in range(n)])]
    ppermute x6, starting transfers between devices: 4.08 us -> 2.72 us  [exchange(): lax.ppermute(messages[k], axis, [(i, i ^ k) for i in range(n)])]
    pallas_call x4 -> x5, Pallas kernels: 15.3 us -> 16.7 us  [the longest x1 12.6 us: scores_back(): call(scores_back_kernel, 'scores_back', 1, 8 + len(w), [SDS((pad, 256), b...]
    all_to_all x1, waiting for transfers between devices: 4.08 us -> 2.94 us  [local(): got = lax.all_to_all(message, 'dp', split_axis=0, concat_axis=0, tiled=True)]
  transfers between devices with their start and end apart: 20 -> 20, of which waited for: 11 -> 11; matrix products, arithmetic and copies ran while one was open for 2% -> 3% of each run, Pallas kernels for 10% -> 24%
where the time goes in v3:
time: 101 us; the launch traced here: 100 us
  waiting for transfers between devices  36.5 us (36%)
  Pallas kernels  34.3 us (34%)
  starting transfers between devices  21.6 us (21%)
  local copies, waits for them, and re-layouts  4.8 us (5%)
  between operations  3.07 us (3%)
    ppermute x12, waiting for transfers between devices, from_peers(): lax.ppermute(x, axis, [(i, i ^ k) for i in range(n)])  15.6 us
    pallas_call x1, Pallas kernels, scores_back(): call(scores_back_kernel, 'scores_back', 1, 8 + len(w), [SDS((pad, 256), b...  12.6 us
    all_to_all x1, waiting for transfers between devices, local(): lax.all_to_all(jnp.swapaxes(mine, 1, 2), 'dp', split_axis=0, concat_axis=...  10.4 us
    pallas_call x1, Pallas kernels, attn_fwd(): call(attn_fwd_kernel, 'attn_fwd', 1, 5 + len(w), [SDS((pad, dim), f32)] +...  9.25 us
    ppermute x12, starting transfers between devices, from_peers(): lax.ppermute(x, axis, [(i, i ^ k) for i in range(n)])  7.78 us
    ppermute x6, waiting for transfers between devices, exchange(): lax.ppermute(messages[k], axis, [(i, i ^ k) for i in range(n)])  7.56 us
    all_to_all x1, starting transfers between devices, local(): lax.all_to_all(jnp.swapaxes(mine, 1, 2), 'dp', split_axis=0, concat_axis=...  7.25 us
    pallas_call x1, Pallas kernels, ffn(): call(ffn_kernel, 'ffn', 1, 3 + len(w), [SDS((SIDE * SIDE, dim), bf16), SD...  5.91 us
  transfers between devices with their start and end apart: 20, of which 11 were waited for; matrix products, arithmetic and copies ran while one was open for 3% of the time, Pallas kernels for 24%

profile of v3, /device:TPU:0, one launch (start us, length us, event | category | flops | bytes accessed | tf_op | source)
XLA Modules:
  0.0 100.4 jit_solution(17173208895741536908)
XLA Ops:
  0.7 0.9 copy-done.1
  1.6 0.9 cast.1
  2.5 7.3 %all-to-all-start = ((bf16[8,2,54,216]{3,1,2,0:T(2,128)(2,1)}), bf16[8,2,54,216]{3,1,2,0:T(2,128)(2,1)S(1)}, u32[]{:S(2)}, u32[]{:S(2)}) async-start(bf16[8,2,54,216]{3,1,2,0:T(2,128)(2,1)} %bitcast.2), calls=%async_computation | async-start | bytes 884736 | tf_op jit(solution)/shard_map/all_to_all | solution.py:594
  11.8 0.2 copy.40.cot_ref
  11.9 0.1 pad_add_fusion.scal
  12.0 10.4 %all-to-all-done = bf16[8,2,54,216]{3,1,2,0:T(2,128)(2,1)S(1)} async-done(((bf16[8,2,54,216]{3,1,2,0:T(2,128)(2,1)}), bf16[8,2,54,216]{3,1,2,0:T(2,128)(2,1)S(1)}, u32[]{:S(2)}, u32[]{:S(2)}) %all-to-all-start) | async-done | bytes 373280 | tf_op jit(solution)/shard_map/all_to_all | solution.py:594
  22.4 0.1 copy.42.every_ref
  22.5 0.6 select.1
  23.2 0.1 collective-permute-start.2
  23.3 1.6 %collective-permute-start.1 = (bf16[4,54,216]{2,1,0:T(8,128)(2,1)S(1)}, bf16[4,54,216]{2,1,0:T(8,128)(2,1)S(1)}, u32[]{:S(2)}, u32[]{:S(2)}) collective-permute-start(bf16[4,54,216]{2,1,0:T(8,128)(2,1)S(1)} %get-tuple-element.81.refs_0_), channel_id=1, source_target_pairs={{0,2},{1,3},{2,0},{3,1},{4,6},{5,7},{6,4},{7,5},{8,10},{9,11},{10,... | collective-permute-start | bytes 279944 | tf_op jit(solution)/shard_map/ppermute | solution.py:552
  24.8 0.3 collective-permute-start
  25.1 1.2 %prep.1 = (f32[224,216]{1,0:T(8,128)S(1)}, bf16[224,216]{1,0:T(8,128)(2,1)S(1)}, f32[224,216]{1,0:T(8,128)S(1)}, bf16[4,192,192]{2,1,0:T(8,128)(2,1)S(1)}, bf16[...) custom-call(s32[4]{0:T(128)S(1)} %pad_add_fusion.scal, bf16[4,196,216]{2,1,0:T(8,128)(2,1)S(1)} %copy.39.tok_ref, ...), custom_call_target="tpu_custom_call" | custom-call | flops 1000000000 | bytes 3000000 | tf_op jit(solution)/shard_map/prep/pallas_call | solution.py:475
  26.4 2.3 %collective-permute-done.2.refs_3_ = bf16[4,54,216]{2,1,0:T(8,128)(2,1)S(1)} collective-permute-done((bf16[4,54,216]{2,1,0:T(8,128)(2,1)S(1)}, bf16[4,54,216]{2,1,0:T(8,128)(2,1)S(1)}, u32[]{:S(2)}, u32[]{:S(2)}) %collective-permute-start.2) | collective-permute-done | bytes 93344 | tf_op jit(solution)/shard_map/ppermute | solution.py:552
  28.6 2.5 %collective-permute-done.1.refs_2_ = bf16[4,54,216]{2,1,0:T(8,128)(2,1)S(1)} collective-permute-done((bf16[4,54,216]{2,1,0:T(8,128)(2,1)S(1)}, bf16[4,54,216]{2,1,0:T(8,128)(2,1)S(1)}, u32[]{:S(2)}, u32[]{:S(2)}) %collective-permute-start.1) | collective-permute-done | bytes 93344 | tf_op jit(solution)/shard_map/ppermute | solution.py:552
  31.1 0.0 collective-permute-start.5
  31.2 1.7 %collective-permute-start.4 = (bf16[9,54,216]{2,1,0:T(8,128)(2,1)S(1)}, bf16[9,54,216]{2,1,0:T(8,128)(2,1)S(1)}, u32[]{:S(2)}, u32[]{:S(2)}) collective-permute-start(bf16[9,54,216]{2,1,0:T(8,128)(2,1)S(1)} %get-tuple-element.88.refs_0_), channel_id=1, source_target_pairs={{0,2},{1,3},{2,0},{3,1},{4,6},{5,7},{6,4},{7,5},{8,10},{9,11},{10,... | collective-permute-start | bytes 629864 | tf_op jit(solution)/shard_map/ppermute | solution.py:552
  32.8 0.2 collective-permute-start.3
  33.0 9.3 %attn_fwd.1 = (f32[224,216]{1,0:T(8,128)S(1)}, bf16[224,256]{1,0:T(8,128)(2,1)S(1)}, bf16[224,256]{1,0:T(8,128)(2,1)S(1)}, bf16[224,256]{1,0:T(8,128)(2,1)S(1)},...) custom-call(s32[4]{0:T(128)S(1)} %pad_add_fusion.scal, ...), custom_call_target="tpu_custom_call" | custom-call | flops 10000000000 | bytes 30000000 | tf_op jit(solution)/shard_map/attn_fwd/pallas_call | solution.py:500
  42.3 2.9 %collective-permute-done.4.refs_2_ = bf16[9,54,216]{2,1,0:T(8,128)(2,1)S(1)} collective-permute-done((bf16[9,54,216]{2,1,0:T(8,128)(2,1)S(1)}, bf16[9,54,216]{2,1,0:T(8,128)(2,1)S(1)}, u32[]{:S(2)}, u32[]{:S(2)}) %collective-permute-start.4) | collective-permute-done | bytes 209984 | tf_op jit(solution)/shard_map/ppermute | solution.py:552
  45.2 5.9 %ffn.1 = (bf16[196,216]{1,0:T(8,128)(2,1)S(1)}, f32[224,216]{1,0:T(8,128)S(1)}, f32[8,216]{1,0:T(8,128)S(1)}, bf16[9,54,216]{2,1,0:T(8,128)(2,1)S(1)}, bf16[9,54...) custom-call(s32[4]{0:T(128)S(1)} %pad_add_fusion.scal, ...), custom_call_target="tpu_custom_call" | custom-call | flops 6000000000 | bytes 18000000 | tf_op jit(solution)/shard_map/ffn/pallas_call | solution.py:511
  51.1 0.1 collective-permute-start.11
  51.2 1.5 %collective-permute-start.10 = (bf16[196,216]{1,0:T(8,128)(2,1)S(1)}, bf16[196,216]{1,0:T(8,128)(2,1)S(1)}, u32[]{:S(2)}, u32[]{:S(2)}) collective-permute-start(bf16[196,216]{1,0:T(8,128)(2,1)S(1)} %get-tuple-element.89.refs_0_), channel_id=1, source_target_pairs={{0,2},{1,3},{2,0},{3,1},{4,6},{5,7},{6,4},{7,5},{8,10},{9,11},{10,... | collective-permute-start | bytes 254024 | tf_op jit(solution)/shard_map/ppermute | solution.py:552
  52.7 0.3 collective-permute-start.9
  53.0 0.2 collective-permute-start.6
  53.2 0.6 collective-permute-start.7
  53.8 2.5 %collective-permute-done.11.refs_3_ = bf16[196,216]{1,0:T(8,128)(2,1)S(1)} collective-permute-done((bf16[196,216]{1,0:T(8,128)(2,1)S(1)}, bf16[196,216]{1,0:T(8,128)(2,1)S(1)}, u32[]{:S(2)}, u32[]{:S(2)}) %collective-permute-start.11) | collective-permute-done | bytes 84704 | tf_op jit(solution)/shard_map/ppermute | solution.py:552
  56.3 12.6 %scores_back.1 = (bf16[224,256]{1,0:T(8,128)(2,1)S(1)}, bf16[224,256]{1,0:T(8,128)(2,1)S(1)}, bf16[224,256]{1,0:T(8,128)(2,1)S(1)}, f32[2,12,12]{2,1,0:T(8,128)S(1)}) custom-call(s32[4]{0:T(128)S(1)} %pad_add_fusion.scal, f32[224,216]{1,0:T(8,128)S(1)} %get-tuple-element.90.dmid_ref, bf16[4,192,192]{2,1,0:T(8,128)(2,1)S(1)} %get-tuple-element.78.kron_ref, ...), custom_call_target="tpu_custom_call" | custom-call | flops 12000000000 | bytes 36000000 | tf_op jit(solution)/shard_map/scores_back/pallas_call | solution.py:528
  68.9 0.0 collective-permute-done.6.refs_5_
  68.9 0.6 collective-permute-done.8.refs_7_
  69.5 1.1 %weights_back.1 = (bf16[196,216]{1,0:T(8,128)(2,1)S(1)}, bf16[5,54,216]{2,1,0:T(8,128)(2,1)S(1)}, bf16[5,54,216]{2,1,0:T(8,128)(2,1)S(1)}, bf16[5,54,216]{2,1,0:T(8,128)(2,1)S(1)}, bf16[5,54,216]{2,1,0:T(8,128)(2,1)S(1)}) custom-call(s32[4]{0:T(128)S(1)} %pad_add_fusion.scal, f32[224,216]{1,0:T(8,128)S(1)} %get-tuple-element.76.x_ref, ...), custom_call_target="tpu_custom_call" | custom-call | flops 3000000000 | bytes 9000000 | tf_op jit(solution)/shard_map/weights_back/pallas_call | solution.py:542
  70.7 0.2 collective-permute-start.12
  70.9 1.4 %collective-permute-start.13 = (bf16[5,54,216]{2,1,0:T(8,128)(2,1)S(1)}, bf16[5,54,216]{2,1,0:T(8,128)(2,1)S(1)}, u32[]{:S(2)}, u32[]{:S(2)}) collective-permute-start(bf16[5,54,216]{2,1,0:T(8,128)(2,1)S(1)} %get-tuple-element.111), channel_id=1, source_target_pairs={{0,2},{1,3},{2,0},{3,1},{4,6},{5,7},{6,4},{7,5},{8,10},{9,11},{10,... | collective-permute-start | bytes 349928 | tf_op jit(solution)/shard_map/ppermute | solution.py:558
  72.3 0.4 collective-permute-start.14
  72.6 4.8 %collective-permute-done.13.refs_2_ = bf16[5,54,216]{2,1,0:T(8,128)(2,1)S(1)} collective-permute-done((bf16[5,54,216]{2,1,0:T(8,128)(2,1)S(1)}, bf16[5,54,216]{2,1,0:T(8,128)(2,1)S(1)}, u32[]{:S(2)}, u32[]{:S(2)}) %collective-permute-start.13) | collective-permute-done | bytes 116672 | tf_op jit(solution)/shard_map/ppermute | solution.py:558
  77.4 2.1 %collective-permute-done.14.refs_3_ = bf16[5,54,216]{2,1,0:T(8,128)(2,1)S(1)} collective-permute-done((bf16[5,54,216]{2,1,0:T(8,128)(2,1)S(1)}, bf16[5,54,216]{2,1,0:T(8,128)(2,1)S(1)}, u32[]{:S(2)}, u32[]{:S(2)}) %collective-permute-start.14) | collective-permute-done | bytes 116672 | tf_op jit(solution)/shard_map/ppermute | solution.py:558
  79.5 0.9 spread.1
  80.5 1.1 %copy.43 = bf16[8,2,54,256]{3,1,2,0:T(2,128)(2,1)} copy(bf16[8,2,54,256]{3,2,1,0:T(8,128)(2,1)S(1)} %spread.1) | data formatting | bytes 884736 | tf_op jit(solution)/shard_map/spread/pallas_call | solution.py:612
  81.6 3.9 %all-to-all-start.1 = ((bf16[8,2,54,256]{3,1,2,0:T(2,128)(2,1)}), bf16[8,2,54,256]{3,1,2,0:T(2,128)(2,1)S(1)}, u32[]{:S(2)}, u32[]{:S(2)}) async-start(bf16[8,2,54,256]{3,1,2,0:T(2,128)(2,1)} %copy.43), calls=%async_computation.1 | async-start | bytes 884736 | tf_op jit(solution)/shard_map/all_to_all | solution.py:616
  85.5 1.0 collective-permute-start.17
  86.5 1.1 %collective-permute-start.16 = (bf16[196,216]{1,0:T(8,128)(2,1)S(1)}, bf16[196,216]{1,0:T(8,128)(2,1)S(1)}, u32[]{:S(2)}, u32[]{:S(2)}) collective-permute-start(bf16[196,216]{1,0:T(8,128)(2,1)S(1)} %get-tuple-element.113.refs_4_), channel_id=1, source_target_pairs={{0,2},{1,3},{2,0},{3,1},{4,6},{5,7},{6,4},{7,5},{8,10},{9,11},{10,... | collective-permute-start | bytes 254024 | tf_op jit(solution)/shard_map/ppermute | solution.py:552
  87.6 2.7 %collective-permute-done.17.refs_7_ = bf16[196,216]{1,0:T(8,128)(2,1)S(1)} collective-permute-done((bf16[196,216]{1,0:T(8,128)(2,1)S(1)}, bf16[196,216]{1,0:T(8,128)(2,1)S(1)}, u32[]{:S(2)}, u32[]{:S(2)}) %collective-permute-start.17) | collective-permute-done | bytes 84704 | tf_op jit(solution)/shard_map/ppermute | solution.py:552
  90.3 2.7 %collective-permute-done.16.refs_6_ = bf16[196,216]{1,0:T(8,128)(2,1)S(1)} collective-permute-done((bf16[196,216]{1,0:T(8,128)(2,1)S(1)}, bf16[196,216]{1,0:T(8,128)(2,1)S(1)}, u32[]{:S(2)}, u32[]{:S(2)}) %collective-permute-start.16) | collective-permute-done | bytes 84704 | tf_op jit(solution)/shard_map/ppermute | solution.py:552
  93.0 0.7 assemble.1
  93.7 1.2 %copy.45 = f32[4,196,216]{2,0,1:T(4,128)} copy(f32[4,196,216]{2,1,0:T(8,128)S(1)} %get-tuple-element.152) | data formatting | bytes 1354752
  94.8 1.2 %copy.46 = f32[4,196,216]{2,0,1:T(4,128)} copy(f32[4,196,216]{2,1,0:T(8,128)S(1)} %get-tuple-element.153) | data formatting | bytes 1354752
  96.0 2.9 %all-to-all-done.1 = bf16[8,2,54,256]{3,1,2,0:T(2,128)(2,1)S(1)} async-done(((bf16[8,2,54,256]{3,1,2,0:T(2,128)(2,1)}), bf16[8,2,54,256]{3,1,2,0:T(2,128)(2,1)S(1)}, u32[]{:S(2)}, u32[]{:S(2)}) %all-to-all-start.1) | async-done | bytes 442400 | tf_op jit(solution)/shard_map/all_to_all | solution.py:616
  99.0 0.1 copy.44.got_ref
  99.1 1.2 %update.1 = (f32[54,2,216]{2,1,0:T(2,128)}, f32[54,2,216]{2,1,0:T(2,128)}, f32[54,2,216]{2,1,0:T(2,128)}, bf16[54,2,216]{2,1,0:T(2,128)(2,1)}, f32[4,216]{1,0:T(...) custom-call(bf16[8,2,54,256]{3,2,1,0:T(8,128)(2,1)S(1)} %copy.44.got, ...), custom_call_target="tpu_custom_call" | custom-call | flops 1000000000 | bytes 3000000 | tf_op jit(solution)/shard_map/update/pallas_call | solution.py:571
  (43 shorter events, 0.2 us)
Async XLA Ops:
  0.6 11.0 %copy-start = (f32[2,12,12]{2,0,1:T(2,128)S(1)}, f32[2,12,12]{2,0,1:T(2,128)}, u32[]{:S(2)}) copy-start(f32[2,12,12]{2,0,1:T(2,128)} %param.30) | copy-start | bytes 3460
  0.7 0.9 copy-start.1
  1.6 10.1 %copy-start.15 = (bf16[4,196,216]{2,0,1:T(4,128)(2,1)S(1)}, bf16[4,196,216]{2,0,1:T(4,128)(2,1)}, u32[]{:S(2)}) copy-start(bf16[4,196,216]{2,0,1:T(4,128)(2,1)} %param.18) | copy-start | bytes 1016068
  1.6 10.2 %copy-start.14 = (f32[4,196,216]{2,0,1:T(4,128)S(1)}, f32[4,196,216]{2,0,1:T(4,128)}, u32[]{:S(2)}) copy-start(f32[4,196,216]{2,0,1:T(4,128)} %param.19) | copy-start | bytes 2032132
  1.6 21.0 %copy-start.5 = (f32[9,216]{1,0:T(8,128)S(1)}, f32[9,216]{1,0:T(8,128)}, u32[]{:S(2)}) copy-start(f32[9,216]{1,0:T(8,128)} %refs_9_.1) | copy-start | bytes 23332
  1.6 21.0 %copy-start.13 = (s32[12]{0:T(128)S(1)}, s32[12]{0:T(128)}, u32[]{:S(2)}) copy-start(s32[12]{0:T(128)} %slot_ref.3) | copy-start | bytes 148
  2.5 20.0 %all-to-all-start = ((bf16[8,2,54,216]{3,1,2,0:T(2,128)(2,1)}), bf16[8,2,54,216]{3,1,2,0:T(2,128)(2,1)S(1)}, u32[]{:S(2)}, u32[]{:S(2)}) async-start(bf16[8,2,54,216]{3,1,2,0:T(2,128)(2,1)} %bitcast.2), calls=%async_computation | async-start | bytes 884736 | tf_op jit(solution)/shard_map/all_to_all | solution.py:594
  11.8 13.3 %copy-start.10 = (f32[4,216]{1,0:T(4,128)S(1)}, f32[4,216]{1,0:T(4,128)}, u32[]{:S(2)}) copy-start(f32[4,216]{1,0:T(4,128)} %refs_3_.1) | copy-start | bytes 10372
  23.2 5.4 %collective-permute-start.2 = (bf16[4,54,216]{2,1,0:T(8,128)(2,1)S(1)}, bf16[4,54,216]{2,1,0:T(8,128)(2,1)S(1)}, u32[]{:S(2)}, u32[]{:S(2)}) collective-permute-start(bf16[4,54,216]{2,1,0:T(8,128)(2,1)S(1)} %get-tuple-element.81.refs_0_), channel_id=1, source_target_pairs={{0,3},{1,2},{2,1},{3,0},{4,7},{5,6},{6,5},{7,4},{8,11},{9,10},{10,... | collective-permute-start | bytes 279944 | tf_op jit(solution)/shard_map/ppermute | solution.py:552
  23.3 7.9 %collective-permute-start.1 = (bf16[4,54,216]{2,1,0:T(8,128)(2,1)S(1)}, bf16[4,54,216]{2,1,0:T(8,128)(2,1)S(1)}, u32[]{:S(2)}, u32[]{:S(2)}) collective-permute-start(bf16[4,54,216]{2,1,0:T(8,128)(2,1)S(1)} %get-tuple-element.81.refs_0_), channel_id=1, source_target_pairs={{0,2},{1,3},{2,0},{3,1},{4,6},{5,7},{6,4},{7,5},{8,10},{9,11},{10,... | collective-permute-start | bytes 279944 | tf_op jit(solution)/shard_map/ppermute | solution.py:552
  24.8 6.3 %collective-permute-start = (bf16[4,54,216]{2,1,0:T(8,128)(2,1)S(1)}, bf16[4,54,216]{2,1,0:T(8,128)(2,1)S(1)}, u32[]{:S(2)}, u32[]{:S(2)}) collective-permute-start(bf16[4,54,216]{2,1,0:T(8,128)(2,1)S(1)} %get-tuple-element.81.refs_0_), channel_id=1, source_target_pairs={{0,1},{1,0},{2,3},{3,2},{4,5},{5,4},{6,7},{7,6},{8,9},{9,8},{10,11... | collective-permute-start | bytes 279944 | tf_op jit(solution)/shard_map/ppermute | solution.py:552
  31.1 11.1 %collective-permute-start.5 = (bf16[9,54,216]{2,1,0:T(8,128)(2,1)S(1)}, bf16[9,54,216]{2,1,0:T(8,128)(2,1)S(1)}, u32[]{:S(2)}, u32[]{:S(2)}) collective-permute-start(bf16[9,54,216]{2,1,0:T(8,128)(2,1)S(1)} %get-tuple-element.88.refs_0_), channel_id=1, source_target_pairs={{0,3},{1,2},{2,1},{3,0},{4,7},{5,6},{6,5},{7,4},{8,11},{9,10},{10,... | collective-permute-start | bytes 629864 | tf_op jit(solution)/shard_map/ppermute | solution.py:552
  31.2 14.0 %collective-permute-start.4 = (bf16[9,54,216]{2,1,0:T(8,128)(2,1)S(1)}, bf16[9,54,216]{2,1,0:T(8,128)(2,1)S(1)}, u32[]{:S(2)}, u32[]{:S(2)}) collective-permute-start(bf16[9,54,216]{2,1,0:T(8,128)(2,1)S(1)} %get-tuple-element.88.refs_0_), channel_id=1, source_target_pairs={{0,2},{1,3},{2,0},{3,1},{4,6},{5,7},{6,4},{7,5},{8,10},{9,11},{10,... | collective-permute-start | bytes 629864 | tf_op jit(solution)/shard_map/ppermute | solution.py:552
  32.8 12.4 %collective-permute-start.3 = (bf16[9,54,216]{2,1,0:T(8,128)(2,1)S(1)}, bf16[9,54,216]{2,1,0:T(8,128)(2,1)S(1)}, u32[]{:S(2)}, u32[]{:S(2)}) collective-permute-start(bf16[9,54,216]{2,1,0:T(8,128)(2,1)S(1)} %get-tuple-element.88.refs_0_), channel_id=1, source_target_pairs={{0,1},{1,0},{2,3},{3,2},{4,5},{5,4},{6,7},{7,6},{8,9},{9,8},{10,11... | collective-permute-start | bytes 629864 | tf_op jit(solution)/shard_map/ppermute | solution.py:552
  51.1 5.2 %collective-permute-start.11 = (bf16[196,216]{1,0:T(8,128)(2,1)S(1)}, bf16[196,216]{1,0:T(8,128)(2,1)S(1)}, u32[]{:S(2)}, u32[]{:S(2)}) collective-permute-start(bf16[196,216]{1,0:T(8,128)(2,1)S(1)} %get-tuple-element.89.refs_0_), channel_id=1, source_target_pairs={{0,3},{1,2},{2,1},{3,0},{4,7},{5,6},{6,5},{7,4},{8,11},{9,10},{10,... | collective-permute-start | bytes 254024 | tf_op jit(solution)/shard_map/ppermute | solution.py:552
  51.2 17.7 %collective-permute-start.10 = (bf16[196,216]{1,0:T(8,128)(2,1)S(1)}, bf16[196,216]{1,0:T(8,128)(2,1)S(1)}, u32[]{:S(2)}, u32[]{:S(2)}) collective-permute-start(bf16[196,216]{1,0:T(8,128)(2,1)S(1)} %get-tuple-element.89.refs_0_), channel_id=1, source_target_pairs={{0,2},{1,3},{2,0},{3,1},{4,6},{5,7},{6,4},{7,5},{8,10},{9,11},{10,... | collective-permute-start | bytes 254024 | tf_op jit(solution)/shard_map/ppermute | solution.py:552
  52.7 16.2 %collective-permute-start.9 = (bf16[196,216]{1,0:T(8,128)(2,1)S(1)}, bf16[196,216]{1,0:T(8,128)(2,1)S(1)}, u32[]{:S(2)}, u32[]{:S(2)}) collective-permute-start(bf16[196,216]{1,0:T(8,128)(2,1)S(1)} %get-tuple-element.89.refs_0_), channel_id=1, source_target_pairs={{0,1},{1,0},{2,3},{3,2},{4,5},{5,4},{6,7},{7,6},{8,9},{9,8},{10,11... | collective-permute-start | bytes 254024 | tf_op jit(solution)/shard_map/ppermute | solution.py:552
  53.0 15.8 %collective-permute-start.6 = (bf16[9,54,216]{2,1,0:T(8,128)(2,1)S(1)}, bf16[9,54,216]{2,1,0:T(8,128)(2,1)S(1)}, u32[]{:S(2)}, u32[]{:S(2)}) collective-permute-start(bf16[9,54,216]{2,1,0:T(8,128)(2,1)S(1)} %get-tuple-element.97), channel_id=1, source_target_pairs={{0,1},{1,0},{2,3},{3,2},{4,5},{5,4},{6,7},{7,6},{8,9},{9,8},{10,11... | collective-permute-start | bytes 629864 | tf_op jit(solution)/shard_map/ppermute | solution.py:558
  53.2 15.7 %collective-permute-start.7 = (bf16[9,54,216]{2,1,0:T(8,128)(2,1)S(1)}, bf16[9,54,216]{2,1,0:T(8,128)(2,1)S(1)}, u32[]{:S(2)}, u32[]{:S(2)}) collective-permute-start(bf16[9,54,216]{2,1,0:T(8,128)(2,1)S(1)} %get-tuple-element.98), channel_id=1, source_target_pairs={{0,2},{1,3},{2,0},{3,1},{4,6},{5,7},{6,4},{7,5},{8,10},{9,11},{10,... | collective-permute-start | bytes 629864 | tf_op jit(solution)/shard_map/ppermute | solution.py:558
  56.3 13.3 %collective-permute-start.8 = (bf16[9,54,216]{2,1,0:T(8,128)(2,1)S(1)}, bf16[9,54,216]{2,1,0:T(8,128)(2,1)S(1)}, u32[]{:S(2)}, u32[]{:S(2)}) collective-permute-start(bf16[9,54,216]{2,1,0:T(8,128)(2,1)S(1)} %get-tuple-element.99), channel_id=1, source_target_pairs={{0,3},{1,2},{2,1},{3,0},{4,7},{5,6},{6,5},{7,4},{8,11},{9,10},{10,... | collective-permute-start | bytes 629864 | tf_op jit(solution)/shard_map/ppermute | solution.py:558
  70.7 2.0 %collective-permute-start.12 = (bf16[5,54,216]{2,1,0:T(8,128)(2,1)S(1)}, bf16[5,54,216]{2,1,0:T(8,128)(2,1)S(1)}, u32[]{:S(2)}, u32[]{:S(2)}) collective-permute-start(bf16[5,54,216]{2,1,0:T(8,128)(2,1)S(1)} %get-tuple-element.110), channel_id=1, source_target_pairs={{0,1},{1,0},{2,3},{3,2},{4,5},{5,4},{6,7},{7,6},{8,9},{9,8},{10,11... | collective-permute-start | bytes 349928 | tf_op jit(solution)/shard_map/ppermute | solution.py:558
  70.9 6.6 %collective-permute-start.13 = (bf16[5,54,216]{2,1,0:T(8,128)(2,1)S(1)}, bf16[5,54,216]{2,1,0:T(8,128)(2,1)S(1)}, u32[]{:S(2)}, u32[]{:S(2)}) collective-permute-start(bf16[5,54,216]{2,1,0:T(8,128)(2,1)S(1)} %get-tuple-element.111), channel_id=1, source_target_pairs={{0,2},{1,3},{2,0},{3,1},{4,6},{5,7},{6,4},{7,5},{8,10},{9,11},{10,... | collective-permute-start | bytes 349928 | tf_op jit(solution)/shard_map/ppermute | solution.py:558
  72.3 7.3 %collective-permute-start.14 = (bf16[5,54,216]{2,1,0:T(8,128)(2,1)S(1)}, bf16[5,54,216]{2,1,0:T(8,128)(2,1)S(1)}, u32[]{:S(2)}, u32[]{:S(2)}) collective-permute-start(bf16[5,54,216]{2,1,0:T(8,128)(2,1)S(1)} %get-tuple-element.112), channel_id=1, source_target_pairs={{0,3},{1,2},{2,1},{3,0},{4,7},{5,6},{6,5},{7,4},{8,11},{9,10},{10,... | collective-permute-start | bytes 349928 | tf_op jit(solution)/shard_map/ppermute | solution.py:558
  81.6 17.4 %all-to-all-start.1 = ((bf16[8,2,54,256]{3,1,2,0:T(2,128)(2,1)}), bf16[8,2,54,256]{3,1,2,0:T(2,128)(2,1)S(1)}, u32[]{:S(2)}, u32[]{:S(2)}) async-start(bf16[8,2,54,256]{3,1,2,0:T(2,128)(2,1)} %copy.43), calls=%async_computation.1 | async-start | bytes 884736 | tf_op jit(solution)/shard_map/all_to_all | solution.py:616
  85.4 13.6 %copy-start.2 = (f32[2,54,216]{2,0,1:T(2,128)S(1)}, f32[2,54,216]{2,0,1:T(2,128)}, u32[]{:S(2)}) copy-start(f32[2,54,216]{2,0,1:T(2,128)} %param.24) | copy-start | bytes 279940
  85.4 13.6 %copy-start.3 = (f32[2,54,216]{2,0,1:T(2,128)S(1)}, f32[2,54,216]{2,0,1:T(2,128)}, u32[]{:S(2)}) copy-start(f32[2,54,216]{2,0,1:T(2,128)} %param.25) | copy-start | bytes 279940
  85.4 13.6 %copy-start.4 = (f32[2,54,216]{2,0,1:T(2,128)S(1)}, f32[2,54,216]{2,0,1:T(2,128)}, u32[]{:S(2)}) copy-start(f32[2,54,216]{2,0,1:T(2,128)} %param.26) | copy-start | bytes 279940
  85.5 13.6 %copy-start.6 = (f32[9,216]{1,0:T(8,128)S(1)}, f32[9,216]{1,0:T(8,128)}, u32[]{:S(2)}) copy-start(f32[9,216]{1,0:T(8,128)} %refs_10_.1) | copy-start | bytes 23332
  85.5 13.6 %copy-start.7 = (f32[9,216]{1,0:T(8,128)S(1)}, f32[9,216]{1,0:T(8,128)}, u32[]{:S(2)}) copy-start(f32[9,216]{1,0:T(8,128)} %refs_11_.1) | copy-start | bytes 23332
  85.5 13.6 %copy-start.8 = (f32[2,12,12]{2,0,1:T(2,128)S(1)}, f32[2,12,12]{2,0,1:T(2,128)}, u32[]{:S(2)}) copy-start(f32[2,12,12]{2,0,1:T(2,128)} %param.31) | copy-start | bytes 3460
  85.5 13.6 %copy-start.9 = (f32[2,12,12]{2,0,1:T(2,128)S(1)}, f32[2,12,12]{2,0,1:T(2,128)}, u32[]{:S(2)}) copy-start(f32[2,12,12]{2,0,1:T(2,128)} %param.32) | copy-start | bytes 3460
  85.5 13.6 %copy-start.11 = (f32[4,216]{1,0:T(4,128)S(1)}, f32[4,216]{1,0:T(4,128)}, u32[]{:S(2)}) copy-start(f32[4,216]{1,0:T(4,128)} %refs_4_.1) | copy-start | bytes 10372
  85.5 13.6 %copy-start.12 = (f32[4,216]{1,0:T(4,128)S(1)}, f32[4,216]{1,0:T(4,128)}, u32[]{:S(2)}) copy-start(f32[4,216]{1,0:T(4,128)} %refs_5_.1) | copy-start | bytes 10372
  85.5 4.8 %collective-permute-start.17 = (bf16[196,216]{1,0:T(8,128)(2,1)S(1)}, bf16[196,216]{1,0:T(8,128)(2,1)S(1)}, u32[]{:S(2)}, u32[]{:S(2)}) collective-permute-start(bf16[196,216]{1,0:T(8,128)(2,1)S(1)} %get-tuple-element.113.refs_4_), channel_id=1, source_target_pairs={{0,3},{1,2},{2,1},{3,0},{4,7},{5,6},{6,5},{7,4},{8,11},{9,10},{10,... | collective-permute-start | bytes 254024 | tf_op jit(solution)/shard_map/ppermute | solution.py:552
  86.5 6.5 %collective-permute-start.16 = (bf16[196,216]{1,0:T(8,128)(2,1)S(1)}, bf16[196,216]{1,0:T(8,128)(2,1)S(1)}, u32[]{:S(2)}, u32[]{:S(2)}) collective-permute-start(bf16[196,216]{1,0:T(8,128)(2,1)S(1)} %get-tuple-element.113.refs_4_), channel_id=1, source_target_pairs={{0,2},{1,3},{2,0},{3,1},{4,6},{5,7},{6,4},{7,5},{8,10},{9,11},{10,... | collective-permute-start | bytes 254024 | tf_op jit(solution)/shard_map/ppermute | solution.py:552
  87.6 5.4 %collective-permute-start.15 = (bf16[196,216]{1,0:T(8,128)(2,1)S(1)}, bf16[196,216]{1,0:T(8,128)(2,1)S(1)}, u32[]{:S(2)}, u32[]{:S(2)}) collective-permute-start(bf16[196,216]{1,0:T(8,128)(2,1)S(1)} %get-tuple-element.113.refs_4_), channel_id=1, source_target_pairs={{0,1},{1,0},{2,3},{3,2},{4,5},{5,4},{6,7},{7,6},{8,9},{9,8},{10,11... | collective-permute-start | bytes 254024 | tf_op jit(solution)/shard_map/ppermute | solution.py:552

commit v4 on v3

v4 whole, which is shorter than its diff:
```python
import functools
import jax
import jax.numpy as jnp
from jax import lax
from jax.experimental import pallas as pl
from jax.experimental.pallas import tpu as pltpu
from jax.sharding import PartitionSpec as P

HD = 18
SIDE = 14
PITCH = 16
MARGIN = 24
FREE = 216
WIDE = 40
norm_eps = 1e-05
bf16 = jnp.bfloat16
f32 = jnp.float32


def nn(a, b):
    return lax.dot_general(a, b, (((1,), (0,)), ((), ())), preferred_element_type=f32)


def nt(a, b):
    return lax.dot_general(a, b, (((1,), (1,)), ((), ())), preferred_element_type=f32)


def tn(a, b):
    return lax.dot_general(a, b, (((0,), (0,)), ((), ())), preferred_element_type=f32)


def iota(shape, dim):
    return lax.broadcasted_iota(jnp.int32, shape, dim)


def split2(v):
    hi = v.astype(bf16)
    return hi, (v - hi.astype(f32)).astype(bf16)


def real_rows(shape):
    return (iota(shape, 0) & (PITCH - 1)) < SIDE


def lane_head(shape, dim, place):
    lane = iota(shape, dim)
    rest = lane & 63
    head = ((lane >> 6) ^ place) * 3 + (rest >= 18).astype(jnp.int32) + (rest >= 36).astype(jnp.int32)
    return jnp.where(rest < 54, head, -1)


def true_head(rows, place):
    return ((rows // (3 * PITCH)) ^ place) * 3 + (rows // PITCH) % 3


def prep_kernel(scal, tok_ref, cot_ref, norm_ref, talk_ref, x_ref, a_ref, dy_ref, mix_ref, bias_ref, tmp_ref):
    x_ref[...] = jnp.zeros_like(x_ref)
    dy_ref[...] = jnp.zeros_like(dy_ref)
    valid = (scal[0] < scal[1]).astype(f32)
    tmp_ref[...] = tok_ref[0].astype(f32)
    for y in range(SIDE):
        x_ref[PITCH * y : PITCH * y + SIDE, :] = tmp_ref[SIDE * y : SIDE * (y + 1), :]
        dy_ref[PITCH * y : PITCH * y + SIDE, :] = cot_ref[0, SIDE * y : SIDE * (y + 1), :] * valid
    x = x_ref[...]
    centred = x - jnp.mean(x, axis=-1, keepdims=True)
    inv = lax.rsqrt(jnp.mean(centred * centred, axis=-1, keepdims=True) + norm_eps)
    a = centred * inv * norm_ref[0:1, :] + norm_ref[1:2, :]
    a_ref[...] = jnp.where(real_rows(a.shape), a, 0.0).astype(bf16)
    heads = talk_ref.shape[1]
    n = heads * PITCH
    ex = (true_head(iota((n, heads), 0), scal[0]) == iota((n, heads), 1)).astype(bf16)
    el = (lane_head((256, heads), 0, scal[0]) == iota((256, heads), 1)).astype(bf16)
    for i in range(2):
        both = []
        for part in split2(talk_ref[i]):
            if i == 0:
                both.append(nt(nn(ex, part).astype(bf16), el))
            else:
                both.append(nt(nt(ex, part).astype(bf16), el))
        mix_ref[i] = (both[0] + both[1]) * (HD**-0.5 if i == 0 else 1.0)
    bias_ref[...] = jnp.where(real_rows(bias_ref.shape), 0.0, -1e30)


def load_weight(dst_ref, w_refs, b):
    for k, w_ref in enumerate(w_refs):
        dst_ref[64 * k : 64 * k + 54, :] = w_ref[b]


def tiled(rows, heads):
    return jnp.concatenate([rows] * heads, axis=0)


def over_heads(rows, heads):
    return jnp.sum(rows.reshape(heads, PITCH, rows.shape[1]), axis=0)


def attn_fwd_kernel(scal, x_ref, a_ref, mix_ref, bias_ref, *refs, parts, unroll):
    w_refs, refs = refs[:parts], refs[parts:]
    mid_ref, q_ref, k_ref, v_ref, o_ref, qw_ref, p_ref, pv_ref, ws_ref = refs
    heads = mix_ref.shape[1] // PITCH
    a = a_ref[...]
    ws_ref[...] = jnp.zeros_like(ws_ref)
    for b, dst in enumerate((q_ref, k_ref, v_ref)):
        load_weight(ws_ref.at[b], w_refs, b)
        dst[...] = nt(a, ws_ref[b]).astype(bf16)
    load_weight(ws_ref.at[3], w_refs, 3)
    head = lane_head((1, 256), 1, scal[0])
    keep = ((head >= 0) & (head < scal[2])).astype(f32)

    def group(y, _):
        rows = pl.ds(pl.multiple_of(y * PITCH, PITCH), PITCH)
        qw = (tiled(q_ref[rows, :].astype(f32), heads) * mix_ref[0]).astype(bf16)
        qw_ref[y] = qw
        t = nt(k_ref[...], qw) + bias_ref[...]
        e = jnp.exp(t - jnp.max(t, axis=0, keepdims=True))
        p = (e * (1.0 / jnp.sum(e, axis=0, keepdims=True))).astype(bf16)
        p_ref[y] = p
        pv = tn(p, v_ref[...])
        pv_ref[y] = pv.astype(bf16)
        o_ref[rows, :] = (over_heads(pv * mix_ref[1], heads) * keep).astype(bf16)
        return 0

    lax.fori_loop(0, SIDE, group, 0, unroll=unroll)
    mid_ref[...] = x_ref[...] + nn(o_ref[...], ws_ref[3])


def ln_stats(v):
    centred = v - jnp.mean(v, axis=-1, keepdims=True)
    inv = lax.rsqrt(jnp.mean(centred * centred, axis=-1, keepdims=True) + norm_eps)
    return centred * inv, inv


def ln_back(grad, scaled, inv, gain):
    gs = grad * gain
    return inv * (
        gs - jnp.mean(gs, axis=-1, keepdims=True) - scaled * jnp.mean(gs * scaled, axis=-1, keepdims=True)
    )


def in_free_lanes(flat, dst_ref, first_row):
    rows = flat.shape[0]
    for j in range(6):
        dst_ref[first_row + rows * j : first_row + rows * (j + 1), :] = pltpu.roll(flat, (FREE - WIDE * j) % 256, 1)


def from_free_lanes(src_ref, first_row, rows):
    lane = iota((rows, 256), 1)
    flat = jnp.zeros((rows, 256), f32)
    for j in range(6):
        moved = pltpu.roll(src_ref[first_row + rows * j : first_row + rows * (j + 1), :], (WIDE * j - FREE) % 256, 1)
        flat = flat + jnp.where((lane >= WIDE * j) & (lane < WIDE * (j + 1)), moved, 0.0)
    return flat


def place(rows=216):
    shape = (rows, 256)
    lane = iota(shape, 1)
    rest = lane & 63
    return ((iota(shape, 0) == (lane >> 6) * 54 + rest) & (rest < 54)).astype(bf16)


def ffn_kernel(
    scal, mid_ref, dy_ref, norm_ref, o_ref, *refs, parts
):
    w_refs, refs = refs[:parts], refs[parts:]
    out_ref, dmid_ref, gn_ref = refs[:3]
    gw_refs, refs = refs[3 : 3 + parts], refs[3 + parts :]
    win_ref, wdn_ref, h_ref, d_ref, gate_ref, dh_ref, cv_ref, gcv_ref, tmp_ref, sm_ref = refs
    hd = parts
    lanes = hd * 256
    win_ref[...] = jnp.zeros_like(win_ref)
    wdn_ref[...] = jnp.zeros_like(wdn_ref)
    pm = place()
    for h in range(hd):
        for j in range(4):
            at = 256 * h + 64 * j
            win_ref[at : at + 54, :] = w_refs[h][j]
            wdn_ref[at : at + 54, :] = w_refs[h][4 + j]
        both = nn(w_refs[h][8], pm)
        cv_ref[:, 256 * h : 256 * (h + 1)] = both[0:9] + both[16:25]
    mid = mid_ref[...]
    z, inv = ln_stats(mid)
    rows = real_rows(mid.shape)
    w = jnp.where(rows, z * norm_ref[2:3, :] + norm_ref[3:4, :], 0.0).astype(bf16)
    dy = dy_ref[...]
    e = dy.astype(bf16)
    tokens = mid.shape[0]
    pad = MARGIN
    zero = jnp.zeros((pad, lanes), f32)
    h_ref[0:pad, :] = zero
    h_ref[pad + tokens :, :] = zero
    d_ref[0:pad, :] = zero
    d_ref[pad + tokens :, :] = zero
    h_ref[pad : pad + tokens, :] = nt(w, win_ref[...])
    d_ref[pad : pad + tokens, :] = nt(e, wdn_ref[...])
    lane = iota((1, 128), 1)
    rmask = real_rows((tokens, 128))
    for c in range(lanes // 128):
        cols = slice(128 * c, 128 * (c + 1))
        glane = lane + 128 * c
        rest = glane & 63
        unit = (((glane >> 8) ^ scal[0]) * 4 + ((glane >> 6) & 3)) * 54 + rest
        keep = ((rest < 54) & (unit < scal[3])).astype(f32)
        act = jnp.zeros((tokens, 128), f32)
        for t in range(9):
            off = PITCH * (t // 3 - 1) + t % 3 - 1
            act = act + cv_ref[t : t + 1, cols] * h_ref[pad + off : pad + off + tokens, cols]
        sig = 1.0 / (1.0 + jnp.exp(-act))
        gate_ref[:, cols] = (act * sig * keep).astype(bf16)
        dact = d_ref[pad : pad + tokens, cols] * keep * sig * (1.0 + act * (1.0 - sig))
        d_ref[pad : pad + tokens, cols] = dact
        dh = jnp.zeros((tokens, 128), f32)
        for t in range(9):
            off = PITCH * (t // 3 - 1) + t % 3 - 1
            gcv_ref[t : t + 1, cols] = jnp.sum(
                dact * h_ref[pad + off : pad + off + tokens, cols], axis=0, keepdims=True
            )
            dh = dh + cv_ref[t : t + 1, cols] * d_ref[pad - off : pad - off + tokens, cols]
        dh_ref[:, cols] = jnp.where(rmask, dh, 0.0).astype(bf16)
    valid = (scal[0] < scal[1]).astype(f32)
    down = nn(gate_ref[...], wdn_ref[...])
    tmp_ref[...] = (mid + down) * valid
    for y in range(SIDE):
        out_ref[SIDE * y : SIDE * (y + 1), :] = tmp_ref[PITCH * y : PITCH * y + SIDE, :].astype(bf16)
    dw = nn(dh_ref[...], win_ref[...])
    gn_ref[...] = jnp.zeros_like(gn_ref)
    gn_ref[0:1, :] = jnp.sum(dw * z, axis=0, keepdims=True)
    gn_ref[1:2, :] = jnp.sum(dw, axis=0, keepdims=True)
    dmid = dy + ln_back(dw, z, inv, norm_ref[2:3, :])
    dmid_ref[...] = dmid
    go = tn(o_ref[...], dmid.astype(bf16)).astype(bf16)
    dim = mid.shape[1]
    free = iota((54, 256), 1) >= FREE
    pm = place(256)
    for h in range(hd):
        cols = slice(256 * h, 256 * (h + 1))
        gi = tn(dh_ref[:, cols], w).astype(bf16)
        gd = tn(gate_ref[:, cols], e).astype(bf16)
        for j in range(4):
            gw_refs[h][1 + j, :, 0:dim] = gi[64 * j : 64 * j + 54]
            gw_refs[h][5 + j, :, 0:dim] = gd[64 * j : 64 * j + 54]
        in_free_lanes(nt(gcv_ref[:, cols].astype(bf16), pm), sm_ref, 0)
        gw_refs[h][0] = jnp.where(free, sm_ref[0:54, :], 0.0).astype(bf16)
        gw_refs[h][0, :, 0:dim] = go[64 * h : 64 * h + 54]


def scores_back_kernel(
    scal, dmid_ref, mix_ref, q_ref, k_ref, v_ref, qw_ref, p_ref, pv_ref, *refs, parts, unroll, part
):
    heads = mix_ref.shape[1] // PITCH
    n = heads * PITCH
    if part == 0:
        w_refs, refs = refs[:parts], refs[parts:]
        do_ref, gq_ref, gk_ref, gv_ref, g0_ref, g1_ref, wo_ref = refs
        wo_ref[...] = jnp.zeros_like(wo_ref)
        load_weight(wo_ref, w_refs, 3)
        f = dmid_ref[...].astype(bf16)
        head = lane_head((1, 256), 1, scal[0])
        keep = ((head >= 0) & (head < scal[2])).astype(f32)
        do_ref[...] = (nt(f, wo_ref[...]) * keep).astype(bf16)
        for ref in (gk_ref, gv_ref, g0_ref, g1_ref):
            ref[...] = jnp.zeros_like(ref)
    else:
        do_ref, *sums, gq_ref, gkb_ref, gvb_ref, gt_ref, gk_ref, gv_ref, g0_ref, g1_ref = refs
        for ref, old in zip((gk_ref, gv_ref, g0_ref, g1_ref), sums):
            ref[...] = old[...]
    first = SIDE // 2 * part

    def group(y, _):
        out_rows = pl.ds(pl.multiple_of(y * PITCH, PITCH), PITCH)
        y = y + first
        rows = pl.ds(pl.multiple_of(y * PITCH, PITCH), PITCH)
        dot = tiled(do_ref[rows, :].astype(f32), heads)
        dw = (dot * mix_ref[1]).astype(bf16)
        dp = nt(v_ref[...], dw)
        p = p_ref[y]
        pf = p.astype(f32)
        dt = (pf * (dp - jnp.sum(dp * pf, axis=0, keepdims=True))).astype(bf16)
        gv_ref[...] += nn(p, dw)
        gk_ref[...] += nn(dt, qw_ref[y])
        dk = tn(dt, k_ref[...])
        gq_ref[out_rows, :] = over_heads(dk * mix_ref[0], heads).astype(bf16)
        g0_ref[...] += dk * tiled(q_ref[rows, :].astype(f32), heads)
        g1_ref[...] += pv_ref[y].astype(f32) * dot
        return 0

    lax.fori_loop(0, SIDE // 2, group, 0, unroll=unroll)
    if part == 0:
        return
    gkb_ref[...] = gk_ref[...].astype(bf16)
    gvb_ref[...] = gv_ref[...].astype(bf16)
    ex = (true_head(iota((n, heads), 0), scal[0]) == iota((n, heads), 1)).astype(bf16)
    el = (lane_head((256, heads), 0, scal[0]) == iota((256, heads), 1)).astype(bf16)
    for i, ref in enumerate((g0_ref, g1_ref)):
        hi, lo = split2(ref[...])
        hi, lo = split2(nn(hi, el) + nn(lo, el))
        if i == 0:
            gt_ref[i] = (tn(ex, hi) + tn(ex, lo)) * HD**-0.5
        else:
            gt_ref[i] = tn(hi, ex) + tn(lo, ex)


def weights_back_kernel(
    scal, x_ref, a_ref, dmid_ref, norm_ref, gn2_ref, gqa_ref, gqb_ref, gk_ref, gv_ref, gt_ref, *refs, parts
):
    w_refs, refs = refs[:parts], refs[parts:]
    tg_ref, gw_refs, refs = refs[0], refs[1 : 1 + parts], refs[1 + parts :]
    ws_ref, tmp_ref, flat_ref, sm_ref = refs
    heads = gt_ref.shape[1]
    dim = x_ref.shape[1]
    ws_ref[...] = jnp.zeros_like(ws_ref)
    for b in range(3):
        load_weight(ws_ref.at[b], w_refs, b)
    gq = jnp.concatenate([gqa_ref[...], gqb_ref[...]], axis=0)
    gk, gv = gk_ref[...], gv_ref[...]
    a = a_ref[...]
    da = nn(gq, ws_ref[0]) + nn(gk, ws_ref[1]) + nn(gv, ws_ref[2])
    z, inv = ln_stats(x_ref[...])
    flat_ref[...] = jnp.zeros_like(flat_ref)
    flat_ref[0:1, 0:dim] = jnp.sum(da * z, axis=0, keepdims=True)
    flat_ref[1:2, 0:dim] = jnp.sum(da, axis=0, keepdims=True)
    flat_ref[2:4, 0:dim] = gn2_ref[0:2, :]
    for i in range(2):
        flat_ref[8 : 8 + heads, 128 * i : 128 * i + heads] = gt_ref[i]
    sm_ref[...] = jnp.zeros_like(sm_ref)
    in_free_lanes(flat_ref[0:4, :], sm_ref, 0)
    mix = flat_ref[8 : 8 + heads, :]
    first = iota(mix.shape, 1) < 128
    mix = jnp.where(first, mix, 0.0) + pltpu.roll(jnp.where(first, 0.0, mix), 128 + heads, 1)
    sm_ref[24 : 24 + heads, :] = pltpu.roll(mix, FREE, 1)
    small = jnp.where(iota((54, 256), 1) >= FREE, sm_ref[0:54, :], 0.0).astype(bf16)
    for h in range(parts):
        gw_refs[h][0] = small
    for b, g in enumerate((gq, gk, gv)):
        gw = tn(g, a).astype(bf16)
        for h in range(parts):
            gw_refs[h][b, :, 0:dim] = gw[64 * h : 64 * h + 54]
    tmp_ref[...] = dmid_ref[...] + ln_back(da, z, inv, norm_ref[0:1, :])
    for y in range(SIDE):
        tg_ref[SIDE * y : SIDE * (y + 1), :] = tmp_ref[PITCH * y : PITCH * y + SIDE, :].astype(bf16)


def cast_kernel(m_hbm, out_ref, m_ref, sem):
    copy = pltpu.make_async_copy(m_hbm, m_ref, sem)
    copy.start()
    copy.wait()
    low = m_ref[...].astype(bf16)
    for i in range(out_ref.shape[0]):
        out_ref[i] = low


def select_kernel(slot_ref, every_ref, conv_ref, attn_ref, ffn_ref):
    per = every_ref.shape[1]
    for b in range(12):
        slot = slot_ref[b]
        block = every_ref[slot // per, slot % per]
        if b < 4:
            attn_ref[b] = block
        else:
            ffn_ref[b - 4] = block
    hi, lo = split2(conv_ref[...])
    ffn_ref[8] = jnp.zeros_like(ffn_ref[8])
    ffn_ref[8, 0:9] = hi
    ffn_ref[8, 16:25] = lo


def total(refs, at):
    acc = refs[0][at].astype(f32)
    for ref in refs[1:]:
        acc = acc + ref[at].astype(f32)
    return acc


def half_sum_kernel(a_ref, b_ref, out_ref):
    out_ref[...] = (a_ref[...].astype(f32) + b_ref[...].astype(f32)).astype(bf16)


def spread_ffn_kernel(slot_ref, *refs, ranks):
    ffn_refs, out_ref = refs[:-1], refs[-1]
    per = out_ref.shape[0] // ranks
    out_ref[...] = jnp.zeros_like(out_ref)
    for b in range(9):
        block = total(ffn_refs, b)
        out_ref[slot_ref[3 + b], :, 0:FREE] = block[:, 0:FREE].astype(bf16)
        if b == 0:
            wide = block[:, FREE:].astype(bf16)
    for r in range(ranks):
        out_ref[r * per, :, FREE:] = wide


def spread_attn_kernel(slot_ref, old_ref, *refs, ranks):
    attn, out_ref = refs[:-1], refs[-1]
    per = out_ref.shape[0] // ranks
    out_ref[...] = old_ref[...]
    for b in range(3):
        block = total(attn, b)
        out_ref[slot_ref[b], :, 0:FREE] = block[:, 0:FREE].astype(bf16)
        if b == 0:
            wide = block[:, FREE:].astype(bf16)
    for r in range(ranks):
        out_ref[r * per + 1, :, FREE:] = wide


def adam(w, g, one, two, rate, decay):
    one_new = 0.5 * one + 0.5 * g
    two_new = 0.5 * two + 0.5 * g * g
    hat_one = one_new / (1.0 - 0.5**3)
    hat_two = two_new / (1.0 - 0.5**3)
    return w - rate * (hat_one / (jnp.sqrt(hat_two) + 1e-08) + decay * w), one_new, two_new


def update_kernel(got_ref, *refs, ranks):
    ins, outs, (g_ref, sm_ref, flat_ref) = refs[0:12], refs[12:25], refs[25:]
    per = got_ref.shape[0] // ranks
    dim = ins[0].shape[2]
    rows = got_ref.shape[1]
    for i in range(per):
        g = got_ref[i].astype(f32)
        for r in range(1, ranks):
            g = g + got_ref[r * per + i].astype(f32)
        g_ref[:, i, :] = g[:, 0:dim]
        sm_ref[i, 0:rows, :] = g
    w, one, two = adam(ins[0][...], g_ref[...], ins[1][...], ins[2][...], 0.06, 0.05)
    outs[0][...], outs[1][...], outs[2][...], outs[3][...] = w, one, two, w.astype(bf16)
    heads = ins[6].shape[0]
    flat_ref[0:9, :] = from_free_lanes(sm_ref.at[0], 0, 9)
    flat_ref[16:20, :] = from_free_lanes(sm_ref.at[1], 0, 4)
    mix = pltpu.roll(sm_ref[1, 24 : 24 + heads, :], 256 - FREE, 1)
    flat_ref[32 : 32 + heads, :] = mix
    flat_ref[48 : 48 + heads, :] = pltpu.roll(mix, 256 - heads, 1)
    outs[4][...], outs[5][...], outs[6][...] = adam(
        ins[3][...], flat_ref[16:20, 0:dim], ins[4][...], ins[5][...], 0.2, 0.0
    )
    for i in range(2):
        w, one, two = adam(
            ins[6][:, i, :], flat_ref[16 * (i + 2) : 16 * (i + 2) + heads, 0:heads], ins[7][:, i, :], ins[8][:, i, :],
            0.2, 0.0,
        )
        outs[7][:, i, :], outs[8][:, i, :], outs[9][:, i, :] = w, one, two
    outs[10][...], outs[11][...], outs[12][...] = adam(
        ins[9][...], flat_ref[0:9, 0:dim], ins[10][...], ins[11][...], 0.2, 0.05
    )


def assemble_kernel(scal, *refs):
    for k, ref in enumerate(refs[:-1]):
        refs[-1][scal[0] ^ k] = ref[...].astype(f32)


VM = pl.BlockSpec(memory_space=pltpu.VMEM)
SM = pl.BlockSpec(memory_space=pltpu.SMEM)
SDS = jax.ShapeDtypeStruct


def call(body, name, n_scalar, n_in, out_shape, scratch=(), mb=16, micros=1, **kw):
    return pl.pallas_call(
        functools.partial(body, **kw) if kw else body,
        in_specs=[SM] * n_scalar + [VM] * n_in,
        out_specs=[VM] * len(out_shape),
        out_shape=out_shape,
        scratch_shapes=scratch,
        compiler_params=pltpu.CompilerParams(vmem_limit_bytes=mb << 20),
        cost_estimate=pl.CostEstimate(flops=micros * 1000000000, transcendentals=0, bytes_accessed=micros * 3000000),
        name=name,
    )


def prep(scal, tokens, cotangent, norm_params, talk):
    tok, dim = tokens.shape[1], tokens.shape[2]
    pad = SIDE * PITCH
    heads = talk.shape[1]
    n = heads * PITCH
    full = lambda *s: pl.BlockSpec(s, lambda i, sc: (0,) * len(s))
    return pl.pallas_call(
        prep_kernel,
        grid_spec=pltpu.PrefetchScalarGridSpec(
            num_scalar_prefetch=1,
            grid=(1,),
            in_specs=[
                pl.BlockSpec((1, tok, dim), lambda i, sc: (sc[0], 0, 0)),
                pl.BlockSpec((1, tok, dim), lambda i, sc: (sc[0], 0, 0)),
                full(*norm_params.shape),
                full(*talk.shape),
            ],
            out_specs=[full(pad, dim), full(pad, dim), full(pad, dim), full(2, n, 256), full(pad, n)],
            scratch_shapes=[pltpu.VMEM((tok, dim), f32)],
        ),
        out_shape=[SDS((pad, dim), f32), SDS((pad, dim), bf16), SDS((pad, dim), f32), SDS((2, n, 256), f32),
                   SDS((pad, n), f32)],
        compiler_params=pltpu.CompilerParams(vmem_limit_bytes=16 << 20),
        cost_estimate=pl.CostEstimate(flops=1000000000, transcendentals=0, bytes_accessed=3000000),
        name="prep",
    )(scal, tokens, cotangent, norm_params, talk)


def attn_fwd(scal, x, a, mix, bias, w, unroll=7):
    pad, dim = x.shape
    n = mix.shape[1]
    return call(
        attn_fwd_kernel, "attn_fwd", 1, 4 + len(w),
        [SDS((pad, dim), f32)] + [SDS((pad, 256), bf16)] * 4
        + [SDS((SIDE, n, 256), bf16), SDS((SIDE, pad, n), bf16), SDS((SIDE, n, 256), bf16)],
        [pltpu.VMEM((4, 256, dim), bf16)],
        mb=24, micros=10, parts=len(w), unroll=unroll,
    )(scal, x, a, mix, bias, *w)


def ffn(scal, mid, dy, norm_params, o, w):
    pad, dim = mid.shape
    lanes = len(w) * 256
    return call(
        ffn_kernel, "ffn", 1, 4 + len(w),
        [SDS((SIDE * SIDE, dim), bf16), SDS((pad, dim), f32), SDS((8, dim), f32)] + [SDS((9, 54, 256), bf16)] * len(w),
        [
            pltpu.VMEM((lanes, dim), bf16), pltpu.VMEM((lanes, dim), bf16),
            pltpu.VMEM((pad + 2 * MARGIN, lanes), f32), pltpu.VMEM((pad + 2 * MARGIN, lanes), f32),
            pltpu.VMEM((pad, lanes), bf16), pltpu.VMEM((pad, lanes), bf16),
            pltpu.VMEM((9, lanes), f32), pltpu.VMEM((9, lanes), f32), pltpu.VMEM((pad, dim), f32),
            pltpu.VMEM((56, 256), f32),
        ],
        mb=24, micros=6, parts=len(w),
    )(scal, mid, dy, norm_params, o, *w)


def scores_back(scal, dmid, mix, q, k, v, qw, p, pv, more, part, unroll=7):
    pad, dim = dmid.shape
    n = mix.shape[1]
    heads = n // PITCH
    sums = [SDS((pad, 256), f32)] * 2 + [SDS((n, 256), f32)] * 2
    half = SDS((pad // 2, 256), bf16)
    if part == 0:
        outs = [SDS((pad, 256), bf16), half] + sums
        scratch = [pltpu.VMEM((256, dim), bf16)]
    else:
        outs = [half] + [SDS((pad, 256), bf16)] * 2 + [SDS((2, heads, heads), f32)]
        scratch = [pltpu.VMEM(t.shape, f32) for t in sums]
    return call(
        scores_back_kernel, "scores_back", 1, 8 + len(more), outs, scratch,
        mb=24, micros=4, parts=len(more), unroll=unroll, part=part,
    )(scal, dmid, mix, q, k, v, qw, p, pv, *more)


def weights_back(scal, x, a, dmid, norm_params, gn2, gqa, gqb, gk, gv, gt, w):
    pad, dim = x.shape
    return call(
        weights_back_kernel, "weights_back", 1, 10 + len(w),
        [SDS((SIDE * SIDE, dim), bf16)] + [SDS((3, 54, 256), bf16)] * len(w),
        [pltpu.VMEM((3, 256, dim), bf16), pltpu.VMEM((pad, dim), f32), pltpu.VMEM((24, 256), f32),
         pltpu.VMEM((56, 256), f32)],
        mb=24, micros=3, parts=len(w),
    )(scal, x, a, dmid, norm_params, gn2, gqa, gqb, gk, gv, gt, *w)


def permute(x, axis, k):
    return lax.ppermute(x, axis, [(i, i ^ k) for i in range(lax.axis_size(axis))])


def swap(t):
    return jnp.swapaxes(t, 0, 1)


def whole(*shape):
    return pl.BlockSpec(shape, lambda i: (0,) * len(shape))


def staged(body, name, ins, outs, scratch=(), micros=1):
    return pl.pallas_call(
        body,
        grid=(1,),
        in_specs=[whole(*t.shape) for t in ins],
        out_specs=[whole(*t.shape) for t in outs],
        out_shape=outs,
        scratch_shapes=scratch,
        compiler_params=pltpu.CompilerParams(vmem_limit_bytes=16 << 20),
        cost_estimate=pl.CostEstimate(flops=micros * 1000000000, transcendentals=0, bytes_accessed=micros * 3000000),
        name=name,
    )(*ins)


def local(
    tokens, cotangent, image_count, subnet_heads, subnet_width, block_slot,
    master, master_m1, master_m2, norm_params, norm_m1, norm_m2, talk, talk_m1, talk_m2, conv, conv_m1, conv_m2,
):
    slots, rows, dim = master.shape
    parts = lax.axis_size("head")
    ranks = lax.axis_size("dp")
    place_id = lax.axis_index("head").astype(jnp.int32)
    scal = jnp.concatenate([place_id[None], image_count, subnet_heads, subnet_width])
    mine = pl.pallas_call(
        cast_kernel,
        grid=(1,),
        in_specs=[pl.BlockSpec(memory_space=pltpu.HBM)],
        out_specs=whole(ranks, rows, slots, dim),
        out_shape=SDS((ranks, rows, slots, dim), bf16),
        scratch_shapes=[pltpu.VMEM((rows, slots, dim), f32), pltpu.SemaphoreType.DMA],
        compiler_params=pltpu.CompilerParams(vmem_limit_bytes=16 << 20),
        name="cast",
    )(swap(master))
    every = lax.all_to_all(jnp.swapaxes(mine, 1, 2), "dp", split_axis=0, concat_axis=0, tiled=True)
    x, a, dy, mix, bias = prep(scal, tokens, cotangent, norm_params, talk)
    every, x = lax.optimization_barrier((every, x))
    attn_w, ffn_w = call(
        select_kernel, "select", 1, 2, [SDS((4, rows, dim), bf16), SDS((9, rows, dim), bf16)]
    )(block_slot, every, conv)
    attn_2, attn_1 = permute(attn_w, "head", 2), permute(attn_w, "head", 1)
    attn_3 = permute(attn_2, "head", 1)
    attn_w = [attn_w, attn_1, attn_2, attn_3]
    ffn_2, ffn_1 = permute(ffn_w, "head", 2), permute(ffn_w, "head", 1)
    mid, q, k, v, o, qw, p, pv = attn_fwd(scal, x, a, mix, bias, attn_w)
    mid, ffn_2 = lax.optimization_barrier((mid, ffn_2))
    ffn_w = [ffn_w, ffn_1, ffn_2, permute(ffn_2, "head", 1)]
    out, dmid, gn2, *ffn_g = ffn(scal, mid, dy, norm_params, o, ffn_w)
    ffn_1, ffn_3 = permute(ffn_g[1], "head", 1), permute(ffn_g[3], "head", 1)
    out_2, out_1 = permute(out, "head", 2), permute(out, "head", 1)
    do, gqa, *sums = scores_back(scal, dmid, mix, q, k, v, qw, p, pv, attn_w, 0)
    do, ffn_1, ffn_3, out_1, out_2 = lax.optimization_barrier((do, ffn_1, ffn_3, out_1, out_2))
    (half,) = call(half_sum_kernel, "half_sum", 0, 2, [SDS(ffn_3.shape, bf16)])(ffn_g[2], ffn_3)
    ffn_2, out_3 = permute(half, "head", 2), permute(out_2, "head", 1)
    gqb, gk, gv, gt = scores_back(scal, dmid, mix, q, k, v, qw, p, pv, [do, *sums], 1)
    tg, *attn_g = weights_back(scal, x, a, dmid, norm_params, gn2, gqa, gqb, gk, gv, gt, attn_w)
    attn_1, attn_3 = permute(attn_g[1], "head", 1), permute(attn_g[3], "head", 1)
    (half,) = call(half_sum_kernel, "half_sum", 0, 2, [SDS(attn_3.shape, bf16)])(attn_g[2], attn_3)
    attn_2 = permute(half, "head", 2)
    (message,) = call(
        spread_ffn_kernel, "spread_ffn", 1, 3, [SDS((ranks * slots, rows, 256), bf16)], ranks=ranks
    )(block_slot, ffn_g[0], ffn_1, ffn_2)
    tg, attn_2, message, out_3 = lax.optimization_barrier((tg, attn_2, message, out_3))
    tg_2, tg_1 = permute(tg, "head", 2), permute(tg, "head", 1)
    tg_3 = permute(tg_2, "head", 1)
    (message,) = call(
        spread_attn_kernel, "spread_attn", 1, 4, [SDS(message.shape, bf16)], ranks=ranks
    )(block_slot, message, attn_g[0], attn_1, attn_2)
    got = lax.all_to_all(message, "dp", split_axis=0, concat_axis=0, tiled=True)
    shape = SDS((parts,) + tokens.shape[1:], f32)
    (output,) = call(assemble_kernel, "assemble", 1, parts, [shape])(scal, out, out_1, out_2, out_3)
    (token_grad,) = call(assemble_kernel, "assemble", 1, parts, [shape])(scal, tg, tg_1, tg_2, tg_3)
    state = [
        swap(master), swap(master_m1), swap(master_m2), norm_params, norm_m1, norm_m2,
        swap(talk), swap(talk_m1), swap(talk_m2), conv, conv_m1, conv_m2,
    ]
    shapes = [SDS(t.shape, f32) for t in state]
    shapes.insert(3, SDS(state[0].shape, bf16))
    new = staged(
        functools.partial(update_kernel, ranks=ranks), "update", [got, *state], shapes,
        [pltpu.VMEM((rows, slots, dim), f32), pltpu.VMEM((slots, 64, 256), f32), pltpu.VMEM((64, 256), f32)],
    )
    new = [swap(t) if t.ndim == 3 else t for t in new]
    return (output, token_grad, *new)


def solution(mesh):
    in_specs = (
        P("dp", None, None),
        P("dp", None, None),
        P("dp"),
        P(),
        P(),
        P(),
        P("dp", None, "head"),
        P("dp", None, "head"),
        P("dp", None, "head"),
        P(),
        P(),
        P(),
        P(),
        P(),
        P(),
        P(None, "head"),
        P(None, "head"),
        P(None, "head"),
    )
    out_specs = (
        P("dp", None, None),
        P("dp", None, None),
        P("dp", None, "head"),
        P("dp", None, "head"),
        P("dp", None, "head"),
        P("dp", None, "head"),
        P(),
        P(),
        P(),
        P(),
        P(),
        P(),
        P(None, "head"),
        P(None, "head"),
        P(None, "head"),
    )
    return jax.shard_map(local, mesh=mesh, in_specs=in_specs, out_specs=out_specs, check_vma=False)
```

time: 101 us -> 81.4 us (0.81)
  waiting for transfers between devices: 36.5 us -> 28 us
  Pallas kernels: 34.3 us -> 26 us
  starting transfers between devices: 21.6 us -> 20.2 us
  local copies, waits for them, and re-layouts: 4.8 us -> 3.63 us
    ppermute x18, waiting for transfers between devices: 23.2 us -> 14.4 us  [permute(): lax.ppermute(x, axis, [(i, i ^ k) for i in range(lax.axis_size(axis))])]
    pallas_call x5 -> x11, Pallas kernels: 29.3 us -> 21.9 us  [the longest x2 6.34 us: scores_back(): call(scores_back_kernel, 'scores_back', 1, 8 + len(more), outs, scratch,...]
    ppermute x18, starting transfers between devices: 10.5 us -> 9.19 us  [permute(): lax.ppermute(x, axis, [(i, i ^ k) for i in range(lax.axis_size(axis))])]
    all_to_all x1, waiting for transfers between devices: 2.94 us -> 4.24 us  [local(): got = lax.all_to_all(message, 'dp', split_axis=0, concat_axis=0, tiled=True)]
    all_to_all x1, waiting for transfers between devices: 10.4 us -> 9.3 us  [local(): lax.all_to_all(jnp.swapaxes(mine, 1, 2), 'dp', split_axis=0, concat_axis=...]
    pallas_call x1 -> x0, local copies, waits for them, and re-layouts: 1.1 us -> none  [local(): call(spread_kernel, 'spread', 1, 2 * parts, [SDS((ranks, slots, rows, 256...]
    pallas_call x2 -> x1, Pallas kernels: 2.05 us -> 1.17 us  [staged(): pl.pallas_call(body, grid=(1,), in_specs=[whole(*t.shape) for t in ins],...]
  transfers between devices with their start and end apart: 20 -> 20, of which waited for: 11 -> 9; matrix products, arithmetic and copies ran while one was open for 3% -> 3% of each run, Pallas kernels for 24% -> 19%
where the time goes in v4:
time: 81.4 us; the launch traced here: 81 us
  waiting for transfers between devices  28 us (34%)
  Pallas kernels  26 us (32%)
  starting transfers between devices  20.2 us (25%)
  local copies, waits for them, and re-layouts  3.63 us (4%)
  between operations  3.08 us (4%)
    ppermute x18, waiting for transfers between devices, permute(): lax.ppermute(x, axis, [(i, i ^ k) for i in range(lax.axis_size(axis))])  14.4 us
    all_to_all x1, waiting for transfers between devices, local(): lax.all_to_all(jnp.swapaxes(mine, 1, 2), 'dp', split_axis=0, concat_axis=...  9.3 us
    ppermute x18, starting transfers between devices, permute(): lax.ppermute(x, axis, [(i, i ^ k) for i in range(lax.axis_size(axis))])  9.19 us
    all_to_all x1, starting transfers between devices, local(): lax.all_to_all(jnp.swapaxes(mine, 1, 2), 'dp', split_axis=0, concat_axis=...  7.26 us
    pallas_call x2, Pallas kernels, scores_back(): call(scores_back_kernel, 'scores_back', 1, 8 + len(more), outs, scratch,...  6.34 us
    pallas_call x1, Pallas kernels, ffn(): call(ffn_kernel, 'ffn', 1, 4 + len(w), [SDS((SIDE * SIDE, dim), bf16), SD...  6.28 us
    pallas_call x1, Pallas kernels, attn_fwd(): call(attn_fwd_kernel, 'attn_fwd', 1, 4 + len(w), [SDS((pad, dim), f32)] +...  4.96 us
    all_to_all x1, waiting for transfers between devices, local(): got = lax.all_to_all(message, 'dp', split_axis=0, concat_axis=0, tiled=True)  4.24 us
  transfers between devices with their start and end apart: 20, of which 9 were waited for; matrix products, arithmetic and copies ran while one was open for 3% of the time, Pallas kernels for 19%

profile of v4, /device:TPU:0, one launch (start us, length us, event | category | flops | bytes accessed | tf_op | source)
XLA Modules:
  0.0 81.0 jit_solution(13320956802607623885)
XLA Ops:
  0.6 0.0 copy-start
  0.7 0.9 %copy-done = f32[2,54,216]{2,0,1:T(2,128)S(1)} copy-done((f32[2,54,216]{2,0,1:T(2,128)S(1)}, f32[2,54,216]{2,0,1:T(2,128)}, u32[]{:S(2)}) %copy-start) | copy-done | bytes 93336
  1.6 1.0 %cast.1 = bf16[8,54,2,216]{3,2,1,0:T(2,128)(2,1)} custom-call(f32[54,2,216]{2,1,0:T(2,128)S(1)} %bitcast.15), custom_call_target="tpu_custom_call" | custom-call | tf_op jit(solution)/shard_map/cast/pallas_call | solution.py:589
  2.6 7.3 %all-to-all-start = ((bf16[8,2,54,216]{3,1,2,0:T(2,128)(2,1)}), bf16[8,2,54,216]{3,1,2,0:T(2,128)(2,1)S(1)}, u32[]{:S(2)}, u32[]{:S(2)}) async-start(bf16[8,2,54,216]{3,1,2,0:T(2,128)(2,1)} %bitcast.2), calls=%async_computation | async-start | bytes 884736 | tf_op jit(solution)/shard_map/all_to_all | solution.py:599
  11.9 0.2 copy.40.cot_ref
  12.1 0.1 pad_add_fusion.scal
  12.2 1.1 %prep.1 = (f32[224,216]{1,0:T(8,128)S(1)}, bf16[224,216]{1,0:T(8,128)(2,1)S(1)}, f32[224,216]{1,0:T(8,128)S(1)}, f32[2,192,256]{2,1,0:T(8,128)S(1)}, f32[224,192]{1,0:T(8,128)S(1)}) custom-call(s32[4]{0:T(128)S(1)} %pad_add_fusion.scal, bf16[4,196,216]{2,1,0:T(8,128)(2,1)S(1)} %copy.39.tok_ref, f32[4,196,216]{2,1,0:T(8,128)S(1)} %copy.40.cot_ref, ...), custom_call_target="tpu_custom_call" | custom-call | flops 1000000000 | bytes 3000000 | tf_op jit(solution)/shard_map/prep/pallas_call | solution.py:474
  13.3 9.3 %all-to-all-done = bf16[8,2,54,216]{3,1,2,0:T(2,128)(2,1)S(1)} async-done(((bf16[8,2,54,216]{3,1,2,0:T(2,128)(2,1)}), bf16[8,2,54,216]{3,1,2,0:T(2,128)(2,1)S(1)}, u32[]{:S(2)}, u32[]{:S(2)}) %all-to-all-start) | async-done | bytes 373280 | tf_op jit(solution)/shard_map/all_to_all | solution.py:599
  22.6 0.1 copy.42.every_ref
  22.7 0.6 select.1
  23.3 1.6 %collective-permute-start.1 = (bf16[4,54,216]{2,1,0:T(8,128)(2,1)S(1)}, bf16[4,54,216]{2,1,0:T(8,128)(2,1)S(1)}, u32[]{:S(2)}, u32[]{:S(2)}) collective-permute-start(bf16[4,54,216]{2,1,0:T(8,128)(2,1)S(1)} %get-tuple-element.84.refs_0_), channel_id=1, source_target_pairs={{0,2},{1,3},{2,0},{3,1},{4,6},{5,7},{6,4},{7,5},{8,10},{9,11},{10,... | collective-permute-start | bytes 279944 | tf_op jit(solution)/shard_map/ppermute | solution.py:555
  24.9 3.3 %collective-permute-done.1.refs_2_ = bf16[4,54,216]{2,1,0:T(8,128)(2,1)S(1)} collective-permute-done((bf16[4,54,216]{2,1,0:T(8,128)(2,1)S(1)}, bf16[4,54,216]{2,1,0:T(8,128)(2,1)S(1)}, u32[]{:S(2)}, u32[]{:S(2)}) %collective-permute-start.1) | collective-permute-done | bytes 93344 | tf_op jit(solution)/shard_map/ppermute | solution.py:555
  28.2 0.5 collective-permute-start.4
  28.7 1.5 %collective-permute-start.3 = (bf16[9,54,216]{2,1,0:T(8,128)(2,1)S(1)}, bf16[9,54,216]{2,1,0:T(8,128)(2,1)S(1)}, u32[]{:S(2)}, u32[]{:S(2)}) collective-permute-start(bf16[9,54,216]{2,1,0:T(8,128)(2,1)S(1)} %get-tuple-element.86.refs_0_), channel_id=1, source_target_pairs={{0,2},{1,3},{2,0},{3,1},{4,6},{5,7},{6,4},{7,5},{8,10},{9,11},{10,... | collective-permute-start | bytes 629864 | tf_op jit(solution)/shard_map/ppermute | solution.py:555
  30.2 5.0 %attn_fwd.1 = (f32[224,216]{1,0:T(8,128)S(1)}, bf16[224,256]{1,0:T(8,128)(2,1)S(1)}, bf16[224,256]{1,0:T(8,128)(2,1)S(1)}, bf16[224,256]{1,0:T(8,128)(2,1)S(1)},...) custom-call(s32[4]{0:T(128)S(1)} %pad_add_fusion.scal, ...), custom_call_target="tpu_custom_call" | custom-call | flops 10000000000 | bytes 30000000 | tf_op jit(solution)/shard_map/attn_fwd/pallas_call | solution.py:499
  35.2 1.6 %collective-permute-done.3.refs_2_ = bf16[9,54,216]{2,1,0:T(8,128)(2,1)S(1)} collective-permute-done((bf16[9,54,216]{2,1,0:T(8,128)(2,1)S(1)}, bf16[9,54,216]{2,1,0:T(8,128)(2,1)S(1)}, u32[]{:S(2)}, u32[]{:S(2)}) %collective-permute-start.3) | collective-permute-done | bytes 209984 | tf_op jit(solution)/shard_map/ppermute | solution.py:555
  36.8 1.5 %collective-permute-done.5.refs_3_ = bf16[9,54,216]{2,1,0:T(8,128)(2,1)S(1)} collective-permute-done((bf16[9,54,216]{2,1,0:T(8,128)(2,1)S(1)}, bf16[9,54,216]{2,1,0:T(8,128)(2,1)S(1)}, u32[]{:S(2)}, u32[]{:S(2)}) %collective-permute-start.5) | collective-permute-done | bytes 209984 | tf_op jit(solution)/shard_map/ppermute | solution.py:555
  38.3 6.3 %ffn.1 = (bf16[196,216]{1,0:T(8,128)(2,1)S(1)}, f32[224,216]{1,0:T(8,128)S(1)}, f32[8,216]{1,0:T(8,128)S(1)}, bf16[9,54,256]{2,1,0:T(8,128)(2,1)S(1)}, bf16[9,54...) custom-call(s32[4]{0:T(128)S(1)} %pad_add_fusion.scal, ...), custom_call_target="tpu_custom_call" | custom-call | flops 6000000000 | bytes 18000000 | tf_op jit(solution)/shard_map/ffn/pallas_call | solution.py:511
  44.6 1.6 %collective-permute-start.9 = (bf16[196,216]{1,0:T(8,128)(2,1)S(1)}, bf16[196,216]{1,0:T(8,128)(2,1)S(1)}, u32[]{:S(2)}, u32[]{:S(2)}) collective-permute-start(bf16[196,216]{1,0:T(8,128)(2,1)S(1)} %get-tuple-element.91.refs_0_), channel_id=1, source_target_pairs={{0,2},{1,3},{2,0},{3,1},{4,6},{5,7},{6,4},{7,5},{8,10},{9,11},{10,... | collective-permute-start | bytes 254024 | tf_op jit(solution)/shard_map/ppermute | solution.py:555
  46.2 0.5 collective-permute-start.6
  46.7 2.9 %scores_back.2 = (bf16[224,256]{1,0:T(8,128)(2,1)S(1)}, bf16[112,256]{1,0:T(8,128)(2,1)S(1)}, f32[224,256]{1,0:T(8,128)S(1)}, f32[224,256]{1,0:T(8,128)S(1)}, f3...) custom-call(s32[4]{0:T(128)S(1)} %pad_add_fusion.scal, f32[224,216]{1,0:T(8,128)S(1)} %get-tuple-element.92.dmid_ref, ...), custom_call_target="tpu_custom_call" | custom-call | flops 4000000000 | bytes 12000000 | tf_op jit(solution)/shard_map/scores_back/pallas_call | solution.py:537
  49.7 0.1 half_sum.3
  49.8 1.5 %collective-permute-start.12 = (bf16[9,54,256]{2,1,0:T(8,128)(2,1)S(1)}, bf16[9,54,256]{2,1,0:T(8,128)(2,1)S(1)}, u32[]{:S(2)}, u32[]{:S(2)}) collective-permute-start(bf16[9,54,256]{2,1,0:T(8,128)(2,1)S(1)} %half_sum.3), channel_id=1, source_target_pairs={{0,2},{1,3},{2,0},{3,1},{4,6},{5,7},{6,4},{7,5},{8,10},{9,11},{10,... | collective-permute-start | bytes 746504 | tf_op jit(solution)/shard_map/ppermute | solution.py:555
  51.3 3.4 %scores_back.3 = (bf16[112,256]{1,0:T(8,128)(2,1)S(1)}, bf16[224,256]{1,0:T(8,128)(2,1)S(1)}, bf16[224,256]{1,0:T(8,128)(2,1)S(1)}, f32[2,12,12]{2,1,0:T(8,128)S(1)}) custom-call(s32[4]{0:T(128)S(1)} %pad_add_fusion.scal, f32[224,216]{1,0:T(8,128)S(1)} %get-tuple-element.92.dmid_ref, f32[2,192,256]{2,1,0:T(8,128)S(1)} %get-tuple-element.81.mix_ref, ...), custom_call_target="tpu_custom_call" | custom-call | flops 4000000000 | bytes 12000000 | tf_op jit(solution)/shard_map/scores_back/pallas_call | solution.py:537
  54.7 1.2 %weights_back.1 = (bf16[196,216]{1,0:T(8,128)(2,1)S(1)}, bf16[3,54,256]{2,1,0:T(8,128)(2,1)S(1)}, bf16[3,54,256]{2,1,0:T(8,128)(2,1)S(1)}, bf16[3,54,256]{2,1,0:T(8,128)(2,1)S(1)}, bf16[3,54,256]{2,1,0:T(8,128)(2,1)S(1)}) custom-call(s32[4]{0:T(128)S(1)} %pad_add_fusion.scal, f32[224,216]{1,0:T(8,128)S(1)} %get-tuple-element.79.x_ref, ...), custom_call_target="tpu_custom_call" | custom-call | flops 3000000000 | bytes 9000000 | tf_op jit(solution)/shard_map/weights_back/pallas_call | solution.py:545
  55.8 0.1 collective-permute-start.10
  55.9 0.5 collective-permute-start.17
  56.4 0.1 collective-permute-start.13
  56.5 0.7 collective-permute-done.10.b_ref
  57.2 0.7 collective-permute-start.11
  57.9 0.6 collective-permute-done.12.refs_2_
  58.5 0.7 spread_ffn.1.old_ref
  59.2 2.7 %collective-permute-done.11.refs_2_ = bf16[3,54,256]{2,1,0:T(8,128)(2,1)S(1)} collective-permute-done((bf16[3,54,256]{2,1,0:T(8,128)(2,1)S(1)}, bf16[3,54,256]{2,1,0:T(8,128)(2,1)S(1)}, u32[]{:S(2)}, u32[]{:S(2)}) %collective-permute-start.11) | collective-permute-done | bytes 82976 | tf_op jit(solution)/shard_map/ppermute | solution.py:555
  61.9 1.4 %spread_attn.1 = bf16[16,54,256]{2,1,0:T(8,128)(2,1)} custom-call(s32[12]{0:T(128)S(1)} %copy-done.13, bf16[16,54,256]{2,1,0:T(8,128)(2,1)S(1)} %spread_ffn.1.old_ref, bf16[3,54,256]{2,1,0:T(8,128)(2,1)S(1)} %get-tuple-element.125.refs_0_, bf16[3,54,256]{2,1,0:T(8,128)(2,1)S(1)} %collective-permute-done.17.refs_1_, ...), custom_call_target="tpu_custom_call" | custom-call | flops 1000000000 | bytes 3000000 | tf_op jit(solution)/shard_map/spread_attn/pallas_call | solution.py:630
  63.3 3.8 %all-to-all-start.1 = ((bf16[16,54,256]{2,1,0:T(8,128)(2,1)}), bf16[16,54,256]{2,1,0:T(8,128)(2,1)S(1)}, u32[]{:S(2)}, u32[]{:S(2)}) async-start(bf16[16,54,256]{2,1,0:T(8,128)(2,1)} %spread_attn.1), calls=%async_computation.1 | async-start | bytes 917504 | tf_op jit(solution)/shard_map/all_to_all | solution.py:633
  67.0 0.7 collective-permute-start.15
  67.7 4.0 %collective-permute-done.15.refs_2_ = bf16[196,216]{1,0:T(8,128)(2,1)S(1)} collective-permute-done((bf16[196,216]{1,0:T(8,128)(2,1)S(1)}, bf16[196,216]{1,0:T(8,128)(2,1)S(1)}, u32[]{:S(2)}, u32[]{:S(2)}) %collective-permute-start.15) | collective-permute-done | bytes 84704 | tf_op jit(solution)/shard_map/ppermute | solution.py:555
  71.7 0.6 assemble.2
  72.3 1.2 %copy.43 = f32[4,196,216]{2,0,1:T(4,128)} copy(f32[4,196,216]{2,1,0:T(8,128)S(1)} %assemble.2) | data formatting | bytes 1354752
  73.5 0.6 assemble.3
  74.1 0.0 copy-start.1
  74.1 0.0 copy-start.3
  74.1 0.0 copy-start.4
  74.2 0.0 copy-start.8
  74.2 0.0 copy-start.9
  74.2 1.2 %copy.44 = f32[4,196,216]{2,0,1:T(4,128)} copy(f32[4,196,216]{2,1,0:T(8,128)S(1)} %assemble.3) | data formatting | bytes 1354752
  75.4 4.2 %all-to-all-done.1.got_ref = bf16[16,54,256]{2,1,0:T(8,128)(2,1)S(1)} async-done(((bf16[16,54,256]{2,1,0:T(8,128)(2,1)}), bf16[16,54,256]{2,1,0:T(8,128)(2,1)S(1)}, u32[]{:S(2)}, u32[]{:S(2)}) %all-to-all-start.1) | async-done | bytes 442400 | tf_op jit(solution)/shard_map/all_to_all | solution.py:633
  79.7 1.2 %update.1 = (f32[54,2,216]{2,1,0:T(2,128)}, f32[54,2,216]{2,1,0:T(2,128)}, f32[54,2,216]{2,1,0:T(2,128)}, bf16[54,2,216]{2,1,0:T(2,128)(2,1)}, f32[4,216]{1,0:T(...) custom-call(bf16[16,54,256]{2,1,0:T(8,128)(2,1)S(1)} %all-to-all-don, ...), custom_call_target="tpu_custom_call" | custom-call | flops 1000000000 | bytes 3000000 | tf_op jit(solution)/shard_map/update/pallas_call | solution.py:567
  (46 shorter events, 0.2 us)
Async XLA Ops:
  0.6 0.9 %copy-start = (f32[2,54,216]{2,0,1:T(2,128)S(1)}, f32[2,54,216]{2,0,1:T(2,128)}, u32[]{:S(2)}) copy-start(f32[2,54,216]{2,0,1:T(2,128)} %param.24) | copy-start | bytes 279940
  1.5 10.3 %copy-start.2 = (f32[2,12,12]{2,0,1:T(2,128)S(1)}, f32[2,12,12]{2,0,1:T(2,128)}, u32[]{:S(2)}) copy-start(f32[2,12,12]{2,0,1:T(2,128)} %param.30) | copy-start | bytes 3460
  1.5 10.3 %copy-start.15 = (bf16[4,196,216]{2,0,1:T(4,128)(2,1)S(1)}, bf16[4,196,216]{2,0,1:T(4,128)(2,1)}, u32[]{:S(2)}) copy-start(bf16[4,196,216]{2,0,1:T(4,128)(2,1)} %param.18) | copy-start | bytes 1016068
  1.6 10.4 %copy-start.14 = (f32[4,196,216]{2,0,1:T(4,128)S(1)}, f32[4,196,216]{2,0,1:T(4,128)}, u32[]{:S(2)}) copy-start(f32[4,196,216]{2,0,1:T(4,128)} %param.19) | copy-start | bytes 2032132
  2.6 20.0 %all-to-all-start = ((bf16[8,2,54,216]{3,1,2,0:T(2,128)(2,1)}), bf16[8,2,54,216]{3,1,2,0:T(2,128)(2,1)S(1)}, u32[]{:S(2)}, u32[]{:S(2)}) async-start(bf16[8,2,54,216]{3,1,2,0:T(2,128)(2,1)} %bitcast.2), calls=%async_computation | async-start | bytes 884736 | tf_op jit(solution)/shard_map/all_to_all | solution.py:599
  9.9 2.3 %copy-start.10 = (f32[4,216]{1,0:T(4,128)S(1)}, f32[4,216]{1,0:T(4,128)}, u32[]{:S(2)}) copy-start(f32[4,216]{1,0:T(4,128)} %refs_3_.1) | copy-start | bytes 10372
  12.2 10.5 %copy-start.5 = (f32[9,216]{1,0:T(8,128)S(1)}, f32[9,216]{1,0:T(8,128)}, u32[]{:S(2)}) copy-start(f32[9,216]{1,0:T(8,128)} %refs_9_.1) | copy-start | bytes 23332
  12.2 10.5 %copy-start.13 = (s32[12]{0:T(128)S(1)}, s32[12]{0:T(128)}, u32[]{:S(2)}) copy-start(s32[12]{0:T(128)} %slot_ref.5) | copy-start | bytes 148
  23.3 4.9 %collective-permute-start.1 = (bf16[4,54,216]{2,1,0:T(8,128)(2,1)S(1)}, bf16[4,54,216]{2,1,0:T(8,128)(2,1)S(1)}, u32[]{:S(2)}, u32[]{:S(2)}) collective-permute-start(bf16[4,54,216]{2,1,0:T(8,128)(2,1)S(1)} %get-tuple-element.84.refs_0_), channel_id=1, source_target_pairs={{0,2},{1,3},{2,0},{3,1},{4,6},{5,7},{6,4},{7,5},{8,10},{9,11},{10,... | collective-permute-start | bytes 279944 | tf_op jit(solution)/shard_map/ppermute | solution.py:555
  24.9 5.3 %collective-permute-start = (bf16[4,54,216]{2,1,0:T(8,128)(2,1)S(1)}, bf16[4,54,216]{2,1,0:T(8,128)(2,1)S(1)}, u32[]{:S(2)}, u32[]{:S(2)}) collective-permute-start(bf16[4,54,216]{2,1,0:T(8,128)(2,1)S(1)} %get-tuple-element.84.refs_0_), channel_id=1, source_target_pairs={{0,1},{1,0},{2,3},{3,2},{4,5},{5,4},{6,7},{7,6},{8,9},{9,8},{10,11... | collective-permute-start | bytes 279944 | tf_op jit(solution)/shard_map/ppermute | solution.py:555
  28.2 2.0 %collective-permute-start.2 = (bf16[4,54,216]{2,1,0:T(8,128)(2,1)S(1)}, bf16[4,54,216]{2,1,0:T(8,128)(2,1)S(1)}, u32[]{:S(2)}, u32[]{:S(2)}) collective-permute-start(bf16[4,54,216]{2,1,0:T(8,128)(2,1)S(1)} %collective-permute-done.1.refs_2_), channel_id=1, source_target_pairs={{0,1},{1,0},{2,3},{3,2},{4,5},{5,4},{6,7},{7,6},{8,9},{9,8},{10,11... | collective-permute-start | bytes 279944 | tf_op jit(solution)/shard_map/ppermute | solution.py:555
  28.2 8.6 %collective-permute-start.4 = (bf16[9,54,216]{2,1,0:T(8,128)(2,1)S(1)}, bf16[9,54,216]{2,1,0:T(8,128)(2,1)S(1)}, u32[]{:S(2)}, u32[]{:S(2)}) collective-permute-start(bf16[9,54,216]{2,1,0:T(8,128)(2,1)S(1)} %get-tuple-element.86.refs_0_), channel_id=1, source_target_pairs={{0,1},{1,0},{2,3},{3,2},{4,5},{5,4},{6,7},{7,6},{8,9},{9,8},{10,11... | collective-permute-start | bytes 629864 | tf_op jit(solution)/shard_map/ppermute | solution.py:555
  28.7 8.1 %collective-permute-start.3 = (bf16[9,54,216]{2,1,0:T(8,128)(2,1)S(1)}, bf16[9,54,216]{2,1,0:T(8,128)(2,1)S(1)}, u32[]{:S(2)}, u32[]{:S(2)}) collective-permute-start(bf16[9,54,216]{2,1,0:T(8,128)(2,1)S(1)} %get-tuple-element.86.refs_0_), channel_id=1, source_target_pairs={{0,2},{1,3},{2,0},{3,1},{4,6},{5,7},{6,4},{7,5},{8,10},{9,11},{10,... | collective-permute-start | bytes 629864 | tf_op jit(solution)/shard_map/ppermute | solution.py:555
  36.8 1.5 %collective-permute-start.5 = (bf16[9,54,216]{2,1,0:T(8,128)(2,1)S(1)}, bf16[9,54,216]{2,1,0:T(8,128)(2,1)S(1)}, u32[]{:S(2)}, u32[]{:S(2)}) collective-permute-start(bf16[9,54,216]{2,1,0:T(8,128)(2,1)S(1)} %collective-permute-done.3.refs_2_), channel_id=1, source_target_pairs={{0,1},{1,0},{2,3},{3,2},{4,5},{5,4},{6,7},{7,6},{8,9},{9,8},{10,11... | collective-permute-start | bytes 629864 | tf_op jit(solution)/shard_map/ppermute | solution.py:555
  44.6 5.1 %collective-permute-start.9 = (bf16[196,216]{1,0:T(8,128)(2,1)S(1)}, bf16[196,216]{1,0:T(8,128)(2,1)S(1)}, u32[]{:S(2)}, u32[]{:S(2)}) collective-permute-start(bf16[196,216]{1,0:T(8,128)(2,1)S(1)} %get-tuple-element.91.refs_0_), channel_id=1, source_target_pairs={{0,2},{1,3},{2,0},{3,1},{4,6},{5,7},{6,4},{7,5},{8,10},{9,11},{10,... | collective-permute-start | bytes 254024 | tf_op jit(solution)/shard_map/ppermute | solution.py:555
  46.2 3.5 %collective-permute-start.8 = (bf16[196,216]{1,0:T(8,128)(2,1)S(1)}, bf16[196,216]{1,0:T(8,128)(2,1)S(1)}, u32[]{:S(2)}, u32[]{:S(2)}) collective-permute-start(bf16[196,216]{1,0:T(8,128)(2,1)S(1)} %get-tuple-element.91.refs_0_), channel_id=1, source_target_pairs={{0,1},{1,0},{2,3},{3,2},{4,5},{5,4},{6,7},{7,6},{8,9},{9,8},{10,11... | collective-permute-start | bytes 254024 | tf_op jit(solution)/shard_map/ppermute | solution.py:555
  46.2 3.5 %collective-permute-start.6 = (bf16[9,54,256]{2,1,0:T(8,128)(2,1)S(1)}, bf16[9,54,256]{2,1,0:T(8,128)(2,1)S(1)}, u32[]{:S(2)}, u32[]{:S(2)}) collective-permute-start(bf16[9,54,256]{2,1,0:T(8,128)(2,1)S(1)} %get-tuple-element.100), channel_id=1, source_target_pairs={{0,1},{1,0},{2,3},{3,2},{4,5},{5,4},{6,7},{7,6},{8,9},{9,8},{10,11... | collective-permute-start | bytes 746504 | tf_op jit(solution)/shard_map/ppermute | solution.py:555
  46.7 3.0 %collective-permute-start.7 = (bf16[9,54,256]{2,1,0:T(8,128)(2,1)S(1)}, bf16[9,54,256]{2,1,0:T(8,128)(2,1)S(1)}, u32[]{:S(2)}, u32[]{:S(2)}) collective-permute-start(bf16[9,54,256]{2,1,0:T(8,128)(2,1)S(1)} %get-tuple-element.101), channel_id=1, source_target_pairs={{0,1},{1,0},{2,3},{3,2},{4,5},{5,4},{6,7},{7,6},{8,9},{9,8},{10,11... | collective-permute-start | bytes 746504 | tf_op jit(solution)/shard_map/ppermute | solution.py:555
  49.8 8.7 %collective-permute-start.12 = (bf16[9,54,256]{2,1,0:T(8,128)(2,1)S(1)}, bf16[9,54,256]{2,1,0:T(8,128)(2,1)S(1)}, u32[]{:S(2)}, u32[]{:S(2)}) collective-permute-start(bf16[9,54,256]{2,1,0:T(8,128)(2,1)S(1)} %half_sum.3), channel_id=1, source_target_pairs={{0,2},{1,3},{2,0},{3,1},{4,6},{5,7},{6,4},{7,5},{8,10},{9,11},{10,... | collective-permute-start | bytes 746504 | tf_op jit(solution)/shard_map/ppermute | solution.py:555
  55.8 1.3 %collective-permute-start.10 = (bf16[3,54,256]{2,1,0:T(8,128)(2,1)S(1)}, bf16[3,54,256]{2,1,0:T(8,128)(2,1)S(1)}, u32[]{:S(2)}, u32[]{:S(2)}) collective-permute-start(bf16[3,54,256]{2,1,0:T(8,128)(2,1)S(1)} %get-tuple-element.117), channel_id=1, source_target_pairs={{0,1},{1,0},{2,3},{3,2},{4,5},{5,4},{6,7},{7,6},{8,9},{9,8},{10,11... | collective-permute-start | bytes 248840 | tf_op jit(solution)/shard_map/ppermute | solution.py:555
  55.9 6.0 %collective-permute-start.17 = (bf16[3,54,256]{2,1,0:T(8,128)(2,1)S(1)}, bf16[3,54,256]{2,1,0:T(8,128)(2,1)S(1)}, u32[]{:S(2)}, u32[]{:S(2)}) collective-permute-start(bf16[3,54,256]{2,1,0:T(8,128)(2,1)S(1)} %get-tuple-element.126), channel_id=1, source_target_pairs={{0,1},{1,0},{2,3},{3,2},{4,5},{5,4},{6,7},{7,6},{8,9},{9,8},{10,11... | collective-permute-start | bytes 248840 | tf_op jit(solution)/shard_map/ppermute | solution.py:555
  56.4 2.7 %collective-permute-start.13 = (bf16[196,216]{1,0:T(8,128)(2,1)S(1)}, bf16[196,216]{1,0:T(8,128)(2,1)S(1)}, u32[]{:S(2)}, u32[]{:S(2)}) collective-permute-start(bf16[196,216]{1,0:T(8,128)(2,1)S(1)} %collective-permute-done.9.refs_2_), channel_id=1, source_target_pairs={{0,1},{1,0},{2,3},{3,2},{4,5},{5,4},{6,7},{7,6},{8,9},{9,8},{10,11... | collective-permute-start | bytes 254024 | tf_op jit(solution)/shard_map/ppermute | solution.py:555
  57.2 4.7 %collective-permute-start.11 = (bf16[3,54,256]{2,1,0:T(8,128)(2,1)S(1)}, bf16[3,54,256]{2,1,0:T(8,128)(2,1)S(1)}, u32[]{:S(2)}, u32[]{:S(2)}) collective-permute-start(bf16[3,54,256]{2,1,0:T(8,128)(2,1)S(1)} %half_sum.2), channel_id=1, source_target_pairs={{0,2},{1,3},{2,0},{3,1},{4,6},{5,7},{6,4},{7,5},{8,10},{9,11},{10,... | collective-permute-start | bytes 248840 | tf_op jit(solution)/shard_map/ppermute | solution.py:555
  63.3 16.4 %all-to-all-start.1 = ((bf16[16,54,256]{2,1,0:T(8,128)(2,1)}), bf16[16,54,256]{2,1,0:T(8,128)(2,1)S(1)}, u32[]{:S(2)}, u32[]{:S(2)}) async-start(bf16[16,54,256]{2,1,0:T(8,128)(2,1)} %spread_attn.1), calls=%async_computation.1 | async-start | bytes 917504 | tf_op jit(solution)/shard_map/all_to_all | solution.py:633
  67.0 4.7 %collective-permute-start.15 = (bf16[196,216]{1,0:T(8,128)(2,1)S(1)}, bf16[196,216]{1,0:T(8,128)(2,1)S(1)}, u32[]{:S(2)}, u32[]{:S(2)}) collective-permute-start(bf16[196,216]{1,0:T(8,128)(2,1)S(1)} %get-tuple-element.123.refs_0_), channel_id=1, source_target_pairs={{0,2},{1,3},{2,0},{3,1},{4,6},{5,7},{6,4},{7,5},{8,10},{9,11},{10,... | collective-permute-start | bytes 254024 | tf_op jit(solution)/shard_map/ppermute | solution.py:555
  67.7 5.8 %collective-permute-start.14 = (bf16[196,216]{1,0:T(8,128)(2,1)S(1)}, bf16[196,216]{1,0:T(8,128)(2,1)S(1)}, u32[]{:S(2)}, u32[]{:S(2)}) collective-permute-start(bf16[196,216]{1,0:T(8,128)(2,1)S(1)} %get-tuple-element.123.refs_0_), channel_id=1, source_target_pairs={{0,1},{1,0},{2,3},{3,2},{4,5},{5,4},{6,7},{7,6},{8,9},{9,8},{10,11... | collective-permute-start | bytes 254024 | tf_op jit(solution)/shard_map/ppermute | solution.py:555
  71.7 1.8 %collective-permute-start.16 = (bf16[196,216]{1,0:T(8,128)(2,1)S(1)}, bf16[196,216]{1,0:T(8,128)(2,1)S(1)}, u32[]{:S(2)}, u32[]{:S(2)}) collective-permute-start(bf16[196,216]{1,0:T(8,128)(2,1)S(1)} %collective-permute-done.15.refs_2_), channel_id=1, source_target_pairs={{0,1},{1,0},{2,3},{3,2},{4,5},{5,4},{6,7},{7,6},{8,9},{9,8},{10,11... | collective-permute-start | bytes 254024 | tf_op jit(solution)/shard_map/ppermute | solution.py:555
  74.1 5.5 %copy-start.1 = (f32[2,54,216]{2,0,1:T(2,128)S(1)}, f32[2,54,216]{2,0,1:T(2,128)}, u32[]{:S(2)}) copy-start(f32[2,54,216]{2,0,1:T(2,128)} %param.24) | copy-start | bytes 279940
  74.1 5.5 %copy-start.3 = (f32[2,54,216]{2,0,1:T(2,128)S(1)}, f32[2,54,216]{2,0,1:T(2,128)}, u32[]{:S(2)}) copy-start(f32[2,54,216]{2,0,1:T(2,128)} %param.25) | copy-start | bytes 279940
  74.1 5.5 %copy-start.4 = (f32[2,54,216]{2,0,1:T(2,128)S(1)}, f32[2,54,216]{2,0,1:T(2,128)}, u32[]{:S(2)}) copy-start(f32[2,54,216]{2,0,1:T(2,128)} %param.26) | copy-start | bytes 279940
  74.2 5.5 %copy-start.6 = (f32[9,216]{1,0:T(8,128)S(1)}, f32[9,216]{1,0:T(8,128)}, u32[]{:S(2)}) copy-start(f32[9,216]{1,0:T(8,128)} %refs_10_.1) | copy-start | bytes 23332
  74.2 5.5 %copy-start.7 = (f32[9,216]{1,0:T(8,128)S(1)}, f32[9,216]{1,0:T(8,128)}, u32[]{:S(2)}) copy-start(f32[9,216]{1,0:T(8,128)} %refs_11_.1) | copy-start | bytes 23332
  74.2 5.5 %copy-start.8 = (f32[2,12,12]{2,0,1:T(2,128)S(1)}, f32[2,12,12]{2,0,1:T(2,128)}, u32[]{:S(2)}) copy-start(f32[2,12,12]{2,0,1:T(2,128)} %param.31) | copy-start | bytes 3460
  74.2 5.5 %copy-start.9 = (f32[2,12,12]{2,0,1:T(2,128)S(1)}, f32[2,12,12]{2,0,1:T(2,128)}, u32[]{:S(2)}) copy-start(f32[2,12,12]{2,0,1:T(2,128)} %param.32) | copy-start | bytes 3460
  74.2 5.5 %copy-start.11 = (f32[4,216]{1,0:T(4,128)S(1)}, f32[4,216]{1,0:T(4,128)}, u32[]{:S(2)}) copy-start(f32[4,216]{1,0:T(4,128)} %refs_4_.1) | copy-start | bytes 10372
  74.2 5.5 %copy-start.12 = (f32[4,216]{1,0:T(4,128)S(1)}, f32[4,216]{1,0:T(4,128)}, u32[]{:S(2)}) copy-start(f32[4,216]{1,0:T(4,128)} %refs_5_.1) | copy-start | bytes 10372

commit v5 on v4

--- a/solution.py
+++ b/solution.py
@@ -301,10 +301,10 @@
 
 
 def weights_back_kernel(
-    scal, x_ref, a_ref, dmid_ref, norm_ref, gn2_ref, gqa_ref, gqb_ref, gk_ref, gv_ref, gt_ref, *refs, parts
+    scal, x_ref, a_ref, dmid_ref, norm_ref, gn2_ref, gqa_ref, gqb_ref, gk_ref, gv_ref, gt_ref, y_ref, *refs, parts
 ):
     w_refs, refs = refs[:parts], refs[parts:]
-    tg_ref, gw_refs, refs = refs[0], refs[1 : 1 + parts], refs[1 + parts :]
+    both_ref, gw_refs, refs = refs[0], refs[1 : 1 + parts], refs[1 + parts :]
     ws_ref, tmp_ref, flat_ref, sm_ref = refs
     heads = gt_ref.shape[1]
     dim = x_ref.shape[1]
@@ -337,23 +337,32 @@
             gw_refs[h][b, :, 0:dim] = gw[64 * h : 64 * h + 54]
     tmp_ref[...] = dmid_ref[...] + ln_back(da, z, inv, norm_ref[0:1, :])
     for y in range(SIDE):
-        tg_ref[SIDE * y : SIDE * (y + 1), :] = tmp_ref[PITCH * y : PITCH * y + SIDE, :].astype(bf16)
+        both_ref[1, SIDE * y : SIDE * (y + 1), :] = tmp_ref[PITCH * y : PITCH * y + SIDE, :].astype(bf16)
+    both_ref[0] = y_ref[...]
 
 
 def cast_kernel(m_hbm, out_ref, m_ref, sem):
     copy = pltpu.make_async_copy(m_hbm, m_ref, sem)
     copy.start()
     copy.wait()
-    low = m_ref[...].astype(bf16)
     for i in range(out_ref.shape[0]):
-        out_ref[i] = low
-
-
-def select_kernel(slot_ref, every_ref, conv_ref, attn_ref, ffn_ref):
-    per = every_ref.shape[1]
+        out_ref[i] = m_ref[:, i, :].astype(bf16)
+
+
+def pair_kernel(own_ref, other_ref, out_ref):
+    out_ref[0] = own_ref[...]
+    out_ref[1] = other_ref[...]
+
+
+def select_kernel(slot_ref, scal, conv_ref, *refs):
+    pairs, (attn_ref, ffn_ref, every_ref) = refs[:-3], refs[-3:]
+    for k, ref in enumerate(pairs):
+        every_ref[scal[5] ^ k] = ref[...]
+    per = every_ref.shape[2]
     for b in range(12):
         slot = slot_ref[b]
-        block = every_ref[slot // per, slot % per]
+        rank = slot // per
+        block = every_ref[rank // 2, (rank % 2) ^ scal[4], slot % per]
         if b < 4:
             attn_ref[b] = block
         else:
@@ -375,30 +384,46 @@
     out_ref[...] = (a_ref[...].astype(f32) + b_ref[...].astype(f32)).astype(bf16)
 
 
-def spread_ffn_kernel(slot_ref, *refs, ranks):
+def spot(slot, scal, per):
+    rank = slot // per
+    return (rank // 2) ^ scal[5], (rank % 2) ^ scal[4], slot % per
+
+
+def spread_ffn_kernel(slot_ref, scal, *refs):
     ffn_refs, out_ref = refs[:-1], refs[-1]
-    per = out_ref.shape[0] // ranks
+    pairs, _, per = out_ref.shape[:3]
     out_ref[...] = jnp.zeros_like(out_ref)
     for b in range(9):
         block = total(ffn_refs, b)
-        out_ref[slot_ref[3 + b], :, 0:FREE] = block[:, 0:FREE].astype(bf16)
+        k, j, i = spot(slot_ref[3 + b], scal, per)
+        out_ref[k, j, i, :, 0:FREE] = block[:, 0:FREE].astype(bf16)
         if b == 0:
             wide = block[:, FREE:].astype(bf16)
-    for r in range(ranks):
-        out_ref[r * per, :, FREE:] = wide
-
-
-def spread_attn_kernel(slot_ref, old_ref, *refs, ranks):
-    attn, out_ref = refs[:-1], refs[-1]
-    per = out_ref.shape[0] // ranks
-    out_ref[...] = old_ref[...]
+    for k in range(pairs):
+        for j in range(2):
+            out_ref[k, j, 0, :, FREE:] = wide
+
+
+def spread_attn_kernel(slot_ref, scal, old_ref, *refs, parts):
+    attn, outs, all_ref = refs[:parts], refs[parts:-1], refs[-1]
+    pairs, _, per = all_ref.shape[:3]
+    all_ref[...] = old_ref[...]
     for b in range(3):
         block = total(attn, b)
-        out_ref[slot_ref[b], :, 0:FREE] = block[:, 0:FREE].astype(bf16)
+        k, j, i = spot(slot_ref[b], scal, per)
+        all_ref[k, j, i, :, 0:FREE] = block[:, 0:FREE].astype(bf16)
         if b == 0:
             wide = block[:, FREE:].astype(bf16)
-    for r in range(ranks):
-        out_ref[r * per + 1, :, FREE:] = wide
+    for k in range(pairs):
+        outs[k][...] = all_ref[k]
+        for j in range(2):
+            outs[k][j, 1, :, FREE:] = wide
+
+
+def pair_sum_kernel(*refs):
+    own_ref, other_ref = refs[-2:]
+    own_ref[...] = total(refs[:-2], 0)
+    other_ref[...] = total(refs[:-2], 1).astype(bf16)
 
 
 def adam(w, g, one, two, rate, decay):
@@ -409,15 +434,12 @@
     return w - rate * (hat_one / (jnp.sqrt(hat_two) + 1e-08) + decay * w), one_new, two_new
 
 
-def update_kernel(got_ref, *refs, ranks):
+def update_kernel(own_ref, other_ref, *refs):
     ins, outs, (g_ref, sm_ref, flat_ref) = refs[0:12], refs[12:25], refs[25:]
-    per = got_ref.shape[0] // ranks
+    per, rows = own_ref.shape[:2]
     dim = ins[0].shape[2]
-    rows = got_ref.shape[1]
     for i in range(per):
-        g = got_ref[i].astype(f32)
-        for r in range(1, ranks):
-            g = g + got_ref[r * per + i].astype(f32)
+        g = own_ref[i] + other_ref[i].astype(f32)
         g_ref[:, i, :] = g[:, 0:dim]
         sm_ref[i, 0:rows, :] = g
     w, one, two = adam(ins[0][...], g_ref[...], ins[1][...], ins[2][...], 0.06, 0.05)
@@ -443,8 +465,22 @@
 
 
 def assemble_kernel(scal, *refs):
-    for k, ref in enumerate(refs[:-1]):
-        refs[-1][scal[0] ^ k] = ref[...].astype(f32)
+    ins, outs, (all_ref,) = refs[:-3], refs[-3:-1], refs[-1:]
+    parts, tokens = len(ins), ins[0].shape[1]
+    step = 32
+    shape = (parts * step, parts * step)
+    row, col = iota(shape, 0), iota(shape, 1)
+    pick = ((row // parts == col % step) & (row % parts == col // step)).astype(bf16)
+    full = all_ref.shape[1]
+    for k in range(parts):
+        all_ref[k, tokens // step * step : full, :] = jnp.zeros((full - tokens // step * step, all_ref.shape[2]), bf16)
+    for i, out_ref in enumerate(outs):
+        for k, ref in enumerate(ins):
+            all_ref[scal[0] ^ k, 0:tokens, :] = ref[i]
+        for at in range(0, tokens, step):
+            mixed = nn(pick, jnp.concatenate([all_ref[k, at : at + step, :] for k in range(parts)], axis=0))
+            for t in range(min(step, tokens - at)):
+                out_ref[at + t] = mixed[parts * t : parts * (t + 1)]
 
 
 VM = pl.BlockSpec(memory_space=pltpu.VMEM)
@@ -501,7 +537,7 @@
         [SDS((pad, dim), f32)] + [SDS((pad, 256), bf16)] * 4
         + [SDS((SIDE, n, 256), bf16), SDS((SIDE, pad, n), bf16), SDS((SIDE, n, 256), bf16)],
         [pltpu.VMEM((4, 256, dim), bf16)],
-        mb=24, micros=10, parts=len(w), unroll=unroll,
+        mb=24, micros=1, parts=len(w), unroll=unroll,
     )(scal, x, a, mix, bias, *w)
 
 
@@ -540,15 +576,15 @@
     )(scal, dmid, mix, q, k, v, qw, p, pv, *more)
 
 
-def weights_back(scal, x, a, dmid, norm_params, gn2, gqa, gqb, gk, gv, gt, w):
+def weights_back(scal, x, a, dmid, norm_params, gn2, gqa, gqb, gk, gv, gt, out, w):
     pad, dim = x.shape
     return call(
-        weights_back_kernel, "weights_back", 1, 10 + len(w),
-        [SDS((SIDE * SIDE, dim), bf16)] + [SDS((3, 54, 256), bf16)] * len(w),
+        weights_back_kernel, "weights_back", 1, 11 + len(w),
+        [SDS((2, SIDE * SIDE, dim), bf16)] + [SDS((3, 54, 256), bf16)] * len(w),
         [pltpu.VMEM((3, 256, dim), bf16), pltpu.VMEM((pad, dim), f32), pltpu.VMEM((24, 256), f32),
          pltpu.VMEM((56, 256), f32)],
         mb=24, micros=3, parts=len(w),
-    )(scal, x, a, dmid, norm_params, gn2, gqa, gqb, gk, gv, gt, *w)
+    )(scal, x, a, dmid, norm_params, gn2, gqa, gqb, gk, gv, gt, out, *w)
 
 
 def permute(x, axis, k):
@@ -585,23 +621,29 @@
     parts = lax.axis_size("head")
     ranks = lax.axis_size("dp")
     place_id = lax.axis_index("head").astype(jnp.int32)
-    scal = jnp.concatenate([place_id[None], image_count, subnet_heads, subnet_width])
+    rank = lax.axis_index("dp").astype(jnp.int32)
+    scal = jnp.concatenate(
+        [place_id[None], image_count, subnet_heads, subnet_width, (rank % 2)[None], (rank // 2)[None]]
+    )
     mine = pl.pallas_call(
         cast_kernel,
         grid=(1,),
         in_specs=[pl.BlockSpec(memory_space=pltpu.HBM)],
-        out_specs=whole(ranks, rows, slots, dim),
-        out_shape=SDS((ranks, rows, slots, dim), bf16),
+        out_specs=whole(slots, rows, dim),
+        out_shape=SDS((slots, rows, dim), bf16),
         scratch_shapes=[pltpu.VMEM((rows, slots, dim), f32), pltpu.SemaphoreType.DMA],
         compiler_params=pltpu.CompilerParams(vmem_limit_bytes=16 << 20),
         name="cast",
     )(swap(master))
-    every = lax.all_to_all(jnp.swapaxes(mine, 1, 2), "dp", split_axis=0, concat_axis=0, tiled=True)
-    x, a, dy, mix, bias = prep(scal, tokens, cotangent, norm_params, talk)
-    every, x = lax.optimization_barrier((every, x))
+    (pair,) = call(pair_kernel, "pair", 0, 2, [SDS((2, slots, rows, dim), bf16)])(mine, permute(mine, "dp", 1))
+    pair, tokens, cotangent, talk_in = lax.optimization_barrier((pair, tokens, cotangent, talk))
+    pairs = [pair] + [permute(pair, "dp", 2 * k) for k in range(1, ranks // 2)]
+    x, a, dy, mix, bias = prep(scal, tokens, cotangent, norm_params, talk_in)
+    pairs[1], x = lax.optimization_barrier((pairs[1], x))
     attn_w, ffn_w = call(
-        select_kernel, "select", 1, 2, [SDS((4, rows, dim), bf16), SDS((9, rows, dim), bf16)]
-    )(block_slot, every, conv)
+        select_kernel, "select", 2, 1 + len(pairs), [SDS((4, rows, dim), bf16), SDS((9, rows, dim), bf16)],
+        [pltpu.VMEM((ranks // 2, 2, slots, rows, dim), bf16)],
+    )(block_slot, scal, conv, *pairs)
     attn_2, attn_1 = permute(attn_w, "head", 2), permute(attn_w, "head", 1)
     attn_3 = permute(attn_2, "head", 1)
     attn_w = [attn_w, attn_1, attn_2, attn_3]
@@ -611,29 +653,43 @@
     ffn_w = [ffn_w, ffn_1, ffn_2, permute(ffn_2, "head", 1)]
     out, dmid, gn2, *ffn_g = ffn(scal, mid, dy, norm_params, o, ffn_w)
     ffn_1, ffn_3 = permute(ffn_g[1], "head", 1), permute(ffn_g[3], "head", 1)
-    out_2, out_1 = permute(out, "head", 2), permute(out, "head", 1)
     do, gqa, *sums = scores_back(scal, dmid, mix, q, k, v, qw, p, pv, attn_w, 0)
-    do, ffn_1, ffn_3, out_1, out_2 = lax.optimization_barrier((do, ffn_1, ffn_3, out_1, out_2))
+    do, ffn_1, ffn_3 = lax.optimization_barrier((do, ffn_1, ffn_3))
     (half,) = call(half_sum_kernel, "half_sum", 0, 2, [SDS(ffn_3.shape, bf16)])(ffn_g[2], ffn_3)
-    ffn_2, out_3 = permute(half, "head", 2), permute(out_2, "head", 1)
+    ffn_2 = permute(half, "head", 2)
     gqb, gk, gv, gt = scores_back(scal, dmid, mix, q, k, v, qw, p, pv, [do, *sums], 1)
-    tg, *attn_g = weights_back(scal, x, a, dmid, norm_params, gn2, gqa, gqb, gk, gv, gt, attn_w)
+    both, *attn_g = weights_back(scal, x, a, dmid, norm_params, gn2, gqa, gqb, gk, gv, gt, out, attn_w)
     attn_1, attn_3 = permute(attn_g[1], "head", 1), permute(attn_g[3], "head", 1)
     (half,) = call(half_sum_kernel, "half_sum", 0, 2, [SDS(attn_3.shape, bf16)])(attn_g[2], attn_3)
     attn_2 = permute(half, "head", 2)
     (message,) = call(
-        spread_ffn_kernel, "spread_ffn", 1, 3, [SDS((ranks * slots, rows, 256), bf16)], ranks=ranks
-    )(block_slot, ffn_g[0], ffn_1, ffn_2)
-    tg, attn_2, message, out_3 = lax.optimization_barrier((tg, attn_2, message, out_3))
-    tg_2, tg_1 = permute(tg, "head", 2), permute(tg, "head", 1)
-    tg_3 = permute(tg_2, "head", 1)
-    (message,) = call(
-        spread_attn_kernel, "spread_attn", 1, 4, [SDS(message.shape, bf16)], ranks=ranks
-    )(block_slot, message, attn_g[0], attn_1, attn_2)
-    got = lax.all_to_all(message, "dp", split_axis=0, concat_axis=0, tiled=True)
-    shape = SDS((parts,) + tokens.shape[1:], f32)
-    (output,) = call(assemble_kernel, "assemble", 1, parts, [shape])(scal, out, out_1, out_2, out_3)
-    (token_grad,) = call(assemble_kernel, "assemble", 1, parts, [shape])(scal, tg, tg_1, tg_2, tg_3)
+        spread_ffn_kernel, "spread_ffn", 2, 3, [SDS((ranks // 2, 2, slots, rows, 256), bf16)]
+    )(block_slot, scal, ffn_g[0], ffn_1, ffn_2)
+    messages = list(call(
+        spread_attn_kernel, "spread_attn", 2, 4, [SDS(message.shape[1:], bf16)] * (ranks // 2),
+        [pltpu.VMEM(message.shape, bf16)], parts=3,
+    )(block_slot, scal, message, attn_g[0], attn_1, attn_2))
+    both, messages[1] = lax.optimization_barrier((both, messages[1]))
+    both_2, both_1 = permute(both, "head", 2), permute(both, "head", 1)
+    both_3 = permute(both_2, "head", 1)
+    messages = [messages[0]] + [permute(messages[k], "dp", 2 * k) for k in range(1, ranks // 2)]
+    own, other = call(
+        pair_sum_kernel, "pair_sum", 0, ranks // 2, [SDS((slots, rows, 256), f32), SDS((slots, rows, 256), bf16)]
+    )(*messages)
+    other = permute(other, "dp", 1)
+    shape = SDS((tokens.shape[1], parts, dim), f32)
+    output, token_grad = pl.pallas_call(
+        assemble_kernel,
+        grid=(1,),
+        in_specs=[SM] + [whole(*both.shape)] * parts,
+        out_specs=[whole(*shape.shape)] * 2,
+        out_shape=[shape, shape],
+        scratch_shapes=[pltpu.VMEM((parts, 224, dim), bf16)],
+        compiler_params=pltpu.CompilerParams(vmem_limit_bytes=16 << 20),
+        cost_estimate=pl.CostEstimate(flops=1000000000, transcendentals=0, bytes_accessed=3000000),
+        name="assemble",
+    )(scal, both, both_1, both_2, both_3)
+    other, output, token_grad = lax.optimization_barrier((other, output, token_grad))
     state = [
         swap(master), swap(master_m1), swap(master_m2), norm_params, norm_m1, norm_m2,
         swap(talk), swap(talk_m1), swap(talk_m2), conv, conv_m1, conv_m2,
@@ -641,11 +697,11 @@
     shapes = [SDS(t.shape, f32) for t in state]
     shapes.insert(3, SDS(state[0].shape, bf16))
     new = staged(
-        functools.partial(update_kernel, ranks=ranks), "update", [got, *state], shapes,
+        update_kernel, "update", [own, other, *state], shapes,
         [pltpu.VMEM((rows, slots, dim), f32), pltpu.VMEM((slots, 64, 256), f32), pltpu.VMEM((64, 256), f32)],
     )
     new = [swap(t) if t.ndim == 3 else t for t in new]
-    return (output, token_grad, *new)
+    return (swap(output), swap(token_grad), *new)
 
 
 def solution(mesh):

time: 81.4 us -> 75.1 us (0.923)
  waiting for transfers between devices: 28 us -> 25 us
  local copies, waits for them, and re-layouts: 3.63 us -> 1.27 us
    all_to_all x2 -> x0, waiting for transfers between devices: 13.5 us -> none  [the longest x1 9.3 us: local(): lax.all_to_all(jnp.swapaxes(mine, 1, 2), 'dp', split_axis=0, concat_axis=...]
    all_to_all x2 -> x0, starting transfers between devices: 11 us -> none  [the longest x1 7.26 us: local(): lax.all_to_all(jnp.swapaxes(mine, 1, 2), 'dp', split_axis=0, concat_axis=...]
    ppermute x18 -> x23, starting transfers between devices: 9.19 us -> 20.1 us  [permute(): lax.ppermute(x, axis, [(i, i ^ k) for i in range(lax.axis_size(axis))])]
    ppermute x18 -> x23, waiting for transfers between devices: 14.4 us -> 25 us  [permute(): lax.ppermute(x, axis, [(i, i ^ k) for i in range(lax.axis_size(axis))])]
    unnamed x37 -> x32, local copies, waits for them, and re-layouts: 3.57 us -> 0.98 us
    pallas_call x6 -> x7, Pallas kernels: 5.02 us -> 5.28 us  [the longest x1 2 us: local(): pl.pallas_call(assemble_kernel, grid=(1,), in_specs=[SM] + [whole(*both.s...]
  transfers between devices with their start and end apart: 20 -> 23, of which waited for: 9 -> 12; matrix products, arithmetic and copies ran while one was open for 3% -> 0% of each run, Pallas kernels for 19% -> 22%
where the time goes in v5:
time: 75.1 us; the launch traced here: 74.9 us
  Pallas kernels  25.4 us (34%)
  waiting for transfers between devices  25 us (33%)
  starting transfers between devices  20.1 us (27%)
  between operations  3.06 us (4%)
  local copies, waits for them, and re-layouts  1.27 us (2%)
    ppermute x23, waiting for transfers between devices, permute(): lax.ppermute(x, axis, [(i, i ^ k) for i in range(lax.axis_size(axis))])  25 us
    ppermute x23, starting transfers between devices, permute(): lax.ppermute(x, axis, [(i, i ^ k) for i in range(lax.axis_size(axis))])  20.1 us
    pallas_call x2, Pallas kernels, scores_back(): call(scores_back_kernel, 'scores_back', 1, 8 + len(more), outs, scratch,...  6.38 us
    pallas_call x1, Pallas kernels, ffn(): call(ffn_kernel, 'ffn', 1, 4 + len(w), [SDS((SIDE * SIDE, dim), bf16), SD...  6.29 us
    pallas_call x1, Pallas kernels, attn_fwd(): call(attn_fwd_kernel, 'attn_fwd', 1, 4 + len(w), [SDS((pad, dim), f32)] +...  4.96 us
    pallas_call x1, Pallas kernels, local(): pl.pallas_call(assemble_kernel, grid=(1,), in_specs=[SM] + [whole(*both.s...  2 us
  transfers between devices with their start and end apart: 23, of which 12 were waited for; matrix products, arithmetic and copies ran while one was open for 0% of the time, Pallas kernels for 22%

profile of v5, /device:TPU:0, one launch (start us, length us, event | category | flops | bytes accessed | tf_op | source)
XLA Modules:
  0.0 74.9 jit_solution(7534435094292674484)
XLA Ops:
  0.6 0.0 copy-start
  0.7 0.9 %copy-done = f32[2,54,216]{2,0,1:T(2,128)S(1)} copy-done((f32[2,54,216]{2,0,1:T(2,128)S(1)}, f32[2,54,216]{2,0,1:T(2,128)}, u32[]{:S(2)}) %copy-start) | copy-done | bytes 93336
  1.5 0.2 cast.1.own_ref
  1.8 3.0 %collective-permute-start = (bf16[2,54,216]{2,1,0:T(8,128)(2,1)S(1)}, bf16[2,54,216]{2,1,0:T(8,128)(2,1)S(1)}, u32[]{:S(2)}, u32[]{:S(2)}) collective-permute-start(bf16[2,54,216]{2,1,0:T(8,128)(2,1)S(1)} %cast.1.own_ref), channel_id=1, source_target_pairs={{0,4},{4,0},{8,12},{12,8},{16,20},{20,16},{24,28},{28,24},{1,5},{5... | collective-permute-start | bytes 139976 | tf_op jit(solution)/shard_map/ppermute | solution.py:591
  6.7 0.1 concatenate.3.scal
  6.8 0.1 collective-permute-done.other_ref
  7.0 4.2 %collective-permute-start.3 = (bf16[2,2,54,216]{3,2,1,0:T(8,128)(2,1)S(1)}, bf16[2,2,54,216]{3,2,1,0:T(8,128)(2,1)S(1)}, u32[]{:S(2)}, u32[]{:S(2)}) collective-permute-start(bf16[2,2,54,216]{3,2,1,0:T(8,128)(2,1)S(1)} %pair.1.refs_0_), channel_id=1, source_target_pairs={{0,24},{4,28},{8,16},{12,20},{16,8},{20,12},{24,0},{28,4},{1,25},{... | collective-permute-start | bytes 279944 | tf_op jit(solution)/shard_map/ppermute | solution.py:591
  11.2 0.6 collective-permute-start.1
  11.9 0.2 copy.34.cot_ref
  12.1 1.1 %prep.1 = (f32[224,216]{1,0:T(8,128)S(1)}, bf16[224,216]{1,0:T(8,128)(2,1)S(1)}, f32[224,216]{1,0:T(8,128)S(1)}, f32[2,192,256]{2,1,0:T(8,128)S(1)}, f32[224,192]{1,0:T(8,128)S(1)}) custom-call(s32[6]{0:T(128)S(1)} %concatenate.3.scal, bf16[4,196,216]{2,1,0:T(8,128)(2,1)S(1)} %copy.33.tok_ref, f32[4,196,216]{2,1,0:T(8,128)S(1)} %copy.34.cot_ref, ...), custom_call_target="tpu_custom_call" | custom-call | flops 1000000000 | bytes 3000000 | tf_op jit(solution)/shard_map/prep/pallas_call | solution.py:510
  13.2 4.4 %collective-permute-done.1.refs_1_ = bf16[2,2,54,216]{3,2,1,0:T(8,128)(2,1)S(1)} collective-permute-done((bf16[2,2,54,216]{3,2,1,0:T(8,128)(2,1)S(1)}, bf16[2,2,54,216]{3,2,1,0:T(8,128)(2,1)S(1)}, u32[]{:S(2)}, u32[]{:S(2)}) %collective-permute-start.1) | collective-permute-done | bytes 93344 | tf_op jit(solution)/shard_map/ppermute | solution.py:591
  17.6 2.3 %collective-permute-done.2.refs_2_ = bf16[2,2,54,216]{3,2,1,0:T(8,128)(2,1)S(1)} collective-permute-done((bf16[2,2,54,216]{3,2,1,0:T(8,128)(2,1)S(1)}, bf16[2,2,54,216]{3,2,1,0:T(8,128)(2,1)S(1)}, u32[]{:S(2)}, u32[]{:S(2)}) %collective-permute-start.2) | collective-permute-done | bytes 93344 | tf_op jit(solution)/shard_map/ppermute | solution.py:591
  19.9 0.7 select.7
  20.7 1.6 %collective-permute-start.5 = (bf16[4,54,216]{2,1,0:T(8,128)(2,1)S(1)}, bf16[4,54,216]{2,1,0:T(8,128)(2,1)S(1)}, u32[]{:S(2)}, u32[]{:S(2)}) collective-permute-start(bf16[4,54,216]{2,1,0:T(8,128)(2,1)S(1)} %get-tuple-element.99.refs_0_), channel_id=1, source_target_pairs={{0,2},{1,3},{2,0},{3,1},{4,6},{5,7},{6,4},{7,5},{8,10},{9,11},{10,... | collective-permute-start | bytes 279944 | tf_op jit(solution)/shard_map/ppermute | solution.py:591
  22.2 0.5 collective-permute-start.7
  22.8 3.9 %collective-permute-done.5.refs_2_ = bf16[4,54,216]{2,1,0:T(8,128)(2,1)S(1)} collective-permute-done((bf16[4,54,216]{2,1,0:T(8,128)(2,1)S(1)}, bf16[4,54,216]{2,1,0:T(8,128)(2,1)S(1)}, u32[]{:S(2)}, u32[]{:S(2)}) %collective-permute-start.5) | collective-permute-done | bytes 93344 | tf_op jit(solution)/shard_map/ppermute | solution.py:591
  26.7 0.5 collective-permute-start.8
  27.2 0.8 %collective-permute-done.6.refs_3_ = bf16[4,54,216]{2,1,0:T(8,128)(2,1)S(1)} collective-permute-done((bf16[4,54,216]{2,1,0:T(8,128)(2,1)S(1)}, bf16[4,54,216]{2,1,0:T(8,128)(2,1)S(1)}, u32[]{:S(2)}, u32[]{:S(2)}) %collective-permute-start.6) | collective-permute-done | bytes 93344 | tf_op jit(solution)/shard_map/ppermute | solution.py:591
  28.0 5.0 %attn_fwd.1 = (f32[224,216]{1,0:T(8,128)S(1)}, bf16[224,256]{1,0:T(8,128)(2,1)S(1)}, bf16[224,256]{1,0:T(8,128)(2,1)S(1)}, bf16[224,256]{1,0:T(8,128)(2,1)S(1)},...) custom-call(s32[6]{0:T(128)S(1)} %concatenate.3.scal, ...), custom_call_target="tpu_custom_call" | custom-call | flops 1000000000 | bytes 3000000 | tf_op jit(solution)/shard_map/attn_fwd/pallas_call | solution.py:535
  33.0 0.2 collective-permute-start.9
  33.2 1.4 %collective-permute-done.9.refs_3_ = bf16[9,54,216]{2,1,0:T(8,128)(2,1)S(1)} collective-permute-done((bf16[9,54,216]{2,1,0:T(8,128)(2,1)S(1)}, bf16[9,54,216]{2,1,0:T(8,128)(2,1)S(1)}, u32[]{:S(2)}, u32[]{:S(2)}) %collective-permute-start.9) | collective-permute-done | bytes 209984 | tf_op jit(solution)/shard_map/ppermute | solution.py:591
  34.6 6.3 %ffn.1 = (bf16[196,216]{1,0:T(8,128)(2,1)S(1)}, f32[224,216]{1,0:T(8,128)S(1)}, f32[8,216]{1,0:T(8,128)S(1)}, bf16[9,54,256]{2,1,0:T(8,128)(2,1)S(1)}, bf16[9,54...) custom-call(s32[6]{0:T(128)S(1)} %concatenate.3.scal, ...), custom_call_target="tpu_custom_call" | custom-call | flops 6000000000 | bytes 18000000 | tf_op jit(solution)/shard_map/ffn/pallas_call | solution.py:547
  40.9 0.2 collective-permute-start.10
  41.1 0.4 collective-permute-start.11
  41.4 3.0 %scores_back.2 = (bf16[224,256]{1,0:T(8,128)(2,1)S(1)}, bf16[112,256]{1,0:T(8,128)(2,1)S(1)}, f32[224,256]{1,0:T(8,128)S(1)}, f32[224,256]{1,0:T(8,128)S(1)}, f3...) custom-call(s32[6]{0:T(128)S(1)} %concatenate.3.scal, f32[224,216]{1,0:T(8,128)S(1)} %get-tuple-element.107.dmid_ref, ...), custom_call_target="tpu_custom_call" | custom-call | flops 4000000000 | bytes 12000000 | tf_op jit(solution)/shard_map/scores_back/pallas_call | solution.py:573
  44.4 0.1 half_sum.2
  44.5 1.7 %collective-permute-start.12 = (bf16[9,54,256]{2,1,0:T(8,128)(2,1)S(1)}, bf16[9,54,256]{2,1,0:T(8,128)(2,1)S(1)}, u32[]{:S(2)}, u32[]{:S(2)}) collective-permute-start(bf16[9,54,256]{2,1,0:T(8,128)(2,1)S(1)} %half_sum.2), channel_id=1, source_target_pairs={{0,2},{1,3},{2,0},{3,1},{4,6},{5,7},{6,4},{7,5},{8,10},{9,11},{10,... | collective-permute-start | bytes 746504 | tf_op jit(solution)/shard_map/ppermute | solution.py:591
  46.2 3.4 %scores_back.3 = (bf16[112,256]{1,0:T(8,128)(2,1)S(1)}, bf16[224,256]{1,0:T(8,128)(2,1)S(1)}, bf16[224,256]{1,0:T(8,128)(2,1)S(1)}, f32[2,12,12]{2,1,0:T(8,128)S(1)}) custom-call(s32[6]{0:T(128)S(1)} %concatenate.3.scal, f32[224,216]{1,0:T(8,128)S(1)} %get-tuple-element.107.dmid_ref, f32[2,192,256]{2,1,0:T(8,128)S(1)} %get-tuple-element.96.mix_ref, ...), custom_call_target="tpu_custom_call" | custom-call | flops 4000000000 | bytes 12000000 | tf_op jit(solution)/shard_map/scores_back/pallas_call | solution.py:573
  49.6 1.2 %weights_back.1 = (bf16[2,196,216]{2,1,0:T(8,128)(2,1)S(1)}, bf16[3,54,256]{2,1,0:T(8,128)(2,1)S(1)}, bf16[3,54,256]{2,1,0:T(8,128)(2,1)S(1)}, bf16[3,54,256]{2,1,0:T(8,128)(2,1)S(1)}, bf16[3,54,256]{2,1,0:T(8,128)(2,1)S(1)}) custom-call(s32[6]{0:T(128)S(1)} %concatenate.3.scal, f32[224,216]{1,0:T(8,128)S(1)} %get-tuple-element.94.x_ref, ...), custom_call_target="tpu_custom_call" | custom-call | flops 3000000000 | bytes 9000000 | tf_op jit(solution)/shard_map/weights_back/pallas_call | solution.py:581
  50.8 0.1 collective-permute-start.14
  50.9 0.5 collective-permute-start.13
  51.4 0.8 %collective-permute-done.14.b_ref = bf16[3,54,256]{2,1,0:T(8,128)(2,1)S(1)} collective-permute-done((bf16[3,54,256]{2,1,0:T(8,128)(2,1)S(1)}, bf16[3,54,256]{2,1,0:T(8,128)(2,1)S(1)}, u32[]{:S(2)}, u32[]{:S(2)}) %collective-permute-start.14) | collective-permute-done | bytes 82976 | tf_op jit(solution)/shard_map/ppermute | solution.py:591
  52.2 0.5 collective-permute-start.15
  52.6 0.2 collective-permute-done.12.refs_2_
  52.9 0.7 spread_ffn.1.old_ref
  53.6 3.3 %collective-permute-done.15.refs_2_ = bf16[3,54,256]{2,1,0:T(8,128)(2,1)S(1)} collective-permute-done((bf16[3,54,256]{2,1,0:T(8,128)(2,1)S(1)}, bf16[3,54,256]{2,1,0:T(8,128)(2,1)S(1)}, u32[]{:S(2)}, u32[]{:S(2)}) %collective-permute-start.15) | collective-permute-done | bytes 82976 | tf_op jit(solution)/shard_map/ppermute | solution.py:591
  56.8 0.7 spread_attn.1
  57.5 0.5 collective-permute-start.21
  57.9 0.1 collective-permute-start.16
  58.0 1.8 %collective-permute-start.17 = (bf16[2,2,54,256]{3,2,1,0:T(8,128)(2,1)S(1)}, bf16[2,2,54,256]{3,2,1,0:T(8,128)(2,1)S(1)}, u32[]{:S(2)}, u32[]{:S(2)}) collective-permute-start(bf16[2,2,54,256]{3,2,1,0:T(8,128)(2,1)S(1)} %get-tuple-element.140), channel_id=1, source_target_pairs={{0,16},{4,20},{8,24},{12,28},{16,0},{20,4},{24,8},{28,12},{1,17},{... | collective-permute-start | bytes 331784 | tf_op jit(solution)/shard_map/ppermute | solution.py:591
  59.8 2.5 %collective-permute-start.18 = (bf16[2,2,54,256]{3,2,1,0:T(8,128)(2,1)S(1)}, bf16[2,2,54,256]{3,2,1,0:T(8,128)(2,1)S(1)}, u32[]{:S(2)}, u32[]{:S(2)}) collective-permute-start(bf16[2,2,54,256]{3,2,1,0:T(8,128)(2,1)S(1)} %get-tuple-element.141), channel_id=1, source_target_pairs={{0,24},{4,28},{8,16},{12,20},{16,8},{20,12},{24,0},{28,4},{1,25},{... | collective-permute-start | bytes 331784 | tf_op jit(solution)/shard_map/ppermute | solution.py:591
  62.3 1.5 %collective-permute-done.21.refs_2_ = bf16[2,196,216]{2,1,0:T(8,128)(2,1)S(1)} collective-permute-done((bf16[2,196,216]{2,1,0:T(8,128)(2,1)S(1)}, bf16[2,196,216]{2,1,0:T(8,128)(2,1)S(1)}, u32[]{:S(2)}, u32[]{:S(2)}) %collective-permute-start.21) | collective-permute-done | bytes 169376 | tf_op jit(solution)/shard_map/ppermute | solution.py:591
  63.9 5.3 %collective-permute-done.17.refs_2_ = bf16[2,2,54,256]{3,2,1,0:T(8,128)(2,1)S(1)} collective-permute-done((bf16[2,2,54,256]{3,2,1,0:T(8,128)(2,1)S(1)}, bf16[2,2,54,256]{3,2,1,0:T(8,128)(2,1)S(1)}, u32[]{:S(2)}, u32[]{:S(2)}) %collective-permute-start.17) | collective-permute-done | bytes 110624 | tf_op jit(solution)/shard_map/ppermute | solution.py:591
  69.2 0.1 pair_sum.1
  69.4 1.3 %collective-permute-start.19 = (bf16[2,54,256]{2,1,0:T(8,128)(2,1)S(1)}, bf16[2,54,256]{2,1,0:T(8,128)(2,1)S(1)}, u32[]{:S(2)}, u32[]{:S(2)}) collective-permute-start(bf16[2,54,256]{2,1,0:T(8,128)(2,1)S(1)} %get-tuple-element.142), channel_id=1, source_target_pairs={{0,4},{4,0},{8,12},{12,8},{16,20},{20,16},{24,28},{28,24},{1,5},{5... | collective-permute-start | bytes 165896 | tf_op jit(solution)/shard_map/ppermute | solution.py:591
  70.7 2.0 %assemble.1 = (f32[196,4,216]{2,1,0:T(4,128)}, f32[196,4,216]{2,1,0:T(4,128)}) custom-call(s32[6]{0:T(128)S(1)} %concatenate.3.scal, bf16[2,196,216]{2,1,0:T(8,128)(2,1)S(1)} %get-tuple-element.143.refs_0_, bf16[2,196,216]{2,1,0:T(8,128)(2,1)S(1)} %collective-permute-done.20.refs_1_, bf16[2,196,216]{2,1,0:T(8,128)(2,1)S(1)} %collective-permute-done.21.refs_2_, ...), custom_call_target="tpu_custom_call" | custom-call | flops 1000000000 | bytes 3000000 | tf_op jit(solution)/shard_map/assemble/pallas_call | solution.py:681
  72.7 0.9 %collective-permute-done.19.other_ref = bf16[2,54,256]{2,1,0:T(8,128)(2,1)S(1)} collective-permute-done((bf16[2,54,256]{2,1,0:T(8,128)(2,1)S(1)}, bf16[2,54,256]{2,1,0:T(8,128)(2,1)S(1)}, u32[]{:S(2)}, u32[]{:S(2)}) %collective-permute-start.19) | collective-permute-done | bytes 55328 | tf_op jit(solution)/shard_map/ppermute | solution.py:591
  73.7 1.1 %update.1 = (f32[54,2,216]{2,1,0:T(2,128)}, f32[54,2,216]{2,1,0:T(2,128)}, f32[54,2,216]{2,1,0:T(2,128)}, bf16[54,2,216]{2,1,0:T(2,128)(2,1)}, f32[4,216]{1,0:T(...) custom-call(f32[2,54,256]{2,1,0:T(8,128)S(1)} %get-tuple-element.148, ...), custom_call_target="tpu_custom_call" | custom-call | flops 1000000000 | bytes 3000000 | tf_op jit(solution)/shard_map/update/pallas_call | solution.py:603
  (50 shorter events, 0.2 us)
Async XLA Ops:
  0.6 0.9 %copy-start = (f32[2,54,216]{2,0,1:T(2,128)S(1)}, f32[2,54,216]{2,0,1:T(2,128)}, u32[]{:S(2)}) copy-start(f32[2,54,216]{2,0,1:T(2,128)} %param.24) | copy-start | bytes 279940
  1.8 5.2 %collective-permute-start = (bf16[2,54,216]{2,1,0:T(8,128)(2,1)S(1)}, bf16[2,54,216]{2,1,0:T(8,128)(2,1)S(1)}, u32[]{:S(2)}, u32[]{:S(2)}) collective-permute-start(bf16[2,54,216]{2,1,0:T(8,128)(2,1)S(1)} %cast.1.own_ref), channel_id=1, source_target_pairs={{0,4},{4,0},{8,12},{12,8},{16,20},{20,16},{24,28},{28,24},{1,5},{5... | collective-permute-start | bytes 139976 | tf_op jit(solution)/shard_map/ppermute | solution.py:591
  6.8 5.0 %copy-start.2 = (f32[2,12,12]{2,0,1:T(2,128)S(1)}, f32[2,12,12]{2,0,1:T(2,128)}, u32[]{:S(2)}) copy-start(f32[2,12,12]{2,0,1:T(2,128)} %param.30) | copy-start | bytes 3460
  6.8 5.0 %copy-start.15 = (bf16[4,196,216]{2,0,1:T(4,128)(2,1)S(1)}, bf16[4,196,216]{2,0,1:T(4,128)(2,1)}, u32[]{:S(2)}) copy-start(bf16[4,196,216]{2,0,1:T(4,128)(2,1)} %param.18) | copy-start | bytes 1016068
  6.8 5.1 %copy-start.14 = (f32[4,196,216]{2,0,1:T(4,128)S(1)}, f32[4,196,216]{2,0,1:T(4,128)}, u32[]{:S(2)}) copy-start(f32[4,196,216]{2,0,1:T(4,128)} %param.19) | copy-start | bytes 2032132
  7.0 5.1 %copy-start.10 = (f32[4,216]{1,0:T(4,128)S(1)}, f32[4,216]{1,0:T(4,128)}, u32[]{:S(2)}) copy-start(f32[4,216]{1,0:T(4,128)} %refs_3_.1) | copy-start | bytes 10372
  7.0 10.7 %collective-permute-start.3 = (bf16[2,2,54,216]{3,2,1,0:T(8,128)(2,1)S(1)}, bf16[2,2,54,216]{3,2,1,0:T(8,128)(2,1)S(1)}, u32[]{:S(2)}, u32[]{:S(2)}) collective-permute-start(bf16[2,2,54,216]{3,2,1,0:T(8,128)(2,1)S(1)} %pair.1.refs_0_), channel_id=1, source_target_pairs={{0,24},{4,28},{8,16},{12,20},{16,8},{20,12},{24,0},{28,4},{1,25},{... | collective-permute-start | bytes 279944 | tf_op jit(solution)/shard_map/ppermute | solution.py:591
  11.2 8.8 %collective-permute-start.2 = (bf16[2,2,54,216]{3,2,1,0:T(8,128)(2,1)S(1)}, bf16[2,2,54,216]{3,2,1,0:T(8,128)(2,1)S(1)}, u32[]{:S(2)}, u32[]{:S(2)}) collective-permute-start(bf16[2,2,54,216]{3,2,1,0:T(8,128)(2,1)S(1)} %pair.1.refs_0_), channel_id=1, source_target_pairs={{0,16},{4,20},{8,24},{12,28},{16,0},{20,4},{24,8},{28,12},{1,17},{... | collective-permute-start | bytes 279944 | tf_op jit(solution)/shard_map/ppermute | solution.py:591
  11.2 6.5 %collective-permute-start.1 = (bf16[2,2,54,216]{3,2,1,0:T(8,128)(2,1)S(1)}, bf16[2,2,54,216]{3,2,1,0:T(8,128)(2,1)S(1)}, u32[]{:S(2)}, u32[]{:S(2)}) collective-permute-start(bf16[2,2,54,216]{3,2,1,0:T(8,128)(2,1)S(1)} %pair.1.refs_0_), channel_id=1, source_target_pairs={{0,8},{4,12},{8,0},{12,4},{16,24},{20,28},{24,16},{28,20},{1,9},{5... | collective-permute-start | bytes 279944 | tf_op jit(solution)/shard_map/ppermute | solution.py:591
  12.1 7.9 %copy-start.5 = (f32[9,216]{1,0:T(8,128)S(1)}, f32[9,216]{1,0:T(8,128)}, u32[]{:S(2)}) copy-start(f32[9,216]{1,0:T(8,128)} %refs_9_.1) | copy-start | bytes 23332
  12.1 7.9 %copy-start.13 = (s32[12]{0:T(128)S(1)}, s32[12]{0:T(128)}, u32[]{:S(2)}) copy-start(s32[12]{0:T(128)} %slot_ref.5) | copy-start | bytes 148
  20.7 6.0 %collective-permute-start.5 = (bf16[4,54,216]{2,1,0:T(8,128)(2,1)S(1)}, bf16[4,54,216]{2,1,0:T(8,128)(2,1)S(1)}, u32[]{:S(2)}, u32[]{:S(2)}) collective-permute-start(bf16[4,54,216]{2,1,0:T(8,128)(2,1)S(1)} %get-tuple-element.99.refs_0_), channel_id=1, source_target_pairs={{0,2},{1,3},{2,0},{3,1},{4,6},{5,7},{6,4},{7,5},{8,10},{9,11},{10,... | collective-permute-start | bytes 279944 | tf_op jit(solution)/shard_map/ppermute | solution.py:591
  22.2 10.7 %collective-permute-start.7 = (bf16[9,54,216]{2,1,0:T(8,128)(2,1)S(1)}, bf16[9,54,216]{2,1,0:T(8,128)(2,1)S(1)}, u32[]{:S(2)}, u32[]{:S(2)}) collective-permute-start(bf16[9,54,216]{2,1,0:T(8,128)(2,1)S(1)} %get-tuple-element.101.refs_0_), channel_id=1, source_target_pairs={{0,2},{1,3},{2,0},{3,1},{4,6},{5,7},{6,4},{7,5},{8,10},{9,11},{10,... | collective-permute-start | bytes 629864 | tf_op jit(solution)/shard_map/ppermute | solution.py:591
  22.7 4.4 %collective-permute-start.4 = (bf16[4,54,216]{2,1,0:T(8,128)(2,1)S(1)}, bf16[4,54,216]{2,1,0:T(8,128)(2,1)S(1)}, u32[]{:S(2)}, u32[]{:S(2)}) collective-permute-start(bf16[4,54,216]{2,1,0:T(8,128)(2,1)S(1)} %get-tuple-element.99.refs_0_), channel_id=1, source_target_pairs={{0,1},{1,0},{2,3},{3,2},{4,5},{5,4},{6,7},{7,6},{8,9},{9,8},{10,11... | collective-permute-start | bytes 279944 | tf_op jit(solution)/shard_map/ppermute | solution.py:591
  26.7 1.3 %collective-permute-start.6 = (bf16[4,54,216]{2,1,0:T(8,128)(2,1)S(1)}, bf16[4,54,216]{2,1,0:T(8,128)(2,1)S(1)}, u32[]{:S(2)}, u32[]{:S(2)}) collective-permute-start(bf16[4,54,216]{2,1,0:T(8,128)(2,1)S(1)} %collective-permute-done.5.refs_2_), channel_id=1, source_target_pairs={{0,1},{1,0},{2,3},{3,2},{4,5},{5,4},{6,7},{7,6},{8,9},{9,8},{10,11... | collective-permute-start | bytes 279944 | tf_op jit(solution)/shard_map/ppermute | solution.py:591
  26.7 6.5 %collective-permute-start.8 = (bf16[9,54,216]{2,1,0:T(8,128)(2,1)S(1)}, bf16[9,54,216]{2,1,0:T(8,128)(2,1)S(1)}, u32[]{:S(2)}, u32[]{:S(2)}) collective-permute-start(bf16[9,54,216]{2,1,0:T(8,128)(2,1)S(1)} %get-tuple-element.101.refs_0_), channel_id=1, source_target_pairs={{0,1},{1,0},{2,3},{3,2},{4,5},{5,4},{6,7},{7,6},{8,9},{9,8},{10,11... | collective-permute-start | bytes 629864 | tf_op jit(solution)/shard_map/ppermute | solution.py:591
  33.0 1.6 %collective-permute-start.9 = (bf16[9,54,216]{2,1,0:T(8,128)(2,1)S(1)}, bf16[9,54,216]{2,1,0:T(8,128)(2,1)S(1)}, u32[]{:S(2)}, u32[]{:S(2)}) collective-permute-start(bf16[9,54,216]{2,1,0:T(8,128)(2,1)S(1)} %collective-permute-done.7.refs_2_), channel_id=1, source_target_pairs={{0,1},{1,0},{2,3},{3,2},{4,5},{5,4},{6,7},{7,6},{8,9},{9,8},{10,11... | collective-permute-start | bytes 629864 | tf_op jit(solution)/shard_map/ppermute | solution.py:591
  40.9 3.6 %collective-permute-start.10 = (bf16[9,54,256]{2,1,0:T(8,128)(2,1)S(1)}, bf16[9,54,256]{2,1,0:T(8,128)(2,1)S(1)}, u32[]{:S(2)}, u32[]{:S(2)}) collective-permute-start(bf16[9,54,256]{2,1,0:T(8,128)(2,1)S(1)} %get-tuple-element.115), channel_id=1, source_target_pairs={{0,1},{1,0},{2,3},{3,2},{4,5},{5,4},{6,7},{7,6},{8,9},{9,8},{10,11... | collective-permute-start | bytes 746504 | tf_op jit(solution)/shard_map/ppermute | solution.py:591
  41.1 3.4 %collective-permute-start.11 = (bf16[9,54,256]{2,1,0:T(8,128)(2,1)S(1)}, bf16[9,54,256]{2,1,0:T(8,128)(2,1)S(1)}, u32[]{:S(2)}, u32[]{:S(2)}) collective-permute-start(bf16[9,54,256]{2,1,0:T(8,128)(2,1)S(1)} %get-tuple-element.116), channel_id=1, source_target_pairs={{0,1},{1,0},{2,3},{3,2},{4,5},{5,4},{6,7},{7,6},{8,9},{9,8},{10,11... | collective-permute-start | bytes 746504 | tf_op jit(solution)/shard_map/ppermute | solution.py:591
  44.5 8.3 %collective-permute-start.12 = (bf16[9,54,256]{2,1,0:T(8,128)(2,1)S(1)}, bf16[9,54,256]{2,1,0:T(8,128)(2,1)S(1)}, u32[]{:S(2)}, u32[]{:S(2)}) collective-permute-start(bf16[9,54,256]{2,1,0:T(8,128)(2,1)S(1)} %half_sum.2), channel_id=1, source_target_pairs={{0,2},{1,3},{2,0},{3,1},{4,6},{5,7},{6,4},{7,5},{8,10},{9,11},{10,... | collective-permute-start | bytes 746504 | tf_op jit(solution)/shard_map/ppermute | solution.py:591
  50.8 1.3 %collective-permute-start.14 = (bf16[3,54,256]{2,1,0:T(8,128)(2,1)S(1)}, bf16[3,54,256]{2,1,0:T(8,128)(2,1)S(1)}, u32[]{:S(2)}, u32[]{:S(2)}) collective-permute-start(bf16[3,54,256]{2,1,0:T(8,128)(2,1)S(1)} %get-tuple-element.135), channel_id=1, source_target_pairs={{0,1},{1,0},{2,3},{3,2},{4,5},{5,4},{6,7},{7,6},{8,9},{9,8},{10,11... | collective-permute-start | bytes 248840 | tf_op jit(solution)/shard_map/ppermute | solution.py:591
  50.9 2.7 %collective-permute-start.13 = (bf16[3,54,256]{2,1,0:T(8,128)(2,1)S(1)}, bf16[3,54,256]{2,1,0:T(8,128)(2,1)S(1)}, u32[]{:S(2)}, u32[]{:S(2)}) collective-permute-start(bf16[3,54,256]{2,1,0:T(8,128)(2,1)S(1)} %get-tuple-element.133), channel_id=1, source_target_pairs={{0,1},{1,0},{2,3},{3,2},{4,5},{5,4},{6,7},{7,6},{8,9},{9,8},{10,11... | collective-permute-start | bytes 248840 | tf_op jit(solution)/shard_map/ppermute | solution.py:591
  52.2 4.7 %collective-permute-start.15 = (bf16[3,54,256]{2,1,0:T(8,128)(2,1)S(1)}, bf16[3,54,256]{2,1,0:T(8,128)(2,1)S(1)}, u32[]{:S(2)}, u32[]{:S(2)}) collective-permute-start(bf16[3,54,256]{2,1,0:T(8,128)(2,1)S(1)} %half_sum.3), channel_id=1, source_target_pairs={{0,2},{1,3},{2,0},{3,1},{4,6},{5,7},{6,4},{7,5},{8,10},{9,11},{10,... | collective-permute-start | bytes 248840 | tf_op jit(solution)/shard_map/ppermute | solution.py:591
  57.5 6.4 %collective-permute-start.21 = (bf16[2,196,216]{2,1,0:T(8,128)(2,1)S(1)}, bf16[2,196,216]{2,1,0:T(8,128)(2,1)S(1)}, u32[]{:S(2)}, u32[]{:S(2)}) collective-permute-start(bf16[2,196,216]{2,1,0:T(8,128)(2,1)S(1)} %get-tuple-element.143.refs_0_), channel_id=1, source_target_pairs={{0,2},{1,3},{2,0},{3,1},{4,6},{5,7},{6,4},{7,5},{8,10},{9,11},{10,... | collective-permute-start | bytes 508040 | tf_op jit(solution)/shard_map/ppermute | solution.py:591
  57.9 5.9 %collective-permute-start.16 = (bf16[2,2,54,256]{3,2,1,0:T(8,128)(2,1)S(1)}, bf16[2,2,54,256]{3,2,1,0:T(8,128)(2,1)S(1)}, u32[]{:S(2)}, u32[]{:S(2)}) collective-permute-start(bf16[2,2,54,256]{3,2,1,0:T(8,128)(2,1)S(1)} %get-tuple-element.139), channel_id=1, source_target_pairs={{0,8},{4,12},{8,0},{12,4},{16,24},{20,28},{24,16},{28,20},{1,9},{5... | collective-permute-start | bytes 331784 | tf_op jit(solution)/shard_map/ppermute | solution.py:591
  58.0 11.1 %collective-permute-start.17 = (bf16[2,2,54,256]{3,2,1,0:T(8,128)(2,1)S(1)}, bf16[2,2,54,256]{3,2,1,0:T(8,128)(2,1)S(1)}, u32[]{:S(2)}, u32[]{:S(2)}) collective-permute-start(bf16[2,2,54,256]{3,2,1,0:T(8,128)(2,1)S(1)} %get-tuple-element.140), channel_id=1, source_target_pairs={{0,16},{4,20},{8,24},{12,28},{16,0},{20,4},{24,8},{28,12},{1,17},{... | collective-permute-start | bytes 331784 | tf_op jit(solution)/shard_map/ppermute | solution.py:591
  59.8 9.4 %collective-permute-start.18 = (bf16[2,2,54,256]{3,2,1,0:T(8,128)(2,1)S(1)}, bf16[2,2,54,256]{3,2,1,0:T(8,128)(2,1)S(1)}, u32[]{:S(2)}, u32[]{:S(2)}) collective-permute-start(bf16[2,2,54,256]{3,2,1,0:T(8,128)(2,1)S(1)} %get-tuple-element.141), channel_id=1, source_target_pairs={{0,24},{4,28},{8,16},{12,20},{16,8},{20,12},{24,0},{28,4},{1,25},{... | collective-permute-start | bytes 331784 | tf_op jit(solution)/shard_map/ppermute | solution.py:591
  62.3 8.3 %collective-permute-start.20 = (bf16[2,196,216]{2,1,0:T(8,128)(2,1)S(1)}, bf16[2,196,216]{2,1,0:T(8,128)(2,1)S(1)}, u32[]{:S(2)}, u32[]{:S(2)}) collective-permute-start(bf16[2,196,216]{2,1,0:T(8,128)(2,1)S(1)} %get-tuple-element.143.refs_0_), channel_id=1, source_target_pairs={{0,1},{1,0},{2,3},{3,2},{4,5},{5,4},{6,7},{7,6},{8,9},{9,8},{10,11... | collective-permute-start | bytes 508040 | tf_op jit(solution)/shard_map/ppermute | solution.py:591
  63.9 6.8 %collective-permute-start.22 = (bf16[2,196,216]{2,1,0:T(8,128)(2,1)S(1)}, bf16[2,196,216]{2,1,0:T(8,128)(2,1)S(1)}, u32[]{:S(2)}, u32[]{:S(2)}) collective-permute-start(bf16[2,196,216]{2,1,0:T(8,128)(2,1)S(1)} %collective-permute-done.21.refs_2_), channel_id=1, source_target_pairs={{0,1},{1,0},{2,3},{3,2},{4,5},{5,4},{6,7},{7,6},{8,9},{9,8},{10,11... | collective-permute-start | bytes 508040 | tf_op jit(solution)/shard_map/ppermute | solution.py:591
  69.2 4.4 %copy-start.1 = (f32[2,54,216]{2,0,1:T(2,128)S(1)}, f32[2,54,216]{2,0,1:T(2,128)}, u32[]{:S(2)}) copy-start(f32[2,54,216]{2,0,1:T(2,128)} %param.24) | copy-start | bytes 279940
  69.3 4.3 %copy-start.3 = (f32[2,54,216]{2,0,1:T(2,128)S(1)}, f32[2,54,216]{2,0,1:T(2,128)}, u32[]{:S(2)}) copy-start(f32[2,54,216]{2,0,1:T(2,128)} %param.25) | copy-start | bytes 279940
  69.3 4.3 %copy-start.4 = (f32[2,54,216]{2,0,1:T(2,128)S(1)}, f32[2,54,216]{2,0,1:T(2,128)}, u32[]{:S(2)}) copy-start(f32[2,54,216]{2,0,1:T(2,128)} %param.26) | copy-start | bytes 279940
  69.3 4.3 %copy-start.6 = (f32[9,216]{1,0:T(8,128)S(1)}, f32[9,216]{1,0:T(8,128)}, u32[]{:S(2)}) copy-start(f32[9,216]{1,0:T(8,128)} %refs_10_.1) | copy-start | bytes 23332
  69.3 4.3 %copy-start.7 = (f32[9,216]{1,0:T(8,128)S(1)}, f32[9,216]{1,0:T(8,128)}, u32[]{:S(2)}) copy-start(f32[9,216]{1,0:T(8,128)} %refs_11_.1) | copy-start | bytes 23332
  69.3 4.3 %copy-start.8 = (f32[2,12,12]{2,0,1:T(2,128)S(1)}, f32[2,12,12]{2,0,1:T(2,128)}, u32[]{:S(2)}) copy-start(f32[2,12,12]{2,0,1:T(2,128)} %param.31) | copy-start | bytes 3460
  69.3 4.3 %copy-start.9 = (f32[2,12,12]{2,0,1:T(2,128)S(1)}, f32[2,12,12]{2,0,1:T(2,128)}, u32[]{:S(2)}) copy-start(f32[2,12,12]{2,0,1:T(2,128)} %param.32) | copy-start | bytes 3460
  69.3 4.3 %copy-start.11 = (f32[4,216]{1,0:T(4,128)S(1)}, f32[4,216]{1,0:T(4,128)}, u32[]{:S(2)}) copy-start(f32[4,216]{1,0:T(4,128)} %refs_4_.1) | copy-start | bytes 10372
  69.3 4.3 %copy-start.12 = (f32[4,216]{1,0:T(4,128)S(1)}, f32[4,216]{1,0:T(4,128)}, u32[]{:S(2)}) copy-start(f32[4,216]{1,0:T(4,128)} %refs_5_.1) | copy-start | bytes 10372
  69.4 4.2 %collective-permute-start.19 = (bf16[2,54,256]{2,1,0:T(8,128)(2,1)S(1)}, bf16[2,54,256]{2,1,0:T(8,128)(2,1)S(1)}, u32[]{:S(2)}, u32[]{:S(2)}) collective-permute-start(bf16[2,54,256]{2,1,0:T(8,128)(2,1)S(1)} %get-tuple-element.142), channel_id=1, source_target_pairs={{0,4},{4,0},{8,12},{12,8},{16,20},{20,16},{24,28},{28,24},{1,5},{5... | collective-permute-start | bytes 165896 | tf_op jit(solution)/shard_map/ppermute | solution.py:591

commit v6 on v5

--- a/solution.py
+++ b/solution.py
@@ -96,7 +96,7 @@
 
 def attn_fwd_kernel(scal, x_ref, a_ref, mix_ref, bias_ref, *refs, parts, unroll):
     w_refs, refs = refs[:parts], refs[parts:]
-    mid_ref, q_ref, k_ref, v_ref, o_ref, qw_ref, p_ref, pv_ref, ws_ref = refs
+    mid_ref, q_ref, k_ref, v_ref, o_ref, qw_ref, p_ref, pv_ref, ws_ref, t_ref = refs
     heads = mix_ref.shape[1] // PITCH
     a = a_ref[...]
     ws_ref[...] = jnp.zeros_like(ws_ref)
@@ -107,20 +107,24 @@
     head = lane_head((1, 256), 1, scal[0])
     keep = ((head >= 0) & (head < scal[2])).astype(f32)
 
-    def group(y, _):
-        rows = pl.ds(pl.multiple_of(y * PITCH, PITCH), PITCH)
-        qw = (tiled(q_ref[rows, :].astype(f32), heads) * mix_ref[0]).astype(bf16)
-        qw_ref[y] = qw
-        t = nt(k_ref[...], qw) + bias_ref[...]
-        e = jnp.exp(t - jnp.max(t, axis=0, keepdims=True))
-        p = (e * (1.0 / jnp.sum(e, axis=0, keepdims=True))).astype(bf16)
-        p_ref[y] = p
-        pv = tn(p, v_ref[...])
-        pv_ref[y] = pv.astype(bf16)
-        o_ref[rows, :] = (over_heads(pv * mix_ref[1], heads) * keep).astype(bf16)
+    def groups(b, _):
+        ys = [b * unroll + u for u in range(unroll)]
+        rows = [pl.ds(pl.multiple_of(y * PITCH, PITCH), PITCH) for y in ys]
+        for u, y in enumerate(ys):
+            qw_ref[y] = (tiled(q_ref[rows[u], :].astype(f32), heads) * mix_ref[0]).astype(bf16)
+        for u, y in enumerate(ys):
+            t_ref[u] = nt(k_ref[...], qw_ref[y]) + bias_ref[...]
+        for u, y in enumerate(ys):
+            t = t_ref[u]
+            e = jnp.exp(t - jnp.max(t, axis=0, keepdims=True))
+            p_ref[y] = (e * (1.0 / jnp.sum(e, axis=0, keepdims=True))).astype(bf16)
+        for u, y in enumerate(ys):
+            pv = tn(p_ref[y], v_ref[...])
+            pv_ref[y] = pv.astype(bf16)
+            o_ref[rows[u], :] = (over_heads(pv * mix_ref[1], heads) * keep).astype(bf16)
         return 0
 
-    lax.fori_loop(0, SIDE, group, 0, unroll=unroll)
+    lax.fori_loop(0, SIDE // unroll, groups, 0)
     mid_ref[...] = x_ref[...] + nn(o_ref[...], ws_ref[3])
 
 
@@ -159,99 +163,111 @@
     return ((iota(shape, 0) == (lane >> 6) * 54 + rest) & (rest < 54)).astype(bf16)
 
 
-def ffn_kernel(
-    scal, mid_ref, dy_ref, norm_ref, o_ref, *refs, parts
-):
+def ffn_kernel(scal, mid_ref, dy_ref, norm_ref, o_ref, *refs, parts):
     w_refs, refs = refs[:parts], refs[parts:]
     out_ref, dmid_ref, gn_ref = refs[:3]
     gw_refs, refs = refs[3 : 3 + parts], refs[3 + parts :]
-    win_ref, wdn_ref, h_ref, d_ref, gate_ref, dh_ref, cv_ref, gcv_ref, tmp_ref, sm_ref = refs
-    hd = parts
-    lanes = hd * 256
-    win_ref[...] = jnp.zeros_like(win_ref)
-    wdn_ref[...] = jnp.zeros_like(wdn_ref)
-    pm = place()
-    for h in range(hd):
-        for j in range(4):
-            at = 256 * h + 64 * j
-            win_ref[at : at + 54, :] = w_refs[h][j]
-            wdn_ref[at : at + 54, :] = w_refs[h][4 + j]
-        both = nn(w_refs[h][8], pm)
-        cv_ref[:, 256 * h : 256 * (h + 1)] = both[0:9] + both[16:25]
+    win_ref, wdn_ref, h_ref, d_ref, gate_ref, dh_ref, cv_ref, gcv_ref, tmp_ref, sm_ref, down_ref, dw_ref = refs
+    pm = place(256)
     mid = mid_ref[...]
+    tokens, dim = mid.shape
     z, inv = ln_stats(mid)
     rows = real_rows(mid.shape)
     w = jnp.where(rows, z * norm_ref[2:3, :] + norm_ref[3:4, :], 0.0).astype(bf16)
     dy = dy_ref[...]
     e = dy.astype(bf16)
-    tokens = mid.shape[0]
     pad = MARGIN
-    zero = jnp.zeros((pad, lanes), f32)
-    h_ref[0:pad, :] = zero
-    h_ref[pad + tokens :, :] = zero
-    d_ref[0:pad, :] = zero
-    d_ref[pad + tokens :, :] = zero
-    h_ref[pad : pad + tokens, :] = nt(w, win_ref[...])
-    d_ref[pad : pad + tokens, :] = nt(e, wdn_ref[...])
+    zero = jnp.zeros((pad, 128), f32)
     lane = iota((1, 128), 1)
-    rmask = real_rows((tokens, 128))
-    for c in range(lanes // 128):
-        cols = slice(128 * c, 128 * (c + 1))
-        glane = lane + 128 * c
-        rest = glane & 63
-        unit = (((glane >> 8) ^ scal[0]) * 4 + ((glane >> 6) & 3)) * 54 + rest
-        keep = ((rest < 54) & (unit < scal[3])).astype(f32)
-        act = jnp.zeros((tokens, 128), f32)
-        for t in range(9):
-            off = PITCH * (t // 3 - 1) + t % 3 - 1
-            act = act + cv_ref[t : t + 1, cols] * h_ref[pad + off : pad + off + tokens, cols]
-        sig = 1.0 / (1.0 + jnp.exp(-act))
-        gate_ref[:, cols] = (act * sig * keep).astype(bf16)
-        dact = d_ref[pad : pad + tokens, cols] * keep * sig * (1.0 + act * (1.0 - sig))
-        d_ref[pad : pad + tokens, cols] = dact
-        dh = jnp.zeros((tokens, 128), f32)
-        for t in range(9):
-            off = PITCH * (t // 3 - 1) + t % 3 - 1
-            gcv_ref[t : t + 1, cols] = jnp.sum(
-                dact * h_ref[pad + off : pad + off + tokens, cols], axis=0, keepdims=True
-            )
-            dh = dh + cv_ref[t : t + 1, cols] * d_ref[pad - off : pad - off + tokens, cols]
-        dh_ref[:, cols] = jnp.where(rmask, dh, 0.0).astype(bf16)
+    free = iota((54, 256), 1) >= FREE
+    for h in range(parts):
+        for j in range(4):
+            at = 64 * j
+            win_ref[h, at : at + 54, :] = w_refs[h][j]
+            wdn_ref[h, at : at + 54, :] = w_refs[h][4 + j]
+            win_ref[h, at + 54 : at + 64, :] = jnp.zeros((10, dim), bf16)
+            wdn_ref[h, at + 54 : at + 64, :] = jnp.zeros((10, dim), bf16)
+        both = nn(w_refs[h][8], pm[0:dim])
+        cv_ref[:, 256 * h : 256 * (h + 1)] = both[0:9] + both[16:25]
+    def up(h):
+        hidden = nt(w, win_ref[h])
+        dgate = nt(e, wdn_ref[h])
+        for half in range(2):
+            c = 2 * h + half
+            mine = slice(128 * half, 128 * (half + 1))
+            for ref, value in ((h_ref, hidden), (d_ref, dgate)):
+                ref[c, 0:pad, :] = zero
+                ref[c, pad + tokens :, :] = zero
+                ref[c, pad : pad + tokens, :] = value[:, mine]
+
+    def middle(h):
+        for half in range(2):
+            c = 2 * h + half
+            cols = slice(128 * c, 128 * (c + 1))
+            mine = slice(128 * half, 128 * (half + 1))
+            glane = lane + 128 * c
+            unit = (((glane >> 8) ^ scal[0]) * 4 + ((glane >> 6) & 3)) * 54 + (glane & 63)
+            keep = (unit < scal[3]).astype(f32)
+            act = None
+            for t in range(9):
+                off = pad + PITCH * (t // 3 - 1) + t % 3 - 1
+                term = cv_ref[t : t + 1, cols] * h_ref[c, off : off + tokens, :]
+                act = term if act is None else act + term
+            sig = 0.5 * jnp.tanh(0.5 * act) + 0.5
+            silu = act * sig
+            gate_ref[h, :, mine] = (silu * keep).astype(bf16)
+            dact = d_ref[c, pad : pad + tokens, :] * keep * (silu + sig * (1.0 - silu))
+            d_ref[c, pad : pad + tokens, :] = dact
+            dh = None
+            for t in range(9):
+                shift = PITCH * (t // 3 - 1) + t % 3 - 1
+                gcv_ref[t : t + 1, cols] = jnp.sum(
+                    dact * h_ref[c, pad + shift : pad + shift + tokens, :], axis=0, keepdims=True
+                )
+                term = cv_ref[t : t + 1, cols] * d_ref[c, pad - shift : pad - shift + tokens, :]
+                dh = term if dh is None else dh + term
+            dh_ref[h, :, mine] = dh.astype(bf16)
+
+    def back(h):
+        gi = tn(dh_ref[h], w).astype(bf16)
+        gd = tn(gate_ref[h], e).astype(bf16)
+        for j in range(4):
+            gw_refs[h][1 + j, :, 0:dim] = gi[64 * j : 64 * j + 54]
+            gw_refs[h][5 + j, :, 0:dim] = gd[64 * j : 64 * j + 54]
+        in_free_lanes(nt(gcv_ref[:, 256 * h : 256 * (h + 1)].astype(bf16), pm), sm_ref.at[h], 0)
+        gw_refs[h][0] = jnp.where(free, sm_ref[h, 0:54, :], 0.0).astype(bf16)
+
+    for h in range(parts):
+        up(h)
+    for h in range(parts):
+        middle(h)
+    down_ref[...] = sum(nn(gate_ref[h], wdn_ref[h]) for h in range(parts))
+    dw_ref[...] = sum(nn(dh_ref[h], win_ref[h]) for h in range(parts))
+    for h in range(parts):
+        back(h)
     valid = (scal[0] < scal[1]).astype(f32)
-    down = nn(gate_ref[...], wdn_ref[...])
-    tmp_ref[...] = (mid + down) * valid
+    tmp_ref[...] = (mid + down_ref[...]) * valid
     for y in range(SIDE):
         out_ref[SIDE * y : SIDE * (y + 1), :] = tmp_ref[PITCH * y : PITCH * y + SIDE, :].astype(bf16)
-    dw = nn(dh_ref[...], win_ref[...])
+    dw = jnp.where(rows, dw_ref[...], 0.0)
     gn_ref[...] = jnp.zeros_like(gn_ref)
     gn_ref[0:1, :] = jnp.sum(dw * z, axis=0, keepdims=True)
     gn_ref[1:2, :] = jnp.sum(dw, axis=0, keepdims=True)
     dmid = dy + ln_back(dw, z, inv, norm_ref[2:3, :])
     dmid_ref[...] = dmid
     go = tn(o_ref[...], dmid.astype(bf16)).astype(bf16)
-    dim = mid.shape[1]
-    free = iota((54, 256), 1) >= FREE
-    pm = place(256)
-    for h in range(hd):
-        cols = slice(256 * h, 256 * (h + 1))
-        gi = tn(dh_ref[:, cols], w).astype(bf16)
-        gd = tn(gate_ref[:, cols], e).astype(bf16)
-        for j in range(4):
-            gw_refs[h][1 + j, :, 0:dim] = gi[64 * j : 64 * j + 54]
-            gw_refs[h][5 + j, :, 0:dim] = gd[64 * j : 64 * j + 54]
-        in_free_lanes(nt(gcv_ref[:, cols].astype(bf16), pm), sm_ref, 0)
-        gw_refs[h][0] = jnp.where(free, sm_ref[0:54, :], 0.0).astype(bf16)
+    for h in range(parts):
         gw_refs[h][0, :, 0:dim] = go[64 * h : 64 * h + 54]
 
 
 def scores_back_kernel(
-    scal, dmid_ref, mix_ref, q_ref, k_ref, v_ref, qw_ref, p_ref, pv_ref, *refs, parts, unroll, part
+    scal, dmid_ref, mix_ref, q_ref, k_ref, v_ref, qw_ref, p_ref, pv_ref, *refs, parts, part
 ):
     heads = mix_ref.shape[1] // PITCH
     n = heads * PITCH
     if part == 0:
         w_refs, refs = refs[:parts], refs[parts:]
-        do_ref, gq_ref, gk_ref, gv_ref, g0_ref, g1_ref, wo_ref = refs
+        do_ref, gq_ref, gk_ref, gv_ref, g0_ref, g1_ref, wo_ref, dw_ref, dp_ref, dt_ref = refs
         wo_ref[...] = jnp.zeros_like(wo_ref)
         load_weight(wo_ref, w_refs, 3)
         f = dmid_ref[...].astype(bf16)
@@ -261,30 +277,29 @@
         for ref in (gk_ref, gv_ref, g0_ref, g1_ref):
             ref[...] = jnp.zeros_like(ref)
     else:
-        do_ref, *sums, gq_ref, gkb_ref, gvb_ref, gt_ref, gk_ref, gv_ref, g0_ref, g1_ref = refs
+        do_ref, *sums, gq_ref, gkb_ref, gvb_ref, gt_ref, gk_ref, gv_ref, g0_ref, g1_ref, dw_ref, dp_ref, dt_ref = refs
         for ref, old in zip((gk_ref, gv_ref, g0_ref, g1_ref), sums):
             ref[...] = old[...]
     first = SIDE // 2 * part
 
-    def group(y, _):
-        out_rows = pl.ds(pl.multiple_of(y * PITCH, PITCH), PITCH)
-        y = y + first
-        rows = pl.ds(pl.multiple_of(y * PITCH, PITCH), PITCH)
-        dot = tiled(do_ref[rows, :].astype(f32), heads)
-        dw = (dot * mix_ref[1]).astype(bf16)
-        dp = nt(v_ref[...], dw)
-        p = p_ref[y]
-        pf = p.astype(f32)
-        dt = (pf * (dp - jnp.sum(dp * pf, axis=0, keepdims=True))).astype(bf16)
-        gv_ref[...] += nn(p, dw)
-        gk_ref[...] += nn(dt, qw_ref[y])
-        dk = tn(dt, k_ref[...])
-        gq_ref[out_rows, :] = over_heads(dk * mix_ref[0], heads).astype(bf16)
-        g0_ref[...] += dk * tiled(q_ref[rows, :].astype(f32), heads)
-        g1_ref[...] += pv_ref[y].astype(f32) * dot
-        return 0
-
-    lax.fori_loop(0, SIDE // 2, group, 0, unroll=unroll)
+    ys = [first + u for u in range(SIDE // 2)]
+    rows = [slice(PITCH * y, PITCH * (y + 1)) for y in ys]
+    for u, y in enumerate(ys):
+        dw_ref[u] = (tiled(do_ref[rows[u], :].astype(f32), heads) * mix_ref[1]).astype(bf16)
+    for u, y in enumerate(ys):
+        dp_ref[u] = nt(v_ref[...], dw_ref[u])
+    for u, y in enumerate(ys):
+        dp = dp_ref[u]
+        p = p_ref[y].astype(f32)
+        dt_ref[u] = (p * (dp - jnp.sum(dp * p, axis=0, keepdims=True))).astype(bf16)
+    gv_ref[...] += sum(nn(p_ref[y], dw_ref[u]) for u, y in enumerate(ys))
+    gk_ref[...] += sum(nn(dt_ref[u], qw_ref[y]) for u, y in enumerate(ys))
+    for u, y in enumerate(ys):
+        dk = tn(dt_ref[u], k_ref[...])
+        gq_ref[PITCH * u : PITCH * (u + 1), :] = over_heads(dk * mix_ref[0], heads).astype(bf16)
+        g0_ref[...] += dk * tiled(q_ref[rows[u], :].astype(f32), heads)
+    for u, y in enumerate(ys):
+        g1_ref[...] += pv_ref[y].astype(f32) * tiled(do_ref[rows[u], :].astype(f32), heads)
     if part == 0:
         return
     gkb_ref[...] = gk_ref[...].astype(bf16)
@@ -529,14 +544,14 @@
     )(scal, tokens, cotangent, norm_params, talk)
 
 
-def attn_fwd(scal, x, a, mix, bias, w, unroll=7):
+def attn_fwd(scal, x, a, mix, bias, w, unroll=14):
     pad, dim = x.shape
     n = mix.shape[1]
     return call(
         attn_fwd_kernel, "attn_fwd", 1, 4 + len(w),
         [SDS((pad, dim), f32)] + [SDS((pad, 256), bf16)] * 4
         + [SDS((SIDE, n, 256), bf16), SDS((SIDE, pad, n), bf16), SDS((SIDE, n, 256), bf16)],
-        [pltpu.VMEM((4, 256, dim), bf16)],
+        [pltpu.VMEM((4, 256, dim), bf16), pltpu.VMEM((unroll, pad, n), f32)],
         mb=24, micros=1, parts=len(w), unroll=unroll,
     )(scal, x, a, mix, bias, *w)
 
@@ -548,17 +563,17 @@
         ffn_kernel, "ffn", 1, 4 + len(w),
         [SDS((SIDE * SIDE, dim), bf16), SDS((pad, dim), f32), SDS((8, dim), f32)] + [SDS((9, 54, 256), bf16)] * len(w),
         [
-            pltpu.VMEM((lanes, dim), bf16), pltpu.VMEM((lanes, dim), bf16),
-            pltpu.VMEM((pad + 2 * MARGIN, lanes), f32), pltpu.VMEM((pad + 2 * MARGIN, lanes), f32),
-            pltpu.VMEM((pad, lanes), bf16), pltpu.VMEM((pad, lanes), bf16),
+            pltpu.VMEM((len(w), 256, dim), bf16), pltpu.VMEM((len(w), 256, dim), bf16),
+            pltpu.VMEM((lanes // 128, pad + 2 * MARGIN, 128), f32), pltpu.VMEM((lanes // 128, pad + 2 * MARGIN, 128), f32),
+            pltpu.VMEM((len(w), pad, 256), bf16), pltpu.VMEM((len(w), pad, 256), bf16),
             pltpu.VMEM((9, lanes), f32), pltpu.VMEM((9, lanes), f32), pltpu.VMEM((pad, dim), f32),
-            pltpu.VMEM((56, 256), f32),
+            pltpu.VMEM((len(w), 56, 256), f32), pltpu.VMEM((pad, dim), f32), pltpu.VMEM((pad, dim), f32),
         ],
         mb=24, micros=6, parts=len(w),
     )(scal, mid, dy, norm_params, o, *w)
 
 
-def scores_back(scal, dmid, mix, q, k, v, qw, p, pv, more, part, unroll=7):
+def scores_back(scal, dmid, mix, q, k, v, qw, p, pv, more, part):
     pad, dim = dmid.shape
     n = mix.shape[1]
     heads = n // PITCH
@@ -570,9 +585,12 @@
     else:
         outs = [half] + [SDS((pad, 256), bf16)] * 2 + [SDS((2, heads, heads), f32)]
         scratch = [pltpu.VMEM(t.shape, f32) for t in sums]
+    scratch += [
+        pltpu.VMEM((SIDE // 2, n, 256), bf16), pltpu.VMEM((SIDE // 2, pad, n), f32), pltpu.VMEM((SIDE // 2, pad, n), bf16)
+    ]
     return call(
         scores_back_kernel, "scores_back", 1, 8 + len(more), outs, scratch,
-        mb=24, micros=4, parts=len(more), unroll=unroll, part=part,
+        mb=24, micros=4, parts=len(more), part=part,
     )(scal, dmid, mix, q, k, v, qw, p, pv, *more)
 
 

time: 75.1 us -> 69.2 us (0.921)
  Pallas kernels: 25.4 us -> 19.6 us
    pallas_call x1, Pallas kernels: 6.29 us -> 3.92 us  [ffn(): call(ffn_kernel, 'ffn', 1, 4 + len(w), [SDS((SIDE * SIDE, dim), bf16), SD...]
    pallas_call x1, Pallas kernels: 4.96 us -> 3.21 us  [attn_fwd(): call(attn_fwd_kernel, 'attn_fwd', 1, 4 + len(w), [SDS((pad, dim), f32)] +...]
    pallas_call x2, Pallas kernels: 6.38 us -> 4.72 us  [scores_back(): call(scores_back_kernel, 'scores_back', 1, 8 + len(more), outs, scratch,...]
  transfers between devices with their start and end apart: 23 -> 23, of which waited for: 12 -> 12; matrix products, arithmetic and copies ran while one was open for 0% -> 0% of each run, Pallas kernels for 22% -> 19%
where the time goes in v6:
time: 69.2 us; the launch traced here: 69 us
  waiting for transfers between devices  25 us (36%)
  starting transfers between devices  20.2 us (29%)
  Pallas kernels  19.6 us (28%)
  between operations  2.92 us (4%)
  local copies, waits for them, and re-layouts  1.27 us (2%)
    ppermute x23, waiting for transfers between devices, permute(): lax.ppermute(x, axis, [(i, i ^ k) for i in range(lax.axis_size(axis))])  25 us
    ppermute x23, starting transfers between devices, permute(): lax.ppermute(x, axis, [(i, i ^ k) for i in range(lax.axis_size(axis))])  20.2 us
    pallas_call x2, Pallas kernels, scores_back(): call(scores_back_kernel, 'scores_back', 1, 8 + len(more), outs, scratch,...  4.72 us
    pallas_call x1, Pallas kernels, ffn(): call(ffn_kernel, 'ffn', 1, 4 + len(w), [SDS((SIDE * SIDE, dim), bf16), SD...  3.92 us
    pallas_call x1, Pallas kernels, attn_fwd(): call(attn_fwd_kernel, 'attn_fwd', 1, 4 + len(w), [SDS((pad, dim), f32)] +...  3.21 us
    pallas_call x1, Pallas kernels, local(): pl.pallas_call(assemble_kernel, grid=(1,), in_specs=[SM] + [whole(*both.s...  2 us
  transfers between devices with their start and end apart: 23, of which 12 were waited for; matrix products, arithmetic and copies ran while one was open for 0% of the time, Pallas kernels for 19%

profile of v6, /device:TPU:0, one launch (start us, length us, event | category | flops | bytes accessed | tf_op | source)
XLA Modules:
  0.0 69.0 jit_solution(8339424070328549041)
XLA Ops:
  0.7 0.9 %copy-done = f32[2,54,216]{2,0,1:T(2,128)S(1)} copy-done((f32[2,54,216]{2,0,1:T(2,128)S(1)}, f32[2,54,216]{2,0,1:T(2,128)}, u32[]{:S(2)}) %copy-start) | copy-done | bytes 93336
  1.5 0.2 cast.1.own_ref
  1.8 3.0 %collective-permute-start = (bf16[2,54,216]{2,1,0:T(8,128)(2,1)S(1)}, bf16[2,54,216]{2,1,0:T(8,128)(2,1)S(1)}, u32[]{:S(2)}, u32[]{:S(2)}) collective-permute-start(bf16[2,54,216]{2,1,0:T(8,128)(2,1)S(1)} %cast.1.own_ref), channel_id=1, source_target_pairs={{0,4},{4,0},{8,12},{12,8},{16,20},{20,16},{24,28},{28,24},{1,5},{5... | collective-permute-start | bytes 139976 | tf_op jit(solution)/shard_map/ppermute | solution.py:609
  6.7 0.1 concatenate.3.scal
  6.8 0.1 collective-permute-done.other_ref
  7.0 4.2 %collective-permute-start.3 = (bf16[2,2,54,216]{3,2,1,0:T(8,128)(2,1)S(1)}, bf16[2,2,54,216]{3,2,1,0:T(8,128)(2,1)S(1)}, u32[]{:S(2)}, u32[]{:S(2)}) collective-permute-start(bf16[2,2,54,216]{3,2,1,0:T(8,128)(2,1)S(1)} %pair.1.refs_0_), channel_id=1, source_target_pairs={{0,24},{4,28},{8,16},{12,20},{16,8},{20,12},{24,0},{28,4},{1,25},{... | collective-permute-start | bytes 279944 | tf_op jit(solution)/shard_map/ppermute | solution.py:609
  11.2 0.6 collective-permute-start.1
  11.9 0.2 copy.34.cot_ref
  12.1 0.0 copy-start.5
  12.1 1.1 %prep.1 = (f32[224,216]{1,0:T(8,128)S(1)}, bf16[224,216]{1,0:T(8,128)(2,1)S(1)}, f32[224,216]{1,0:T(8,128)S(1)}, f32[2,192,256]{2,1,0:T(8,128)S(1)}, f32[224,192]{1,0:T(8,128)S(1)}) custom-call(s32[6]{0:T(128)S(1)} %concatenate.3.scal, bf16[4,196,216]{2,1,0:T(8,128)(2,1)S(1)} %copy.33.tok_ref, f32[4,196,216]{2,1,0:T(8,128)S(1)} %copy.34.cot_ref, ...), custom_call_target="tpu_custom_call" | custom-call | flops 1000000000 | bytes 3000000 | tf_op jit(solution)/shard_map/prep/pallas_call | solution.py:525
  13.2 4.4 %collective-permute-done.1.refs_1_ = bf16[2,2,54,216]{3,2,1,0:T(8,128)(2,1)S(1)} collective-permute-done((bf16[2,2,54,216]{3,2,1,0:T(8,128)(2,1)S(1)}, bf16[2,2,54,216]{3,2,1,0:T(8,128)(2,1)S(1)}, u32[]{:S(2)}, u32[]{:S(2)}) %collective-permute-start.1) | collective-permute-done | bytes 93344 | tf_op jit(solution)/shard_map/ppermute | solution.py:609
  17.6 2.3 %collective-permute-done.2.refs_2_ = bf16[2,2,54,216]{3,2,1,0:T(8,128)(2,1)S(1)} collective-permute-done((bf16[2,2,54,216]{3,2,1,0:T(8,128)(2,1)S(1)}, bf16[2,2,54,216]{3,2,1,0:T(8,128)(2,1)S(1)}, u32[]{:S(2)}, u32[]{:S(2)}) %collective-permute-start.2) | collective-permute-done | bytes 93344 | tf_op jit(solution)/shard_map/ppermute | solution.py:609
  19.9 0.7 %select.7 = (bf16[4,54,216]{2,1,0:T(8,128)(2,1)S(1)}, bf16[9,54,216]{2,1,0:T(8,128)(2,1)S(1)}) custom-call(s32[12]{0:T(128)S(1)} %copy-done.13, s32[6]{0:T(128)S(1)} %concatenate.3.scal, f32[9,216]{1,0:T(8,128)S(1)} %copy-done.5, bf16[2,2,54,216]{3,2,1,0:T(8,128)(2,1)S(1)} %pair.1.refs_0_, bf16[2,2,54,216]{3,2,1,0:T(8,128)(2,1)S(1)} %collective-permute-done.1.refs_1_, ...), custom_call_target="tpu_custom_call" | custom-call | flops 1000000000 | bytes 3000000 | tf_op jit(solution)/shard_map/select/pallas_call | solution.py:661
  20.7 1.6 %collective-permute-start.5 = (bf16[4,54,216]{2,1,0:T(8,128)(2,1)S(1)}, bf16[4,54,216]{2,1,0:T(8,128)(2,1)S(1)}, u32[]{:S(2)}, u32[]{:S(2)}) collective-permute-start(bf16[4,54,216]{2,1,0:T(8,128)(2,1)S(1)} %get-tuple-element.99.refs_0_), channel_id=1, source_target_pairs={{0,2},{1,3},{2,0},{3,1},{4,6},{5,7},{6,4},{7,5},{8,10},{9,11},{10,... | collective-permute-start | bytes 279944 | tf_op jit(solution)/shard_map/ppermute | solution.py:609
  22.2 0.5 collective-permute-start.7
  22.8 3.9 %collective-permute-done.5.refs_2_ = bf16[4,54,216]{2,1,0:T(8,128)(2,1)S(1)} collective-permute-done((bf16[4,54,216]{2,1,0:T(8,128)(2,1)S(1)}, bf16[4,54,216]{2,1,0:T(8,128)(2,1)S(1)}, u32[]{:S(2)}, u32[]{:S(2)}) %collective-permute-start.5) | collective-permute-done | bytes 93344 | tf_op jit(solution)/shard_map/ppermute | solution.py:609
  26.7 0.5 collective-permute-start.8
  27.2 0.8 %collective-permute-done.6.refs_3_ = bf16[4,54,216]{2,1,0:T(8,128)(2,1)S(1)} collective-permute-done((bf16[4,54,216]{2,1,0:T(8,128)(2,1)S(1)}, bf16[4,54,216]{2,1,0:T(8,128)(2,1)S(1)}, u32[]{:S(2)}, u32[]{:S(2)}) %collective-permute-start.6) | collective-permute-done | bytes 93344 | tf_op jit(solution)/shard_map/ppermute | solution.py:609
  28.0 3.2 %attn_fwd.1 = (f32[224,216]{1,0:T(8,128)S(1)}, bf16[224,256]{1,0:T(8,128)(2,1)S(1)}, bf16[224,256]{1,0:T(8,128)(2,1)S(1)}, bf16[224,256]{1,0:T(8,128)(2,1)S(1)},...) custom-call(s32[6]{0:T(128)S(1)} %concatenate.3.scal, ...), custom_call_target="tpu_custom_call" | custom-call | flops 1000000000 | bytes 3000000 | tf_op jit(solution)/shard_map/attn_fwd/pallas_call | solution.py:550
  31.2 0.2 collective-permute-start.9
  31.4 1.4 %collective-permute-done.9.refs_3_ = bf16[9,54,216]{2,1,0:T(8,128)(2,1)S(1)} collective-permute-done((bf16[9,54,216]{2,1,0:T(8,128)(2,1)S(1)}, bf16[9,54,216]{2,1,0:T(8,128)(2,1)S(1)}, u32[]{:S(2)}, u32[]{:S(2)}) %collective-permute-start.9) | collective-permute-done | bytes 209984 | tf_op jit(solution)/shard_map/ppermute | solution.py:609
  32.8 3.9 %ffn.1 = (bf16[196,216]{1,0:T(8,128)(2,1)S(1)}, f32[224,216]{1,0:T(8,128)S(1)}, f32[8,216]{1,0:T(8,128)S(1)}, bf16[9,54,256]{2,1,0:T(8,128)(2,1)S(1)}, bf16[9,54...) custom-call(s32[6]{0:T(128)S(1)} %concatenate.3.scal, ...), custom_call_target="tpu_custom_call" | custom-call | flops 6000000000 | bytes 18000000 | tf_op jit(solution)/shard_map/ffn/pallas_call | solution.py:562
  36.8 0.2 collective-permute-start.10
  37.0 0.4 collective-permute-start.11
  37.3 2.2 %scores_back.2 = (bf16[224,256]{1,0:T(8,128)(2,1)S(1)}, bf16[112,256]{1,0:T(8,128)(2,1)S(1)}, f32[224,256]{1,0:T(8,128)S(1)}, f32[224,256]{1,0:T(8,128)S(1)}, f3...) custom-call(s32[6]{0:T(128)S(1)} %concatenate.3.scal, f32[224,216]{1,0:T(8,128)S(1)} %get-tuple-element.107.dmid_ref, ...), custom_call_target="tpu_custom_call" | custom-call | flops 4000000000 | bytes 12000000 | tf_op jit(solution)/shard_map/scores_back/pallas_call | solution.py:591
  39.6 0.1 half_sum.2
  39.6 1.7 %collective-permute-start.12 = (bf16[9,54,256]{2,1,0:T(8,128)(2,1)S(1)}, bf16[9,54,256]{2,1,0:T(8,128)(2,1)S(1)}, u32[]{:S(2)}, u32[]{:S(2)}) collective-permute-start(bf16[9,54,256]{2,1,0:T(8,128)(2,1)S(1)} %half_sum.2), channel_id=1, source_target_pairs={{0,2},{1,3},{2,0},{3,1},{4,6},{5,7},{6,4},{7,5},{8,10},{9,11},{10,... | collective-permute-start | bytes 746504 | tf_op jit(solution)/shard_map/ppermute | solution.py:609
  41.4 2.5 %scores_back.3 = (bf16[112,256]{1,0:T(8,128)(2,1)S(1)}, bf16[224,256]{1,0:T(8,128)(2,1)S(1)}, bf16[224,256]{1,0:T(8,128)(2,1)S(1)}, f32[2,12,12]{2,1,0:T(8,128)S(1)}) custom-call(s32[6]{0:T(128)S(1)} %concatenate.3.scal, f32[224,216]{1,0:T(8,128)S(1)} %get-tuple-element.107.dmid_ref, f32[2,192,256]{2,1,0:T(8,128)S(1)} %get-tuple-element.96.mix_ref, ...), custom_call_target="tpu_custom_call" | custom-call | flops 4000000000 | bytes 12000000 | tf_op jit(solution)/shard_map/scores_back/pallas_call | solution.py:591
  43.9 1.1 %weights_back.1 = (bf16[2,196,216]{2,1,0:T(8,128)(2,1)S(1)}, bf16[3,54,256]{2,1,0:T(8,128)(2,1)S(1)}, bf16[3,54,256]{2,1,0:T(8,128)(2,1)S(1)}, bf16[3,54,256]{2,1,0:T(8,128)(2,1)S(1)}, bf16[3,54,256]{2,1,0:T(8,128)(2,1)S(1)}) custom-call(s32[6]{0:T(128)S(1)} %concatenate.3.scal, f32[224,216]{1,0:T(8,128)S(1)} %get-tuple-element.94.x_ref, ...), custom_call_target="tpu_custom_call" | custom-call | flops 3000000000 | bytes 9000000 | tf_op jit(solution)/shard_map/weights_back/pallas_call | solution.py:599
  45.0 0.1 collective-permute-start.14
  45.1 0.5 collective-permute-start.13
  45.6 0.8 %collective-permute-done.14.b_ref = bf16[3,54,256]{2,1,0:T(8,128)(2,1)S(1)} collective-permute-done((bf16[3,54,256]{2,1,0:T(8,128)(2,1)S(1)}, bf16[3,54,256]{2,1,0:T(8,128)(2,1)S(1)}, u32[]{:S(2)}, u32[]{:S(2)}) %collective-permute-start.14) | collective-permute-done | bytes 82976 | tf_op jit(solution)/shard_map/ppermute | solution.py:609
  46.4 0.4 collective-permute-start.15
  46.8 1.2 %collective-permute-done.12.refs_2_ = bf16[9,54,256]{2,1,0:T(8,128)(2,1)S(1)} collective-permute-done((bf16[9,54,256]{2,1,0:T(8,128)(2,1)S(1)}, bf16[9,54,256]{2,1,0:T(8,128)(2,1)S(1)}, u32[]{:S(2)}, u32[]{:S(2)}) %collective-permute-start.12) | collective-permute-done | bytes 248864 | tf_op jit(solution)/shard_map/ppermute | solution.py:609
  48.0 0.7 spread_ffn.1.old_ref
  48.7 2.3 %collective-permute-done.15.refs_2_ = bf16[3,54,256]{2,1,0:T(8,128)(2,1)S(1)} collective-permute-done((bf16[3,54,256]{2,1,0:T(8,128)(2,1)S(1)}, bf16[3,54,256]{2,1,0:T(8,128)(2,1)S(1)}, u32[]{:S(2)}, u32[]{:S(2)}) %collective-permute-start.15) | collective-permute-done | bytes 82976 | tf_op jit(solution)/shard_map/ppermute | solution.py:609
  51.0 0.7 spread_attn.1
  51.7 0.5 collective-permute-start.21
  52.2 0.1 collective-permute-start.16
  52.3 1.8 %collective-permute-start.17 = (bf16[2,2,54,256]{3,2,1,0:T(8,128)(2,1)S(1)}, bf16[2,2,54,256]{3,2,1,0:T(8,128)(2,1)S(1)}, u32[]{:S(2)}, u32[]{:S(2)}) collective-permute-start(bf16[2,2,54,256]{3,2,1,0:T(8,128)(2,1)S(1)} %get-tuple-element.140), channel_id=1, source_target_pairs={{0,16},{4,20},{8,24},{12,28},{16,0},{20,4},{24,8},{28,12},{1,17},{... | collective-permute-start | bytes 331784 | tf_op jit(solution)/shard_map/ppermute | solution.py:609
  54.0 2.6 %collective-permute-start.18 = (bf16[2,2,54,256]{3,2,1,0:T(8,128)(2,1)S(1)}, bf16[2,2,54,256]{3,2,1,0:T(8,128)(2,1)S(1)}, u32[]{:S(2)}, u32[]{:S(2)}) collective-permute-start(bf16[2,2,54,256]{3,2,1,0:T(8,128)(2,1)S(1)} %get-tuple-element.141), channel_id=1, source_target_pairs={{0,24},{4,28},{8,16},{12,20},{16,8},{20,12},{24,0},{28,4},{1,25},{... | collective-permute-start | bytes 331784 | tf_op jit(solution)/shard_map/ppermute | solution.py:609
  56.6 1.5 %collective-permute-done.21.refs_2_ = bf16[2,196,216]{2,1,0:T(8,128)(2,1)S(1)} collective-permute-done((bf16[2,196,216]{2,1,0:T(8,128)(2,1)S(1)}, bf16[2,196,216]{2,1,0:T(8,128)(2,1)S(1)}, u32[]{:S(2)}, u32[]{:S(2)}) %collective-permute-start.21) | collective-permute-done | bytes 169376 | tf_op jit(solution)/shard_map/ppermute | solution.py:609
  58.1 5.4 %collective-permute-done.17.refs_2_ = bf16[2,2,54,256]{3,2,1,0:T(8,128)(2,1)S(1)} collective-permute-done((bf16[2,2,54,256]{3,2,1,0:T(8,128)(2,1)S(1)}, bf16[2,2,54,256]{3,2,1,0:T(8,128)(2,1)S(1)}, u32[]{:S(2)}, u32[]{:S(2)}) %collective-permute-start.17) | collective-permute-done | bytes 110624 | tf_op jit(solution)/shard_map/ppermute | solution.py:609
  63.4 0.1 pair_sum.1
  63.6 1.3 %collective-permute-start.19 = (bf16[2,54,256]{2,1,0:T(8,128)(2,1)S(1)}, bf16[2,54,256]{2,1,0:T(8,128)(2,1)S(1)}, u32[]{:S(2)}, u32[]{:S(2)}) collective-permute-start(bf16[2,54,256]{2,1,0:T(8,128)(2,1)S(1)} %get-tuple-element.142), channel_id=1, source_target_pairs={{0,4},{4,0},{8,12},{12,8},{16,20},{20,16},{24,28},{28,24},{1,5},{5... | collective-permute-start | bytes 165896 | tf_op jit(solution)/shard_map/ppermute | solution.py:609
  64.9 2.0 %assemble.1 = (f32[196,4,216]{2,1,0:T(4,128)}, f32[196,4,216]{2,1,0:T(4,128)}) custom-call(s32[6]{0:T(128)S(1)} %concatenate.3.scal, bf16[2,196,216]{2,1,0:T(8,128)(2,1)S(1)} %get-tuple-element.143.refs_0_, bf16[2,196,216]{2,1,0:T(8,128)(2,1)S(1)} %collective-permute-done.20.refs_1_, bf16[2,196,216]{2,1,0:T(8,128)(2,1)S(1)} %collective-permute-done.21.refs_2_, ...), custom_call_target="tpu_custom_call" | custom-call | flops 1000000000 | bytes 3000000 | tf_op jit(solution)/shard_map/assemble/pallas_call | solution.py:699
  66.9 0.9 %collective-permute-done.19.other_ref = bf16[2,54,256]{2,1,0:T(8,128)(2,1)S(1)} collective-permute-done((bf16[2,54,256]{2,1,0:T(8,128)(2,1)S(1)}, bf16[2,54,256]{2,1,0:T(8,128)(2,1)S(1)}, u32[]{:S(2)}, u32[]{:S(2)}) %collective-permute-start.19) | collective-permute-done | bytes 55328 | tf_op jit(solution)/shard_map/ppermute | solution.py:609
  67.9 1.1 %update.1 = (f32[54,2,216]{2,1,0:T(2,128)}, f32[54,2,216]{2,1,0:T(2,128)}, f32[54,2,216]{2,1,0:T(2,128)}, bf16[54,2,216]{2,1,0:T(2,128)(2,1)}, f32[4,216]{1,0:T(...) custom-call(f32[2,54,256]{2,1,0:T(8,128)S(1)} %get-tuple-element.148, ...), custom_call_target="tpu_custom_call" | custom-call | flops 1000000000 | bytes 3000000 | tf_op jit(solution)/shard_map/update/pallas_call | solution.py:621
  (50 shorter events, 0.2 us)
Async XLA Ops:
  0.6 0.9 %copy-start = (f32[2,54,216]{2,0,1:T(2,128)S(1)}, f32[2,54,216]{2,0,1:T(2,128)}, u32[]{:S(2)}) copy-start(f32[2,54,216]{2,0,1:T(2,128)} %param.24) | copy-start | bytes 279940
  1.8 5.2 %collective-permute-start = (bf16[2,54,216]{2,1,0:T(8,128)(2,1)S(1)}, bf16[2,54,216]{2,1,0:T(8,128)(2,1)S(1)}, u32[]{:S(2)}, u32[]{:S(2)}) collective-permute-start(bf16[2,54,216]{2,1,0:T(8,128)(2,1)S(1)} %cast.1.own_ref), channel_id=1, source_target_pairs={{0,4},{4,0},{8,12},{12,8},{16,20},{20,16},{24,28},{28,24},{1,5},{5... | collective-permute-start | bytes 139976 | tf_op jit(solution)/shard_map/ppermute | solution.py:609
  6.8 5.0 %copy-start.2 = (f32[2,12,12]{2,0,1:T(2,128)S(1)}, f32[2,12,12]{2,0,1:T(2,128)}, u32[]{:S(2)}) copy-start(f32[2,12,12]{2,0,1:T(2,128)} %param.30) | copy-start | bytes 3460
  6.8 5.0 %copy-start.15 = (bf16[4,196,216]{2,0,1:T(4,128)(2,1)S(1)}, bf16[4,196,216]{2,0,1:T(4,128)(2,1)}, u32[]{:S(2)}) copy-start(bf16[4,196,216]{2,0,1:T(4,128)(2,1)} %param.18) | copy-start | bytes 1016068
  6.8 5.1 %copy-start.14 = (f32[4,196,216]{2,0,1:T(4,128)S(1)}, f32[4,196,216]{2,0,1:T(4,128)}, u32[]{:S(2)}) copy-start(f32[4,196,216]{2,0,1:T(4,128)} %param.19) | copy-start | bytes 2032132
  7.0 5.1 %copy-start.10 = (f32[4,216]{1,0:T(4,128)S(1)}, f32[4,216]{1,0:T(4,128)}, u32[]{:S(2)}) copy-start(f32[4,216]{1,0:T(4,128)} %refs_3_.1) | copy-start | bytes 10372
  7.0 10.7 %collective-permute-start.3 = (bf16[2,2,54,216]{3,2,1,0:T(8,128)(2,1)S(1)}, bf16[2,2,54,216]{3,2,1,0:T(8,128)(2,1)S(1)}, u32[]{:S(2)}, u32[]{:S(2)}) collective-permute-start(bf16[2,2,54,216]{3,2,1,0:T(8,128)(2,1)S(1)} %pair.1.refs_0_), channel_id=1, source_target_pairs={{0,24},{4,28},{8,16},{12,20},{16,8},{20,12},{24,0},{28,4},{1,25},{... | collective-permute-start | bytes 279944 | tf_op jit(solution)/shard_map/ppermute | solution.py:609
  11.2 8.8 %collective-permute-start.2 = (bf16[2,2,54,216]{3,2,1,0:T(8,128)(2,1)S(1)}, bf16[2,2,54,216]{3,2,1,0:T(8,128)(2,1)S(1)}, u32[]{:S(2)}, u32[]{:S(2)}) collective-permute-start(bf16[2,2,54,216]{3,2,1,0:T(8,128)(2,1)S(1)} %pair.1.refs_0_), channel_id=1, source_target_pairs={{0,16},{4,20},{8,24},{12,28},{16,0},{20,4},{24,8},{28,12},{1,17},{... | collective-permute-start | bytes 279944 | tf_op jit(solution)/shard_map/ppermute | solution.py:609
  11.2 6.5 %collective-permute-start.1 = (bf16[2,2,54,216]{3,2,1,0:T(8,128)(2,1)S(1)}, bf16[2,2,54,216]{3,2,1,0:T(8,128)(2,1)S(1)}, u32[]{:S(2)}, u32[]{:S(2)}) collective-permute-start(bf16[2,2,54,216]{3,2,1,0:T(8,128)(2,1)S(1)} %pair.1.refs_0_), channel_id=1, source_target_pairs={{0,8},{4,12},{8,0},{12,4},{16,24},{20,28},{24,16},{28,20},{1,9},{5... | collective-permute-start | bytes 279944 | tf_op jit(solution)/shard_map/ppermute | solution.py:609
  12.1 7.9 %copy-start.5 = (f32[9,216]{1,0:T(8,128)S(1)}, f32[9,216]{1,0:T(8,128)}, u32[]{:S(2)}) copy-start(f32[9,216]{1,0:T(8,128)} %refs_9_.1) | copy-start | bytes 23332
  12.1 7.9 %copy-start.13 = (s32[12]{0:T(128)S(1)}, s32[12]{0:T(128)}, u32[]{:S(2)}) copy-start(s32[12]{0:T(128)} %slot_ref.5) | copy-start | bytes 148
  20.7 6.0 %collective-permute-start.5 = (bf16[4,54,216]{2,1,0:T(8,128)(2,1)S(1)}, bf16[4,54,216]{2,1,0:T(8,128)(2,1)S(1)}, u32[]{:S(2)}, u32[]{:S(2)}) collective-permute-start(bf16[4,54,216]{2,1,0:T(8,128)(2,1)S(1)} %get-tuple-element.99.refs_0_), channel_id=1, source_target_pairs={{0,2},{1,3},{2,0},{3,1},{4,6},{5,7},{6,4},{7,5},{8,10},{9,11},{10,... | collective-permute-start | bytes 279944 | tf_op jit(solution)/shard_map/ppermute | solution.py:609
  22.2 9.0 %collective-permute-start.7 = (bf16[9,54,216]{2,1,0:T(8,128)(2,1)S(1)}, bf16[9,54,216]{2,1,0:T(8,128)(2,1)S(1)}, u32[]{:S(2)}, u32[]{:S(2)}) collective-permute-start(bf16[9,54,216]{2,1,0:T(8,128)(2,1)S(1)} %get-tuple-element.101.refs_0_), channel_id=1, source_target_pairs={{0,2},{1,3},{2,0},{3,1},{4,6},{5,7},{6,4},{7,5},{8,10},{9,11},{10,... | collective-permute-start | bytes 629864 | tf_op jit(solution)/shard_map/ppermute | solution.py:609
  22.7 4.4 %collective-permute-start.4 = (bf16[4,54,216]{2,1,0:T(8,128)(2,1)S(1)}, bf16[4,54,216]{2,1,0:T(8,128)(2,1)S(1)}, u32[]{:S(2)}, u32[]{:S(2)}) collective-permute-start(bf16[4,54,216]{2,1,0:T(8,128)(2,1)S(1)} %get-tuple-element.99.refs_0_), channel_id=1, source_target_pairs={{0,1},{1,0},{2,3},{3,2},{4,5},{5,4},{6,7},{7,6},{8,9},{9,8},{10,11... | collective-permute-start | bytes 279944 | tf_op jit(solution)/shard_map/ppermute | solution.py:609
  26.7 1.3 %collective-permute-start.6 = (bf16[4,54,216]{2,1,0:T(8,128)(2,1)S(1)}, bf16[4,54,216]{2,1,0:T(8,128)(2,1)S(1)}, u32[]{:S(2)}, u32[]{:S(2)}) collective-permute-start(bf16[4,54,216]{2,1,0:T(8,128)(2,1)S(1)} %collective-permute-done.5.refs_2_), channel_id=1, source_target_pairs={{0,1},{1,0},{2,3},{3,2},{4,5},{5,4},{6,7},{7,6},{8,9},{9,8},{10,11... | collective-permute-start | bytes 279944 | tf_op jit(solution)/shard_map/ppermute | solution.py:609
  26.7 4.8 %collective-permute-start.8 = (bf16[9,54,216]{2,1,0:T(8,128)(2,1)S(1)}, bf16[9,54,216]{2,1,0:T(8,128)(2,1)S(1)}, u32[]{:S(2)}, u32[]{:S(2)}) collective-permute-start(bf16[9,54,216]{2,1,0:T(8,128)(2,1)S(1)} %get-tuple-element.101.refs_0_), channel_id=1, source_target_pairs={{0,1},{1,0},{2,3},{3,2},{4,5},{5,4},{6,7},{7,6},{8,9},{9,8},{10,11... | collective-permute-start | bytes 629864 | tf_op jit(solution)/shard_map/ppermute | solution.py:609
  31.2 1.6 %collective-permute-start.9 = (bf16[9,54,216]{2,1,0:T(8,128)(2,1)S(1)}, bf16[9,54,216]{2,1,0:T(8,128)(2,1)S(1)}, u32[]{:S(2)}, u32[]{:S(2)}) collective-permute-start(bf16[9,54,216]{2,1,0:T(8,128)(2,1)S(1)} %collective-permute-done.7.refs_2_), channel_id=1, source_target_pairs={{0,1},{1,0},{2,3},{3,2},{4,5},{5,4},{6,7},{7,6},{8,9},{9,8},{10,11... | collective-permute-start | bytes 629864 | tf_op jit(solution)/shard_map/ppermute | solution.py:609
  36.8 2.8 %collective-permute-start.10 = (bf16[9,54,256]{2,1,0:T(8,128)(2,1)S(1)}, bf16[9,54,256]{2,1,0:T(8,128)(2,1)S(1)}, u32[]{:S(2)}, u32[]{:S(2)}) collective-permute-start(bf16[9,54,256]{2,1,0:T(8,128)(2,1)S(1)} %get-tuple-element.115), channel_id=1, source_target_pairs={{0,1},{1,0},{2,3},{3,2},{4,5},{5,4},{6,7},{7,6},{8,9},{9,8},{10,11... | collective-permute-start | bytes 746504 | tf_op jit(solution)/shard_map/ppermute | solution.py:609
  37.0 2.6 %collective-permute-start.11 = (bf16[9,54,256]{2,1,0:T(8,128)(2,1)S(1)}, bf16[9,54,256]{2,1,0:T(8,128)(2,1)S(1)}, u32[]{:S(2)}, u32[]{:S(2)}) collective-permute-start(bf16[9,54,256]{2,1,0:T(8,128)(2,1)S(1)} %get-tuple-element.116), channel_id=1, source_target_pairs={{0,1},{1,0},{2,3},{3,2},{4,5},{5,4},{6,7},{7,6},{8,9},{9,8},{10,11... | collective-permute-start | bytes 746504 | tf_op jit(solution)/shard_map/ppermute | solution.py:609
  39.6 8.3 %collective-permute-start.12 = (bf16[9,54,256]{2,1,0:T(8,128)(2,1)S(1)}, bf16[9,54,256]{2,1,0:T(8,128)(2,1)S(1)}, u32[]{:S(2)}, u32[]{:S(2)}) collective-permute-start(bf16[9,54,256]{2,1,0:T(8,128)(2,1)S(1)} %half_sum.2), channel_id=1, source_target_pairs={{0,2},{1,3},{2,0},{3,1},{4,6},{5,7},{6,4},{7,5},{8,10},{9,11},{10,... | collective-permute-start | bytes 746504 | tf_op jit(solution)/shard_map/ppermute | solution.py:609
  45.0 1.3 %collective-permute-start.14 = (bf16[3,54,256]{2,1,0:T(8,128)(2,1)S(1)}, bf16[3,54,256]{2,1,0:T(8,128)(2,1)S(1)}, u32[]{:S(2)}, u32[]{:S(2)}) collective-permute-start(bf16[3,54,256]{2,1,0:T(8,128)(2,1)S(1)} %get-tuple-element.135), channel_id=1, source_target_pairs={{0,1},{1,0},{2,3},{3,2},{4,5},{5,4},{6,7},{7,6},{8,9},{9,8},{10,11... | collective-permute-start | bytes 248840 | tf_op jit(solution)/shard_map/ppermute | solution.py:609
  45.1 3.6 %collective-permute-start.13 = (bf16[3,54,256]{2,1,0:T(8,128)(2,1)S(1)}, bf16[3,54,256]{2,1,0:T(8,128)(2,1)S(1)}, u32[]{:S(2)}, u32[]{:S(2)}) collective-permute-start(bf16[3,54,256]{2,1,0:T(8,128)(2,1)S(1)} %get-tuple-element.133), channel_id=1, source_target_pairs={{0,1},{1,0},{2,3},{3,2},{4,5},{5,4},{6,7},{7,6},{8,9},{9,8},{10,11... | collective-permute-start | bytes 248840 | tf_op jit(solution)/shard_map/ppermute | solution.py:609
  46.4 4.7 %collective-permute-start.15 = (bf16[3,54,256]{2,1,0:T(8,128)(2,1)S(1)}, bf16[3,54,256]{2,1,0:T(8,128)(2,1)S(1)}, u32[]{:S(2)}, u32[]{:S(2)}) collective-permute-start(bf16[3,54,256]{2,1,0:T(8,128)(2,1)S(1)} %half_sum.3), channel_id=1, source_target_pairs={{0,2},{1,3},{2,0},{3,1},{4,6},{5,7},{6,4},{7,5},{8,10},{9,11},{10,... | collective-permute-start | bytes 248840 | tf_op jit(solution)/shard_map/ppermute | solution.py:609
  51.7 6.4 %collective-permute-start.21 = (bf16[2,196,216]{2,1,0:T(8,128)(2,1)S(1)}, bf16[2,196,216]{2,1,0:T(8,128)(2,1)S(1)}, u32[]{:S(2)}, u32[]{:S(2)}) collective-permute-start(bf16[2,196,216]{2,1,0:T(8,128)(2,1)S(1)} %get-tuple-element.143.refs_0_), channel_id=1, source_target_pairs={{0,2},{1,3},{2,0},{3,1},{4,6},{5,7},{6,4},{7,5},{8,10},{9,11},{10,... | collective-permute-start | bytes 508040 | tf_op jit(solution)/shard_map/ppermute | solution.py:609
  52.2 5.9 %collective-permute-start.16 = (bf16[2,2,54,256]{3,2,1,0:T(8,128)(2,1)S(1)}, bf16[2,2,54,256]{3,2,1,0:T(8,128)(2,1)S(1)}, u32[]{:S(2)}, u32[]{:S(2)}) collective-permute-start(bf16[2,2,54,256]{3,2,1,0:T(8,128)(2,1)S(1)} %get-tuple-element.139), channel_id=1, source_target_pairs={{0,8},{4,12},{8,0},{12,4},{16,24},{20,28},{24,16},{28,20},{1,9},{5... | collective-permute-start | bytes 331784 | tf_op jit(solution)/shard_map/ppermute | solution.py:609
  52.3 11.2 %collective-permute-start.17 = (bf16[2,2,54,256]{3,2,1,0:T(8,128)(2,1)S(1)}, bf16[2,2,54,256]{3,2,1,0:T(8,128)(2,1)S(1)}, u32[]{:S(2)}, u32[]{:S(2)}) collective-permute-start(bf16[2,2,54,256]{3,2,1,0:T(8,128)(2,1)S(1)} %get-tuple-element.140), channel_id=1, source_target_pairs={{0,16},{4,20},{8,24},{12,28},{16,0},{20,4},{24,8},{28,12},{1,17},{... | collective-permute-start | bytes 331784 | tf_op jit(solution)/shard_map/ppermute | solution.py:609
  54.0 9.4 %collective-permute-start.18 = (bf16[2,2,54,256]{3,2,1,0:T(8,128)(2,1)S(1)}, bf16[2,2,54,256]{3,2,1,0:T(8,128)(2,1)S(1)}, u32[]{:S(2)}, u32[]{:S(2)}) collective-permute-start(bf16[2,2,54,256]{3,2,1,0:T(8,128)(2,1)S(1)} %get-tuple-element.141), channel_id=1, source_target_pairs={{0,24},{4,28},{8,16},{12,20},{16,8},{20,12},{24,0},{28,4},{1,25},{... | collective-permute-start | bytes 331784 | tf_op jit(solution)/shard_map/ppermute | solution.py:609
  56.6 8.3 %collective-permute-start.20 = (bf16[2,196,216]{2,1,0:T(8,128)(2,1)S(1)}, bf16[2,196,216]{2,1,0:T(8,128)(2,1)S(1)}, u32[]{:S(2)}, u32[]{:S(2)}) collective-permute-start(bf16[2,196,216]{2,1,0:T(8,128)(2,1)S(1)} %get-tuple-element.143.refs_0_), channel_id=1, source_target_pairs={{0,1},{1,0},{2,3},{3,2},{4,5},{5,4},{6,7},{7,6},{8,9},{9,8},{10,11... | collective-permute-start | bytes 508040 | tf_op jit(solution)/shard_map/ppermute | solution.py:609
  58.1 6.9 %collective-permute-start.22 = (bf16[2,196,216]{2,1,0:T(8,128)(2,1)S(1)}, bf16[2,196,216]{2,1,0:T(8,128)(2,1)S(1)}, u32[]{:S(2)}, u32[]{:S(2)}) collective-permute-start(bf16[2,196,216]{2,1,0:T(8,128)(2,1)S(1)} %collective-permute-done.21.refs_2_), channel_id=1, source_target_pairs={{0,1},{1,0},{2,3},{3,2},{4,5},{5,4},{6,7},{7,6},{8,9},{9,8},{10,11... | collective-permute-start | bytes 508040 | tf_op jit(solution)/shard_map/ppermute | solution.py:609
  63.5 4.4 %copy-start.1 = (f32[2,54,216]{2,0,1:T(2,128)S(1)}, f32[2,54,216]{2,0,1:T(2,128)}, u32[]{:S(2)}) copy-start(f32[2,54,216]{2,0,1:T(2,128)} %param.24) | copy-start | bytes 279940
  63.5 4.3 %copy-start.3 = (f32[2,54,216]{2,0,1:T(2,128)S(1)}, f32[2,54,216]{2,0,1:T(2,128)}, u32[]{:S(2)}) copy-start(f32[2,54,216]{2,0,1:T(2,128)} %param.25) | copy-start | bytes 279940
  63.5 4.3 %copy-start.4 = (f32[2,54,216]{2,0,1:T(2,128)S(1)}, f32[2,54,216]{2,0,1:T(2,128)}, u32[]{:S(2)}) copy-start(f32[2,54,216]{2,0,1:T(2,128)} %param.26) | copy-start | bytes 279940
  63.5 4.3 %copy-start.6 = (f32[9,216]{1,0:T(8,128)S(1)}, f32[9,216]{1,0:T(8,128)}, u32[]{:S(2)}) copy-start(f32[9,216]{1,0:T(8,128)} %refs_10_.1) | copy-start | bytes 23332
  63.6 4.3 %copy-start.7 = (f32[9,216]{1,0:T(8,128)S(1)}, f32[9,216]{1,0:T(8,128)}, u32[]{:S(2)}) copy-start(f32[9,216]{1,0:T(8,128)} %refs_11_.1) | copy-start | bytes 23332
  63.6 4.3 %copy-start.8 = (f32[2,12,12]{2,0,1:T(2,128)S(1)}, f32[2,12,12]{2,0,1:T(2,128)}, u32[]{:S(2)}) copy-start(f32[2,12,12]{2,0,1:T(2,128)} %param.31) | copy-start | bytes 3460
  63.6 4.3 %copy-start.9 = (f32[2,12,12]{2,0,1:T(2,128)S(1)}, f32[2,12,12]{2,0,1:T(2,128)}, u32[]{:S(2)}) copy-start(f32[2,12,12]{2,0,1:T(2,128)} %param.32) | copy-start | bytes 3460
  63.6 4.3 %copy-start.11 = (f32[4,216]{1,0:T(4,128)S(1)}, f32[4,216]{1,0:T(4,128)}, u32[]{:S(2)}) copy-start(f32[4,216]{1,0:T(4,128)} %refs_4_.1) | copy-start | bytes 10372
  63.6 4.3 %copy-start.12 = (f32[4,216]{1,0:T(4,128)S(1)}, f32[4,216]{1,0:T(4,128)}, u32[]{:S(2)}) copy-start(f32[4,216]{1,0:T(4,128)} %refs_5_.1) | copy-start | bytes 10372
  63.6 4.2 %collective-permute-start.19 = (bf16[2,54,256]{2,1,0:T(8,128)(2,1)S(1)}, bf16[2,54,256]{2,1,0:T(8,128)(2,1)S(1)}, u32[]{:S(2)}, u32[]{:S(2)}) collective-permute-start(bf16[2,54,256]{2,1,0:T(8,128)(2,1)S(1)} %get-tuple-element.142), channel_id=1, source_target_pairs={{0,4},{4,0},{8,12},{12,8},{16,20},{20,16},{24,28},{28,24},{1,5},{5... | collective-permute-start | bytes 165896 | tf_op jit(solution)/shard_map/ppermute | solution.py:609

commit v7 on v6

--- a/solution.py
+++ b/solution.py
@@ -10,6 +10,13 @@
 SIDE = 14
 PITCH = 16
 MARGIN = 24
+BUNCH = 4
+EARLY = 4
+
+
+def bunches(first, last):
+    return [(y, min(BUNCH, last - y)) for y in range(first, last, BUNCH)]
+
 FREE = 216
 WIDE = 40
 norm_eps = 1e-05
@@ -50,7 +57,9 @@
 
 
 def true_head(rows, place):
-    return ((rows // (3 * PITCH)) ^ place) * 3 + (rows // PITCH) % 3
+    head = rows >> 4
+    part = (head >= 3).astype(jnp.int32) + (head >= 6).astype(jnp.int32) + (head >= 9).astype(jnp.int32)
+    return (part ^ place) * 3 + (head - 3 * part)
 
 
 def prep_kernel(scal, tok_ref, cot_ref, norm_ref, talk_ref, x_ref, a_ref, dy_ref, mix_ref, bias_ref, tmp_ref):
@@ -94,7 +103,7 @@
     return jnp.sum(rows.reshape(heads, PITCH, rows.shape[1]), axis=0)
 
 
-def attn_fwd_kernel(scal, x_ref, a_ref, mix_ref, bias_ref, *refs, parts, unroll):
+def attn_fwd_kernel(scal, x_ref, a_ref, mix_ref, bias_ref, *refs, parts):
     w_refs, refs = refs[:parts], refs[parts:]
     mid_ref, q_ref, k_ref, v_ref, o_ref, qw_ref, p_ref, pv_ref, ws_ref, t_ref = refs
     heads = mix_ref.shape[1] // PITCH
@@ -107,24 +116,23 @@
     head = lane_head((1, 256), 1, scal[0])
     keep = ((head >= 0) & (head < scal[2])).astype(f32)
 
-    def groups(b, _):
-        ys = [b * unroll + u for u in range(unroll)]
-        rows = [pl.ds(pl.multiple_of(y * PITCH, PITCH), PITCH) for y in ys]
-        for u, y in enumerate(ys):
-            qw_ref[y] = (tiled(q_ref[rows[u], :].astype(f32), heads) * mix_ref[0]).astype(bf16)
-        for u, y in enumerate(ys):
-            t_ref[u] = nt(k_ref[...], qw_ref[y]) + bias_ref[...]
-        for u, y in enumerate(ys):
-            t = t_ref[u]
+    n = heads * PITCH
+    for y in range(SIDE):
+        q = q_ref[PITCH * y : PITCH * (y + 1), :].astype(f32)
+        qw_ref[n * y : n * (y + 1), :] = (tiled(q, heads) * mix_ref[0]).astype(bf16)
+    for b, (y, count) in enumerate(bunches(0, SIDE)):
+        t_ref[b, :, 0 : n * count] = nt(k_ref[...], qw_ref[n * y : n * (y + count), :])
+    for b, (y, count) in enumerate(bunches(0, SIDE)):
+        for at in range(0, n * count, 128):
+            t = t_ref[b, :, at : at + 128] + bias_ref[...]
             e = jnp.exp(t - jnp.max(t, axis=0, keepdims=True))
-            p_ref[y] = (e * (1.0 / jnp.sum(e, axis=0, keepdims=True))).astype(bf16)
-        for u, y in enumerate(ys):
-            pv = tn(p_ref[y], v_ref[...])
-            pv_ref[y] = pv.astype(bf16)
-            o_ref[rows[u], :] = (over_heads(pv * mix_ref[1], heads) * keep).astype(bf16)
-        return 0
-
-    lax.fori_loop(0, SIDE // unroll, groups, 0)
+            p_ref[b, :, at : at + 128] = (e * (1.0 / jnp.sum(e, axis=0, keepdims=True))).astype(bf16)
+    for b, (first, count) in enumerate(bunches(0, SIDE)):
+        pv = tn(p_ref[b, :, 0 : n * count], v_ref[...])
+        pv_ref[n * first : n * (first + count), :] = pv.astype(bf16)
+        for u in range(count):
+            o = over_heads(pv[n * u : n * (u + 1)] * mix_ref[1], heads)
+            o_ref[PITCH * (first + u) : PITCH * (first + u + 1), :] = (o * keep).astype(bf16)
     mid_ref[...] = x_ref[...] + nn(o_ref[...], ws_ref[3])
 
 
@@ -163,97 +171,119 @@
     return ((iota(shape, 0) == (lane >> 6) * 54 + rest) & (rest < 54)).astype(bf16)
 
 
-def ffn_kernel(scal, mid_ref, dy_ref, norm_ref, o_ref, *refs, parts):
+def up(w_ref, w, e, win_ref, wdn_ref, h_ref, d_ref, cv_ref):
+    tokens, dim = w.shape
+    pad = MARGIN
+    for j in range(4):
+        at = 64 * j
+        win_ref[at : at + 54, :] = w_ref[j]
+        wdn_ref[at : at + 54, :] = w_ref[4 + j]
+        win_ref[at + 54 : at + 64, :] = jnp.zeros((10, dim), bf16)
+        wdn_ref[at + 54 : at + 64, :] = jnp.zeros((10, dim), bf16)
+    both = nn(w_ref[8], place(dim))
+    cv_ref[...] = both[0:9] + both[16:25]
+    hidden = nt(w, win_ref[...])
+    dgate = nt(e, wdn_ref[...])
+    zero = jnp.zeros((pad, 128), f32)
+    for half in range(2):
+        mine = slice(128 * half, 128 * (half + 1))
+        for ref, value in ((h_ref, hidden), (d_ref, dgate)):
+            ref[half, 0:pad, :] = zero
+            ref[half, pad + tokens :, :] = zero
+            ref[half, pad : pad + tokens, :] = value[:, mine]
+
+
+def middle(scal, k, h_ref, d_ref, gate_ref, dh_ref, cv_ref, gcv_ref):
+    tokens = gate_ref.shape[0]
+    pad = MARGIN
+    for half in range(2):
+        cols = slice(128 * half, 128 * (half + 1))
+        lane = iota((1, 128), 1) + 128 * half
+        unit = ((k ^ scal[0]) * 4 + (lane >> 6)) * 54 + (lane & 63)
+        keep = (unit < scal[3]).astype(f32)
+        act = None
+        for t in range(9):
+            off = pad + PITCH * (t // 3 - 1) + t % 3 - 1
+            term = cv_ref[t : t + 1, cols] * h_ref[half, off : off + tokens, :]
+            act = term if act is None else act + term
+        sig = 0.5 * jnp.tanh(0.5 * act) + 0.5
+        silu = act * sig
+        gate_ref[:, cols] = (silu * keep).astype(bf16)
+        dact = d_ref[half, pad : pad + tokens, :] * keep * (silu + sig * (1.0 - silu))
+        d_ref[half, pad : pad + tokens, :] = dact
+        dh = None
+        for t in range(9):
+            shift = PITCH * (t // 3 - 1) + t % 3 - 1
+            gcv_ref[t : t + 1, cols] = jnp.sum(
+                dact * h_ref[half, pad + shift : pad + shift + tokens, :], axis=0, keepdims=True
+            )
+            term = cv_ref[t : t + 1, cols] * d_ref[half, pad - shift : pad - shift + tokens, :]
+            dh = term if dh is None else dh + term
+        dh_ref[:, cols] = dh.astype(bf16)
+
+
+def ffn_first_kernel(scal, mid_ref, dy_ref, norm_ref, *refs, parts):
     w_refs, refs = refs[:parts], refs[parts:]
-    out_ref, dmid_ref, gn_ref = refs[:3]
-    gw_refs, refs = refs[3 : 3 + parts], refs[3 + parts :]
-    win_ref, wdn_ref, h_ref, d_ref, gate_ref, dh_ref, cv_ref, gcv_ref, tmp_ref, sm_ref, down_ref, dw_ref = refs
-    pm = place(256)
-    mid = mid_ref[...]
-    tokens, dim = mid.shape
-    z, inv = ln_stats(mid)
-    rows = real_rows(mid.shape)
-    w = jnp.where(rows, z * norm_ref[2:3, :] + norm_ref[3:4, :], 0.0).astype(bf16)
-    dy = dy_ref[...]
-    e = dy.astype(bf16)
-    pad = MARGIN
-    zero = jnp.zeros((pad, 128), f32)
-    lane = iota((1, 128), 1)
-    free = iota((54, 256), 1) >= FREE
-    for h in range(parts):
-        for j in range(4):
-            at = 64 * j
-            win_ref[h, at : at + 54, :] = w_refs[h][j]
-            wdn_ref[h, at : at + 54, :] = w_refs[h][4 + j]
-            win_ref[h, at + 54 : at + 64, :] = jnp.zeros((10, dim), bf16)
-            wdn_ref[h, at + 54 : at + 64, :] = jnp.zeros((10, dim), bf16)
-        both = nn(w_refs[h][8], pm[0:dim])
-        cv_ref[:, 256 * h : 256 * (h + 1)] = both[0:9] + both[16:25]
-    def up(h):
-        hidden = nt(w, win_ref[h])
-        dgate = nt(e, wdn_ref[h])
-        for half in range(2):
-            c = 2 * h + half
-            mine = slice(128 * half, 128 * (half + 1))
-            for ref, value in ((h_ref, hidden), (d_ref, dgate)):
-                ref[c, 0:pad, :] = zero
-                ref[c, pad + tokens :, :] = zero
-                ref[c, pad : pad + tokens, :] = value[:, mine]
-
-    def middle(h):
-        for half in range(2):
-            c = 2 * h + half
-            cols = slice(128 * c, 128 * (c + 1))
-            mine = slice(128 * half, 128 * (half + 1))
-            glane = lane + 128 * c
-            unit = (((glane >> 8) ^ scal[0]) * 4 + ((glane >> 6) & 3)) * 54 + (glane & 63)
-            keep = (unit < scal[3]).astype(f32)
-            act = None
-            for t in range(9):
-                off = pad + PITCH * (t // 3 - 1) + t % 3 - 1
-                term = cv_ref[t : t + 1, cols] * h_ref[c, off : off + tokens, :]
-                act = term if act is None else act + term
-            sig = 0.5 * jnp.tanh(0.5 * act) + 0.5
-            silu = act * sig
-            gate_ref[h, :, mine] = (silu * keep).astype(bf16)
-            dact = d_ref[c, pad : pad + tokens, :] * keep * (silu + sig * (1.0 - silu))
-            d_ref[c, pad : pad + tokens, :] = dact
-            dh = None
-            for t in range(9):
-                shift = PITCH * (t // 3 - 1) + t % 3 - 1
-                gcv_ref[t : t + 1, cols] = jnp.sum(
-                    dact * h_ref[c, pad + shift : pad + shift + tokens, :], axis=0, keepdims=True
-                )
-                term = cv_ref[t : t + 1, cols] * d_ref[c, pad - shift : pad - shift + tokens, :]
-                dh = term if dh is None else dh + term
-            dh_ref[h, :, mine] = dh.astype(bf16)
-
-    def back(h):
-        gi = tn(dh_ref[h], w).astype(bf16)
-        gd = tn(gate_ref[h], e).astype(bf16)
+    z_ref, inv_ref, w_ref, e_ref, win_ref, wdn_ref, gate_ref, dh_ref, gcv_ref, h_ref, d_ref, cv_ref = refs
+    z, inv = ln_stats(mid_ref[...])
+    z_ref[...] = z
+    inv_ref[...] = jnp.broadcast_to(inv, inv_ref.shape)
+    w = jnp.where(real_rows(z.shape), z * norm_ref[2:3, :] + norm_ref[3:4, :], 0.0).astype(bf16)
+    e = dy_ref[...].astype(bf16)
+    w_ref[...] = w
+    e_ref[...] = e
+    for k in range(parts):
+        up(w_refs[k], w, e, win_ref.at[k], wdn_ref.at[k], h_ref.at[k], d_ref.at[k], cv_ref.at[k])
+    for k in range(parts):
+        middle(
+            scal, k, h_ref.at[k], d_ref.at[k], gate_ref.at[k], dh_ref.at[k], cv_ref.at[k], gcv_ref.at[k]
+        )
+
+
+def ffn_last_kernel(
+    scal, mid_ref, dy_ref, norm_ref, o_ref, z_ref, inv_ref, w_ref, e_ref, *refs, parts
+):
+    wins, wdns, gates, dhs, gcvs, last_ref = refs[:6]
+    out_ref, dmid_ref, gn_ref = refs[6:9]
+    gw_refs, refs = refs[9 : 9 + parts], refs[9 + parts :]
+    win_ref, wdn_ref, gate_ref, dh_ref, gcv_ref, h_ref, d_ref, cv_ref, tmp_ref, sm_ref, dw_ref = refs
+    w, e = w_ref[...], e_ref[...]
+    dim = w.shape[1]
+    k = parts - 1
+    up(last_ref, w, e, win_ref, wdn_ref, h_ref, d_ref, cv_ref)
+    for h in range(k):
+        gi = tn(dhs[h], w).astype(bf16)
+        gd = tn(gates[h], e).astype(bf16)
         for j in range(4):
             gw_refs[h][1 + j, :, 0:dim] = gi[64 * j : 64 * j + 54]
             gw_refs[h][5 + j, :, 0:dim] = gd[64 * j : 64 * j + 54]
-        in_free_lanes(nt(gcv_ref[:, 256 * h : 256 * (h + 1)].astype(bf16), pm), sm_ref.at[h], 0)
+    middle(scal, k, h_ref, d_ref, gate_ref, dh_ref, cv_ref, gcv_ref)
+    wins, wdns, gates, dhs, gcvs = [
+        [ref.at[i] for i in range(k)] + [own]
+        for ref, own in ((wins, win_ref), (wdns, wdn_ref), (gates, gate_ref), (dhs, dh_ref), (gcvs, gcv_ref))
+    ]
+    dw_ref[...] = sum(nn(dhs[h][...], wins[h][...]) for h in range(parts))
+    valid = (scal[0] < scal[1]).astype(f32)
+    tmp_ref[...] = (mid_ref[...] + sum(nn(gates[h][...], wdns[h][...]) for h in range(parts))) * valid
+    free = iota((54, 256), 1) >= FREE
+    pm = place(256)
+    for h in range(parts):
+        if h == k:
+            gi = tn(dhs[h][...], w).astype(bf16)
+            gd = tn(gates[h][...], e).astype(bf16)
+            for j in range(4):
+                gw_refs[h][1 + j, :, 0:dim] = gi[64 * j : 64 * j + 54]
+                gw_refs[h][5 + j, :, 0:dim] = gd[64 * j : 64 * j + 54]
+        in_free_lanes(nt(gcvs[h][...].astype(bf16), pm), sm_ref.at[h], 0)
         gw_refs[h][0] = jnp.where(free, sm_ref[h, 0:54, :], 0.0).astype(bf16)
-
-    for h in range(parts):
-        up(h)
-    for h in range(parts):
-        middle(h)
-    down_ref[...] = sum(nn(gate_ref[h], wdn_ref[h]) for h in range(parts))
-    dw_ref[...] = sum(nn(dh_ref[h], win_ref[h]) for h in range(parts))
-    for h in range(parts):
-        back(h)
-    valid = (scal[0] < scal[1]).astype(f32)
-    tmp_ref[...] = (mid + down_ref[...]) * valid
     for y in range(SIDE):
         out_ref[SIDE * y : SIDE * (y + 1), :] = tmp_ref[PITCH * y : PITCH * y + SIDE, :].astype(bf16)
-    dw = jnp.where(rows, dw_ref[...], 0.0)
+    z, inv = z_ref[...], inv_ref[:, 0:1]
+    dw = jnp.where(real_rows(z.shape), dw_ref[...], 0.0)
     gn_ref[...] = jnp.zeros_like(gn_ref)
     gn_ref[0:1, :] = jnp.sum(dw * z, axis=0, keepdims=True)
     gn_ref[1:2, :] = jnp.sum(dw, axis=0, keepdims=True)
-    dmid = dy + ln_back(dw, z, inv, norm_ref[2:3, :])
+    dmid = dy_ref[...] + ln_back(dw, z, inv, norm_ref[2:3, :])
     dmid_ref[...] = dmid
     go = tn(o_ref[...], dmid.astype(bf16)).astype(bf16)
     for h in range(parts):
@@ -280,26 +310,37 @@
         do_ref, *sums, gq_ref, gkb_ref, gvb_ref, gt_ref, gk_ref, gv_ref, g0_ref, g1_ref, dw_ref, dp_ref, dt_ref = refs
         for ref, old in zip((gk_ref, gv_ref, g0_ref, g1_ref), sums):
             ref[...] = old[...]
-    first = SIDE // 2 * part
-
-    ys = [first + u for u in range(SIDE // 2)]
-    rows = [slice(PITCH * y, PITCH * (y + 1)) for y in ys]
-    for u, y in enumerate(ys):
-        dw_ref[u] = (tiled(do_ref[rows[u], :].astype(f32), heads) * mix_ref[1]).astype(bf16)
-    for u, y in enumerate(ys):
-        dp_ref[u] = nt(v_ref[...], dw_ref[u])
-    for u, y in enumerate(ys):
-        dp = dp_ref[u]
-        p = p_ref[y].astype(f32)
-        dt_ref[u] = (p * (dp - jnp.sum(dp * p, axis=0, keepdims=True))).astype(bf16)
-    gv_ref[...] += sum(nn(p_ref[y], dw_ref[u]) for u, y in enumerate(ys))
-    gk_ref[...] += sum(nn(dt_ref[u], qw_ref[y]) for u, y in enumerate(ys))
-    for u, y in enumerate(ys):
-        dk = tn(dt_ref[u], k_ref[...])
-        gq_ref[PITCH * u : PITCH * (u + 1), :] = over_heads(dk * mix_ref[0], heads).astype(bf16)
-        g0_ref[...] += dk * tiled(q_ref[rows[u], :].astype(f32), heads)
-    for u, y in enumerate(ys):
-        g1_ref[...] += pv_ref[y].astype(f32) * tiled(do_ref[rows[u], :].astype(f32), heads)
+    first, last = (0, EARLY) if part == 0 else (EARLY, SIDE)
+    for y in range(first, last):
+        do = do_ref[PITCH * y : PITCH * (y + 1), :].astype(f32)
+        at = n * (y - first)
+        dw_ref[at : at + n, :] = (tiled(do, heads) * mix_ref[1]).astype(bf16)
+    groups = [(b, b + first // BUNCH, y, count) for b, (y, count) in enumerate(bunches(first, last))]
+    for b, _, y, count in groups:
+        at = n * (y - first)
+        dp_ref[b, :, 0 : n * count] = nt(v_ref[...], dw_ref[at : at + n * count, :])
+    for b, whole_b, y, count in groups:
+        for at in range(0, n * count, 128):
+            dp = dp_ref[b, :, at : at + 128]
+            p = p_ref[whole_b, :, at : at + 128].astype(f32)
+            dt_ref[b, :, at : at + 128] = (p * (dp - jnp.sum(dp * p, axis=0, keepdims=True))).astype(bf16)
+    gv, gk = gv_ref[...], gk_ref[...]
+    for b, whole_b, y, count in groups:
+        at = n * (y - first)
+        gv = gv + nn(p_ref[whole_b, :, 0 : n * count], dw_ref[at : at + n * count, :])
+        gk = gk + nn(dt_ref[b, :, 0 : n * count], qw_ref[n * y : n * (y + count), :])
+    gv_ref[...] = gv
+    gk_ref[...] = gk
+    for b, _, y, count in groups:
+        dk = tn(dt_ref[b, :, 0 : n * count], k_ref[...])
+        for u in range(count):
+            mine = dk[n * u : n * (u + 1)]
+            at = PITCH * (y + u)
+            gq_ref[at - PITCH * first : at - PITCH * first + PITCH, :] = over_heads(mine * mix_ref[0], heads).astype(bf16)
+            g0_ref[...] += mine * tiled(q_ref[at : at + PITCH, :].astype(f32), heads)
+    for y in range(first, last):
+        do = do_ref[PITCH * y : PITCH * (y + 1), :].astype(f32)
+        g1_ref[...] += pv_ref[n * y : n * (y + 1), :].astype(f32) * tiled(do, heads)
     if part == 0:
         return
     gkb_ref[...] = gk_ref[...].astype(bf16)
@@ -364,20 +405,23 @@
         out_ref[i] = m_ref[:, i, :].astype(bf16)
 
 
-def pair_kernel(own_ref, other_ref, out_ref):
-    out_ref[0] = own_ref[...]
-    out_ref[1] = other_ref[...]
-
-
-def select_kernel(slot_ref, scal, conv_ref, *refs):
-    pairs, (attn_ref, ffn_ref, every_ref) = refs[:-3], refs[-3:]
-    for k, ref in enumerate(pairs):
-        every_ref[scal[5] ^ k] = ref[...]
-    per = every_ref.shape[2]
+def spot(slot, per):
+    bits = per.bit_length() - 1
+    return slot >> (bits + 1), (slot >> bits) & 1, slot & (per - 1)
+
+
+def stack_kernel(*refs):
+    for k, ref in enumerate(refs[:-1]):
+        refs[-1][k] = ref[...]
+
+
+def select_kernel(slot_ref, scal, conv_ref, own_ref, other_ref, attn_ref, ffn_ref, every_ref):
+    every_ref[0] = own_ref[...]
+    every_ref[1] = other_ref[...]
+    per = own_ref.shape[1]
     for b in range(12):
-        slot = slot_ref[b]
-        rank = slot // per
-        block = every_ref[rank // 2, (rank % 2) ^ scal[4], slot % per]
+        pair, place, own = spot(slot_ref[b], per)
+        block = every_ref[place ^ scal[4], pair ^ scal[5], own]
         if b < 4:
             attn_ref[b] = block
         else:
@@ -399,19 +443,14 @@
     out_ref[...] = (a_ref[...].astype(f32) + b_ref[...].astype(f32)).astype(bf16)
 
 
-def spot(slot, scal, per):
-    rank = slot // per
-    return (rank // 2) ^ scal[5], (rank % 2) ^ scal[4], slot % per
-
-
 def spread_ffn_kernel(slot_ref, scal, *refs):
     ffn_refs, out_ref = refs[:-1], refs[-1]
     pairs, _, per = out_ref.shape[:3]
     out_ref[...] = jnp.zeros_like(out_ref)
     for b in range(9):
         block = total(ffn_refs, b)
-        k, j, i = spot(slot_ref[3 + b], scal, per)
-        out_ref[k, j, i, :, 0:FREE] = block[:, 0:FREE].astype(bf16)
+        k, j, i = spot(slot_ref[3 + b], per)
+        out_ref[k ^ scal[5], j ^ scal[4], i, :, 0:FREE] = block[:, 0:FREE].astype(bf16)
         if b == 0:
             wide = block[:, FREE:].astype(bf16)
     for k in range(pairs):
@@ -425,20 +464,19 @@
     all_ref[...] = old_ref[...]
     for b in range(3):
         block = total(attn, b)
-        k, j, i = spot(slot_ref[b], scal, per)
-        all_ref[k, j, i, :, 0:FREE] = block[:, 0:FREE].astype(bf16)
+        k, j, i = spot(slot_ref[b], per)
+        all_ref[k ^ scal[5], j ^ scal[4], i, :, 0:FREE] = block[:, 0:FREE].astype(bf16)
         if b == 0:
             wide = block[:, FREE:].astype(bf16)
-    for k in range(pairs):
-        outs[k][...] = all_ref[k]
-        for j in range(2):
-            outs[k][j, 1, :, FREE:] = wide
-
-
-def pair_sum_kernel(*refs):
-    own_ref, other_ref = refs[-2:]
-    own_ref[...] = total(refs[:-2], 0)
-    other_ref[...] = total(refs[:-2], 1).astype(bf16)
+    for j in range(2):
+        outs[j][...] = all_ref[:, j]
+        for k in range(pairs):
+            outs[j][k, 1, :, FREE:] = wide
+
+
+def place_sum_kernel(own_ref, other_ref, *outs):
+    for k, out_ref in enumerate(outs):
+        out_ref[...] = (own_ref[k].astype(f32) + other_ref[k].astype(f32)).astype(out_ref.dtype)
 
 
 def adam(w, g, one, two, rate, decay):
@@ -449,12 +487,13 @@
     return w - rate * (hat_one / (jnp.sqrt(hat_two) + 1e-08) + decay * w), one_new, two_new
 
 
-def update_kernel(own_ref, other_ref, *refs):
+def update_kernel(*refs):
+    got, refs = refs[:-28], refs[-28:]
     ins, outs, (g_ref, sm_ref, flat_ref) = refs[0:12], refs[12:25], refs[25:]
-    per, rows = own_ref.shape[:2]
+    per, rows = got[0].shape[:2]
     dim = ins[0].shape[2]
     for i in range(per):
-        g = own_ref[i] + other_ref[i].astype(f32)
+        g = total(got, i)
         g_ref[:, i, :] = g[:, 0:dim]
         sm_ref[i, 0:rows, :] = g
     w, one, two = adam(ins[0][...], g_ref[...], ins[1][...], ins[2][...], 0.06, 0.05)
@@ -485,7 +524,8 @@
     step = 32
     shape = (parts * step, parts * step)
     row, col = iota(shape, 0), iota(shape, 1)
-    pick = ((row // parts == col % step) & (row % parts == col // step)).astype(bf16)
+    bits = parts.bit_length() - 1
+    pick = ((row >> bits == col & (step - 1)) & (row & (parts - 1) == col >> 5)).astype(bf16)
     full = all_ref.shape[1]
     for k in range(parts):
         all_ref[k, tokens // step * step : full, :] = jnp.zeros((full - tokens // step * step, all_ref.shape[2]), bf16)
@@ -533,44 +573,58 @@
                 full(*norm_params.shape),
                 full(*talk.shape),
             ],
-            out_specs=[full(pad, dim), full(pad, dim), full(pad, dim), full(2, n, 256), full(pad, n)],
+            out_specs=[full(pad, dim), full(pad, dim), full(pad, dim), full(2, n, 256), full(pad, 128)],
             scratch_shapes=[pltpu.VMEM((tok, dim), f32)],
         ),
         out_shape=[SDS((pad, dim), f32), SDS((pad, dim), bf16), SDS((pad, dim), f32), SDS((2, n, 256), f32),
-                   SDS((pad, n), f32)],
+                   SDS((pad, 128), f32)],
         compiler_params=pltpu.CompilerParams(vmem_limit_bytes=16 << 20),
         cost_estimate=pl.CostEstimate(flops=1000000000, transcendentals=0, bytes_accessed=3000000),
         name="prep",
     )(scal, tokens, cotangent, norm_params, talk)
 
 
-def attn_fwd(scal, x, a, mix, bias, w, unroll=14):
+def attn_fwd(scal, x, a, mix, bias, w):
     pad, dim = x.shape
     n = mix.shape[1]
+    grid = (len(bunches(0, SIDE)), pad, n * BUNCH)
     return call(
         attn_fwd_kernel, "attn_fwd", 1, 4 + len(w),
         [SDS((pad, dim), f32)] + [SDS((pad, 256), bf16)] * 4
-        + [SDS((SIDE, n, 256), bf16), SDS((SIDE, pad, n), bf16), SDS((SIDE, n, 256), bf16)],
-        [pltpu.VMEM((4, 256, dim), bf16), pltpu.VMEM((unroll, pad, n), f32)],
-        mb=24, micros=1, parts=len(w), unroll=unroll,
+        + [SDS((SIDE * n, 256), bf16), SDS(grid, bf16), SDS((SIDE * n, 256), bf16)],
+        [pltpu.VMEM((4, 256, dim), bf16), pltpu.VMEM(grid, f32)],
+        mb=24, micros=1, parts=len(w),
     )(scal, x, a, mix, bias, *w)
 
 
-def ffn(scal, mid, dy, norm_params, o, w):
+def ffn_first(scal, mid, dy, norm_params, w):
     pad, dim = mid.shape
-    lanes = len(w) * 256
+    count = len(w)
+    lanes = [(count, 256, dim)] * 2 + [(count, pad, 256)] * 2
+    grids = [pltpu.VMEM((count, 2, pad + 2 * MARGIN, 128), f32)] * 2
     return call(
-        ffn_kernel, "ffn", 1, 4 + len(w),
-        [SDS((SIDE * SIDE, dim), bf16), SDS((pad, dim), f32), SDS((8, dim), f32)] + [SDS((9, 54, 256), bf16)] * len(w),
-        [
-            pltpu.VMEM((len(w), 256, dim), bf16), pltpu.VMEM((len(w), 256, dim), bf16),
-            pltpu.VMEM((lanes // 128, pad + 2 * MARGIN, 128), f32), pltpu.VMEM((lanes // 128, pad + 2 * MARGIN, 128), f32),
-            pltpu.VMEM((len(w), pad, 256), bf16), pltpu.VMEM((len(w), pad, 256), bf16),
-            pltpu.VMEM((9, lanes), f32), pltpu.VMEM((9, lanes), f32), pltpu.VMEM((pad, dim), f32),
-            pltpu.VMEM((len(w), 56, 256), f32), pltpu.VMEM((pad, dim), f32), pltpu.VMEM((pad, dim), f32),
+        ffn_first_kernel, "ffn_first", 1, 3 + count,
+        [SDS((pad, dim), f32), SDS((pad, 128), f32), SDS((pad, dim), bf16), SDS((pad, dim), bf16)]
+        + [SDS(t, bf16) for t in lanes] + [SDS((count, 9, 256), f32)],
+        grids + [pltpu.VMEM((count, 9, 256), f32)],
+        mb=24, micros=3, parts=count,
+    )(scal, mid, dy, norm_params, *w)
+
+
+def ffn_last(scal, mid, dy, norm_params, o, first, w):
+    pad, dim = mid.shape
+    parts = first[4].shape[0] + 1
+    grids = [pltpu.VMEM((2, pad + 2 * MARGIN, 128), f32)] * 2
+    return call(
+        ffn_last_kernel, "ffn_last", 1, 14,
+        [SDS((SIDE * SIDE, dim), bf16), SDS((pad, dim), f32), SDS((8, dim), f32)] + [SDS((9, 54, 256), bf16)] * parts,
+        [pltpu.VMEM((256, dim), bf16)] * 2 + [pltpu.VMEM((pad, 256), bf16)] * 2 + [pltpu.VMEM((9, 256), f32)] + grids
+        + [
+            pltpu.VMEM((9, 256), f32), pltpu.VMEM((pad, dim), f32), pltpu.VMEM((parts, 56, 256), f32),
+            pltpu.VMEM((pad, dim), f32),
         ],
-        mb=24, micros=6, parts=len(w),
-    )(scal, mid, dy, norm_params, o, *w)
+        mb=24, micros=4, parts=parts,
+    )(scal, mid, dy, norm_params, o, *first, w)
 
 
 def scores_back(scal, dmid, mix, q, k, v, qw, p, pv, more, part):
@@ -578,7 +632,8 @@
     n = mix.shape[1]
     heads = n // PITCH
     sums = [SDS((pad, 256), f32)] * 2 + [SDS((n, 256), f32)] * 2
-    half = SDS((pad // 2, 256), bf16)
+    count = EARLY if part == 0 else SIDE - EARLY
+    half = SDS((PITCH * count, 256), bf16)
     if part == 0:
         outs = [SDS((pad, 256), bf16), half] + sums
         scratch = [pltpu.VMEM((256, dim), bf16)]
@@ -586,7 +641,8 @@
         outs = [half] + [SDS((pad, 256), bf16)] * 2 + [SDS((2, heads, heads), f32)]
         scratch = [pltpu.VMEM(t.shape, f32) for t in sums]
     scratch += [
-        pltpu.VMEM((SIDE // 2, n, 256), bf16), pltpu.VMEM((SIDE // 2, pad, n), f32), pltpu.VMEM((SIDE // 2, pad, n), bf16)
+        pltpu.VMEM((n * count, 256), bf16), pltpu.VMEM((-(-count // BUNCH), pad, n * BUNCH), f32),
+        pltpu.VMEM((-(-count // BUNCH), pad, n * BUNCH), bf16),
     ]
     return call(
         scores_back_kernel, "scores_back", 1, 8 + len(more), outs, scratch,
@@ -621,7 +677,7 @@
     return pl.pallas_call(
         body,
         grid=(1,),
-        in_specs=[whole(*t.shape) for t in ins],
+        in_specs=[VM] * len(ins),
         out_specs=[whole(*t.shape) for t in outs],
         out_shape=outs,
         scratch_shapes=scratch,
@@ -653,23 +709,29 @@
         compiler_params=pltpu.CompilerParams(vmem_limit_bytes=16 << 20),
         name="cast",
     )(swap(master))
-    (pair,) = call(pair_kernel, "pair", 0, 2, [SDS((2, slots, rows, dim), bf16)])(mine, permute(mine, "dp", 1))
-    pair, tokens, cotangent, talk_in = lax.optimization_barrier((pair, tokens, cotangent, talk))
-    pairs = [pair] + [permute(pair, "dp", 2 * k) for k in range(1, ranks // 2)]
+    pairs = ranks // 2
+    far = {k: permute(mine, "dp", 2 * k) for k in (*range(2, pairs), 1)}
+    (own,) = call(stack_kernel, "stack", 0, pairs, [SDS((pairs, slots, rows, dim), bf16)])(
+        mine, *[far[k] for k in range(1, pairs)]
+    )
+    own, tokens, cotangent, talk_in = lax.optimization_barrier((own, tokens, cotangent, talk))
+    other = permute(own, "dp", 1)
     x, a, dy, mix, bias = prep(scal, tokens, cotangent, norm_params, talk_in)
-    pairs[1], x = lax.optimization_barrier((pairs[1], x))
+    other, x = lax.optimization_barrier((other, x))
     attn_w, ffn_w = call(
-        select_kernel, "select", 2, 1 + len(pairs), [SDS((4, rows, dim), bf16), SDS((9, rows, dim), bf16)],
-        [pltpu.VMEM((ranks // 2, 2, slots, rows, dim), bf16)],
-    )(block_slot, scal, conv, *pairs)
+        select_kernel, "select", 2, 3, [SDS((4, rows, dim), bf16), SDS((9, rows, dim), bf16)],
+        [pltpu.VMEM((2, pairs, slots, rows, dim), bf16)],
+    )(block_slot, scal, conv, own, other)
     attn_2, attn_1 = permute(attn_w, "head", 2), permute(attn_w, "head", 1)
     attn_3 = permute(attn_2, "head", 1)
     attn_w = [attn_w, attn_1, attn_2, attn_3]
     ffn_2, ffn_1 = permute(ffn_w, "head", 2), permute(ffn_w, "head", 1)
     mid, q, k, v, o, qw, p, pv = attn_fwd(scal, x, a, mix, bias, attn_w)
     mid, ffn_2 = lax.optimization_barrier((mid, ffn_2))
-    ffn_w = [ffn_w, ffn_1, ffn_2, permute(ffn_2, "head", 1)]
-    out, dmid, gn2, *ffn_g = ffn(scal, mid, dy, norm_params, o, ffn_w)
+    ffn_3 = permute(ffn_2, "head", 1)
+    first = list(ffn_first(scal, mid, dy, norm_params, [ffn_w, ffn_1, ffn_2]))
+    first[0], ffn_3 = lax.optimization_barrier((first[0], ffn_3))
+    out, dmid, gn2, *ffn_g = ffn_last(scal, mid, dy, norm_params, o, first, ffn_3)
     ffn_1, ffn_3 = permute(ffn_g[1], "head", 1), permute(ffn_g[3], "head", 1)
     do, gqa, *sums = scores_back(scal, dmid, mix, q, k, v, qw, p, pv, attn_w, 0)
     do, ffn_1, ffn_3 = lax.optimization_barrier((do, ffn_1, ffn_3))
@@ -683,18 +745,19 @@
     (message,) = call(
         spread_ffn_kernel, "spread_ffn", 2, 3, [SDS((ranks // 2, 2, slots, rows, 256), bf16)]
     )(block_slot, scal, ffn_g[0], ffn_1, ffn_2)
-    messages = list(call(
-        spread_attn_kernel, "spread_attn", 2, 4, [SDS(message.shape[1:], bf16)] * (ranks // 2),
-        [pltpu.VMEM(message.shape, bf16)], parts=3,
-    )(block_slot, scal, message, attn_g[0], attn_1, attn_2))
-    both, messages[1] = lax.optimization_barrier((both, messages[1]))
+    both, message = lax.optimization_barrier((both, message))
     both_2, both_1 = permute(both, "head", 2), permute(both, "head", 1)
     both_3 = permute(both_2, "head", 1)
-    messages = [messages[0]] + [permute(messages[k], "dp", 2 * k) for k in range(1, ranks // 2)]
     own, other = call(
-        pair_sum_kernel, "pair_sum", 0, ranks // 2, [SDS((slots, rows, 256), f32), SDS((slots, rows, 256), bf16)]
-    )(*messages)
-    other = permute(other, "dp", 1)
+        spread_attn_kernel, "spread_attn", 2, 4, [SDS((pairs,) + message.shape[2:], bf16)] * 2,
+        [pltpu.VMEM(message.shape, bf16)], parts=3,
+    )(block_slot, scal, message, attn_g[0], attn_1, attn_2)
+    slot_shape = (slots, rows, 256)
+    got = list(call(
+        place_sum_kernel, "place_sum", 0, 2, [SDS(slot_shape, f32)] + [SDS(slot_shape, bf16)] * (pairs - 1)
+    )(own, permute(other, "dp", 1)))
+    far = {k: permute(got[k], "dp", 2 * k) for k in (*range(2, pairs), 1)}
+    got[1:] = [far[k] for k in range(1, pairs)]
     shape = SDS((tokens.shape[1], parts, dim), f32)
     output, token_grad = pl.pallas_call(
         assemble_kernel,
@@ -707,7 +770,7 @@
         cost_estimate=pl.CostEstimate(flops=1000000000, transcendentals=0, bytes_accessed=3000000),
         name="assemble",
     )(scal, both, both_1, both_2, both_3)
-    other, output, token_grad = lax.optimization_barrier((other, output, token_grad))
+    got[-1], output, token_grad = lax.optimization_barrier((got[-1], output, token_grad))
     state = [
         swap(master), swap(master_m1), swap(master_m2), norm_params, norm_m1, norm_m2,
         swap(talk), swap(talk_m1), swap(talk_m2), conv, conv_m1, conv_m2,
@@ -715,7 +778,7 @@
     shapes = [SDS(t.shape, f32) for t in state]
     shapes.insert(3, SDS(state[0].shape, bf16))
     new = staged(
-        update_kernel, "update", [own, other, *state], shapes,
+        update_kernel, "update", [*got, *state], shapes,
         [pltpu.VMEM((rows, slots, dim), f32), pltpu.VMEM((slots, 64, 256), f32), pltpu.VMEM((64, 256), f32)],
     )
     new = [swap(t) if t.ndim == 3 else t for t in new]

time: 69.2 us -> 64.7 us (0.935)
  waiting for transfers between devices: 25 us -> 19.5 us
  starting transfers between devices: 20.2 us -> 21.1 us
    ppermute x23, waiting for transfers between devices: 25 us -> 19.5 us  [permute(): lax.ppermute(x, axis, [(i, i ^ k) for i in range(lax.axis_size(axis))])]
    pallas_call x6 -> x7, Pallas kernels: 6.47 us -> 7.43 us  [the longest x1 2.77 us: ffn_first(): call(ffn_first_kernel, 'ffn_first', 1, 3 + count, [SDS((pad, dim), f32),...]
    ppermute x23, starting transfers between devices: 20.2 us -> 21.1 us  [permute(): lax.ppermute(x, axis, [(i, i ^ k) for i in range(lax.axis_size(axis))])]
  transfers between devices with their start and end apart: 23 -> 23, of which waited for: 12 -> 11; matrix products, arithmetic and copies ran while one was open for 0% -> 0% of each run, Pallas kernels for 19% -> 24%
where the time goes in v7:
time: 64.7 us; the launch traced here: 64.5 us
  starting transfers between devices  21.1 us (33%)
  Pallas kernels  19.7 us (30%)
  waiting for transfers between devices  19.5 us (30%)
  between operations  2.94 us (5%)
  local copies, waits for them, and re-layouts  1.27 us (2%)
    ppermute x23, starting transfers between devices, permute(): lax.ppermute(x, axis, [(i, i ^ k) for i in range(lax.axis_size(axis))])  21.1 us
    ppermute x23, waiting for transfers between devices, permute(): lax.ppermute(x, axis, [(i, i ^ k) for i in range(lax.axis_size(axis))])  19.5 us
    pallas_call x2, Pallas kernels, scores_back(): call(scores_back_kernel, 'scores_back', 1, 8 + len(more), outs, scratch,...  4.39 us
    pallas_call x1, Pallas kernels, ffn_first(): call(ffn_first_kernel, 'ffn_first', 1, 3 + count, [SDS((pad, dim), f32),...  2.77 us
    pallas_call x1, Pallas kernels, attn_fwd(): call(attn_fwd_kernel, 'attn_fwd', 1, 4 + len(w), [SDS((pad, dim), f32)] +...  2.67 us
    pallas_call x1, Pallas kernels, ffn_last(): call(ffn_last_kernel, 'ffn_last', 1, 14, [SDS((SIDE * SIDE, dim), bf16),...  2.19 us
    pallas_call x1, Pallas kernels, local(): pl.pallas_call(assemble_kernel, grid=(1,), in_specs=[SM] + [whole(*both.s...  2 us
  transfers between devices with their start and end apart: 23, of which 11 were waited for; matrix products, arithmetic and copies ran while one was open for 0% of the time, Pallas kernels for 24%

profile of v7, /device:TPU:0, one launch (start us, length us, event | category | flops | bytes accessed | tf_op | source)
XLA Modules:
  0.0 64.5 jit_solution(14998125577299033096)
XLA Ops:
  0.6 0.0 copy-start
  0.7 0.9 %copy-done = f32[2,54,216]{2,0,1:T(2,128)S(1)} copy-done((f32[2,54,216]{2,0,1:T(2,128)S(1)}, f32[2,54,216]{2,0,1:T(2,128)}, u32[]{:S(2)}) %copy-start) | copy-done | bytes 93336
  1.5 0.2 cast.1.refs_0_
  1.8 0.0 copy-start.2
  1.8 5.1 %collective-permute-start.2 = (bf16[2,54,216]{2,1,0:T(8,128)(2,1)S(1)}, bf16[2,54,216]{2,1,0:T(8,128)(2,1)S(1)}, u32[]{:S(2)}, u32[]{:S(2)}) collective-permute-start(bf16[2,54,216]{2,1,0:T(8,128)(2,1)S(1)} %cast.1.refs_0_), channel_id=1, source_target_pairs={{0,24},{4,28},{8,16},{12,20},{16,8},{20,12},{24,0},{28,4},{1,25},{... | collective-permute-start | bytes 139976 | tf_op jit(solution)/shard_map/ppermute | solution.py:665
  6.9 0.6 collective-permute-start
  7.6 1.8 %collective-permute-done.2.refs_3_ = bf16[2,54,216]{2,1,0:T(8,128)(2,1)S(1)} collective-permute-done((bf16[2,54,216]{2,1,0:T(8,128)(2,1)S(1)}, bf16[2,54,216]{2,1,0:T(8,128)(2,1)S(1)}, u32[]{:S(2)}, u32[]{:S(2)}) %collective-permute-start.2) | collective-permute-done | bytes 46688 | tf_op jit(solution)/shard_map/ppermute | solution.py:665
  9.3 2.7 %collective-permute-done.1.refs_2_ = bf16[2,54,216]{2,1,0:T(8,128)(2,1)S(1)} collective-permute-done((bf16[2,54,216]{2,1,0:T(8,128)(2,1)S(1)}, bf16[2,54,216]{2,1,0:T(8,128)(2,1)S(1)}, u32[]{:S(2)}, u32[]{:S(2)}) %collective-permute-start.1) | collective-permute-done | bytes 46688 | tf_op jit(solution)/shard_map/ppermute | solution.py:665
  12.1 1.6 %collective-permute-start.3 = (bf16[4,2,54,216]{3,2,1,0:T(8,128)(2,1)S(1)}, bf16[4,2,54,216]{3,2,1,0:T(8,128)(2,1)S(1)}, u32[]{:S(2)}, u32[]{:S(2)}) collective-permute-start(bf16[4,2,54,216]{3,2,1,0:T(8,128)(2,1)S(1)} %stack.1.own_ref), channel_id=1, source_target_pairs={{0,4},{4,0},{8,12},{12,8},{16,20},{20,16},{24,28},{28,24},{1,5},{5... | collective-permute-start | bytes 559880 | tf_op jit(solution)/shard_map/ppermute | solution.py:665
  15.6 0.1 concatenate.3.scal
  15.7 0.2 copy.34.cot_ref
  15.9 1.1 %prep.1 = (f32[224,216]{1,0:T(8,128)S(1)}, bf16[224,216]{1,0:T(8,128)(2,1)S(1)}, f32[224,216]{1,0:T(8,128)S(1)}, f32[2,192,256]{2,1,0:T(8,128)S(1)}, f32[224,128]{1,0:T(8,128)S(1)}) custom-call(s32[6]{0:T(128)S(1)} %concatenate.3.scal, bf16[4,196,216]{2,1,0:T(8,128)(2,1)S(1)} %copy.33.tok_ref, f32[4,196,216]{2,1,0:T(8,128)S(1)} %copy.34.cot_ref, ...), custom_call_target="tpu_custom_call" | custom-call | flops 1000000000 | bytes 3000000 | tf_op jit(solution)/shard_map/prep/pallas_call | solution.py:565
  17.0 1.7 %collective-permute-done.3.other_ref = bf16[4,2,54,216]{3,2,1,0:T(8,128)(2,1)S(1)} collective-permute-done((bf16[4,2,54,216]{3,2,1,0:T(8,128)(2,1)S(1)}, bf16[4,2,54,216]{3,2,1,0:T(8,128)(2,1)S(1)}, u32[]{:S(2)}, u32[]{:S(2)}) %collective-permute-start.3) | collective-permute-done | bytes 186656 | tf_op jit(solution)/shard_map/ppermute | solution.py:665
  18.8 0.6 select.7
  19.4 1.7 %collective-permute-start.5 = (bf16[4,54,216]{2,1,0:T(8,128)(2,1)S(1)}, bf16[4,54,216]{2,1,0:T(8,128)(2,1)S(1)}, u32[]{:S(2)}, u32[]{:S(2)}) collective-permute-start(bf16[4,54,216]{2,1,0:T(8,128)(2,1)S(1)} %get-tuple-element.110.refs_0_), channel_id=1, source_target_pairs={{0,2},{1,3},{2,0},{3,1},{4,6},{5,7},{6,4},{7,5},{8,10},{9,11},{10,... | collective-permute-start | bytes 279944 | tf_op jit(solution)/shard_map/ppermute | solution.py:665
  21.1 0.4 collective-permute-start.7
  21.5 0.5 collective-permute-start.4
  22.0 3.5 %collective-permute-done.5.refs_2_ = bf16[4,54,216]{2,1,0:T(8,128)(2,1)S(1)} collective-permute-done((bf16[4,54,216]{2,1,0:T(8,128)(2,1)S(1)}, bf16[4,54,216]{2,1,0:T(8,128)(2,1)S(1)}, u32[]{:S(2)}, u32[]{:S(2)}) %collective-permute-start.5) | collective-permute-done | bytes 93344 | tf_op jit(solution)/shard_map/ppermute | solution.py:665
  25.5 1.3 %collective-permute-done.6.refs_3_ = bf16[4,54,216]{2,1,0:T(8,128)(2,1)S(1)} collective-permute-done((bf16[4,54,216]{2,1,0:T(8,128)(2,1)S(1)}, bf16[4,54,216]{2,1,0:T(8,128)(2,1)S(1)}, u32[]{:S(2)}, u32[]{:S(2)}) %collective-permute-start.6) | collective-permute-done | bytes 93344 | tf_op jit(solution)/shard_map/ppermute | solution.py:665
  26.8 2.7 %attn_fwd.1 = (f32[224,216]{1,0:T(8,128)S(1)}, bf16[224,256]{1,0:T(8,128)(2,1)S(1)}, bf16[224,256]{1,0:T(8,128)(2,1)S(1)}, bf16[224,256]{1,0:T(8,128)(2,1)S(1)},...) custom-call(s32[6]{0:T(128)S(1)} %concatenate.3.scal, ...), custom_call_target="tpu_custom_call" | custom-call | flops 1000000000 | bytes 3000000 | tf_op jit(solution)/shard_map/attn_fwd/pallas_call | solution.py:591
  29.5 0.2 collective-permute-start.9
  29.8 2.8 %ffn_first.1 = (f32[224,216]{1,0:T(8,128)S(1)}, f32[224,128]{1,0:T(8,128)S(1)}, bf16[224,216]{1,0:T(8,128)(2,1)S(1)}, bf16[224,216]{1,0:T(8,128)(2,1)S(1)}, bf16...) custom-call(s32[6]{0:T(128)S(1)} %concatenate.3.scal, ...), custom_call_target="tpu_custom_call" | custom-call | flops 3000000000 | bytes 9000000 | tf_op jit(solution)/shard_map/ffn_first/pallas_call | solution.py:605
  32.5 2.2 %ffn_last.1 = (bf16[196,216]{1,0:T(8,128)(2,1)S(1)}, f32[224,216]{1,0:T(8,128)S(1)}, f32[8,216]{1,0:T(8,128)S(1)}, bf16[9,54,256]{2,1,0:T(8,128)(2,1)S(1)}, bf16...) custom-call(s32[6]{0:T(128)S(1)} %concatenate.3.scal, ...), custom_call_target="tpu_custom_call" | custom-call | flops 4000000000 | bytes 12000000 | tf_op jit(solution)/shard_map/ffn_last/pallas_call | solution.py:618
  34.7 0.4 collective-permute-start.10
  35.2 0.2 collective-permute-start.11
  35.3 1.6 %scores_back.2 = (bf16[224,256]{1,0:T(8,128)(2,1)S(1)}, bf16[64,256]{1,0:T(8,128)(2,1)S(1)}, f32[224,256]{1,0:T(8,128)S(1)}, f32[224,256]{1,0:T(8,128)S(1)}, f32...) custom-call(s32[6]{0:T(128)S(1)} %concatenate.3.scal, f32[224,216]{1,0:T(8,128)S(1)} %get-tuple-element.128.dmid_ref, ...), custom_call_target="tpu_custom_call" | custom-call | flops 4000000000 | bytes 12000000 | tf_op jit(solution)/shard_map/scores_back/pallas_call | solution.py:647
  36.9 0.1 half_sum.2
  37.0 1.7 %collective-permute-start.12 = (bf16[9,54,256]{2,1,0:T(8,128)(2,1)S(1)}, bf16[9,54,256]{2,1,0:T(8,128)(2,1)S(1)}, u32[]{:S(2)}, u32[]{:S(2)}) collective-permute-start(bf16[9,54,256]{2,1,0:T(8,128)(2,1)S(1)} %half_sum.2), channel_id=1, source_target_pairs={{0,2},{1,3},{2,0},{3,1},{4,6},{5,7},{6,4},{7,5},{8,10},{9,11},{10,... | collective-permute-start | bytes 746504 | tf_op jit(solution)/shard_map/ppermute | solution.py:665
  38.7 2.8 %scores_back.3 = (bf16[160,256]{1,0:T(8,128)(2,1)S(1)}, bf16[224,256]{1,0:T(8,128)(2,1)S(1)}, bf16[224,256]{1,0:T(8,128)(2,1)S(1)}, f32[2,12,12]{2,1,0:T(8,128)S(1)}) custom-call(s32[6]{0:T(128)S(1)} %concatenate.3.scal, f32[224,216]{1,0:T(8,128)S(1)} %get-tuple-element.128.dmid_ref, f32[2,192,256]{2,1,0:T(8,128)S(1)} %get-tuple-element.107.mix_ref, ...), custom_call_target="tpu_custom_call" | custom-call | flops 4000000000 | bytes 12000000 | tf_op jit(solution)/shard_map/scores_back/pallas_call | solution.py:647
  41.5 1.1 %weights_back.1 = (bf16[2,196,216]{2,1,0:T(8,128)(2,1)S(1)}, bf16[3,54,256]{2,1,0:T(8,128)(2,1)S(1)}, bf16[3,54,256]{2,1,0:T(8,128)(2,1)S(1)}, bf16[3,54,256]{2,1,0:T(8,128)(2,1)S(1)}, bf16[3,54,256]{2,1,0:T(8,128)(2,1)S(1)}) custom-call(s32[6]{0:T(128)S(1)} %concatenate.3.scal, f32[224,216]{1,0:T(8,128)S(1)} %get-tuple-element.105.x_ref, ...), custom_call_target="tpu_custom_call" | custom-call | flops 3000000000 | bytes 9000000 | tf_op jit(solution)/shard_map/weights_back/pallas_call | solution.py:655
  42.7 0.1 collective-permute-start.14
  42.8 0.4 collective-permute-start.13
  43.2 0.8 %collective-permute-done.14.b_ref = bf16[3,54,256]{2,1,0:T(8,128)(2,1)S(1)} collective-permute-done((bf16[3,54,256]{2,1,0:T(8,128)(2,1)S(1)}, bf16[3,54,256]{2,1,0:T(8,128)(2,1)S(1)}, u32[]{:S(2)}, u32[]{:S(2)}) %collective-permute-start.14) | collective-permute-done | bytes 82976 | tf_op jit(solution)/shard_map/ppermute | solution.py:665
  44.0 0.5 collective-permute-start.15
  44.5 1.0 %collective-permute-done.12.refs_2_ = bf16[9,54,256]{2,1,0:T(8,128)(2,1)S(1)} collective-permute-done((bf16[9,54,256]{2,1,0:T(8,128)(2,1)S(1)}, bf16[9,54,256]{2,1,0:T(8,128)(2,1)S(1)}, u32[]{:S(2)}, u32[]{:S(2)}) %collective-permute-start.12) | collective-permute-done | bytes 248864 | tf_op jit(solution)/shard_map/ppermute | solution.py:665
  45.5 0.7 %spread_ffn.1.old_ref = bf16[4,2,2,54,256]{4,3,2,1,0:T(8,128)(2,1)S(1)} custom-call(s32[12]{0:T(128)S(1)} %copy-done.13, s32[6]{0:T(128)S(1)} %concatenate.3.scal, bf16[9,54,256]{2,1,0:T(8,128)(2,1)S(1)} %get-tuple-element.151.refs_0_, bf16[9,54,256]{2,1,0:T(8,128)(2,1)S(1)} %collective-permute-done.10.refs_1_, ...), custom_call_target="tpu_custom_call" | custom-call | flops 1000000000 | bytes 3000000 | tf_op jit(solution)/shard_map/spread_ffn/pallas_call | solution.py:745
  46.2 1.7 %collective-permute-start.19 = (bf16[2,196,216]{2,1,0:T(8,128)(2,1)S(1)}, bf16[2,196,216]{2,1,0:T(8,128)(2,1)S(1)}, u32[]{:S(2)}, u32[]{:S(2)}) collective-permute-start(bf16[2,196,216]{2,1,0:T(8,128)(2,1)S(1)} %get-tuple-element.163.refs_0_), channel_id=1, source_target_pairs={{0,2},{1,3},{2,0},{3,1},{4,6},{5,7},{6,4},{7,5},{8,10},{9,11},{10,... | collective-permute-start | bytes 508040 | tf_op jit(solution)/shard_map/ppermute | solution.py:665
  47.9 1.1 %collective-permute-done.15.refs_2_ = bf16[3,54,256]{2,1,0:T(8,128)(2,1)S(1)} collective-permute-done((bf16[3,54,256]{2,1,0:T(8,128)(2,1)S(1)}, bf16[3,54,256]{2,1,0:T(8,128)(2,1)S(1)}, u32[]{:S(2)}, u32[]{:S(2)}) %collective-permute-start.15) | collective-permute-done | bytes 82976 | tf_op jit(solution)/shard_map/ppermute | solution.py:665
  49.0 0.7 %spread_attn.1 = (bf16[4,2,54,256]{3,2,1,0:T(8,128)(2,1)S(1)}, bf16[4,2,54,256]{3,2,1,0:T(8,128)(2,1)S(1)}) custom-call(s32[12]{0:T(128)S(1)} %copy-done.13, s32[6]{0:T(128)S(1)} %concatenate.3.scal, bf16[4,2,2,54,256]{4,3,2,1,0:T(8,128)(2,1)S(1)} %spread_ffn.1.old_ref, bf16[3,54,256]{2,1,0:T(8,128)(2,1)S(1)} %get-tuple-element.156.refs_0_, ...), custom_call_target="tpu_custom_call" | custom-call | flops 1000000000 | bytes 3000000 | tf_op jit(solution)/shard_map/spread_attn/pallas_call | solution.py:751
  49.7 1.4 %collective-permute-start.16 = (bf16[4,2,54,256]{3,2,1,0:T(8,128)(2,1)S(1)}, bf16[4,2,54,256]{3,2,1,0:T(8,128)(2,1)S(1)}, u32[]{:S(2)}, u32[]{:S(2)}) collective-permute-start(bf16[4,2,54,256]{3,2,1,0:T(8,128)(2,1)S(1)} %get-tuple-element.161), channel_id=1, source_target_pairs={{0,4},{4,0},{8,12},{12,8},{16,20},{20,16},{24,28},{28,24},{1,5},{5... | collective-permute-start | bytes 663560 | tf_op jit(solution)/shard_map/ppermute | solution.py:665
  51.1 2.0 %collective-permute-done.19.refs_2_ = bf16[2,196,216]{2,1,0:T(8,128)(2,1)S(1)} collective-permute-done((bf16[2,196,216]{2,1,0:T(8,128)(2,1)S(1)}, bf16[2,196,216]{2,1,0:T(8,128)(2,1)S(1)}, u32[]{:S(2)}, u32[]{:S(2)}) %collective-permute-start.19) | collective-permute-done | bytes 169376 | tf_op jit(solution)/shard_map/ppermute | solution.py:665
  53.1 3.2 %collective-permute-done.16.other_ref = bf16[4,2,54,256]{3,2,1,0:T(8,128)(2,1)S(1)} collective-permute-done((bf16[4,2,54,256]{3,2,1,0:T(8,128)(2,1)S(1)}, bf16[4,2,54,256]{3,2,1,0:T(8,128)(2,1)S(1)}, u32[]{:S(2)}, u32[]{:S(2)}) %collective-permute-start.16) | collective-permute-done | bytes 221216 | tf_op jit(solution)/shard_map/ppermute | solution.py:665
  56.2 0.1 place_sum.1
  56.3 1.6 %collective-permute-start.17 = (bf16[2,54,256]{2,1,0:T(8,128)(2,1)S(1)}, bf16[2,54,256]{2,1,0:T(8,128)(2,1)S(1)}, u32[]{:S(2)}, u32[]{:S(2)}) collective-permute-start(bf16[2,54,256]{2,1,0:T(8,128)(2,1)S(1)} %get-tuple-element.162), channel_id=1, source_target_pairs={{0,24},{4,28},{8,16},{12,20},{16,8},{20,12},{24,0},{28,4},{1,25},{... | collective-permute-start | bytes 165896 | tf_op jit(solution)/shard_map/ppermute | solution.py:665
  58.0 2.9 %collective-permute-start.22 = (bf16[2,54,256]{2,1,0:T(8,128)(2,1)S(1)}, bf16[2,54,256]{2,1,0:T(8,128)(2,1)S(1)}, u32[]{:S(2)}, u32[]{:S(2)}) collective-permute-start(bf16[2,54,256]{2,1,0:T(8,128)(2,1)S(1)} %get-tuple-element.170), channel_id=1, source_target_pairs={{0,16},{4,20},{8,24},{12,28},{16,0},{20,4},{24,8},{28,12},{1,17},{... | collective-permute-start | bytes 165896 | tf_op jit(solution)/shard_map/ppermute | solution.py:665
  60.9 2.0 %assemble.1 = (f32[196,4,216]{2,1,0:T(4,128)}, f32[196,4,216]{2,1,0:T(4,128)}) custom-call(s32[6]{0:T(128)S(1)} %concatenate.3.scal, bf16[2,196,216]{2,1,0:T(8,128)(2,1)S(1)} %get-tuple-element.163.refs_0_, bf16[2,196,216]{2,1,0:T(8,128)(2,1)S(1)} %collective-permute-done.18.refs_1_, bf16[2,196,216]{2,1,0:T(8,128)(2,1)S(1)} %collective-permute-done.19.refs_2_, ...), custom_call_target="tpu_custom_call" | custom-call | flops 1000000000 | bytes 3000000 | tf_op jit(solution)/shard_map/assemble/pallas_call | solution.py:762
  62.9 0.4 collective-permute-done.21.refs_1_
  63.4 1.1 %update.1 = (f32[54,2,216]{2,1,0:T(2,128)}, f32[54,2,216]{2,1,0:T(2,128)}, f32[54,2,216]{2,1,0:T(2,128)}, bf16[54,2,216]{2,1,0:T(2,128)(2,1)}, f32[4,216]{1,0:T(...) custom-call(f32[2,54,256]{2,1,0:T(8,128)S(1)} %get-tuple-element.168, ...), custom_call_target="tpu_custom_call" | custom-call | flops 1000000000 | bytes 3000000 | tf_op jit(solution)/shard_map/update/pallas_call | solution.py:677
  (51 shorter events, 0.2 us)
Async XLA Ops:
  0.6 0.9 %copy-start = (f32[2,54,216]{2,0,1:T(2,128)S(1)}, f32[2,54,216]{2,0,1:T(2,128)}, u32[]{:S(2)}) copy-start(f32[2,54,216]{2,0,1:T(2,128)} %param.24) | copy-start | bytes 279940
  1.8 13.9 %copy-start.2 = (f32[2,12,12]{2,0,1:T(2,128)S(1)}, f32[2,12,12]{2,0,1:T(2,128)}, u32[]{:S(2)}) copy-start(f32[2,12,12]{2,0,1:T(2,128)} %param.30) | copy-start | bytes 3460
  1.8 13.9 %copy-start.15 = (bf16[4,196,216]{2,0,1:T(4,128)(2,1)S(1)}, bf16[4,196,216]{2,0,1:T(4,128)(2,1)}, u32[]{:S(2)}) copy-start(bf16[4,196,216]{2,0,1:T(4,128)(2,1)} %param.18) | copy-start | bytes 1016068
  1.8 7.5 %collective-permute-start.2 = (bf16[2,54,216]{2,1,0:T(8,128)(2,1)S(1)}, bf16[2,54,216]{2,1,0:T(8,128)(2,1)S(1)}, u32[]{:S(2)}, u32[]{:S(2)}) collective-permute-start(bf16[2,54,216]{2,1,0:T(8,128)(2,1)S(1)} %cast.1.refs_0_), channel_id=1, source_target_pairs={{0,24},{4,28},{8,16},{12,20},{16,8},{20,12},{24,0},{28,4},{1,25},{... | collective-permute-start | bytes 139976 | tf_op jit(solution)/shard_map/ppermute | solution.py:665
  6.9 5.1 %collective-permute-start.1 = (bf16[2,54,216]{2,1,0:T(8,128)(2,1)S(1)}, bf16[2,54,216]{2,1,0:T(8,128)(2,1)S(1)}, u32[]{:S(2)}, u32[]{:S(2)}) collective-permute-start(bf16[2,54,216]{2,1,0:T(8,128)(2,1)S(1)} %cast.1.refs_0_), channel_id=1, source_target_pairs={{0,16},{4,20},{8,24},{12,28},{16,0},{20,4},{24,8},{28,12},{1,17},{... | collective-permute-start | bytes 139976 | tf_op jit(solution)/shard_map/ppermute | solution.py:665
  6.9 5.1 %collective-permute-start = (bf16[2,54,216]{2,1,0:T(8,128)(2,1)S(1)}, bf16[2,54,216]{2,1,0:T(8,128)(2,1)S(1)}, u32[]{:S(2)}, u32[]{:S(2)}) collective-permute-start(bf16[2,54,216]{2,1,0:T(8,128)(2,1)S(1)} %cast.1.refs_0_), channel_id=1, source_target_pairs={{0,8},{4,12},{8,0},{12,4},{16,24},{20,28},{24,16},{28,20},{1,9},{5... | collective-permute-start | bytes 139976 | tf_op jit(solution)/shard_map/ppermute | solution.py:665
  12.0 3.7 %copy-start.14 = (f32[4,196,216]{2,0,1:T(4,128)S(1)}, f32[4,196,216]{2,0,1:T(4,128)}, u32[]{:S(2)}) copy-start(f32[4,196,216]{2,0,1:T(4,128)} %param.19) | copy-start | bytes 2032132
  12.0 3.9 %copy-start.10 = (f32[4,216]{1,0:T(4,128)S(1)}, f32[4,216]{1,0:T(4,128)}, u32[]{:S(2)}) copy-start(f32[4,216]{1,0:T(4,128)} %refs_7_.1) | copy-start | bytes 10372
  12.1 6.7 %collective-permute-start.3 = (bf16[4,2,54,216]{3,2,1,0:T(8,128)(2,1)S(1)}, bf16[4,2,54,216]{3,2,1,0:T(8,128)(2,1)S(1)}, u32[]{:S(2)}, u32[]{:S(2)}) collective-permute-start(bf16[4,2,54,216]{3,2,1,0:T(8,128)(2,1)S(1)} %stack.1.own_ref), channel_id=1, source_target_pairs={{0,4},{4,0},{8,12},{12,8},{16,20},{20,16},{24,28},{28,24},{1,5},{5... | collective-permute-start | bytes 559880 | tf_op jit(solution)/shard_map/ppermute | solution.py:665
  15.9 2.8 %copy-start.5 = (f32[9,216]{1,0:T(8,128)S(1)}, f32[9,216]{1,0:T(8,128)}, u32[]{:S(2)}) copy-start(f32[9,216]{1,0:T(8,128)} %refs_13_.1) | copy-start | bytes 23332
  15.9 2.8 %copy-start.13 = (s32[12]{0:T(128)S(1)}, s32[12]{0:T(128)}, u32[]{:S(2)}) copy-start(s32[12]{0:T(128)} %slot_ref.5) | copy-start | bytes 148
  19.4 6.1 %collective-permute-start.5 = (bf16[4,54,216]{2,1,0:T(8,128)(2,1)S(1)}, bf16[4,54,216]{2,1,0:T(8,128)(2,1)S(1)}, u32[]{:S(2)}, u32[]{:S(2)}) collective-permute-start(bf16[4,54,216]{2,1,0:T(8,128)(2,1)S(1)} %get-tuple-element.110.refs_0_), channel_id=1, source_target_pairs={{0,2},{1,3},{2,0},{3,1},{4,6},{5,7},{6,4},{7,5},{8,10},{9,11},{10,... | collective-permute-start | bytes 279944 | tf_op jit(solution)/shard_map/ppermute | solution.py:665
  21.1 8.5 %collective-permute-start.7 = (bf16[9,54,216]{2,1,0:T(8,128)(2,1)S(1)}, bf16[9,54,216]{2,1,0:T(8,128)(2,1)S(1)}, u32[]{:S(2)}, u32[]{:S(2)}) collective-permute-start(bf16[9,54,216]{2,1,0:T(8,128)(2,1)S(1)} %get-tuple-element.112.refs_0_), channel_id=1, source_target_pairs={{0,2},{1,3},{2,0},{3,1},{4,6},{5,7},{6,4},{7,5},{8,10},{9,11},{10,... | collective-permute-start | bytes 629864 | tf_op jit(solution)/shard_map/ppermute | solution.py:665
  21.5 8.3 %collective-permute-start.8 = (bf16[9,54,216]{2,1,0:T(8,128)(2,1)S(1)}, bf16[9,54,216]{2,1,0:T(8,128)(2,1)S(1)}, u32[]{:S(2)}, u32[]{:S(2)}) collective-permute-start(bf16[9,54,216]{2,1,0:T(8,128)(2,1)S(1)} %get-tuple-element.112.refs_0_), channel_id=1, source_target_pairs={{0,1},{1,0},{2,3},{3,2},{4,5},{5,4},{6,7},{7,6},{8,9},{9,8},{10,11... | collective-permute-start | bytes 629864 | tf_op jit(solution)/shard_map/ppermute | solution.py:665
  21.5 4.0 %collective-permute-start.4 = (bf16[4,54,216]{2,1,0:T(8,128)(2,1)S(1)}, bf16[4,54,216]{2,1,0:T(8,128)(2,1)S(1)}, u32[]{:S(2)}, u32[]{:S(2)}) collective-permute-start(bf16[4,54,216]{2,1,0:T(8,128)(2,1)S(1)} %get-tuple-element.110.refs_0_), channel_id=1, source_target_pairs={{0,1},{1,0},{2,3},{3,2},{4,5},{5,4},{6,7},{7,6},{8,9},{9,8},{10,11... | collective-permute-start | bytes 279944 | tf_op jit(solution)/shard_map/ppermute | solution.py:665
  25.5 1.3 %collective-permute-start.6 = (bf16[4,54,216]{2,1,0:T(8,128)(2,1)S(1)}, bf16[4,54,216]{2,1,0:T(8,128)(2,1)S(1)}, u32[]{:S(2)}, u32[]{:S(2)}) collective-permute-start(bf16[4,54,216]{2,1,0:T(8,128)(2,1)S(1)} %collective-permute-done.5.refs_2_), channel_id=1, source_target_pairs={{0,1},{1,0},{2,3},{3,2},{4,5},{5,4},{6,7},{7,6},{8,9},{9,8},{10,11... | collective-permute-start | bytes 279944 | tf_op jit(solution)/shard_map/ppermute | solution.py:665
  29.5 3.0 %collective-permute-start.9 = (bf16[9,54,216]{2,1,0:T(8,128)(2,1)S(1)}, bf16[9,54,216]{2,1,0:T(8,128)(2,1)S(1)}, u32[]{:S(2)}, u32[]{:S(2)}) collective-permute-start(bf16[9,54,216]{2,1,0:T(8,128)(2,1)S(1)} %collective-permute-done.7.refs_2_), channel_id=1, source_target_pairs={{0,1},{1,0},{2,3},{3,2},{4,5},{5,4},{6,7},{7,6},{8,9},{9,8},{10,11... | collective-permute-start | bytes 629864 | tf_op jit(solution)/shard_map/ppermute | solution.py:665
  34.7 2.2 %collective-permute-start.10 = (bf16[9,54,256]{2,1,0:T(8,128)(2,1)S(1)}, bf16[9,54,256]{2,1,0:T(8,128)(2,1)S(1)}, u32[]{:S(2)}, u32[]{:S(2)}) collective-permute-start(bf16[9,54,256]{2,1,0:T(8,128)(2,1)S(1)} %get-tuple-element.138), channel_id=1, source_target_pairs={{0,1},{1,0},{2,3},{3,2},{4,5},{5,4},{6,7},{7,6},{8,9},{9,8},{10,11... | collective-permute-start | bytes 746504 | tf_op jit(solution)/shard_map/ppermute | solution.py:665
  35.2 1.7 %collective-permute-start.11 = (bf16[9,54,256]{2,1,0:T(8,128)(2,1)S(1)}, bf16[9,54,256]{2,1,0:T(8,128)(2,1)S(1)}, u32[]{:S(2)}, u32[]{:S(2)}) collective-permute-start(bf16[9,54,256]{2,1,0:T(8,128)(2,1)S(1)} %get-tuple-element.139), channel_id=1, source_target_pairs={{0,1},{1,0},{2,3},{3,2},{4,5},{5,4},{6,7},{7,6},{8,9},{9,8},{10,11... | collective-permute-start | bytes 746504 | tf_op jit(solution)/shard_map/ppermute | solution.py:665
  37.0 8.5 %collective-permute-start.12 = (bf16[9,54,256]{2,1,0:T(8,128)(2,1)S(1)}, bf16[9,54,256]{2,1,0:T(8,128)(2,1)S(1)}, u32[]{:S(2)}, u32[]{:S(2)}) collective-permute-start(bf16[9,54,256]{2,1,0:T(8,128)(2,1)S(1)} %half_sum.2), channel_id=1, source_target_pairs={{0,2},{1,3},{2,0},{3,1},{4,6},{5,7},{6,4},{7,5},{8,10},{9,11},{10,... | collective-permute-start | bytes 746504 | tf_op jit(solution)/shard_map/ppermute | solution.py:665
  42.7 1.3 %collective-permute-start.14 = (bf16[3,54,256]{2,1,0:T(8,128)(2,1)S(1)}, bf16[3,54,256]{2,1,0:T(8,128)(2,1)S(1)}, u32[]{:S(2)}, u32[]{:S(2)}) collective-permute-start(bf16[3,54,256]{2,1,0:T(8,128)(2,1)S(1)} %get-tuple-element.159), channel_id=1, source_target_pairs={{0,1},{1,0},{2,3},{3,2},{4,5},{5,4},{6,7},{7,6},{8,9},{9,8},{10,11... | collective-permute-start | bytes 248840 | tf_op jit(solution)/shard_map/ppermute | solution.py:665
  42.8 5.1 %collective-permute-start.13 = (bf16[3,54,256]{2,1,0:T(8,128)(2,1)S(1)}, bf16[3,54,256]{2,1,0:T(8,128)(2,1)S(1)}, u32[]{:S(2)}, u32[]{:S(2)}) collective-permute-start(bf16[3,54,256]{2,1,0:T(8,128)(2,1)S(1)} %get-tuple-element.157), channel_id=1, source_target_pairs={{0,1},{1,0},{2,3},{3,2},{4,5},{5,4},{6,7},{7,6},{8,9},{9,8},{10,11... | collective-permute-start | bytes 248840 | tf_op jit(solution)/shard_map/ppermute | solution.py:665
  44.0 5.0 %collective-permute-start.15 = (bf16[3,54,256]{2,1,0:T(8,128)(2,1)S(1)}, bf16[3,54,256]{2,1,0:T(8,128)(2,1)S(1)}, u32[]{:S(2)}, u32[]{:S(2)}) collective-permute-start(bf16[3,54,256]{2,1,0:T(8,128)(2,1)S(1)} %half_sum.3), channel_id=1, source_target_pairs={{0,2},{1,3},{2,0},{3,1},{4,6},{5,7},{6,4},{7,5},{8,10},{9,11},{10,... | collective-permute-start | bytes 248840 | tf_op jit(solution)/shard_map/ppermute | solution.py:665
  46.2 6.9 %collective-permute-start.19 = (bf16[2,196,216]{2,1,0:T(8,128)(2,1)S(1)}, bf16[2,196,216]{2,1,0:T(8,128)(2,1)S(1)}, u32[]{:S(2)}, u32[]{:S(2)}) collective-permute-start(bf16[2,196,216]{2,1,0:T(8,128)(2,1)S(1)} %get-tuple-element.163.refs_0_), channel_id=1, source_target_pairs={{0,2},{1,3},{2,0},{3,1},{4,6},{5,7},{6,4},{7,5},{8,10},{9,11},{10,... | collective-permute-start | bytes 508040 | tf_op jit(solution)/shard_map/ppermute | solution.py:665
  49.7 6.6 %collective-permute-start.16 = (bf16[4,2,54,256]{3,2,1,0:T(8,128)(2,1)S(1)}, bf16[4,2,54,256]{3,2,1,0:T(8,128)(2,1)S(1)}, u32[]{:S(2)}, u32[]{:S(2)}) collective-permute-start(bf16[4,2,54,256]{3,2,1,0:T(8,128)(2,1)S(1)} %get-tuple-element.161), channel_id=1, source_target_pairs={{0,4},{4,0},{8,12},{12,8},{16,20},{20,16},{24,28},{28,24},{1,5},{5... | collective-permute-start | bytes 663560 | tf_op jit(solution)/shard_map/ppermute | solution.py:665
  51.1 9.8 %collective-permute-start.18 = (bf16[2,196,216]{2,1,0:T(8,128)(2,1)S(1)}, bf16[2,196,216]{2,1,0:T(8,128)(2,1)S(1)}, u32[]{:S(2)}, u32[]{:S(2)}) collective-permute-start(bf16[2,196,216]{2,1,0:T(8,128)(2,1)S(1)} %get-tuple-element.163.refs_0_), channel_id=1, source_target_pairs={{0,1},{1,0},{2,3},{3,2},{4,5},{5,4},{6,7},{7,6},{8,9},{9,8},{10,11... | collective-permute-start | bytes 508040 | tf_op jit(solution)/shard_map/ppermute | solution.py:665
  53.1 7.8 %collective-permute-start.20 = (bf16[2,196,216]{2,1,0:T(8,128)(2,1)S(1)}, bf16[2,196,216]{2,1,0:T(8,128)(2,1)S(1)}, u32[]{:S(2)}, u32[]{:S(2)}) collective-permute-start(bf16[2,196,216]{2,1,0:T(8,128)(2,1)S(1)} %collective-permute-done.19.refs_2_), channel_id=1, source_target_pairs={{0,1},{1,0},{2,3},{3,2},{4,5},{5,4},{6,7},{7,6},{8,9},{9,8},{10,11... | collective-permute-start | bytes 508040 | tf_op jit(solution)/shard_map/ppermute | solution.py:665
  56.3 6.6 %collective-permute-start.17 = (bf16[2,54,256]{2,1,0:T(8,128)(2,1)S(1)}, bf16[2,54,256]{2,1,0:T(8,128)(2,1)S(1)}, u32[]{:S(2)}, u32[]{:S(2)}) collective-permute-start(bf16[2,54,256]{2,1,0:T(8,128)(2,1)S(1)} %get-tuple-element.162), channel_id=1, source_target_pairs={{0,24},{4,28},{8,16},{12,20},{16,8},{20,12},{24,0},{28,4},{1,25},{... | collective-permute-start | bytes 165896 | tf_op jit(solution)/shard_map/ppermute | solution.py:665
  57.9 5.4 %collective-permute-start.21 = (bf16[2,54,256]{2,1,0:T(8,128)(2,1)S(1)}, bf16[2,54,256]{2,1,0:T(8,128)(2,1)S(1)}, u32[]{:S(2)}, u32[]{:S(2)}) collective-permute-start(bf16[2,54,256]{2,1,0:T(8,128)(2,1)S(1)} %get-tuple-element.169), channel_id=1, source_target_pairs={{0,8},{4,12},{8,0},{12,4},{16,24},{20,28},{24,16},{28,20},{1,9},{5... | collective-permute-start | bytes 165896 | tf_op jit(solution)/shard_map/ppermute | solution.py:665
  57.9 5.4 %copy-start.1 = (f32[2,54,216]{2,0,1:T(2,128)S(1)}, f32[2,54,216]{2,0,1:T(2,128)}, u32[]{:S(2)}) copy-start(f32[2,54,216]{2,0,1:T(2,128)} %param.24) | copy-start | bytes 279940
  57.9 5.4 %copy-start.3 = (f32[2,54,216]{2,0,1:T(2,128)S(1)}, f32[2,54,216]{2,0,1:T(2,128)}, u32[]{:S(2)}) copy-start(f32[2,54,216]{2,0,1:T(2,128)} %param.25) | copy-start | bytes 279940
  57.9 5.4 %copy-start.4 = (f32[2,54,216]{2,0,1:T(2,128)S(1)}, f32[2,54,216]{2,0,1:T(2,128)}, u32[]{:S(2)}) copy-start(f32[2,54,216]{2,0,1:T(2,128)} %param.26) | copy-start | bytes 279940
  57.9 5.4 %copy-start.6 = (f32[9,216]{1,0:T(8,128)S(1)}, f32[9,216]{1,0:T(8,128)}, u32[]{:S(2)}) copy-start(f32[9,216]{1,0:T(8,128)} %refs_14_.1) | copy-start | bytes 23332
  57.9 5.4 %copy-start.7 = (f32[9,216]{1,0:T(8,128)S(1)}, f32[9,216]{1,0:T(8,128)}, u32[]{:S(2)}) copy-start(f32[9,216]{1,0:T(8,128)} %refs_15_.1) | copy-start | bytes 23332
  58.0 5.4 %copy-start.8 = (f32[2,12,12]{2,0,1:T(2,128)S(1)}, f32[2,12,12]{2,0,1:T(2,128)}, u32[]{:S(2)}) copy-start(f32[2,12,12]{2,0,1:T(2,128)} %param.31) | copy-start | bytes 3460
  58.0 5.4 %copy-start.9 = (f32[2,12,12]{2,0,1:T(2,128)S(1)}, f32[2,12,12]{2,0,1:T(2,128)}, u32[]{:S(2)}) copy-start(f32[2,12,12]{2,0,1:T(2,128)} %param.32) | copy-start | bytes 3460
  58.0 5.4 %copy-start.11 = (f32[4,216]{1,0:T(4,128)S(1)}, f32[4,216]{1,0:T(4,128)}, u32[]{:S(2)}) copy-start(f32[4,216]{1,0:T(4,128)} %refs_8_.1) | copy-start | bytes 10372
  58.0 5.4 %copy-start.12 = (f32[4,216]{1,0:T(4,128)S(1)}, f32[4,216]{1,0:T(4,128)}, u32[]{:S(2)}) copy-start(f32[4,216]{1,0:T(4,128)} %refs_9_.1) | copy-start | bytes 10372
  58.0 5.3 %collective-permute-start.22 = (bf16[2,54,256]{2,1,0:T(8,128)(2,1)S(1)}, bf16[2,54,256]{2,1,0:T(8,128)(2,1)S(1)}, u32[]{:S(2)}, u32[]{:S(2)}) collective-permute-start(bf16[2,54,256]{2,1,0:T(8,128)(2,1)S(1)} %get-tuple-element.170), channel_id=1, source_target_pairs={{0,16},{4,20},{8,24},{12,28},{16,0},{20,4},{24,8},{28,12},{1,17},{... | collective-permute-start | bytes 165896 | tf_op jit(solution)/shard_map/ppermute | solution.py:665

commit v8 on v7

--- a/solution.py
+++ b/solution.py
@@ -241,39 +241,44 @@
 
 
 def ffn_last_kernel(
-    scal, mid_ref, dy_ref, norm_ref, o_ref, z_ref, inv_ref, w_ref, e_ref, *refs, parts
+    scal, mid_ref, dy_ref, norm_ref, o_ref, z_ref, inv_ref, w_ref, e_ref, *refs, parts, late
 ):
-    wins, wdns, gates, dhs, gcvs, last_ref = refs[:6]
-    out_ref, dmid_ref, gn_ref = refs[6:9]
-    gw_refs, refs = refs[9 : 9 + parts], refs[9 + parts :]
+    early = parts - late
+    wins, wdns, gates, dhs, gcvs = refs[:5]
+    last_refs, refs = refs[5 : 5 + late], refs[5 + late :]
+    out_ref, dmid_ref, gn_ref = refs[:3]
+    gw_refs, refs = refs[3 : 3 + parts], refs[3 + parts :]
     win_ref, wdn_ref, gate_ref, dh_ref, gcv_ref, h_ref, d_ref, cv_ref, tmp_ref, sm_ref, dw_ref = refs
     w, e = w_ref[...], e_ref[...]
     dim = w.shape[1]
-    k = parts - 1
-    up(last_ref, w, e, win_ref, wdn_ref, h_ref, d_ref, cv_ref)
-    for h in range(k):
-        gi = tn(dhs[h], w).astype(bf16)
-        gd = tn(gates[h], e).astype(bf16)
+    wins, wdns, gates, dhs, gcvs = [
+        [ref.at[i] for i in range(early)] + [own.at[i] for i in range(late)]
+        for ref, own in ((wins, win_ref), (wdns, wdn_ref), (gates, gate_ref), (dhs, dh_ref), (gcvs, gcv_ref))
+    ]
+
+    def back(h):
+        gi = tn(dhs[h][...], w).astype(bf16)
+        gd = tn(gates[h][...], e).astype(bf16)
         for j in range(4):
             gw_refs[h][1 + j, :, 0:dim] = gi[64 * j : 64 * j + 54]
             gw_refs[h][5 + j, :, 0:dim] = gd[64 * j : 64 * j + 54]
-    middle(scal, k, h_ref, d_ref, gate_ref, dh_ref, cv_ref, gcv_ref)
-    wins, wdns, gates, dhs, gcvs = [
-        [ref.at[i] for i in range(k)] + [own]
-        for ref, own in ((wins, win_ref), (wdns, wdn_ref), (gates, gate_ref), (dhs, dh_ref), (gcvs, gcv_ref))
-    ]
+
+    for i in range(late):
+        up(last_refs[i], w, e, win_ref.at[i], wdn_ref.at[i], h_ref.at[i], d_ref.at[i], cv_ref.at[i])
+    for h in range(early):
+        back(h)
+    for i in range(late):
+        middle(
+            scal, early + i, h_ref.at[i], d_ref.at[i], gate_ref.at[i], dh_ref.at[i], cv_ref.at[i], gcv_ref.at[i]
+        )
     dw_ref[...] = sum(nn(dhs[h][...], wins[h][...]) for h in range(parts))
     valid = (scal[0] < scal[1]).astype(f32)
     tmp_ref[...] = (mid_ref[...] + sum(nn(gates[h][...], wdns[h][...]) for h in range(parts))) * valid
     free = iota((54, 256), 1) >= FREE
     pm = place(256)
     for h in range(parts):
-        if h == k:
-            gi = tn(dhs[h][...], w).astype(bf16)
-            gd = tn(gates[h][...], e).astype(bf16)
-            for j in range(4):
-                gw_refs[h][1 + j, :, 0:dim] = gi[64 * j : 64 * j + 54]
-                gw_refs[h][5 + j, :, 0:dim] = gd[64 * j : 64 * j + 54]
+        if h >= early:
+            back(h)
         in_free_lanes(nt(gcvs[h][...].astype(bf16), pm), sm_ref.at[h], 0)
         gw_refs[h][0] = jnp.where(free, sm_ref[h, 0:54, :], 0.0).astype(bf16)
     for y in range(SIDE):
@@ -415,10 +420,12 @@
         refs[-1][k] = ref[...]
 
 
-def select_kernel(slot_ref, scal, conv_ref, own_ref, other_ref, attn_ref, ffn_ref, every_ref):
-    every_ref[0] = own_ref[...]
-    every_ref[1] = other_ref[...]
-    per = own_ref.shape[1]
+def select_kernel(slot_ref, scal, conv_ref, *refs):
+    sources, (attn_ref, ffn_ref, every_ref) = refs[:4], refs[4:]
+    per = sources[0].shape[0]
+    for i in range(2):
+        every_ref[i, 0] = sources[2 * i][...]
+        every_ref[i, 1:] = sources[2 * i + 1][...]
     for b in range(12):
         pair, place, own = spot(slot_ref[b], per)
         block = every_ref[place ^ scal[4], pair ^ scal[5], own]
@@ -459,19 +466,26 @@
 
 
 def spread_attn_kernel(slot_ref, scal, old_ref, *refs, parts):
-    attn, outs, all_ref = refs[:parts], refs[parts:-1], refs[-1]
-    pairs, _, per = all_ref.shape[:3]
-    all_ref[...] = old_ref[...]
+    attn, outs = refs[:parts], refs[parts:]
+    half, per = outs[0].shape[:2]
+    for i, ref in enumerate(outs):
+        ref[...] = old_ref[half * (i % 2) : half * (i % 2 + 1), i // 2]
     for b in range(3):
         block = total(attn, b)
-        k, j, i = spot(slot_ref[b], per)
-        all_ref[k ^ scal[5], j ^ scal[4], i, :, 0:FREE] = block[:, 0:FREE].astype(bf16)
+        low = block[:, 0:FREE].astype(bf16)
         if b == 0:
             wide = block[:, FREE:].astype(bf16)
-    for j in range(2):
-        outs[j][...] = all_ref[:, j]
-        for k in range(pairs):
-            outs[j][k, 1, :, FREE:] = wide
+        pair, place, own = spot(slot_ref[b], per)
+        pair, place = pair ^ scal[5], place ^ scal[4]
+        for i, ref in enumerate(outs):
+
+            @pl.when((place == i // 2) & ((pair >= half) == (i % 2 == 1)))
+            def _():
+                ref[pair & (half - 1), own, :, 0:FREE] = low
+
+    for ref in outs:
+        for k in range(half):
+            ref[k, 1, :, FREE:] = wide
 
 
 def place_sum_kernel(own_ref, other_ref, *outs):
@@ -613,18 +627,20 @@
 
 def ffn_last(scal, mid, dy, norm_params, o, first, w):
     pad, dim = mid.shape
-    parts = first[4].shape[0] + 1
-    grids = [pltpu.VMEM((2, pad + 2 * MARGIN, 128), f32)] * 2
+    late = len(w)
+    parts = first[4].shape[0] + late
+    grids = [pltpu.VMEM((late, 2, pad + 2 * MARGIN, 128), f32)] * 2
     return call(
-        ffn_last_kernel, "ffn_last", 1, 14,
+        ffn_last_kernel, "ffn_last", 1, 13 + late,
         [SDS((SIDE * SIDE, dim), bf16), SDS((pad, dim), f32), SDS((8, dim), f32)] + [SDS((9, 54, 256), bf16)] * parts,
-        [pltpu.VMEM((256, dim), bf16)] * 2 + [pltpu.VMEM((pad, 256), bf16)] * 2 + [pltpu.VMEM((9, 256), f32)] + grids
+        [pltpu.VMEM((late, 256, dim), bf16)] * 2 + [pltpu.VMEM((late, pad, 256), bf16)] * 2
+        + [pltpu.VMEM((late, 9, 256), f32)] + grids
         + [
-            pltpu.VMEM((9, 256), f32), pltpu.VMEM((pad, dim), f32), pltpu.VMEM((parts, 56, 256), f32),
+            pltpu.VMEM((late, 9, 256), f32), pltpu.VMEM((pad, dim), f32), pltpu.VMEM((parts, 56, 256), f32),
             pltpu.VMEM((pad, dim), f32),
         ],
-        mb=24, micros=4, parts=parts,
-    )(scal, mid, dy, norm_params, o, *first, w)
+        mb=24, micros=4, parts=parts, late=late,
+    )(scal, mid, dy, norm_params, o, *first, *w)
 
 
 def scores_back(scal, dmid, mix, q, k, v, qw, p, pv, more, part):
@@ -710,18 +726,22 @@
         name="cast",
     )(swap(master))
     pairs = ranks // 2
-    far = {k: permute(mine, "dp", 2 * k) for k in (*range(2, pairs), 1)}
-    (own,) = call(stack_kernel, "stack", 0, pairs, [SDS((pairs, slots, rows, dim), bf16)])(
-        mine, *[far[k] for k in range(1, pairs)]
+    half = pairs // 2
+    near, far = range(1, half), range(half, pairs)
+    apart = {k: permute(mine, "dp", 2 * k) for k in (*far, *near)}
+    near_other = permute(mine, "dp", 1)
+    apart[1], near_other = lax.optimization_barrier((apart[1], near_other))
+    apart[half], tokens, cotangent, talk_in = lax.optimization_barrier((apart[half], tokens, cotangent, talk))
+    (far_own,) = call(stack_kernel, "stack", 0, pairs - 1, [SDS((pairs - 1, slots, rows, dim), bf16)])(
+        *[apart[k] for k in range(1, pairs)]
     )
-    own, tokens, cotangent, talk_in = lax.optimization_barrier((own, tokens, cotangent, talk))
-    other = permute(own, "dp", 1)
+    far_other = permute(far_own, "dp", 1)
     x, a, dy, mix, bias = prep(scal, tokens, cotangent, norm_params, talk_in)
-    other, x = lax.optimization_barrier((other, x))
+    far_other, x = lax.optimization_barrier((far_other, x))
     attn_w, ffn_w = call(
-        select_kernel, "select", 2, 3, [SDS((4, rows, dim), bf16), SDS((9, rows, dim), bf16)],
+        select_kernel, "select", 2, 5, [SDS((4, rows, dim), bf16), SDS((9, rows, dim), bf16)],
         [pltpu.VMEM((2, pairs, slots, rows, dim), bf16)],
-    )(block_slot, scal, conv, own, other)
+    )(block_slot, scal, conv, mine, far_own, near_other, far_other)
     attn_2, attn_1 = permute(attn_w, "head", 2), permute(attn_w, "head", 1)
     attn_3 = permute(attn_2, "head", 1)
     attn_w = [attn_w, attn_1, attn_2, attn_3]
@@ -729,35 +749,37 @@
     mid, q, k, v, o, qw, p, pv = attn_fwd(scal, x, a, mix, bias, attn_w)
     mid, ffn_2 = lax.optimization_barrier((mid, ffn_2))
     ffn_3 = permute(ffn_2, "head", 1)
-    first = list(ffn_first(scal, mid, dy, norm_params, [ffn_w, ffn_1, ffn_2]))
+    first = list(ffn_first(scal, mid, dy, norm_params, [ffn_w, ffn_1]))
     first[0], ffn_3 = lax.optimization_barrier((first[0], ffn_3))
-    out, dmid, gn2, *ffn_g = ffn_last(scal, mid, dy, norm_params, o, first, ffn_3)
+    out, dmid, gn2, *ffn_g = ffn_last(scal, mid, dy, norm_params, o, first, [ffn_2, ffn_3])
     ffn_1, ffn_3 = permute(ffn_g[1], "head", 1), permute(ffn_g[3], "head", 1)
     do, gqa, *sums = scores_back(scal, dmid, mix, q, k, v, qw, p, pv, attn_w, 0)
     do, ffn_1, ffn_3 = lax.optimization_barrier((do, ffn_1, ffn_3))
-    (half,) = call(half_sum_kernel, "half_sum", 0, 2, [SDS(ffn_3.shape, bf16)])(ffn_g[2], ffn_3)
-    ffn_2 = permute(half, "head", 2)
+    (summed,) = call(half_sum_kernel, "half_sum", 0, 2, [SDS(ffn_3.shape, bf16)])(ffn_g[2], ffn_3)
+    ffn_2 = permute(summed, "head", 2)
     gqb, gk, gv, gt = scores_back(scal, dmid, mix, q, k, v, qw, p, pv, [do, *sums], 1)
     both, *attn_g = weights_back(scal, x, a, dmid, norm_params, gn2, gqa, gqb, gk, gv, gt, out, attn_w)
     attn_1, attn_3 = permute(attn_g[1], "head", 1), permute(attn_g[3], "head", 1)
-    (half,) = call(half_sum_kernel, "half_sum", 0, 2, [SDS(attn_3.shape, bf16)])(attn_g[2], attn_3)
-    attn_2 = permute(half, "head", 2)
+    (summed,) = call(half_sum_kernel, "half_sum", 0, 2, [SDS(attn_3.shape, bf16)])(attn_g[2], attn_3)
+    attn_2 = permute(summed, "head", 2)
     (message,) = call(
         spread_ffn_kernel, "spread_ffn", 2, 3, [SDS((ranks // 2, 2, slots, rows, 256), bf16)]
     )(block_slot, scal, ffn_g[0], ffn_1, ffn_2)
     both, message = lax.optimization_barrier((both, message))
     both_2, both_1 = permute(both, "head", 2), permute(both, "head", 1)
     both_3 = permute(both_2, "head", 1)
-    own, other = call(
-        spread_attn_kernel, "spread_attn", 2, 4, [SDS((pairs,) + message.shape[2:], bf16)] * 2,
-        [pltpu.VMEM(message.shape, bf16)], parts=3,
+    near_own, far_own, near_other, far_other = call(
+        spread_attn_kernel, "spread_attn", 2, 4, [SDS((half,) + message.shape[2:], bf16)] * 4, parts=3,
     )(block_slot, scal, message, attn_g[0], attn_1, attn_2)
     slot_shape = (slots, rows, 256)
-    got = list(call(
-        place_sum_kernel, "place_sum", 0, 2, [SDS(slot_shape, f32)] + [SDS(slot_shape, bf16)] * (pairs - 1)
-    )(own, permute(other, "dp", 1)))
-    far = {k: permute(got[k], "dp", 2 * k) for k in (*range(2, pairs), 1)}
-    got[1:] = [far[k] for k in range(1, pairs)]
+    far_other = permute(far_other, "dp", 1)
+    near_other = permute(near_other, "dp", 1)
+    far_sum = call(place_sum_kernel, "place_sum", 0, 2, [SDS(slot_shape, bf16)] * half)(far_own, far_other)
+    far_sum = [permute(far_sum[k - half], "dp", 2 * k) for k in far]
+    own, *near_sum = call(
+        place_sum_kernel, "place_sum", 0, 2, [SDS(slot_shape, f32)] + [SDS(slot_shape, bf16)] * (half - 1)
+    )(near_own, near_other)
+    got = [own] + [permute(near_sum[k - 1], "dp", 2 * k) for k in near] + far_sum
     shape = SDS((tokens.shape[1], parts, dim), f32)
     output, token_grad = pl.pallas_call(
         assemble_kernel,

time: 64.7 us -> 63.8 us (0.986)
  waiting for transfers between devices: 19.5 us -> 17.9 us
  starting transfers between devices: 21.1 us -> 21.9 us
    ppermute x23 -> x25, waiting for transfers between devices: 19.5 us -> 17.9 us  [permute(): lax.ppermute(x, axis, [(i, i ^ k) for i in range(lax.axis_size(axis))])]
    ppermute x23 -> x25, starting transfers between devices: 21.1 us -> 21.9 us  [permute(): lax.ppermute(x, axis, [(i, i ^ k) for i in range(lax.axis_size(axis))])]
    pallas_call x1, Pallas kernels: 2.77 us -> 2.11 us  [ffn_first(): call(ffn_first_kernel, 'ffn_first', 1, 3 + count, [SDS((pad, dim), f32),...]
    pallas_call x4 -> x5, Pallas kernels: 3.47 us -> 4.12 us  [the longest x1 2.79 us: ffn_last(): call(ffn_last_kernel, 'ffn_last', 1, 13 + late, [SDS((SIDE * SIDE, dim),...]
  transfers between devices with their start and end apart: 23 -> 25, of which waited for: 11 -> 13; matrix products, arithmetic and copies ran while one was open for 0% -> 0% of each run, Pallas kernels for 24% -> 23%
where the time goes in v8:
time: 63.8 us; the launch traced here: 63.7 us
  starting transfers between devices  21.9 us (34%)
  Pallas kernels  19.6 us (31%)
  waiting for transfers between devices  17.9 us (28%)
  between operations  2.96 us (5%)
  local copies, waits for them, and re-layouts  1.27 us (2%)
    ppermute x25, starting transfers between devices, permute(): lax.ppermute(x, axis, [(i, i ^ k) for i in range(lax.axis_size(axis))])  21.9 us
    ppermute x25, waiting for transfers between devices, permute(): lax.ppermute(x, axis, [(i, i ^ k) for i in range(lax.axis_size(axis))])  17.9 us
    pallas_call x2, Pallas kernels, scores_back(): call(scores_back_kernel, 'scores_back', 1, 8 + len(more), outs, scratch,...  4.37 us
    pallas_call x1, Pallas kernels, ffn_last(): call(ffn_last_kernel, 'ffn_last', 1, 13 + late, [SDS((SIDE * SIDE, dim),...  2.79 us
    pallas_call x1, Pallas kernels, attn_fwd(): call(attn_fwd_kernel, 'attn_fwd', 1, 4 + len(w), [SDS((pad, dim), f32)] +...  2.65 us
    pallas_call x1, Pallas kernels, ffn_first(): call(ffn_first_kernel, 'ffn_first', 1, 3 + count, [SDS((pad, dim), f32),...  2.11 us
    pallas_call x1, Pallas kernels, local(): pl.pallas_call(assemble_kernel, grid=(1,), in_specs=[SM] + [whole(*both.s...  2 us
  transfers between devices with their start and end apart: 25, of which 13 were waited for; matrix products, arithmetic and copies ran while one was open for 0% of the time, Pallas kernels for 23%

profile of v8, /device:TPU:0, one launch (start us, length us, event | category | flops | bytes accessed | tf_op | source)
XLA Modules:
  0.0 63.7 jit_solution(12646601863918731205)
XLA Ops:
  0.7 0.9 %copy-done = f32[2,54,216]{2,0,1:T(2,128)S(1)} copy-done((f32[2,54,216]{2,0,1:T(2,128)S(1)}, f32[2,54,216]{2,0,1:T(2,128)}, u32[]{:S(2)}) %copy-start) | copy-done | bytes 93336
  1.5 0.2 cast.1.refs_0_
  1.8 4.1 %collective-permute-start.2 = (bf16[2,54,216]{2,1,0:T(8,128)(2,1)S(1)}, bf16[2,54,216]{2,1,0:T(8,128)(2,1)S(1)}, u32[]{:S(2)}, u32[]{:S(2)}) collective-permute-start(bf16[2,54,216]{2,1,0:T(8,128)(2,1)S(1)} %cast.1.refs_0_), channel_id=1, source_target_pairs={{0,16},{4,20},{8,24},{12,28},{16,0},{20,4},{24,8},{28,12},{1,17},{... | collective-permute-start | bytes 139976 | tf_op jit(solution)/shard_map/ppermute | solution.py:681
  5.9 1.5 %collective-permute-start.1 = (bf16[2,54,216]{2,1,0:T(8,128)(2,1)S(1)}, bf16[2,54,216]{2,1,0:T(8,128)(2,1)S(1)}, u32[]{:S(2)}, u32[]{:S(2)}) collective-permute-start(bf16[2,54,216]{2,1,0:T(8,128)(2,1)S(1)} %cast.1.refs_0_), channel_id=1, source_target_pairs={{0,4},{4,0},{8,12},{12,8},{16,20},{20,16},{24,28},{28,24},{1,5},{5... | collective-permute-start | bytes 139976 | tf_op jit(solution)/shard_map/ppermute | solution.py:681
  7.4 1.6 %collective-permute-start = (bf16[2,54,216]{2,1,0:T(8,128)(2,1)S(1)}, bf16[2,54,216]{2,1,0:T(8,128)(2,1)S(1)}, u32[]{:S(2)}, u32[]{:S(2)}) collective-permute-start(bf16[2,54,216]{2,1,0:T(8,128)(2,1)S(1)} %cast.1.refs_0_), channel_id=1, source_target_pairs={{0,8},{4,12},{8,0},{12,4},{16,24},{20,28},{24,16},{28,20},{1,9},{5... | collective-permute-start | bytes 139976 | tf_op jit(solution)/shard_map/ppermute | solution.py:681
  9.0 0.2 collective-permute-start.3
  9.2 0.9 %collective-permute-done.1.refs_2_ = bf16[2,54,216]{2,1,0:T(8,128)(2,1)S(1)} collective-permute-done((bf16[2,54,216]{2,1,0:T(8,128)(2,1)S(1)}, bf16[2,54,216]{2,1,0:T(8,128)(2,1)S(1)}, u32[]{:S(2)}, u32[]{:S(2)}) %collective-permute-start.1) | collective-permute-done | bytes 46688 | tf_op jit(solution)/shard_map/ppermute | solution.py:681
  10.1 1.5 %collective-permute-done.refs_0_ = bf16[2,54,216]{2,1,0:T(8,128)(2,1)S(1)} collective-permute-done((bf16[2,54,216]{2,1,0:T(8,128)(2,1)S(1)}, bf16[2,54,216]{2,1,0:T(8,128)(2,1)S(1)}, u32[]{:S(2)}, u32[]{:S(2)}) %collective-permute-start) | collective-permute-done | bytes 46688 | tf_op jit(solution)/shard_map/ppermute | solution.py:681
  11.6 3.4 %collective-permute-done.3.refs_2_ = bf16[2,54,216]{2,1,0:T(8,128)(2,1)S(1)} collective-permute-done((bf16[2,54,216]{2,1,0:T(8,128)(2,1)S(1)}, bf16[2,54,216]{2,1,0:T(8,128)(2,1)S(1)}, u32[]{:S(2)}, u32[]{:S(2)}) %collective-permute-start.3) | collective-permute-done | bytes 46688 | tf_op jit(solution)/shard_map/ppermute | solution.py:681
  15.0 0.6 collective-permute-start.4
  17.7 0.2 copy.34.cot_ref
  17.9 1.1 %prep.1 = (f32[224,216]{1,0:T(8,128)S(1)}, bf16[224,216]{1,0:T(8,128)(2,1)S(1)}, f32[224,216]{1,0:T(8,128)S(1)}, f32[2,192,256]{2,1,0:T(8,128)S(1)}, f32[224,128]{1,0:T(8,128)S(1)}) custom-call(s32[6]{0:T(128)S(1)} %concatenate.3.scal, bf16[4,196,216]{2,1,0:T(8,128)(2,1)S(1)} %copy.33.tok_ref, f32[4,196,216]{2,1,0:T(8,128)S(1)} %copy.34.cot_ref, ...), custom_call_target="tpu_custom_call" | custom-call | flops 1000000000 | bytes 3000000 | tf_op jit(solution)/shard_map/prep/pallas_call | solution.py:579
  19.0 1.5 %collective-permute-done.4.refs_3_ = bf16[3,2,54,216]{3,2,1,0:T(8,128)(2,1)S(1)} collective-permute-done((bf16[3,2,54,216]{3,2,1,0:T(8,128)(2,1)S(1)}, bf16[3,2,54,216]{3,2,1,0:T(8,128)(2,1)S(1)}, u32[]{:S(2)}, u32[]{:S(2)}) %collective-permute-start.4) | collective-permute-done | bytes 140000 | tf_op jit(solution)/shard_map/ppermute | solution.py:681
  20.5 0.6 select.7
  21.1 1.6 %collective-permute-start.6 = (bf16[4,54,216]{2,1,0:T(8,128)(2,1)S(1)}, bf16[4,54,216]{2,1,0:T(8,128)(2,1)S(1)}, u32[]{:S(2)}, u32[]{:S(2)}) collective-permute-start(bf16[4,54,216]{2,1,0:T(8,128)(2,1)S(1)} %get-tuple-element.116.refs_0_), channel_id=1, source_target_pairs={{0,2},{1,3},{2,0},{3,1},{4,6},{5,7},{6,4},{7,5},{8,10},{9,11},{10,... | collective-permute-start | bytes 279944 | tf_op jit(solution)/shard_map/ppermute | solution.py:681
  22.7 0.5 collective-permute-start.8
  23.2 0.5 collective-permute-start.5
  23.7 2.3 %collective-permute-done.6.refs_2_ = bf16[4,54,216]{2,1,0:T(8,128)(2,1)S(1)} collective-permute-done((bf16[4,54,216]{2,1,0:T(8,128)(2,1)S(1)}, bf16[4,54,216]{2,1,0:T(8,128)(2,1)S(1)}, u32[]{:S(2)}, u32[]{:S(2)}) %collective-permute-start.6) | collective-permute-done | bytes 93344 | tf_op jit(solution)/shard_map/ppermute | solution.py:681
  26.0 1.3 %collective-permute-done.7.refs_3_ = bf16[4,54,216]{2,1,0:T(8,128)(2,1)S(1)} collective-permute-done((bf16[4,54,216]{2,1,0:T(8,128)(2,1)S(1)}, bf16[4,54,216]{2,1,0:T(8,128)(2,1)S(1)}, u32[]{:S(2)}, u32[]{:S(2)}) %collective-permute-start.7) | collective-permute-done | bytes 93344 | tf_op jit(solution)/shard_map/ppermute | solution.py:681
  27.3 2.6 %attn_fwd.1 = (f32[224,216]{1,0:T(8,128)S(1)}, bf16[224,256]{1,0:T(8,128)(2,1)S(1)}, bf16[224,256]{1,0:T(8,128)(2,1)S(1)}, bf16[224,256]{1,0:T(8,128)(2,1)S(1)},...) custom-call(s32[6]{0:T(128)S(1)} %concatenate.3.scal, ...), custom_call_target="tpu_custom_call" | custom-call | flops 1000000000 | bytes 3000000 | tf_op jit(solution)/shard_map/attn_fwd/pallas_call | solution.py:605
  29.9 0.2 collective-permute-start.10
  30.2 2.1 %ffn_first.1 = (f32[224,216]{1,0:T(8,128)S(1)}, f32[224,128]{1,0:T(8,128)S(1)}, bf16[224,216]{1,0:T(8,128)(2,1)S(1)}, bf16[224,216]{1,0:T(8,128)(2,1)S(1)}, bf16...) custom-call(s32[6]{0:T(128)S(1)} %concatenate.3.scal, ...), custom_call_target="tpu_custom_call" | custom-call | flops 3000000000 | bytes 9000000 | tf_op jit(solution)/shard_map/ffn_first/pallas_call | solution.py:619
  32.3 2.8 %ffn_last.1 = (bf16[196,216]{1,0:T(8,128)(2,1)S(1)}, f32[224,216]{1,0:T(8,128)S(1)}, f32[8,216]{1,0:T(8,128)S(1)}, bf16[9,54,256]{2,1,0:T(8,128)(2,1)S(1)}, bf16...) custom-call(s32[6]{0:T(128)S(1)} %concatenate.3.scal, ...), custom_call_target="tpu_custom_call" | custom-call | flops 4000000000 | bytes 12000000 | tf_op jit(solution)/shard_map/ffn_last/pallas_call | solution.py:633
  35.1 0.4 collective-permute-start.11
  35.5 0.2 collective-permute-start.12
  35.7 1.6 %scores_back.2 = (bf16[224,256]{1,0:T(8,128)(2,1)S(1)}, bf16[64,256]{1,0:T(8,128)(2,1)S(1)}, f32[224,256]{1,0:T(8,128)S(1)}, f32[224,256]{1,0:T(8,128)S(1)}, f32...) custom-call(s32[6]{0:T(128)S(1)} %concatenate.3.scal, f32[224,216]{1,0:T(8,128)S(1)} %get-tuple-element.134.dmid_ref, ...), custom_call_target="tpu_custom_call" | custom-call | flops 4000000000 | bytes 12000000 | tf_op jit(solution)/shard_map/scores_back/pallas_call | solution.py:663
  37.3 1.6 %collective-permute-start.13 = (bf16[9,54,256]{2,1,0:T(8,128)(2,1)S(1)}, bf16[9,54,256]{2,1,0:T(8,128)(2,1)S(1)}, u32[]{:S(2)}, u32[]{:S(2)}) collective-permute-start(bf16[9,54,256]{2,1,0:T(8,128)(2,1)S(1)} %half_sum.2), channel_id=1, source_target_pairs={{0,2},{1,3},{2,0},{3,1},{4,6},{5,7},{6,4},{7,5},{8,10},{9,11},{10,... | collective-permute-start | bytes 746504 | tf_op jit(solution)/shard_map/ppermute | solution.py:681
  38.9 2.8 %scores_back.3 = (bf16[160,256]{1,0:T(8,128)(2,1)S(1)}, bf16[224,256]{1,0:T(8,128)(2,1)S(1)}, bf16[224,256]{1,0:T(8,128)(2,1)S(1)}, f32[2,12,12]{2,1,0:T(8,128)S(1)}) custom-call(s32[6]{0:T(128)S(1)} %concatenate.3.scal, f32[224,216]{1,0:T(8,128)S(1)} %get-tuple-element.134.dmid_ref, f32[2,192,256]{2,1,0:T(8,128)S(1)} %get-tuple-element.112.mix_ref, ...), custom_call_target="tpu_custom_call" | custom-call | flops 4000000000 | bytes 12000000 | tf_op jit(solution)/shard_map/scores_back/pallas_call | solution.py:663
  41.7 1.1 %weights_back.1 = (bf16[2,196,216]{2,1,0:T(8,128)(2,1)S(1)}, bf16[3,54,256]{2,1,0:T(8,128)(2,1)S(1)}, bf16[3,54,256]{2,1,0:T(8,128)(2,1)S(1)}, bf16[3,54,256]{2,1,0:T(8,128)(2,1)S(1)}, bf16[3,54,256]{2,1,0:T(8,128)(2,1)S(1)}) custom-call(s32[6]{0:T(128)S(1)} %concatenate.3.scal, f32[224,216]{1,0:T(8,128)S(1)} %get-tuple-element.110.x_ref, ...), custom_call_target="tpu_custom_call" | custom-call | flops 3000000000 | bytes 9000000 | tf_op jit(solution)/shard_map/weights_back/pallas_call | solution.py:671
  42.9 0.1 collective-permute-start.15
  43.0 0.4 collective-permute-start.14
  43.4 0.8 %collective-permute-done.15.b_ref = bf16[3,54,256]{2,1,0:T(8,128)(2,1)S(1)} collective-permute-done((bf16[3,54,256]{2,1,0:T(8,128)(2,1)S(1)}, bf16[3,54,256]{2,1,0:T(8,128)(2,1)S(1)}, u32[]{:S(2)}, u32[]{:S(2)}) %collective-permute-start.15) | collective-permute-done | bytes 82976 | tf_op jit(solution)/shard_map/ppermute | solution.py:681
  44.2 0.6 collective-permute-start.16
  44.8 1.1 %collective-permute-done.13.refs_2_ = bf16[9,54,256]{2,1,0:T(8,128)(2,1)S(1)} collective-permute-done((bf16[9,54,256]{2,1,0:T(8,128)(2,1)S(1)}, bf16[9,54,256]{2,1,0:T(8,128)(2,1)S(1)}, u32[]{:S(2)}, u32[]{:S(2)}) %collective-permute-start.13) | collective-permute-done | bytes 248864 | tf_op jit(solution)/shard_map/ppermute | solution.py:681
  45.9 0.7 %spread_ffn.1.old_ref = bf16[4,2,2,54,256]{4,3,2,1,0:T(8,128)(2,1)S(1)} custom-call(s32[12]{0:T(128)S(1)} %copy-done.13, s32[6]{0:T(128)S(1)} %concatenate.3.scal, bf16[9,54,256]{2,1,0:T(8,128)(2,1)S(1)} %get-tuple-element.157.refs_0_, bf16[9,54,256]{2,1,0:T(8,128)(2,1)S(1)} %collective-permute-done.11.refs_1_, ...), custom_call_target="tpu_custom_call" | custom-call | flops 1000000000 | bytes 3000000 | tf_op jit(solution)/shard_map/spread_ffn/pallas_call | solution.py:765
  46.6 1.6 %collective-permute-start.20 = (bf16[2,196,216]{2,1,0:T(8,128)(2,1)S(1)}, bf16[2,196,216]{2,1,0:T(8,128)(2,1)S(1)}, u32[]{:S(2)}, u32[]{:S(2)}) collective-permute-start(bf16[2,196,216]{2,1,0:T(8,128)(2,1)S(1)} %get-tuple-element.169.refs_0_), channel_id=1, source_target_pairs={{0,2},{1,3},{2,0},{3,1},{4,6},{5,7},{6,4},{7,5},{8,10},{9,11},{10,... | collective-permute-start | bytes 508040 | tf_op jit(solution)/shard_map/ppermute | solution.py:681
  48.1 0.9 %collective-permute-done.16.refs_2_ = bf16[3,54,256]{2,1,0:T(8,128)(2,1)S(1)} collective-permute-done((bf16[3,54,256]{2,1,0:T(8,128)(2,1)S(1)}, bf16[3,54,256]{2,1,0:T(8,128)(2,1)S(1)}, u32[]{:S(2)}, u32[]{:S(2)}) %collective-permute-start.16) | collective-permute-done | bytes 82976 | tf_op jit(solution)/shard_map/ppermute | solution.py:681
  49.1 0.7 %spread_attn.1 = (bf16[2,2,54,256]{3,2,1,0:T(8,128)(2,1)S(1)}, bf16[2,2,54,256]{3,2,1,0:T(8,128)(2,1)S(1)}, bf16[2,2,54,256]{3,2,1,0:T(8,128)(2,1)S(1)}, bf16[2,2,54,256]{3,2,1,0:T(8,128)(2,1)S(1)}) custom-call(s32[12]{0:T(128)S(1)} %copy-done.13, s32[6]{0:T(128)S(1)} %concatenate.3.scal, bf16[4,2,2,54,256]{4,3,2,1,0:T(8,128)(2,1)S(1)} %spread_ffn.1.old_ref, ...), custom_call_target="tpu_custom_call" | custom-call | flops 1000000000 | bytes 3000000 | tf_op jit(solution)/shard_map/spread_attn/pallas_call | solution.py:771
  49.8 0.7 %collective-permute-start.17 = (bf16[2,2,54,256]{3,2,1,0:T(8,128)(2,1)S(1)}, bf16[2,2,54,256]{3,2,1,0:T(8,128)(2,1)S(1)}, u32[]{:S(2)}, u32[]{:S(2)}) collective-permute-start(bf16[2,2,54,256]{3,2,1,0:T(8,128)(2,1)S(1)} %get-tuple-element.167), channel_id=1, source_target_pairs={{0,4},{4,0},{8,12},{12,8},{16,20},{20,16},{24,28},{28,24},{1,5},{5... | collective-permute-start | bytes 331784 | tf_op jit(solution)/shard_map/ppermute | solution.py:681
  50.5 1.4 %collective-permute-start.22 = (bf16[2,2,54,256]{3,2,1,0:T(8,128)(2,1)S(1)}, bf16[2,2,54,256]{3,2,1,0:T(8,128)(2,1)S(1)}, u32[]{:S(2)}, u32[]{:S(2)}) collective-permute-start(bf16[2,2,54,256]{3,2,1,0:T(8,128)(2,1)S(1)} %get-tuple-element.175), channel_id=1, source_target_pairs={{0,4},{4,0},{8,12},{12,8},{16,20},{20,16},{24,28},{28,24},{1,5},{5... | collective-permute-start | bytes 331784 | tf_op jit(solution)/shard_map/ppermute | solution.py:681
  51.9 1.4 %collective-permute-done.20.refs_2_ = bf16[2,196,216]{2,1,0:T(8,128)(2,1)S(1)} collective-permute-done((bf16[2,196,216]{2,1,0:T(8,128)(2,1)S(1)}, bf16[2,196,216]{2,1,0:T(8,128)(2,1)S(1)}, u32[]{:S(2)}, u32[]{:S(2)}) %collective-permute-start.20) | collective-permute-done | bytes 169376 | tf_op jit(solution)/shard_map/ppermute | solution.py:681
  53.3 2.0 %collective-permute-done.17.other_ref = bf16[2,2,54,256]{3,2,1,0:T(8,128)(2,1)S(1)} collective-permute-done((bf16[2,2,54,256]{3,2,1,0:T(8,128)(2,1)S(1)}, bf16[2,2,54,256]{3,2,1,0:T(8,128)(2,1)S(1)}, u32[]{:S(2)}, u32[]{:S(2)}) %collective-permute-start.17) | collective-permute-done | bytes 110624 | tf_op jit(solution)/shard_map/ppermute | solution.py:681
  55.3 0.8 %collective-permute-start.18 = (bf16[2,54,256]{2,1,0:T(8,128)(2,1)S(1)}, bf16[2,54,256]{2,1,0:T(8,128)(2,1)S(1)}, u32[]{:S(2)}, u32[]{:S(2)}) collective-permute-start(bf16[2,54,256]{2,1,0:T(8,128)(2,1)S(1)} %get-tuple-element.168), channel_id=1, source_target_pairs={{0,24},{4,28},{8,16},{12,20},{16,8},{20,12},{24,0},{28,4},{1,25},{... | collective-permute-start | bytes 165896 | tf_op jit(solution)/shard_map/ppermute | solution.py:681
  56.1 0.4 collective-permute-done.22.other_ref
  56.6 3.3 %collective-permute-start.23 = (bf16[2,54,256]{2,1,0:T(8,128)(2,1)S(1)}, bf16[2,54,256]{2,1,0:T(8,128)(2,1)S(1)}, u32[]{:S(2)}, u32[]{:S(2)}) collective-permute-start(bf16[2,54,256]{2,1,0:T(8,128)(2,1)S(1)} %get-tuple-element.177), channel_id=1, source_target_pairs={{0,8},{4,12},{8,0},{12,4},{16,24},{20,28},{24,16},{28,20},{1,9},{5... | collective-permute-start | bytes 165896 | tf_op jit(solution)/shard_map/ppermute | solution.py:681
  60.0 2.0 %assemble.1 = (f32[196,4,216]{2,1,0:T(4,128)}, f32[196,4,216]{2,1,0:T(4,128)}) custom-call(s32[6]{0:T(128)S(1)} %concatenate.3.scal, bf16[2,196,216]{2,1,0:T(8,128)(2,1)S(1)} %get-tuple-element.169.refs_0_, bf16[2,196,216]{2,1,0:T(8,128)(2,1)S(1)} %collective-permute-done.19.refs_1_, bf16[2,196,216]{2,1,0:T(8,128)(2,1)S(1)} %collective-permute-done.20.refs_2_, ...), custom_call_target="tpu_custom_call" | custom-call | flops 1000000000 | bytes 3000000 | tf_op jit(solution)/shard_map/assemble/pallas_call | solution.py:784
  62.0 0.5 collective-permute-done.24.refs_2_
  62.5 1.1 %update.1 = (f32[54,2,216]{2,1,0:T(2,128)}, f32[54,2,216]{2,1,0:T(2,128)}, f32[54,2,216]{2,1,0:T(2,128)}, bf16[54,2,216]{2,1,0:T(2,128)(2,1)}, f32[4,216]{1,0:T(...) custom-call(f32[2,54,256]{2,1,0:T(8,128)S(1)} %get-tuple-element.176, ...), custom_call_target="tpu_custom_call" | custom-call | flops 1000000000 | bytes 3000000 | tf_op jit(solution)/shard_map/update/pallas_call | solution.py:693
  (56 shorter events, 0.4 us)
Async XLA Ops:
  0.6 0.9 %copy-start = (f32[2,54,216]{2,0,1:T(2,128)S(1)}, f32[2,54,216]{2,0,1:T(2,128)}, u32[]{:S(2)}) copy-start(f32[2,54,216]{2,0,1:T(2,128)} %param.24) | copy-start | bytes 279940
  1.8 15.8 %copy-start.2 = (f32[2,12,12]{2,0,1:T(2,128)S(1)}, f32[2,12,12]{2,0,1:T(2,128)}, u32[]{:S(2)}) copy-start(f32[2,12,12]{2,0,1:T(2,128)} %param.30) | copy-start | bytes 3460
  1.8 15.8 %copy-start.15 = (bf16[4,196,216]{2,0,1:T(4,128)(2,1)S(1)}, bf16[4,196,216]{2,0,1:T(4,128)(2,1)}, u32[]{:S(2)}) copy-start(bf16[4,196,216]{2,0,1:T(4,128)(2,1)} %param.18) | copy-start | bytes 1016068
  1.8 7.4 %collective-permute-start.2 = (bf16[2,54,216]{2,1,0:T(8,128)(2,1)S(1)}, bf16[2,54,216]{2,1,0:T(8,128)(2,1)S(1)}, u32[]{:S(2)}, u32[]{:S(2)}) collective-permute-start(bf16[2,54,216]{2,1,0:T(8,128)(2,1)S(1)} %cast.1.refs_0_), channel_id=1, source_target_pairs={{0,16},{4,20},{8,24},{12,28},{16,0},{20,4},{24,8},{28,12},{1,17},{... | collective-permute-start | bytes 139976 | tf_op jit(solution)/shard_map/ppermute | solution.py:681
  5.9 4.2 %collective-permute-start.1 = (bf16[2,54,216]{2,1,0:T(8,128)(2,1)S(1)}, bf16[2,54,216]{2,1,0:T(8,128)(2,1)S(1)}, u32[]{:S(2)}, u32[]{:S(2)}) collective-permute-start(bf16[2,54,216]{2,1,0:T(8,128)(2,1)S(1)} %cast.1.refs_0_), channel_id=1, source_target_pairs={{0,4},{4,0},{8,12},{12,8},{16,20},{20,16},{24,28},{28,24},{1,5},{5... | collective-permute-start | bytes 139976 | tf_op jit(solution)/shard_map/ppermute | solution.py:681
  7.4 4.2 %collective-permute-start = (bf16[2,54,216]{2,1,0:T(8,128)(2,1)S(1)}, bf16[2,54,216]{2,1,0:T(8,128)(2,1)S(1)}, u32[]{:S(2)}, u32[]{:S(2)}) collective-permute-start(bf16[2,54,216]{2,1,0:T(8,128)(2,1)S(1)} %cast.1.refs_0_), channel_id=1, source_target_pairs={{0,8},{4,12},{8,0},{12,4},{16,24},{20,28},{24,16},{28,20},{1,9},{5... | collective-permute-start | bytes 139976 | tf_op jit(solution)/shard_map/ppermute | solution.py:681
  9.0 6.0 %collective-permute-start.3 = (bf16[2,54,216]{2,1,0:T(8,128)(2,1)S(1)}, bf16[2,54,216]{2,1,0:T(8,128)(2,1)S(1)}, u32[]{:S(2)}, u32[]{:S(2)}) collective-permute-start(bf16[2,54,216]{2,1,0:T(8,128)(2,1)S(1)} %cast.1.refs_0_), channel_id=1, source_target_pairs={{0,24},{4,28},{8,16},{12,20},{16,8},{20,12},{24,0},{28,4},{1,25},{... | collective-permute-start | bytes 139976 | tf_op jit(solution)/shard_map/ppermute | solution.py:681
  15.0 2.7 %copy-start.14 = (f32[4,196,216]{2,0,1:T(4,128)S(1)}, f32[4,196,216]{2,0,1:T(4,128)}, u32[]{:S(2)}) copy-start(f32[4,196,216]{2,0,1:T(4,128)} %param.19) | copy-start | bytes 2032132
  15.0 2.9 %copy-start.10 = (f32[4,216]{1,0:T(4,128)S(1)}, f32[4,216]{1,0:T(4,128)}, u32[]{:S(2)}) copy-start(f32[4,216]{1,0:T(4,128)} %refs_7_.1) | copy-start | bytes 10372
  15.0 5.5 %collective-permute-start.4 = (bf16[3,2,54,216]{3,2,1,0:T(8,128)(2,1)S(1)}, bf16[3,2,54,216]{3,2,1,0:T(8,128)(2,1)S(1)}, u32[]{:S(2)}, u32[]{:S(2)}) collective-permute-start(bf16[3,2,54,216]{3,2,1,0:T(8,128)(2,1)S(1)} %stack.1.refs_1_), channel_id=1, source_target_pairs={{0,4},{4,0},{8,12},{12,8},{16,20},{20,16},{24,28},{28,24},{1,5},{5... | collective-permute-start | bytes 419912 | tf_op jit(solution)/shard_map/ppermute | solution.py:681
  17.9 2.6 %copy-start.5 = (f32[9,216]{1,0:T(8,128)S(1)}, f32[9,216]{1,0:T(8,128)}, u32[]{:S(2)}) copy-start(f32[9,216]{1,0:T(8,128)} %refs_13_.1) | copy-start | bytes 23332
  17.9 2.6 %copy-start.13 = (s32[12]{0:T(128)S(1)}, s32[12]{0:T(128)}, u32[]{:S(2)}) copy-start(s32[12]{0:T(128)} %slot_ref.5) | copy-start | bytes 148
  21.1 4.9 %collective-permute-start.6 = (bf16[4,54,216]{2,1,0:T(8,128)(2,1)S(1)}, bf16[4,54,216]{2,1,0:T(8,128)(2,1)S(1)}, u32[]{:S(2)}, u32[]{:S(2)}) collective-permute-start(bf16[4,54,216]{2,1,0:T(8,128)(2,1)S(1)} %get-tuple-element.116.refs_0_), channel_id=1, source_target_pairs={{0,2},{1,3},{2,0},{3,1},{4,6},{5,7},{6,4},{7,5},{8,10},{9,11},{10,... | collective-permute-start | bytes 279944 | tf_op jit(solution)/shard_map/ppermute | solution.py:681
  22.7 7.2 %collective-permute-start.8 = (bf16[9,54,216]{2,1,0:T(8,128)(2,1)S(1)}, bf16[9,54,216]{2,1,0:T(8,128)(2,1)S(1)}, u32[]{:S(2)}, u32[]{:S(2)}) collective-permute-start(bf16[9,54,216]{2,1,0:T(8,128)(2,1)S(1)} %get-tuple-element.118.refs_0_), channel_id=1, source_target_pairs={{0,2},{1,3},{2,0},{3,1},{4,6},{5,7},{6,4},{7,5},{8,10},{9,11},{10,... | collective-permute-start | bytes 629864 | tf_op jit(solution)/shard_map/ppermute | solution.py:681
  23.2 7.0 %collective-permute-start.9 = (bf16[9,54,216]{2,1,0:T(8,128)(2,1)S(1)}, bf16[9,54,216]{2,1,0:T(8,128)(2,1)S(1)}, u32[]{:S(2)}, u32[]{:S(2)}) collective-permute-start(bf16[9,54,216]{2,1,0:T(8,128)(2,1)S(1)} %get-tuple-element.118.refs_0_), channel_id=1, source_target_pairs={{0,1},{1,0},{2,3},{3,2},{4,5},{5,4},{6,7},{7,6},{8,9},{9,8},{10,11... | collective-permute-start | bytes 629864 | tf_op jit(solution)/shard_map/ppermute | solution.py:681
  23.2 2.8 %collective-permute-start.5 = (bf16[4,54,216]{2,1,0:T(8,128)(2,1)S(1)}, bf16[4,54,216]{2,1,0:T(8,128)(2,1)S(1)}, u32[]{:S(2)}, u32[]{:S(2)}) collective-permute-start(bf16[4,54,216]{2,1,0:T(8,128)(2,1)S(1)} %get-tuple-element.116.refs_0_), channel_id=1, source_target_pairs={{0,1},{1,0},{2,3},{3,2},{4,5},{5,4},{6,7},{7,6},{8,9},{9,8},{10,11... | collective-permute-start | bytes 279944 | tf_op jit(solution)/shard_map/ppermute | solution.py:681
  26.0 1.3 %collective-permute-start.7 = (bf16[4,54,216]{2,1,0:T(8,128)(2,1)S(1)}, bf16[4,54,216]{2,1,0:T(8,128)(2,1)S(1)}, u32[]{:S(2)}, u32[]{:S(2)}) collective-permute-start(bf16[4,54,216]{2,1,0:T(8,128)(2,1)S(1)} %collective-permute-done.6.refs_2_), channel_id=1, source_target_pairs={{0,1},{1,0},{2,3},{3,2},{4,5},{5,4},{6,7},{7,6},{8,9},{9,8},{10,11... | collective-permute-start | bytes 279944 | tf_op jit(solution)/shard_map/ppermute | solution.py:681
  29.9 2.3 %collective-permute-start.10 = (bf16[9,54,216]{2,1,0:T(8,128)(2,1)S(1)}, bf16[9,54,216]{2,1,0:T(8,128)(2,1)S(1)}, u32[]{:S(2)}, u32[]{:S(2)}) collective-permute-start(bf16[9,54,216]{2,1,0:T(8,128)(2,1)S(1)} %collective-permute-done.8.refs_5_), channel_id=1, source_target_pairs={{0,1},{1,0},{2,3},{3,2},{4,5},{5,4},{6,7},{7,6},{8,9},{9,8},{10,11... | collective-permute-start | bytes 629864 | tf_op jit(solution)/shard_map/ppermute | solution.py:681
  35.1 2.2 %collective-permute-start.11 = (bf16[9,54,256]{2,1,0:T(8,128)(2,1)S(1)}, bf16[9,54,256]{2,1,0:T(8,128)(2,1)S(1)}, u32[]{:S(2)}, u32[]{:S(2)}) collective-permute-start(bf16[9,54,256]{2,1,0:T(8,128)(2,1)S(1)} %get-tuple-element.144), channel_id=1, source_target_pairs={{0,1},{1,0},{2,3},{3,2},{4,5},{5,4},{6,7},{7,6},{8,9},{9,8},{10,11... | collective-permute-start | bytes 746504 | tf_op jit(solution)/shard_map/ppermute | solution.py:681
  35.5 1.7 %collective-permute-start.12 = (bf16[9,54,256]{2,1,0:T(8,128)(2,1)S(1)}, bf16[9,54,256]{2,1,0:T(8,128)(2,1)S(1)}, u32[]{:S(2)}, u32[]{:S(2)}) collective-permute-start(bf16[9,54,256]{2,1,0:T(8,128)(2,1)S(1)} %get-tuple-element.145), channel_id=1, source_target_pairs={{0,1},{1,0},{2,3},{3,2},{4,5},{5,4},{6,7},{7,6},{8,9},{9,8},{10,11... | collective-permute-start | bytes 746504 | tf_op jit(solution)/shard_map/ppermute | solution.py:681
  37.3 8.5 %collective-permute-start.13 = (bf16[9,54,256]{2,1,0:T(8,128)(2,1)S(1)}, bf16[9,54,256]{2,1,0:T(8,128)(2,1)S(1)}, u32[]{:S(2)}, u32[]{:S(2)}) collective-permute-start(bf16[9,54,256]{2,1,0:T(8,128)(2,1)S(1)} %half_sum.2), channel_id=1, source_target_pairs={{0,2},{1,3},{2,0},{3,1},{4,6},{5,7},{6,4},{7,5},{8,10},{9,11},{10,... | collective-permute-start | bytes 746504 | tf_op jit(solution)/shard_map/ppermute | solution.py:681
  42.9 1.3 %collective-permute-start.15 = (bf16[3,54,256]{2,1,0:T(8,128)(2,1)S(1)}, bf16[3,54,256]{2,1,0:T(8,128)(2,1)S(1)}, u32[]{:S(2)}, u32[]{:S(2)}) collective-permute-start(bf16[3,54,256]{2,1,0:T(8,128)(2,1)S(1)} %get-tuple-element.165), channel_id=1, source_target_pairs={{0,1},{1,0},{2,3},{3,2},{4,5},{5,4},{6,7},{7,6},{8,9},{9,8},{10,11... | collective-permute-start | bytes 248840 | tf_op jit(solution)/shard_map/ppermute | solution.py:681
  43.0 5.1 %collective-permute-start.14 = (bf16[3,54,256]{2,1,0:T(8,128)(2,1)S(1)}, bf16[3,54,256]{2,1,0:T(8,128)(2,1)S(1)}, u32[]{:S(2)}, u32[]{:S(2)}) collective-permute-start(bf16[3,54,256]{2,1,0:T(8,128)(2,1)S(1)} %get-tuple-element.163), channel_id=1, source_target_pairs={{0,1},{1,0},{2,3},{3,2},{4,5},{5,4},{6,7},{7,6},{8,9},{9,8},{10,11... | collective-permute-start | bytes 248840 | tf_op jit(solution)/shard_map/ppermute | solution.py:681
  44.2 4.8 %collective-permute-start.16 = (bf16[3,54,256]{2,1,0:T(8,128)(2,1)S(1)}, bf16[3,54,256]{2,1,0:T(8,128)(2,1)S(1)}, u32[]{:S(2)}, u32[]{:S(2)}) collective-permute-start(bf16[3,54,256]{2,1,0:T(8,128)(2,1)S(1)} %half_sum.3), channel_id=1, source_target_pairs={{0,2},{1,3},{2,0},{3,1},{4,6},{5,7},{6,4},{7,5},{8,10},{9,11},{10,... | collective-permute-start | bytes 248840 | tf_op jit(solution)/shard_map/ppermute | solution.py:681
  46.6 6.7 %collective-permute-start.20 = (bf16[2,196,216]{2,1,0:T(8,128)(2,1)S(1)}, bf16[2,196,216]{2,1,0:T(8,128)(2,1)S(1)}, u32[]{:S(2)}, u32[]{:S(2)}) collective-permute-start(bf16[2,196,216]{2,1,0:T(8,128)(2,1)S(1)} %get-tuple-element.169.refs_0_), channel_id=1, source_target_pairs={{0,2},{1,3},{2,0},{3,1},{4,6},{5,7},{6,4},{7,5},{8,10},{9,11},{10,... | collective-permute-start | bytes 508040 | tf_op jit(solution)/shard_map/ppermute | solution.py:681
  49.8 5.5 %collective-permute-start.17 = (bf16[2,2,54,256]{3,2,1,0:T(8,128)(2,1)S(1)}, bf16[2,2,54,256]{3,2,1,0:T(8,128)(2,1)S(1)}, u32[]{:S(2)}, u32[]{:S(2)}) collective-permute-start(bf16[2,2,54,256]{3,2,1,0:T(8,128)(2,1)S(1)} %get-tuple-element.167), channel_id=1, source_target_pairs={{0,4},{4,0},{8,12},{12,8},{16,20},{20,16},{24,28},{28,24},{1,5},{5... | collective-permute-start | bytes 331784 | tf_op jit(solution)/shard_map/ppermute | solution.py:681
  50.5 6.0 %collective-permute-start.22 = (bf16[2,2,54,256]{3,2,1,0:T(8,128)(2,1)S(1)}, bf16[2,2,54,256]{3,2,1,0:T(8,128)(2,1)S(1)}, u32[]{:S(2)}, u32[]{:S(2)}) collective-permute-start(bf16[2,2,54,256]{3,2,1,0:T(8,128)(2,1)S(1)} %get-tuple-element.175), channel_id=1, source_target_pairs={{0,4},{4,0},{8,12},{12,8},{16,20},{20,16},{24,28},{28,24},{1,5},{5... | collective-permute-start | bytes 331784 | tf_op jit(solution)/shard_map/ppermute | solution.py:681
  51.9 8.1 %collective-permute-start.19 = (bf16[2,196,216]{2,1,0:T(8,128)(2,1)S(1)}, bf16[2,196,216]{2,1,0:T(8,128)(2,1)S(1)}, u32[]{:S(2)}, u32[]{:S(2)}) collective-permute-start(bf16[2,196,216]{2,1,0:T(8,128)(2,1)S(1)} %get-tuple-element.169.refs_0_), channel_id=1, source_target_pairs={{0,1},{1,0},{2,3},{3,2},{4,5},{5,4},{6,7},{7,6},{8,9},{9,8},{10,11... | collective-permute-start | bytes 508040 | tf_op jit(solution)/shard_map/ppermute | solution.py:681
  53.3 6.7 %collective-permute-start.21 = (bf16[2,196,216]{2,1,0:T(8,128)(2,1)S(1)}, bf16[2,196,216]{2,1,0:T(8,128)(2,1)S(1)}, u32[]{:S(2)}, u32[]{:S(2)}) collective-permute-start(bf16[2,196,216]{2,1,0:T(8,128)(2,1)S(1)} %collective-permute-done.20.refs_2_), channel_id=1, source_target_pairs={{0,1},{1,0},{2,3},{3,2},{4,5},{5,4},{6,7},{7,6},{8,9},{9,8},{10,11... | collective-permute-start | bytes 508040 | tf_op jit(solution)/shard_map/ppermute | solution.py:681
  55.3 6.7 %collective-permute-start.18 = (bf16[2,54,256]{2,1,0:T(8,128)(2,1)S(1)}, bf16[2,54,256]{2,1,0:T(8,128)(2,1)S(1)}, u32[]{:S(2)}, u32[]{:S(2)}) collective-permute-start(bf16[2,54,256]{2,1,0:T(8,128)(2,1)S(1)} %get-tuple-element.168), channel_id=1, source_target_pairs={{0,24},{4,28},{8,16},{12,20},{16,8},{20,12},{24,0},{28,4},{1,25},{... | collective-permute-start | bytes 165896 | tf_op jit(solution)/shard_map/ppermute | solution.py:681
  56.1 6.4 %collective-permute-start.24 = (bf16[2,54,256]{2,1,0:T(8,128)(2,1)S(1)}, bf16[2,54,256]{2,1,0:T(8,128)(2,1)S(1)}, u32[]{:S(2)}, u32[]{:S(2)}) collective-permute-start(bf16[2,54,256]{2,1,0:T(8,128)(2,1)S(1)} %get-tuple-element.178), channel_id=1, source_target_pairs={{0,16},{4,20},{8,24},{12,28},{16,0},{20,4},{24,8},{28,12},{1,17},{... | collective-permute-start | bytes 165896 | tf_op jit(solution)/shard_map/ppermute | solution.py:681
  56.5 5.9 %copy-start.1 = (f32[2,54,216]{2,0,1:T(2,128)S(1)}, f32[2,54,216]{2,0,1:T(2,128)}, u32[]{:S(2)}) copy-start(f32[2,54,216]{2,0,1:T(2,128)} %param.24) | copy-start | bytes 279940
  56.5 5.9 %copy-start.3 = (f32[2,54,216]{2,0,1:T(2,128)S(1)}, f32[2,54,216]{2,0,1:T(2,128)}, u32[]{:S(2)}) copy-start(f32[2,54,216]{2,0,1:T(2,128)} %param.25) | copy-start | bytes 279940
  56.5 5.9 %copy-start.4 = (f32[2,54,216]{2,0,1:T(2,128)S(1)}, f32[2,54,216]{2,0,1:T(2,128)}, u32[]{:S(2)}) copy-start(f32[2,54,216]{2,0,1:T(2,128)} %param.26) | copy-start | bytes 279940
  56.6 5.9 %copy-start.6 = (f32[9,216]{1,0:T(8,128)S(1)}, f32[9,216]{1,0:T(8,128)}, u32[]{:S(2)}) copy-start(f32[9,216]{1,0:T(8,128)} %refs_14_.1) | copy-start | bytes 23332
  56.6 5.9 %copy-start.7 = (f32[9,216]{1,0:T(8,128)S(1)}, f32[9,216]{1,0:T(8,128)}, u32[]{:S(2)}) copy-start(f32[9,216]{1,0:T(8,128)} %refs_15_.1) | copy-start | bytes 23332
  56.6 5.9 %copy-start.8 = (f32[2,12,12]{2,0,1:T(2,128)S(1)}, f32[2,12,12]{2,0,1:T(2,128)}, u32[]{:S(2)}) copy-start(f32[2,12,12]{2,0,1:T(2,128)} %param.31) | copy-start | bytes 3460
  56.6 5.9 %copy-start.9 = (f32[2,12,12]{2,0,1:T(2,128)S(1)}, f32[2,12,12]{2,0,1:T(2,128)}, u32[]{:S(2)}) copy-start(f32[2,12,12]{2,0,1:T(2,128)} %param.32) | copy-start | bytes 3460
  56.6 5.9 %copy-start.11 = (f32[4,216]{1,0:T(4,128)S(1)}, f32[4,216]{1,0:T(4,128)}, u32[]{:S(2)}) copy-start(f32[4,216]{1,0:T(4,128)} %refs_8_.1) | copy-start | bytes 10372
  56.6 5.9 %copy-start.12 = (f32[4,216]{1,0:T(4,128)S(1)}, f32[4,216]{1,0:T(4,128)}, u32[]{:S(2)}) copy-start(f32[4,216]{1,0:T(4,128)} %refs_9_.1) | copy-start | bytes 10372
  56.6 5.8 %collective-permute-start.23 = (bf16[2,54,256]{2,1,0:T(8,128)(2,1)S(1)}, bf16[2,54,256]{2,1,0:T(8,128)(2,1)S(1)}, u32[]{:S(2)}, u32[]{:S(2)}) collective-permute-start(bf16[2,54,256]{2,1,0:T(8,128)(2,1)S(1)} %get-tuple-element.177), channel_id=1, source_target_pairs={{0,8},{4,12},{8,0},{12,4},{16,24},{20,28},{24,16},{28,20},{1,9},{5... | collective-permute-start | bytes 165896 | tf_op jit(solution)/shard_map/ppermute | solution.py:681

commit v9 on v8

--- a/solution.py
+++ b/solution.py
@@ -62,7 +62,9 @@
     return (part ^ place) * 3 + (head - 3 * part)
 
 
-def prep_kernel(scal, tok_ref, cot_ref, norm_ref, talk_ref, x_ref, a_ref, dy_ref, mix_ref, bias_ref, tmp_ref):
+def prep_kernel(
+    scal, tok_ref, cot_ref, norm_ref, talk_ref, x_ref, a_ref, dy_ref, mix_ref, bias_ref, keep_ref, ex_ref, el_ref, tmp_ref
+):
     x_ref[...] = jnp.zeros_like(x_ref)
     dy_ref[...] = jnp.zeros_like(dy_ref)
     valid = (scal[0] < scal[1]).astype(f32)
@@ -88,6 +90,15 @@
                 both.append(nt(nt(ex, part).astype(bf16), el))
         mix_ref[i] = (both[0] + both[1]) * (HD**-0.5 if i == 0 else 1.0)
     bias_ref[...] = jnp.where(real_rows(bias_ref.shape), 0.0, -1e30)
+    lanes = lane_head((1, 256), 1, scal[0])
+    keep_ref[0:1, :] = ((lanes >= 0) & (lanes < scal[2])).astype(f32)
+    lane = iota((1, 256), 1)
+    for k in range(keep_ref.shape[0] - 2):
+        unit = ((k ^ scal[0]) * 4 + (lane >> 6)) * 54 + (lane & 63)
+        keep_ref[1 + k : 2 + k, :] = (unit < scal[3]).astype(f32)
+    keep_ref[keep_ref.shape[0] - 1 :, :] = jnp.broadcast_to(valid, (1, 256))
+    ex_ref[...] = ex
+    el_ref[...] = el
 
 
 def load_weight(dst_ref, w_refs, b):
@@ -103,7 +114,7 @@
     return jnp.sum(rows.reshape(heads, PITCH, rows.shape[1]), axis=0)
 
 
-def attn_fwd_kernel(scal, x_ref, a_ref, mix_ref, bias_ref, *refs, parts):
+def attn_fwd_kernel(x_ref, a_ref, mix_ref, bias_ref, keep_ref, *refs, parts):
     w_refs, refs = refs[:parts], refs[parts:]
     mid_ref, q_ref, k_ref, v_ref, o_ref, qw_ref, p_ref, pv_ref, ws_ref, t_ref = refs
     heads = mix_ref.shape[1] // PITCH
@@ -113,8 +124,7 @@
         load_weight(ws_ref.at[b], w_refs, b)
         dst[...] = nt(a, ws_ref[b]).astype(bf16)
     load_weight(ws_ref.at[3], w_refs, 3)
-    head = lane_head((1, 256), 1, scal[0])
-    keep = ((head >= 0) & (head < scal[2])).astype(f32)
+    keep = keep_ref[0:1, :]
 
     n = heads * PITCH
     for y in range(SIDE):
@@ -193,14 +203,12 @@
             ref[half, pad : pad + tokens, :] = value[:, mine]
 
 
-def middle(scal, k, h_ref, d_ref, gate_ref, dh_ref, cv_ref, gcv_ref):
+def middle(keep, h_ref, d_ref, gate_ref, dh_ref, cv_ref, gcv_ref):
     tokens = gate_ref.shape[0]
     pad = MARGIN
     for half in range(2):
         cols = slice(128 * half, 128 * (half + 1))
-        lane = iota((1, 128), 1) + 128 * half
-        unit = ((k ^ scal[0]) * 4 + (lane >> 6)) * 54 + (lane & 63)
-        keep = (unit < scal[3]).astype(f32)
+        on = keep[:, cols]
         act = None
         for t in range(9):
             off = pad + PITCH * (t // 3 - 1) + t % 3 - 1
@@ -208,8 +216,8 @@
             act = term if act is None else act + term
         sig = 0.5 * jnp.tanh(0.5 * act) + 0.5
         silu = act * sig
-        gate_ref[:, cols] = (silu * keep).astype(bf16)
-        dact = d_ref[half, pad : pad + tokens, :] * keep * (silu + sig * (1.0 - silu))
+        gate_ref[:, cols] = (silu * on).astype(bf16)
+        dact = d_ref[half, pad : pad + tokens, :] * on * (silu + sig * (1.0 - silu))
         d_ref[half, pad : pad + tokens, :] = dact
         dh = None
         for t in range(9):
@@ -222,7 +230,7 @@
         dh_ref[:, cols] = dh.astype(bf16)
 
 
-def ffn_first_kernel(scal, mid_ref, dy_ref, norm_ref, *refs, parts):
+def ffn_first_kernel(mid_ref, dy_ref, norm_ref, keep_ref, *refs, parts):
     w_refs, refs = refs[:parts], refs[parts:]
     z_ref, inv_ref, w_ref, e_ref, win_ref, wdn_ref, gate_ref, dh_ref, gcv_ref, h_ref, d_ref, cv_ref = refs
     z, inv = ln_stats(mid_ref[...])
@@ -236,12 +244,12 @@
         up(w_refs[k], w, e, win_ref.at[k], wdn_ref.at[k], h_ref.at[k], d_ref.at[k], cv_ref.at[k])
     for k in range(parts):
         middle(
-            scal, k, h_ref.at[k], d_ref.at[k], gate_ref.at[k], dh_ref.at[k], cv_ref.at[k], gcv_ref.at[k]
+            keep_ref[1 + k : 2 + k, :], h_ref.at[k], d_ref.at[k], gate_ref.at[k], dh_ref.at[k], cv_ref.at[k], gcv_ref.at[k]
         )
 
 
 def ffn_last_kernel(
-    scal, mid_ref, dy_ref, norm_ref, o_ref, z_ref, inv_ref, w_ref, e_ref, *refs, parts, late
+    mid_ref, dy_ref, norm_ref, keep_ref, o_ref, z_ref, inv_ref, w_ref, e_ref, *refs, parts, late
 ):
     early = parts - late
     wins, wdns, gates, dhs, gcvs = refs[:5]
@@ -269,10 +277,10 @@
         back(h)
     for i in range(late):
         middle(
-            scal, early + i, h_ref.at[i], d_ref.at[i], gate_ref.at[i], dh_ref.at[i], cv_ref.at[i], gcv_ref.at[i]
+            keep_ref[1 + early + i : 2 + early + i, :], h_ref.at[i], d_ref.at[i], gate_ref.at[i], dh_ref.at[i], cv_ref.at[i], gcv_ref.at[i]
         )
     dw_ref[...] = sum(nn(dhs[h][...], wins[h][...]) for h in range(parts))
-    valid = (scal[0] < scal[1]).astype(f32)
+    valid = keep_ref[parts + 1 : parts + 2, 0:1]
     tmp_ref[...] = (mid_ref[...] + sum(nn(gates[h][...], wdns[h][...]) for h in range(parts))) * valid
     free = iota((54, 256), 1) >= FREE
     pm = place(256)
@@ -296,7 +304,7 @@
 
 
 def scores_back_kernel(
-    scal, dmid_ref, mix_ref, q_ref, k_ref, v_ref, qw_ref, p_ref, pv_ref, *refs, parts, part
+    dmid_ref, mix_ref, keep_ref, ex_ref, el_ref, q_ref, k_ref, v_ref, qw_ref, p_ref, pv_ref, *refs, parts, part
 ):
     heads = mix_ref.shape[1] // PITCH
     n = heads * PITCH
@@ -306,8 +314,7 @@
         wo_ref[...] = jnp.zeros_like(wo_ref)
         load_weight(wo_ref, w_refs, 3)
         f = dmid_ref[...].astype(bf16)
-        head = lane_head((1, 256), 1, scal[0])
-        keep = ((head >= 0) & (head < scal[2])).astype(f32)
+        keep = keep_ref[0:1, :]
         do_ref[...] = (nt(f, wo_ref[...]) * keep).astype(bf16)
         for ref in (gk_ref, gv_ref, g0_ref, g1_ref):
             ref[...] = jnp.zeros_like(ref)
@@ -350,8 +357,7 @@
         return
     gkb_ref[...] = gk_ref[...].astype(bf16)
     gvb_ref[...] = gv_ref[...].astype(bf16)
-    ex = (true_head(iota((n, heads), 0), scal[0]) == iota((n, heads), 1)).astype(bf16)
-    el = (lane_head((256, heads), 0, scal[0]) == iota((256, heads), 1)).astype(bf16)
+    ex, el = ex_ref[...], el_ref[...]
     for i, ref in enumerate((g0_ref, g1_ref)):
         hi, lo = split2(ref[...])
         hi, lo = split2(nn(hi, el) + nn(lo, el))
@@ -362,7 +368,7 @@
 
 
 def weights_back_kernel(
-    scal, x_ref, a_ref, dmid_ref, norm_ref, gn2_ref, gqa_ref, gqb_ref, gk_ref, gv_ref, gt_ref, y_ref, *refs, parts
+    x_ref, a_ref, dmid_ref, norm_ref, gn2_ref, gqa_ref, gqb_ref, gk_ref, gv_ref, gt_ref, y_ref, *refs, parts
 ):
     w_refs, refs = refs[:parts], refs[parts:]
     both_ref, gw_refs, refs = refs[0], refs[1 : 1 + parts], refs[1 + parts :]
@@ -570,7 +576,7 @@
     )
 
 
-def prep(scal, tokens, cotangent, norm_params, talk):
+def prep(scal, tokens, cotangent, norm_params, talk, parts):
     tok, dim = tokens.shape[1], tokens.shape[2]
     pad = SIDE * PITCH
     heads = talk.shape[1]
@@ -587,51 +593,53 @@
                 full(*norm_params.shape),
                 full(*talk.shape),
             ],
-            out_specs=[full(pad, dim), full(pad, dim), full(pad, dim), full(2, n, 256), full(pad, 128)],
+            out_specs=[full(pad, dim), full(pad, dim), full(pad, dim), full(2, n, 256), full(pad, 128),
+                full(parts + 2, 256), full(n, heads), full(256, heads),
+            ],
             scratch_shapes=[pltpu.VMEM((tok, dim), f32)],
         ),
         out_shape=[SDS((pad, dim), f32), SDS((pad, dim), bf16), SDS((pad, dim), f32), SDS((2, n, 256), f32),
-                   SDS((pad, 128), f32)],
+                   SDS((pad, 128), f32), SDS((parts + 2, 256), f32), SDS((n, heads), bf16), SDS((256, heads), bf16)],
         compiler_params=pltpu.CompilerParams(vmem_limit_bytes=16 << 20),
         cost_estimate=pl.CostEstimate(flops=1000000000, transcendentals=0, bytes_accessed=3000000),
         name="prep",
     )(scal, tokens, cotangent, norm_params, talk)
 
 
-def attn_fwd(scal, x, a, mix, bias, w):
+def attn_fwd(x, a, mix, bias, keep, w):
     pad, dim = x.shape
     n = mix.shape[1]
     grid = (len(bunches(0, SIDE)), pad, n * BUNCH)
     return call(
-        attn_fwd_kernel, "attn_fwd", 1, 4 + len(w),
+        attn_fwd_kernel, "attn_fwd", 0, 5 + len(w),
         [SDS((pad, dim), f32)] + [SDS((pad, 256), bf16)] * 4
         + [SDS((SIDE * n, 256), bf16), SDS(grid, bf16), SDS((SIDE * n, 256), bf16)],
         [pltpu.VMEM((4, 256, dim), bf16), pltpu.VMEM(grid, f32)],
         mb=24, micros=1, parts=len(w),
-    )(scal, x, a, mix, bias, *w)
-
-
-def ffn_first(scal, mid, dy, norm_params, w):
+    )(x, a, mix, bias, keep, *w)
+
+
+def ffn_first(mid, dy, norm_params, keep, w):
     pad, dim = mid.shape
     count = len(w)
     lanes = [(count, 256, dim)] * 2 + [(count, pad, 256)] * 2
     grids = [pltpu.VMEM((count, 2, pad + 2 * MARGIN, 128), f32)] * 2
     return call(
-        ffn_first_kernel, "ffn_first", 1, 3 + count,
+        ffn_first_kernel, "ffn_first", 0, 4 + count,
         [SDS((pad, dim), f32), SDS((pad, 128), f32), SDS((pad, dim), bf16), SDS((pad, dim), bf16)]
         + [SDS(t, bf16) for t in lanes] + [SDS((count, 9, 256), f32)],
         grids + [pltpu.VMEM((count, 9, 256), f32)],
         mb=24, micros=3, parts=count,
-    )(scal, mid, dy, norm_params, *w)
-
-
-def ffn_last(scal, mid, dy, norm_params, o, first, w):
+    )(mid, dy, norm_params, keep, *w)
+
+
+def ffn_last(mid, dy, norm_params, keep, o, first, w):
     pad, dim = mid.shape
     late = len(w)
     parts = first[4].shape[0] + late
     grids = [pltpu.VMEM((late, 2, pad + 2 * MARGIN, 128), f32)] * 2
     return call(
-        ffn_last_kernel, "ffn_last", 1, 13 + late,
+        ffn_last_kernel, "ffn_last", 0, 14 + late,
         [SDS((SIDE * SIDE, dim), bf16), SDS((pad, dim), f32), SDS((8, dim), f32)] + [SDS((9, 54, 256), bf16)] * parts,
         [pltpu.VMEM((late, 256, dim), bf16)] * 2 + [pltpu.VMEM((late, pad, 256), bf16)] * 2
         + [pltpu.VMEM((late, 9, 256), f32)] + grids
@@ -640,10 +648,10 @@
             pltpu.VMEM((pad, dim), f32),
         ],
         mb=24, micros=4, parts=parts, late=late,
-    )(scal, mid, dy, norm_params, o, *first, *w)
-
-
-def scores_back(scal, dmid, mix, q, k, v, qw, p, pv, more, part):
+    )(mid, dy, norm_params, keep, o, *first, *w)
+
+
+def scores_back(dmid, mix, keep, ex, el, q, k, v, qw, p, pv, more, part):
     pad, dim = dmid.shape
     n = mix.shape[1]
     heads = n // PITCH
@@ -661,20 +669,20 @@
         pltpu.VMEM((-(-count // BUNCH), pad, n * BUNCH), bf16),
     ]
     return call(
-        scores_back_kernel, "scores_back", 1, 8 + len(more), outs, scratch,
+        scores_back_kernel, "scores_back", 0, 11 + len(more), outs, scratch,
         mb=24, micros=4, parts=len(more), part=part,
-    )(scal, dmid, mix, q, k, v, qw, p, pv, *more)
-
-
-def weights_back(scal, x, a, dmid, norm_params, gn2, gqa, gqb, gk, gv, gt, out, w):
+    )(dmid, mix, keep, ex, el, q, k, v, qw, p, pv, *more)
+
+
+def weights_back(x, a, dmid, norm_params, gn2, gqa, gqb, gk, gv, gt, out, w):
     pad, dim = x.shape
     return call(
-        weights_back_kernel, "weights_back", 1, 11 + len(w),
+        weights_back_kernel, "weights_back", 0, 11 + len(w),
         [SDS((2, SIDE * SIDE, dim), bf16)] + [SDS((3, 54, 256), bf16)] * len(w),
         [pltpu.VMEM((3, 256, dim), bf16), pltpu.VMEM((pad, dim), f32), pltpu.VMEM((24, 256), f32),
          pltpu.VMEM((56, 256), f32)],
         mb=24, micros=3, parts=len(w),
-    )(scal, x, a, dmid, norm_params, gn2, gqa, gqb, gk, gv, gt, out, *w)
+    )(x, a, dmid, norm_params, gn2, gqa, gqb, gk, gv, gt, out, *w)
 
 
 def permute(x, axis, k):
@@ -736,7 +744,7 @@
         *[apart[k] for k in range(1, pairs)]
     )
     far_other = permute(far_own, "dp", 1)
-    x, a, dy, mix, bias = prep(scal, tokens, cotangent, norm_params, talk_in)
+    x, a, dy, mix, bias, keep, ex, el = prep(scal, tokens, cotangent, norm_params, talk_in, parts)
     far_other, x = lax.optimization_barrier((far_other, x))
     attn_w, ffn_w = call(
         select_kernel, "select", 2, 5, [SDS((4, rows, dim), bf16), SDS((9, rows, dim), bf16)],
@@ -746,19 +754,19 @@
     attn_3 = permute(attn_2, "head", 1)
     attn_w = [attn_w, attn_1, attn_2, attn_3]
     ffn_2, ffn_1 = permute(ffn_w, "head", 2), permute(ffn_w, "head", 1)
-    mid, q, k, v, o, qw, p, pv = attn_fwd(scal, x, a, mix, bias, attn_w)
+    mid, q, k, v, o, qw, p, pv = attn_fwd(x, a, mix, bias, keep, attn_w)
     mid, ffn_2 = lax.optimization_barrier((mid, ffn_2))
     ffn_3 = permute(ffn_2, "head", 1)
-    first = list(ffn_first(scal, mid, dy, norm_params, [ffn_w, ffn_1]))
+    first = list(ffn_first(mid, dy, norm_params, keep, [ffn_w, ffn_1]))
     first[0], ffn_3 = lax.optimization_barrier((first[0], ffn_3))
-    out, dmid, gn2, *ffn_g = ffn_last(scal, mid, dy, norm_params, o, first, [ffn_2, ffn_3])
+    out, dmid, gn2, *ffn_g = ffn_last(mid, dy, norm_params, keep, o, first, [ffn_2, ffn_3])
     ffn_1, ffn_3 = permute(ffn_g[1], "head", 1), permute(ffn_g[3], "head", 1)
-    do, gqa, *sums = scores_back(scal, dmid, mix, q, k, v, qw, p, pv, attn_w, 0)
+    do, gqa, *sums = scores_back(dmid, mix, keep, ex, el, q, k, v, qw, p, pv, attn_w, 0)
     do, ffn_1, ffn_3 = lax.optimization_barrier((do, ffn_1, ffn_3))
     (summed,) = call(half_sum_kernel, "half_sum", 0, 2, [SDS(ffn_3.shape, bf16)])(ffn_g[2], ffn_3)
     ffn_2 = permute(summed, "head", 2)
-    gqb, gk, gv, gt = scores_back(scal, dmid, mix, q, k, v, qw, p, pv, [do, *sums], 1)
-    both, *attn_g = weights_back(scal, x, a, dmid, norm_params, gn2, gqa, gqb, gk, gv, gt, out, attn_w)
+    gqb, gk, gv, gt = scores_back(dmid, mix, keep, ex, el, q, k, v, qw, p, pv, [do, *sums], 1)
+    both, *attn_g = weights_back(x, a, dmid, norm_params, gn2, gqa, gqb, gk, gv, gt, out, attn_w)
     attn_1, attn_3 = permute(attn_g[1], "head", 1), permute(attn_g[3], "head", 1)
     (summed,) = call(half_sum_kernel, "half_sum", 0, 2, [SDS(attn_3.shape, bf16)])(attn_g[2], attn_3)
     attn_2 = permute(summed, "head", 2)

time: 63.8 us -> 61.2 us (0.959)
  Pallas kernels: 19.6 us -> 16.5 us
    pallas_call x6, Pallas kernels: 13.1 us -> 9.94 us  [the longest x2 3.32 us: scores_back(): call(scores_back_kernel, 'scores_back', 0, 11 + len(more), outs, scratch,...]
  transfers between devices with their start and end apart: 25 -> 25, of which waited for: 13 -> 13; matrix products, arithmetic and copies ran while one was open for 0% -> 0% of each run, Pallas kernels for 23% -> 20%
where the time goes in v9:
time: 61.2 us; the launch traced here: 61 us
  starting transfers between devices  22.5 us (37%)
  waiting for transfers between devices  17.8 us (29%)
  Pallas kernels  16.5 us (27%)
  between operations  2.95 us (5%)
  local copies, waits for them, and re-layouts  1.27 us (2%)
    ppermute x25, starting transfers between devices, permute(): lax.ppermute(x, axis, [(i, i ^ k) for i in range(lax.axis_size(axis))])  22.5 us
    ppermute x25, waiting for transfers between devices, permute(): lax.ppermute(x, axis, [(i, i ^ k) for i in range(lax.axis_size(axis))])  17.8 us
    pallas_call x2, Pallas kernels, scores_back(): call(scores_back_kernel, 'scores_back', 0, 11 + len(more), outs, scratch,...  3.32 us
    pallas_call x1, Pallas kernels, ffn_last(): call(ffn_last_kernel, 'ffn_last', 0, 14 + late, [SDS((SIDE * SIDE, dim),...  2.33 us
    pallas_call x1, Pallas kernels, attn_fwd(): call(attn_fwd_kernel, 'attn_fwd', 0, 5 + len(w), [SDS((pad, dim), f32)] +...  2.12 us
    pallas_call x1, Pallas kernels, local(): pl.pallas_call(assemble_kernel, grid=(1,), in_specs=[SM] + [whole(*both.s...  1.99 us
    pallas_call x1, Pallas kernels, ffn_first(): call(ffn_first_kernel, 'ffn_first', 0, 4 + count, [SDS((pad, dim), f32),...  1.57 us
  transfers between devices with their start and end apart: 25, of which 13 were waited for; matrix products, arithmetic and copies ran while one was open for 0% of the time, Pallas kernels for 20%

profile of v9, /device:TPU:0, one launch (start us, length us, event | category | flops | bytes accessed | tf_op | source)
XLA Modules:
  0.0 61.0 jit_solution(8009544409232144378)
XLA Ops:
  0.7 0.9 %copy-done = f32[2,54,216]{2,0,1:T(2,128)S(1)} copy-done((f32[2,54,216]{2,0,1:T(2,128)S(1)}, f32[2,54,216]{2,0,1:T(2,128)}, u32[]{:S(2)}) %copy-start) | copy-done | bytes 93336
  1.5 0.2 cast.1.refs_0_
  1.8 4.1 %collective-permute-start.2 = (bf16[2,54,216]{2,1,0:T(8,128)(2,1)S(1)}, bf16[2,54,216]{2,1,0:T(8,128)(2,1)S(1)}, u32[]{:S(2)}, u32[]{:S(2)}) collective-permute-start(bf16[2,54,216]{2,1,0:T(8,128)(2,1)S(1)} %cast.1.refs_0_), channel_id=1, source_target_pairs={{0,16},{4,20},{8,24},{12,28},{16,0},{20,4},{24,8},{28,12},{1,17},{... | collective-permute-start | bytes 139976 | tf_op jit(solution)/shard_map/ppermute | solution.py:689
  5.9 1.5 %collective-permute-start.1 = (bf16[2,54,216]{2,1,0:T(8,128)(2,1)S(1)}, bf16[2,54,216]{2,1,0:T(8,128)(2,1)S(1)}, u32[]{:S(2)}, u32[]{:S(2)}) collective-permute-start(bf16[2,54,216]{2,1,0:T(8,128)(2,1)S(1)} %cast.1.refs_0_), channel_id=1, source_target_pairs={{0,4},{4,0},{8,12},{12,8},{16,20},{20,16},{24,28},{28,24},{1,5},{5... | collective-permute-start | bytes 139976 | tf_op jit(solution)/shard_map/ppermute | solution.py:689
  7.4 1.6 %collective-permute-start = (bf16[2,54,216]{2,1,0:T(8,128)(2,1)S(1)}, bf16[2,54,216]{2,1,0:T(8,128)(2,1)S(1)}, u32[]{:S(2)}, u32[]{:S(2)}) collective-permute-start(bf16[2,54,216]{2,1,0:T(8,128)(2,1)S(1)} %cast.1.refs_0_), channel_id=1, source_target_pairs={{0,8},{4,12},{8,0},{12,4},{16,24},{20,28},{24,16},{28,20},{1,9},{5... | collective-permute-start | bytes 139976 | tf_op jit(solution)/shard_map/ppermute | solution.py:689
  9.0 0.2 collective-permute-start.3
  9.2 0.9 %collective-permute-done.1.refs_2_ = bf16[2,54,216]{2,1,0:T(8,128)(2,1)S(1)} collective-permute-done((bf16[2,54,216]{2,1,0:T(8,128)(2,1)S(1)}, bf16[2,54,216]{2,1,0:T(8,128)(2,1)S(1)}, u32[]{:S(2)}, u32[]{:S(2)}) %collective-permute-start.1) | collective-permute-done | bytes 46688 | tf_op jit(solution)/shard_map/ppermute | solution.py:689
  10.1 1.5 %collective-permute-done.refs_0_ = bf16[2,54,216]{2,1,0:T(8,128)(2,1)S(1)} collective-permute-done((bf16[2,54,216]{2,1,0:T(8,128)(2,1)S(1)}, bf16[2,54,216]{2,1,0:T(8,128)(2,1)S(1)}, u32[]{:S(2)}, u32[]{:S(2)}) %collective-permute-start) | collective-permute-done | bytes 46688 | tf_op jit(solution)/shard_map/ppermute | solution.py:689
  11.6 3.4 %collective-permute-done.3.refs_2_ = bf16[2,54,216]{2,1,0:T(8,128)(2,1)S(1)} collective-permute-done((bf16[2,54,216]{2,1,0:T(8,128)(2,1)S(1)}, bf16[2,54,216]{2,1,0:T(8,128)(2,1)S(1)}, u32[]{:S(2)}, u32[]{:S(2)}) %collective-permute-start.3) | collective-permute-done | bytes 46688 | tf_op jit(solution)/shard_map/ppermute | solution.py:689
  15.0 0.6 collective-permute-start.4
  17.7 0.2 copy.34.cot_ref
  17.9 1.1 %prep.1 = (f32[224,216]{1,0:T(8,128)S(1)}, bf16[224,216]{1,0:T(8,128)(2,1)S(1)}, f32[224,216]{1,0:T(8,128)S(1)}, f32[2,192,256]{2,1,0:T(8,128)S(1)}, f32[224,128...) custom-call(s32[6]{0:T(128)S(1)} %concatenate.3.scal, ...), custom_call_target="tpu_custom_call" | custom-call | flops 1000000000 | bytes 3000000 | tf_op jit(solution)/shard_map/prep/pallas_call | solution.py:585
  19.0 1.4 %collective-permute-done.4.refs_3_ = bf16[3,2,54,216]{3,2,1,0:T(8,128)(2,1)S(1)} collective-permute-done((bf16[3,2,54,216]{3,2,1,0:T(8,128)(2,1)S(1)}, bf16[3,2,54,216]{3,2,1,0:T(8,128)(2,1)S(1)}, u32[]{:S(2)}, u32[]{:S(2)}) %collective-permute-start.4) | collective-permute-done | bytes 140000 | tf_op jit(solution)/shard_map/ppermute | solution.py:689
  20.5 0.6 %select.7 = (bf16[4,54,216]{2,1,0:T(8,128)(2,1)S(1)}, bf16[9,54,216]{2,1,0:T(8,128)(2,1)S(1)}) custom-call(s32[12]{0:T(128)S(1)} %copy-done.13, s32[6]{0:T(128)S(1)} %concatenate.3.scal, f32[9,216]{1,0:T(8,128)S(1)} %copy-done.5, bf16[2,54,216]{2,1,0:T(8,128)(2,1)S(1)} %cast.1.refs_0_, bf16[3,2,54,216]{3,2,1,0:T(8,128)(2,1)S(1)} %stack.1.refs_1_, ...), custom_call_target="tpu_custom_call" | custom-call | flops 1000000000 | bytes 3000000 | tf_op jit(solution)/shard_map/select/pallas_call | solution.py:749
  21.1 1.6 %collective-permute-start.6 = (bf16[4,54,216]{2,1,0:T(8,128)(2,1)S(1)}, bf16[4,54,216]{2,1,0:T(8,128)(2,1)S(1)}, u32[]{:S(2)}, u32[]{:S(2)}) collective-permute-start(bf16[4,54,216]{2,1,0:T(8,128)(2,1)S(1)} %get-tuple-element.120.refs_0_), channel_id=1, source_target_pairs={{0,2},{1,3},{2,0},{3,1},{4,6},{5,7},{6,4},{7,5},{8,10},{9,11},{10,... | collective-permute-start | bytes 279944 | tf_op jit(solution)/shard_map/ppermute | solution.py:689
  22.7 0.5 collective-permute-start.8
  23.2 0.5 collective-permute-start.5
  23.7 2.3 %collective-permute-done.6.refs_2_ = bf16[4,54,216]{2,1,0:T(8,128)(2,1)S(1)} collective-permute-done((bf16[4,54,216]{2,1,0:T(8,128)(2,1)S(1)}, bf16[4,54,216]{2,1,0:T(8,128)(2,1)S(1)}, u32[]{:S(2)}, u32[]{:S(2)}) %collective-permute-start.6) | collective-permute-done | bytes 93344 | tf_op jit(solution)/shard_map/ppermute | solution.py:689
  26.0 1.3 %collective-permute-done.7.refs_3_ = bf16[4,54,216]{2,1,0:T(8,128)(2,1)S(1)} collective-permute-done((bf16[4,54,216]{2,1,0:T(8,128)(2,1)S(1)}, bf16[4,54,216]{2,1,0:T(8,128)(2,1)S(1)}, u32[]{:S(2)}, u32[]{:S(2)}) %collective-permute-start.7) | collective-permute-done | bytes 93344 | tf_op jit(solution)/shard_map/ppermute | solution.py:689
  27.3 2.1 %attn_fwd.1 = (f32[224,216]{1,0:T(8,128)S(1)}, bf16[224,256]{1,0:T(8,128)(2,1)S(1)}, bf16[224,256]{1,0:T(8,128)(2,1)S(1)}, bf16[224,256]{1,0:T(8,128)(2,1)S(1)},...) custom-call(f32[224,216]{1,0:T(8,128)S(1)} %get-tuple-element.113.x_, ...), custom_call_target="tpu_custom_call" | custom-call | flops 1000000000 | bytes 3000000 | tf_op jit(solution)/shard_map/attn_fwd/pallas_call | solution.py:613
  29.4 0.2 collective-permute-start.10
  29.6 1.6 %ffn_first.1 = (f32[224,216]{1,0:T(8,128)S(1)}, f32[224,128]{1,0:T(8,128)S(1)}, bf16[224,216]{1,0:T(8,128)(2,1)S(1)}, bf16[224,216]{1,0:T(8,128)(2,1)S(1)}, bf16...) custom-call(f32[224,216]{1,0:T(8,128)S(1)} %get-tuple-element.123.mi, ...), custom_call_target="tpu_custom_call" | custom-call | flops 3000000000 | bytes 9000000 | tf_op jit(solution)/shard_map/ffn_first/pallas_call | solution.py:627
  31.2 2.3 %ffn_last.1 = (bf16[196,216]{1,0:T(8,128)(2,1)S(1)}, f32[224,216]{1,0:T(8,128)S(1)}, f32[8,216]{1,0:T(8,128)S(1)}, bf16[9,54,256]{2,1,0:T(8,128)(2,1)S(1)}, bf16...) custom-call(f32[224,216]{1,0:T(8,128)S(1)} %get-tuple-element.123.mid_ref, ...), custom_call_target="tpu_custom_call" | custom-call | flops 4000000000 | bytes 12000000 | tf_op jit(solution)/shard_map/ffn_last/pallas_call | solution.py:641
  33.6 0.4 collective-permute-start.11
  34.0 0.2 collective-permute-start.12
  34.1 1.0 %scores_back.2 = (bf16[224,256]{1,0:T(8,128)(2,1)S(1)}, bf16[64,256]{1,0:T(8,128)(2,1)S(1)}, f32[224,256]{1,0:T(8,128)S(1)}, f32[224,256]{1,0:T(8,128)S(1)}, f32...) custom-call(f32[224,216]{1,0:T(8,128)S(1)} %get-tuple-element.138.dmid_ref, f32[2,192,256]{2,1,0:T(8,128)S(1)} %get-tuple-element.115.mix_ref, ...), custom_call_target="tpu_custom_call" | custom-call | flops 4000000000 | bytes 12000000 | tf_op jit(solution)/shard_map/scores_back/pallas_call | solution.py:671
  35.2 0.3 collective-permute-done.12.b_ref
  35.6 1.6 %collective-permute-start.13 = (bf16[9,54,256]{2,1,0:T(8,128)(2,1)S(1)}, bf16[9,54,256]{2,1,0:T(8,128)(2,1)S(1)}, u32[]{:S(2)}, u32[]{:S(2)}) collective-permute-start(bf16[9,54,256]{2,1,0:T(8,128)(2,1)S(1)} %half_sum.2), channel_id=1, source_target_pairs={{0,2},{1,3},{2,0},{3,1},{4,6},{5,7},{6,4},{7,5},{8,10},{9,11},{10,... | collective-permute-start | bytes 746504 | tf_op jit(solution)/shard_map/ppermute | solution.py:689
  37.2 2.3 %scores_back.3 = (bf16[160,256]{1,0:T(8,128)(2,1)S(1)}, bf16[224,256]{1,0:T(8,128)(2,1)S(1)}, bf16[224,256]{1,0:T(8,128)(2,1)S(1)}, f32[2,12,12]{2,1,0:T(8,128)S(1)}) custom-call(f32[224,216]{1,0:T(8,128)S(1)} %get-tuple-element.138.dmid_ref, f32[2,192,256]{2,1,0:T(8,128)S(1)} %get-tuple-element.115.mix_ref, f32[6,256]{1,0:T(8,128)S(1)} %get-tuple-element.117.keep_ref, ...), custom_call_target="tpu_custom_call" | custom-call | flops 4000000000 | bytes 12000000 | tf_op jit(solution)/shard_map/scores_back/pallas_call | solution.py:671
  39.5 0.6 weights_back.1
  40.1 0.1 collective-permute-start.15
  40.2 0.4 collective-permute-start.14
  40.6 0.8 %collective-permute-done.15.b_ref = bf16[3,54,256]{2,1,0:T(8,128)(2,1)S(1)} collective-permute-done((bf16[3,54,256]{2,1,0:T(8,128)(2,1)S(1)}, bf16[3,54,256]{2,1,0:T(8,128)(2,1)S(1)}, u32[]{:S(2)}, u32[]{:S(2)}) %collective-permute-start.15) | collective-permute-done | bytes 82976 | tf_op jit(solution)/shard_map/ppermute | solution.py:689
  41.4 0.6 collective-permute-start.16
  42.0 2.1 %collective-permute-done.13.refs_2_ = bf16[9,54,256]{2,1,0:T(8,128)(2,1)S(1)} collective-permute-done((bf16[9,54,256]{2,1,0:T(8,128)(2,1)S(1)}, bf16[9,54,256]{2,1,0:T(8,128)(2,1)S(1)}, u32[]{:S(2)}, u32[]{:S(2)}) %collective-permute-start.13) | collective-permute-done | bytes 248864 | tf_op jit(solution)/shard_map/ppermute | solution.py:689
  44.1 0.7 %spread_ffn.1.old_ref = bf16[4,2,2,54,256]{4,3,2,1,0:T(8,128)(2,1)S(1)} custom-call(s32[12]{0:T(128)S(1)} %copy-done.13, s32[6]{0:T(128)S(1)} %concatenate.3.scal, bf16[9,54,256]{2,1,0:T(8,128)(2,1)S(1)} %get-tuple-element.163.refs_0_, bf16[9,54,256]{2,1,0:T(8,128)(2,1)S(1)} %collective-permute-done.11.refs_1_, ...), custom_call_target="tpu_custom_call" | custom-call | flops 1000000000 | bytes 3000000 | tf_op jit(solution)/shard_map/spread_ffn/pallas_call | solution.py:773
  44.8 2.1 %collective-permute-start.20 = (bf16[2,196,216]{2,1,0:T(8,128)(2,1)S(1)}, bf16[2,196,216]{2,1,0:T(8,128)(2,1)S(1)}, u32[]{:S(2)}, u32[]{:S(2)}) collective-permute-start(bf16[2,196,216]{2,1,0:T(8,128)(2,1)S(1)} %get-tuple-element.175.refs_0_), channel_id=1, source_target_pairs={{0,2},{1,3},{2,0},{3,1},{4,6},{5,7},{6,4},{7,5},{8,10},{9,11},{10,... | collective-permute-start | bytes 508040 | tf_op jit(solution)/shard_map/ppermute | solution.py:689
  47.0 0.7 %spread_attn.1 = (bf16[2,2,54,256]{3,2,1,0:T(8,128)(2,1)S(1)}, bf16[2,2,54,256]{3,2,1,0:T(8,128)(2,1)S(1)}, bf16[2,2,54,256]{3,2,1,0:T(8,128)(2,1)S(1)}, bf16[2,2,54,256]{3,2,1,0:T(8,128)(2,1)S(1)}) custom-call(s32[12]{0:T(128)S(1)} %copy-done.13, s32[6]{0:T(128)S(1)} %concatenate.3.scal, bf16[4,2,2,54,256]{4,3,2,1,0:T(8,128)(2,1)S(1)} %spread_ffn.1.old_ref, ...), custom_call_target="tpu_custom_call" | custom-call | flops 1000000000 | bytes 3000000 | tf_op jit(solution)/shard_map/spread_attn/pallas_call | solution.py:779
  47.7 0.8 %collective-permute-start.17 = (bf16[2,2,54,256]{3,2,1,0:T(8,128)(2,1)S(1)}, bf16[2,2,54,256]{3,2,1,0:T(8,128)(2,1)S(1)}, u32[]{:S(2)}, u32[]{:S(2)}) collective-permute-start(bf16[2,2,54,256]{3,2,1,0:T(8,128)(2,1)S(1)} %get-tuple-element.173), channel_id=1, source_target_pairs={{0,4},{4,0},{8,12},{12,8},{16,20},{20,16},{24,28},{28,24},{1,5},{5... | collective-permute-start | bytes 331784 | tf_op jit(solution)/shard_map/ppermute | solution.py:689
  48.4 1.3 %collective-permute-start.22 = (bf16[2,2,54,256]{3,2,1,0:T(8,128)(2,1)S(1)}, bf16[2,2,54,256]{3,2,1,0:T(8,128)(2,1)S(1)}, u32[]{:S(2)}, u32[]{:S(2)}) collective-permute-start(bf16[2,2,54,256]{3,2,1,0:T(8,128)(2,1)S(1)} %get-tuple-element.181), channel_id=1, source_target_pairs={{0,4},{4,0},{8,12},{12,8},{16,20},{20,16},{24,28},{28,24},{1,5},{5... | collective-permute-start | bytes 331784 | tf_op jit(solution)/shard_map/ppermute | solution.py:689
  49.7 1.7 %collective-permute-done.20.refs_2_ = bf16[2,196,216]{2,1,0:T(8,128)(2,1)S(1)} collective-permute-done((bf16[2,196,216]{2,1,0:T(8,128)(2,1)S(1)}, bf16[2,196,216]{2,1,0:T(8,128)(2,1)S(1)}, u32[]{:S(2)}, u32[]{:S(2)}) %collective-permute-start.20) | collective-permute-done | bytes 169376 | tf_op jit(solution)/shard_map/ppermute | solution.py:689
  51.4 1.3 %collective-permute-done.17.other_ref = bf16[2,2,54,256]{3,2,1,0:T(8,128)(2,1)S(1)} collective-permute-done((bf16[2,2,54,256]{3,2,1,0:T(8,128)(2,1)S(1)}, bf16[2,2,54,256]{3,2,1,0:T(8,128)(2,1)S(1)}, u32[]{:S(2)}, u32[]{:S(2)}) %collective-permute-start.17) | collective-permute-done | bytes 110624 | tf_op jit(solution)/shard_map/ppermute | solution.py:689
  52.7 0.8 %collective-permute-start.18 = (bf16[2,54,256]{2,1,0:T(8,128)(2,1)S(1)}, bf16[2,54,256]{2,1,0:T(8,128)(2,1)S(1)}, u32[]{:S(2)}, u32[]{:S(2)}) collective-permute-start(bf16[2,54,256]{2,1,0:T(8,128)(2,1)S(1)} %get-tuple-element.174), channel_id=1, source_target_pairs={{0,24},{4,28},{8,16},{12,20},{16,8},{20,12},{24,0},{28,4},{1,25},{... | collective-permute-start | bytes 165896 | tf_op jit(solution)/shard_map/ppermute | solution.py:689
  53.5 0.4 collective-permute-done.22.other_ref
  54.1 3.3 %collective-permute-start.23 = (bf16[2,54,256]{2,1,0:T(8,128)(2,1)S(1)}, bf16[2,54,256]{2,1,0:T(8,128)(2,1)S(1)}, u32[]{:S(2)}, u32[]{:S(2)}) collective-permute-start(bf16[2,54,256]{2,1,0:T(8,128)(2,1)S(1)} %get-tuple-element.183), channel_id=1, source_target_pairs={{0,8},{4,12},{8,0},{12,4},{16,24},{20,28},{24,16},{28,20},{1,9},{5... | collective-permute-start | bytes 165896 | tf_op jit(solution)/shard_map/ppermute | solution.py:689
  57.4 2.0 %assemble.1 = (f32[196,4,216]{2,1,0:T(4,128)}, f32[196,4,216]{2,1,0:T(4,128)}) custom-call(s32[6]{0:T(128)S(1)} %concatenate.3.scal, bf16[2,196,216]{2,1,0:T(8,128)(2,1)S(1)} %get-tuple-element.175.refs_0_, bf16[2,196,216]{2,1,0:T(8,128)(2,1)S(1)} %collective-permute-done.19.refs_1_, bf16[2,196,216]{2,1,0:T(8,128)(2,1)S(1)} %collective-permute-done.20.refs_2_, ...), custom_call_target="tpu_custom_call" | custom-call | flops 1000000000 | bytes 3000000 | tf_op jit(solution)/shard_map/assemble/pallas_call | solution.py:792
  59.4 0.4 collective-permute-done.24.refs_2_
  59.9 1.1 %update.1 = (f32[54,2,216]{2,1,0:T(2,128)}, f32[54,2,216]{2,1,0:T(2,128)}, f32[54,2,216]{2,1,0:T(2,128)}, bf16[54,2,216]{2,1,0:T(2,128)(2,1)}, f32[4,216]{1,0:T(...) custom-call(f32[2,54,256]{2,1,0:T(8,128)S(1)} %get-tuple-element.182, ...), custom_call_target="tpu_custom_call" | custom-call | flops 1000000000 | bytes 3000000 | tf_op jit(solution)/shard_map/update/pallas_call | solution.py:701
  (56 shorter events, 0.4 us)
Async XLA Ops:
  0.6 0.9 %copy-start = (f32[2,54,216]{2,0,1:T(2,128)S(1)}, f32[2,54,216]{2,0,1:T(2,128)}, u32[]{:S(2)}) copy-start(f32[2,54,216]{2,0,1:T(2,128)} %param.24) | copy-start | bytes 279940
  1.8 15.8 %copy-start.2 = (f32[2,12,12]{2,0,1:T(2,128)S(1)}, f32[2,12,12]{2,0,1:T(2,128)}, u32[]{:S(2)}) copy-start(f32[2,12,12]{2,0,1:T(2,128)} %param.30) | copy-start | bytes 3460
  1.8 15.8 %copy-start.15 = (bf16[4,196,216]{2,0,1:T(4,128)(2,1)S(1)}, bf16[4,196,216]{2,0,1:T(4,128)(2,1)}, u32[]{:S(2)}) copy-start(bf16[4,196,216]{2,0,1:T(4,128)(2,1)} %param.18) | copy-start | bytes 1016068
  1.8 7.4 %collective-permute-start.2 = (bf16[2,54,216]{2,1,0:T(8,128)(2,1)S(1)}, bf16[2,54,216]{2,1,0:T(8,128)(2,1)S(1)}, u32[]{:S(2)}, u32[]{:S(2)}) collective-permute-start(bf16[2,54,216]{2,1,0:T(8,128)(2,1)S(1)} %cast.1.refs_0_), channel_id=1, source_target_pairs={{0,16},{4,20},{8,24},{12,28},{16,0},{20,4},{24,8},{28,12},{1,17},{... | collective-permute-start | bytes 139976 | tf_op jit(solution)/shard_map/ppermute | solution.py:689
  5.9 4.2 %collective-permute-start.1 = (bf16[2,54,216]{2,1,0:T(8,128)(2,1)S(1)}, bf16[2,54,216]{2,1,0:T(8,128)(2,1)S(1)}, u32[]{:S(2)}, u32[]{:S(2)}) collective-permute-start(bf16[2,54,216]{2,1,0:T(8,128)(2,1)S(1)} %cast.1.refs_0_), channel_id=1, source_target_pairs={{0,4},{4,0},{8,12},{12,8},{16,20},{20,16},{24,28},{28,24},{1,5},{5... | collective-permute-start | bytes 139976 | tf_op jit(solution)/shard_map/ppermute | solution.py:689
  7.4 4.2 %collective-permute-start = (bf16[2,54,216]{2,1,0:T(8,128)(2,1)S(1)}, bf16[2,54,216]{2,1,0:T(8,128)(2,1)S(1)}, u32[]{:S(2)}, u32[]{:S(2)}) collective-permute-start(bf16[2,54,216]{2,1,0:T(8,128)(2,1)S(1)} %cast.1.refs_0_), channel_id=1, source_target_pairs={{0,8},{4,12},{8,0},{12,4},{16,24},{20,28},{24,16},{28,20},{1,9},{5... | collective-permute-start | bytes 139976 | tf_op jit(solution)/shard_map/ppermute | solution.py:689
  9.0 6.0 %collective-permute-start.3 = (bf16[2,54,216]{2,1,0:T(8,128)(2,1)S(1)}, bf16[2,54,216]{2,1,0:T(8,128)(2,1)S(1)}, u32[]{:S(2)}, u32[]{:S(2)}) collective-permute-start(bf16[2,54,216]{2,1,0:T(8,128)(2,1)S(1)} %cast.1.refs_0_), channel_id=1, source_target_pairs={{0,24},{4,28},{8,16},{12,20},{16,8},{20,12},{24,0},{28,4},{1,25},{... | collective-permute-start | bytes 139976 | tf_op jit(solution)/shard_map/ppermute | solution.py:689
  15.0 2.7 %copy-start.14 = (f32[4,196,216]{2,0,1:T(4,128)S(1)}, f32[4,196,216]{2,0,1:T(4,128)}, u32[]{:S(2)}) copy-start(f32[4,196,216]{2,0,1:T(4,128)} %param.19) | copy-start | bytes 2032132
  15.0 2.9 %copy-start.10 = (f32[4,216]{1,0:T(4,128)S(1)}, f32[4,216]{1,0:T(4,128)}, u32[]{:S(2)}) copy-start(f32[4,216]{1,0:T(4,128)} %refs_7_.1) | copy-start | bytes 10372
  15.0 5.5 %collective-permute-start.4 = (bf16[3,2,54,216]{3,2,1,0:T(8,128)(2,1)S(1)}, bf16[3,2,54,216]{3,2,1,0:T(8,128)(2,1)S(1)}, u32[]{:S(2)}, u32[]{:S(2)}) collective-permute-start(bf16[3,2,54,216]{3,2,1,0:T(8,128)(2,1)S(1)} %stack.1.refs_1_), channel_id=1, source_target_pairs={{0,4},{4,0},{8,12},{12,8},{16,20},{20,16},{24,28},{28,24},{1,5},{5... | collective-permute-start | bytes 419912 | tf_op jit(solution)/shard_map/ppermute | solution.py:689
  17.9 2.6 %copy-start.5 = (f32[9,216]{1,0:T(8,128)S(1)}, f32[9,216]{1,0:T(8,128)}, u32[]{:S(2)}) copy-start(f32[9,216]{1,0:T(8,128)} %refs_13_.1) | copy-start | bytes 23332
  17.9 2.6 %copy-start.13 = (s32[12]{0:T(128)S(1)}, s32[12]{0:T(128)}, u32[]{:S(2)}) copy-start(s32[12]{0:T(128)} %slot_ref.5) | copy-start | bytes 148
  21.1 4.9 %collective-permute-start.6 = (bf16[4,54,216]{2,1,0:T(8,128)(2,1)S(1)}, bf16[4,54,216]{2,1,0:T(8,128)(2,1)S(1)}, u32[]{:S(2)}, u32[]{:S(2)}) collective-permute-start(bf16[4,54,216]{2,1,0:T(8,128)(2,1)S(1)} %get-tuple-element.120.refs_0_), channel_id=1, source_target_pairs={{0,2},{1,3},{2,0},{3,1},{4,6},{5,7},{6,4},{7,5},{8,10},{9,11},{10,... | collective-permute-start | bytes 279944 | tf_op jit(solution)/shard_map/ppermute | solution.py:689
  22.7 6.7 %collective-permute-start.8 = (bf16[9,54,216]{2,1,0:T(8,128)(2,1)S(1)}, bf16[9,54,216]{2,1,0:T(8,128)(2,1)S(1)}, u32[]{:S(2)}, u32[]{:S(2)}) collective-permute-start(bf16[9,54,216]{2,1,0:T(8,128)(2,1)S(1)} %get-tuple-element.122.refs_0_), channel_id=1, source_target_pairs={{0,2},{1,3},{2,0},{3,1},{4,6},{5,7},{6,4},{7,5},{8,10},{9,11},{10,... | collective-permute-start | bytes 629864 | tf_op jit(solution)/shard_map/ppermute | solution.py:689
  23.2 6.5 %collective-permute-start.9 = (bf16[9,54,216]{2,1,0:T(8,128)(2,1)S(1)}, bf16[9,54,216]{2,1,0:T(8,128)(2,1)S(1)}, u32[]{:S(2)}, u32[]{:S(2)}) collective-permute-start(bf16[9,54,216]{2,1,0:T(8,128)(2,1)S(1)} %get-tuple-element.122.refs_0_), channel_id=1, source_target_pairs={{0,1},{1,0},{2,3},{3,2},{4,5},{5,4},{6,7},{7,6},{8,9},{9,8},{10,11... | collective-permute-start | bytes 629864 | tf_op jit(solution)/shard_map/ppermute | solution.py:689
  23.2 2.8 %collective-permute-start.5 = (bf16[4,54,216]{2,1,0:T(8,128)(2,1)S(1)}, bf16[4,54,216]{2,1,0:T(8,128)(2,1)S(1)}, u32[]{:S(2)}, u32[]{:S(2)}) collective-permute-start(bf16[4,54,216]{2,1,0:T(8,128)(2,1)S(1)} %get-tuple-element.120.refs_0_), channel_id=1, source_target_pairs={{0,1},{1,0},{2,3},{3,2},{4,5},{5,4},{6,7},{7,6},{8,9},{9,8},{10,11... | collective-permute-start | bytes 279944 | tf_op jit(solution)/shard_map/ppermute | solution.py:689
  26.0 1.3 %collective-permute-start.7 = (bf16[4,54,216]{2,1,0:T(8,128)(2,1)S(1)}, bf16[4,54,216]{2,1,0:T(8,128)(2,1)S(1)}, u32[]{:S(2)}, u32[]{:S(2)}) collective-permute-start(bf16[4,54,216]{2,1,0:T(8,128)(2,1)S(1)} %collective-permute-done.6.refs_2_), channel_id=1, source_target_pairs={{0,1},{1,0},{2,3},{3,2},{4,5},{5,4},{6,7},{7,6},{8,9},{9,8},{10,11... | collective-permute-start | bytes 279944 | tf_op jit(solution)/shard_map/ppermute | solution.py:689
  29.4 1.8 %collective-permute-start.10 = (bf16[9,54,216]{2,1,0:T(8,128)(2,1)S(1)}, bf16[9,54,216]{2,1,0:T(8,128)(2,1)S(1)}, u32[]{:S(2)}, u32[]{:S(2)}) collective-permute-start(bf16[9,54,216]{2,1,0:T(8,128)(2,1)S(1)} %collective-permute-done.8.refs_5_), channel_id=1, source_target_pairs={{0,1},{1,0},{2,3},{3,2},{4,5},{5,4},{6,7},{7,6},{8,9},{9,8},{10,11... | collective-permute-start | bytes 629864 | tf_op jit(solution)/shard_map/ppermute | solution.py:689
  33.6 1.6 %collective-permute-start.11 = (bf16[9,54,256]{2,1,0:T(8,128)(2,1)S(1)}, bf16[9,54,256]{2,1,0:T(8,128)(2,1)S(1)}, u32[]{:S(2)}, u32[]{:S(2)}) collective-permute-start(bf16[9,54,256]{2,1,0:T(8,128)(2,1)S(1)} %get-tuple-element.150), channel_id=1, source_target_pairs={{0,1},{1,0},{2,3},{3,2},{4,5},{5,4},{6,7},{7,6},{8,9},{9,8},{10,11... | collective-permute-start | bytes 746504 | tf_op jit(solution)/shard_map/ppermute | solution.py:689
  34.0 1.5 %collective-permute-start.12 = (bf16[9,54,256]{2,1,0:T(8,128)(2,1)S(1)}, bf16[9,54,256]{2,1,0:T(8,128)(2,1)S(1)}, u32[]{:S(2)}, u32[]{:S(2)}) collective-permute-start(bf16[9,54,256]{2,1,0:T(8,128)(2,1)S(1)} %get-tuple-element.151), channel_id=1, source_target_pairs={{0,1},{1,0},{2,3},{3,2},{4,5},{5,4},{6,7},{7,6},{8,9},{9,8},{10,11... | collective-permute-start | bytes 746504 | tf_op jit(solution)/shard_map/ppermute | solution.py:689
  35.6 8.5 %collective-permute-start.13 = (bf16[9,54,256]{2,1,0:T(8,128)(2,1)S(1)}, bf16[9,54,256]{2,1,0:T(8,128)(2,1)S(1)}, u32[]{:S(2)}, u32[]{:S(2)}) collective-permute-start(bf16[9,54,256]{2,1,0:T(8,128)(2,1)S(1)} %half_sum.2), channel_id=1, source_target_pairs={{0,2},{1,3},{2,0},{3,1},{4,6},{5,7},{6,4},{7,5},{8,10},{9,11},{10,... | collective-permute-start | bytes 746504 | tf_op jit(solution)/shard_map/ppermute | solution.py:689
  40.1 1.3 %collective-permute-start.15 = (bf16[3,54,256]{2,1,0:T(8,128)(2,1)S(1)}, bf16[3,54,256]{2,1,0:T(8,128)(2,1)S(1)}, u32[]{:S(2)}, u32[]{:S(2)}) collective-permute-start(bf16[3,54,256]{2,1,0:T(8,128)(2,1)S(1)} %get-tuple-element.171), channel_id=1, source_target_pairs={{0,1},{1,0},{2,3},{3,2},{4,5},{5,4},{6,7},{7,6},{8,9},{9,8},{10,11... | collective-permute-start | bytes 248840 | tf_op jit(solution)/shard_map/ppermute | solution.py:689
  40.2 6.7 %collective-permute-start.14 = (bf16[3,54,256]{2,1,0:T(8,128)(2,1)S(1)}, bf16[3,54,256]{2,1,0:T(8,128)(2,1)S(1)}, u32[]{:S(2)}, u32[]{:S(2)}) collective-permute-start(bf16[3,54,256]{2,1,0:T(8,128)(2,1)S(1)} %get-tuple-element.169), channel_id=1, source_target_pairs={{0,1},{1,0},{2,3},{3,2},{4,5},{5,4},{6,7},{7,6},{8,9},{9,8},{10,11... | collective-permute-start | bytes 248840 | tf_op jit(solution)/shard_map/ppermute | solution.py:689
  41.4 5.5 %collective-permute-start.16 = (bf16[3,54,256]{2,1,0:T(8,128)(2,1)S(1)}, bf16[3,54,256]{2,1,0:T(8,128)(2,1)S(1)}, u32[]{:S(2)}, u32[]{:S(2)}) collective-permute-start(bf16[3,54,256]{2,1,0:T(8,128)(2,1)S(1)} %half_sum.3), channel_id=1, source_target_pairs={{0,2},{1,3},{2,0},{3,1},{4,6},{5,7},{6,4},{7,5},{8,10},{9,11},{10,... | collective-permute-start | bytes 248840 | tf_op jit(solution)/shard_map/ppermute | solution.py:689
  44.8 6.6 %collective-permute-start.20 = (bf16[2,196,216]{2,1,0:T(8,128)(2,1)S(1)}, bf16[2,196,216]{2,1,0:T(8,128)(2,1)S(1)}, u32[]{:S(2)}, u32[]{:S(2)}) collective-permute-start(bf16[2,196,216]{2,1,0:T(8,128)(2,1)S(1)} %get-tuple-element.175.refs_0_), channel_id=1, source_target_pairs={{0,2},{1,3},{2,0},{3,1},{4,6},{5,7},{6,4},{7,5},{8,10},{9,11},{10,... | collective-permute-start | bytes 508040 | tf_op jit(solution)/shard_map/ppermute | solution.py:689
  47.7 5.1 %collective-permute-start.17 = (bf16[2,2,54,256]{3,2,1,0:T(8,128)(2,1)S(1)}, bf16[2,2,54,256]{3,2,1,0:T(8,128)(2,1)S(1)}, u32[]{:S(2)}, u32[]{:S(2)}) collective-permute-start(bf16[2,2,54,256]{3,2,1,0:T(8,128)(2,1)S(1)} %get-tuple-element.173), channel_id=1, source_target_pairs={{0,4},{4,0},{8,12},{12,8},{16,20},{20,16},{24,28},{28,24},{1,5},{5... | collective-permute-start | bytes 331784 | tf_op jit(solution)/shard_map/ppermute | solution.py:689
  48.4 5.5 %collective-permute-start.22 = (bf16[2,2,54,256]{3,2,1,0:T(8,128)(2,1)S(1)}, bf16[2,2,54,256]{3,2,1,0:T(8,128)(2,1)S(1)}, u32[]{:S(2)}, u32[]{:S(2)}) collective-permute-start(bf16[2,2,54,256]{3,2,1,0:T(8,128)(2,1)S(1)} %get-tuple-element.181), channel_id=1, source_target_pairs={{0,4},{4,0},{8,12},{12,8},{16,20},{20,16},{24,28},{28,24},{1,5},{5... | collective-permute-start | bytes 331784 | tf_op jit(solution)/shard_map/ppermute | solution.py:689
  49.7 7.7 %collective-permute-start.19 = (bf16[2,196,216]{2,1,0:T(8,128)(2,1)S(1)}, bf16[2,196,216]{2,1,0:T(8,128)(2,1)S(1)}, u32[]{:S(2)}, u32[]{:S(2)}) collective-permute-start(bf16[2,196,216]{2,1,0:T(8,128)(2,1)S(1)} %get-tuple-element.175.refs_0_), channel_id=1, source_target_pairs={{0,1},{1,0},{2,3},{3,2},{4,5},{5,4},{6,7},{7,6},{8,9},{9,8},{10,11... | collective-permute-start | bytes 508040 | tf_op jit(solution)/shard_map/ppermute | solution.py:689
  51.4 6.0 %collective-permute-start.21 = (bf16[2,196,216]{2,1,0:T(8,128)(2,1)S(1)}, bf16[2,196,216]{2,1,0:T(8,128)(2,1)S(1)}, u32[]{:S(2)}, u32[]{:S(2)}) collective-permute-start(bf16[2,196,216]{2,1,0:T(8,128)(2,1)S(1)} %collective-permute-done.20.refs_2_), channel_id=1, source_target_pairs={{0,1},{1,0},{2,3},{3,2},{4,5},{5,4},{6,7},{7,6},{8,9},{9,8},{10,11... | collective-permute-start | bytes 508040 | tf_op jit(solution)/shard_map/ppermute | solution.py:689
  52.7 6.7 %collective-permute-start.18 = (bf16[2,54,256]{2,1,0:T(8,128)(2,1)S(1)}, bf16[2,54,256]{2,1,0:T(8,128)(2,1)S(1)}, u32[]{:S(2)}, u32[]{:S(2)}) collective-permute-start(bf16[2,54,256]{2,1,0:T(8,128)(2,1)S(1)} %get-tuple-element.174), channel_id=1, source_target_pairs={{0,24},{4,28},{8,16},{12,20},{16,8},{20,12},{24,0},{28,4},{1,25},{... | collective-permute-start | bytes 165896 | tf_op jit(solution)/shard_map/ppermute | solution.py:689
  53.5 6.3 %collective-permute-start.24 = (bf16[2,54,256]{2,1,0:T(8,128)(2,1)S(1)}, bf16[2,54,256]{2,1,0:T(8,128)(2,1)S(1)}, u32[]{:S(2)}, u32[]{:S(2)}) collective-permute-start(bf16[2,54,256]{2,1,0:T(8,128)(2,1)S(1)} %get-tuple-element.184), channel_id=1, source_target_pairs={{0,16},{4,20},{8,24},{12,28},{16,0},{20,4},{24,8},{28,12},{1,17},{... | collective-permute-start | bytes 165896 | tf_op jit(solution)/shard_map/ppermute | solution.py:689
  54.0 5.9 %copy-start.1 = (f32[2,54,216]{2,0,1:T(2,128)S(1)}, f32[2,54,216]{2,0,1:T(2,128)}, u32[]{:S(2)}) copy-start(f32[2,54,216]{2,0,1:T(2,128)} %param.24) | copy-start | bytes 279940
  54.0 5.9 %copy-start.3 = (f32[2,54,216]{2,0,1:T(2,128)S(1)}, f32[2,54,216]{2,0,1:T(2,128)}, u32[]{:S(2)}) copy-start(f32[2,54,216]{2,0,1:T(2,128)} %param.25) | copy-start | bytes 279940
  54.0 5.8 %copy-start.4 = (f32[2,54,216]{2,0,1:T(2,128)S(1)}, f32[2,54,216]{2,0,1:T(2,128)}, u32[]{:S(2)}) copy-start(f32[2,54,216]{2,0,1:T(2,128)} %param.26) | copy-start | bytes 279940
  54.0 5.8 %copy-start.6 = (f32[9,216]{1,0:T(8,128)S(1)}, f32[9,216]{1,0:T(8,128)}, u32[]{:S(2)}) copy-start(f32[9,216]{1,0:T(8,128)} %refs_14_.1) | copy-start | bytes 23332
  54.0 5.8 %copy-start.7 = (f32[9,216]{1,0:T(8,128)S(1)}, f32[9,216]{1,0:T(8,128)}, u32[]{:S(2)}) copy-start(f32[9,216]{1,0:T(8,128)} %refs_15_.1) | copy-start | bytes 23332
  54.0 5.8 %copy-start.8 = (f32[2,12,12]{2,0,1:T(2,128)S(1)}, f32[2,12,12]{2,0,1:T(2,128)}, u32[]{:S(2)}) copy-start(f32[2,12,12]{2,0,1:T(2,128)} %param.31) | copy-start | bytes 3460
  54.0 5.8 %copy-start.9 = (f32[2,12,12]{2,0,1:T(2,128)S(1)}, f32[2,12,12]{2,0,1:T(2,128)}, u32[]{:S(2)}) copy-start(f32[2,12,12]{2,0,1:T(2,128)} %param.32) | copy-start | bytes 3460
  54.1 5.8 %copy-start.11 = (f32[4,216]{1,0:T(4,128)S(1)}, f32[4,216]{1,0:T(4,128)}, u32[]{:S(2)}) copy-start(f32[4,216]{1,0:T(4,128)} %refs_8_.1) | copy-start | bytes 10372
  54.1 5.8 %copy-start.12 = (f32[4,216]{1,0:T(4,128)S(1)}, f32[4,216]{1,0:T(4,128)}, u32[]{:S(2)}) copy-start(f32[4,216]{1,0:T(4,128)} %refs_9_.1) | copy-start | bytes 10372
  54.1 5.8 %collective-permute-start.23 = (bf16[2,54,256]{2,1,0:T(8,128)(2,1)S(1)}, bf16[2,54,256]{2,1,0:T(8,128)(2,1)S(1)}, u32[]{:S(2)}, u32[]{:S(2)}) collective-permute-start(bf16[2,54,256]{2,1,0:T(8,128)(2,1)S(1)} %get-tuple-element.183), channel_id=1, source_target_pairs={{0,8},{4,12},{8,0},{12,4},{16,24},{20,28},{24,16},{28,20},{1,9},{5... | collective-permute-start | bytes 165896 | tf_op jit(solution)/shard_map/ppermute | solution.py:689

commit v10 on v9

--- a/solution.py
+++ b/solution.py
@@ -62,8 +62,13 @@
     return (part ^ place) * 3 + (head - 3 * part)
 
 
+def spot(slot, per):
+    bits = per.bit_length() - 1
+    return slot >> (bits + 1), (slot >> bits) & 1, slot & (per - 1)
+
+
 def prep_kernel(
-    scal, tok_ref, cot_ref, norm_ref, talk_ref, x_ref, a_ref, dy_ref, mix_ref, bias_ref, keep_ref, ex_ref, el_ref, tmp_ref
+    scal, slot_ref, tok_ref, cot_ref, norm_ref, talk_ref, x_ref, a_ref, dy_ref, mix_ref, bias_ref, keep_ref, ex_ref, el_ref, sel_ref, tmp_ref, *, pairs
 ):
     x_ref[...] = jnp.zeros_like(x_ref)
     dy_ref[...] = jnp.zeros_like(dy_ref)
@@ -99,6 +104,12 @@
     keep_ref[keep_ref.shape[0] - 1 :, :] = jnp.broadcast_to(valid, (1, 256))
     ex_ref[...] = ex
     el_ref[...] = el
+    blocks, slots = sel_ref.shape[:2]
+    per = slots // (2 * pairs)
+    for b in range(blocks):
+        pair, place, own = spot(slot_ref[b], per)
+        at = ((place ^ scal[4]) * pairs + (pair ^ scal[5])) * per + own
+        sel_ref[b] = (iota(sel_ref.shape[1:], 0) == at).astype(f32)
 
 
 def load_weight(dst_ref, w_refs, b):
@@ -416,29 +427,38 @@
         out_ref[i] = m_ref[:, i, :].astype(bf16)
 
 
-def spot(slot, per):
-    bits = per.bit_length() - 1
-    return slot >> (bits + 1), (slot >> bits) & 1, slot & (per - 1)
-
-
 def stack_kernel(*refs):
     for k, ref in enumerate(refs[:-1]):
         refs[-1][k] = ref[...]
 
 
-def select_kernel(slot_ref, scal, conv_ref, *refs):
-    sources, (attn_ref, ffn_ref, every_ref) = refs[:4], refs[4:]
-    per = sources[0].shape[0]
-    for i in range(2):
-        every_ref[i, 0] = sources[2 * i][...]
-        every_ref[i, 1:] = sources[2 * i + 1][...]
-    for b in range(12):
-        pair, place, own = spot(slot_ref[b], per)
-        block = every_ref[place ^ scal[4], pair ^ scal[5], own]
-        if b < 4:
-            attn_ref[b] = block
-        else:
-            ffn_ref[b - 4] = block
+def slots_of(sources):
+    found = []
+    for i, ref in enumerate(sources):
+        ranks = [ref] if i % 2 == 0 else [ref.at[k] for k in range(ref.shape[0])]
+        found += [rank[own] for rank in ranks for own in range(rank.shape[0])]
+    return found
+
+
+def pick(sel_ref, b, slots):
+    dim = slots[0].shape[1]
+    block = None
+    for i, slot in enumerate(slots):
+        term = sel_ref[b, i : i + 1, 0:dim] * slot.astype(f32)
+        block = term if block is None else block + term
+    return block.astype(bf16)
+
+
+def select_attn_kernel(sel_ref, *refs):
+    slots = slots_of(refs[:-1])
+    for b in range(4):
+        refs[-1][b] = pick(sel_ref, b, slots)
+
+
+def select_ffn_kernel(sel_ref, conv_ref, *refs):
+    slots, ffn_ref = slots_of(refs[:-1]), refs[-1]
+    for b in range(8):
+        ffn_ref[b] = pick(sel_ref, 4 + b, slots)
     hi, lo = split2(conv_ref[...])
     ffn_ref[8] = jnp.zeros_like(ffn_ref[8])
     ffn_ref[8, 0:9] = hi
@@ -471,26 +491,23 @@
             out_ref[k, j, 0, :, FREE:] = wide
 
 
-def spread_attn_kernel(slot_ref, scal, old_ref, *refs, parts):
+def spread_attn_kernel(sel_ref, old_ref, *refs, parts):
     attn, outs = refs[:parts], refs[parts:]
     half, per = outs[0].shape[:2]
+    blocks = [total(attn, b) for b in range(3)]
+    wide = blocks[0][:, FREE:].astype(bf16)
+    blocks = [block[:, 0:FREE] for block in blocks]
     for i, ref in enumerate(outs):
-        ref[...] = old_ref[half * (i % 2) : half * (i % 2 + 1), i // 2]
-    for b in range(3):
-        block = total(attn, b)
-        low = block[:, 0:FREE].astype(bf16)
-        if b == 0:
-            wide = block[:, FREE:].astype(bf16)
-        pair, place, own = spot(slot_ref[b], per)
-        pair, place = pair ^ scal[5], place ^ scal[4]
-        for i, ref in enumerate(outs):
-
-            @pl.when((place == i // 2) & ((pair >= half) == (i % 2 == 1)))
-            def _():
-                ref[pair & (half - 1), own, :, 0:FREE] = low
-
-    for ref in outs:
         for k in range(half):
+            pair = half * (i % 2) + k
+            for own in range(per):
+                old = old_ref[pair, i // 2, own]
+                at = (i // 2 * 2 * half + pair) * per + own
+                low = old[:, 0:FREE].astype(f32)
+                for b in range(3):
+                    low = low + sel_ref[b, at : at + 1, 0:FREE] * blocks[b]
+                ref[k, own] = old
+                ref[k, own, :, 0:FREE] = low.astype(bf16)
             ref[k, 1, :, FREE:] = wide
 
 
@@ -576,34 +593,36 @@
     )
 
 
-def prep(scal, tokens, cotangent, norm_params, talk, parts):
+def prep(scal, block_slot, tokens, cotangent, norm_params, talk, parts, pairs, slots):
     tok, dim = tokens.shape[1], tokens.shape[2]
     pad = SIDE * PITCH
     heads = talk.shape[1]
     n = heads * PITCH
-    full = lambda *s: pl.BlockSpec(s, lambda i, sc: (0,) * len(s))
+    full = lambda *s: pl.BlockSpec(s, lambda i, sc, bs: (0,) * len(s))
     return pl.pallas_call(
-        prep_kernel,
+        functools.partial(prep_kernel, pairs=pairs),
         grid_spec=pltpu.PrefetchScalarGridSpec(
-            num_scalar_prefetch=1,
+            num_scalar_prefetch=2,
             grid=(1,),
             in_specs=[
-                pl.BlockSpec((1, tok, dim), lambda i, sc: (sc[0], 0, 0)),
-                pl.BlockSpec((1, tok, dim), lambda i, sc: (sc[0], 0, 0)),
+                pl.BlockSpec((1, tok, dim), lambda i, sc, bs: (sc[0], 0, 0)),
+                pl.BlockSpec((1, tok, dim), lambda i, sc, bs: (sc[0], 0, 0)),
                 full(*norm_params.shape),
                 full(*talk.shape),
             ],
             out_specs=[full(pad, dim), full(pad, dim), full(pad, dim), full(2, n, 256), full(pad, 128),
                 full(parts + 2, 256), full(n, heads), full(256, heads),
+                full(12, slots, 256),
             ],
             scratch_shapes=[pltpu.VMEM((tok, dim), f32)],
         ),
         out_shape=[SDS((pad, dim), f32), SDS((pad, dim), bf16), SDS((pad, dim), f32), SDS((2, n, 256), f32),
-                   SDS((pad, 128), f32), SDS((parts + 2, 256), f32), SDS((n, heads), bf16), SDS((256, heads), bf16)],
+                   SDS((pad, 128), f32), SDS((parts + 2, 256), f32), SDS((n, heads), bf16), SDS((256, heads), bf16),
+                   SDS((12, slots, 256), f32)],
         compiler_params=pltpu.CompilerParams(vmem_limit_bytes=16 << 20),
         cost_estimate=pl.CostEstimate(flops=1000000000, transcendentals=0, bytes_accessed=3000000),
         name="prep",
-    )(scal, tokens, cotangent, norm_params, talk)
+    )(scal, block_slot, tokens, cotangent, norm_params, talk)
 
 
 def attn_fwd(x, a, mix, bias, keep, w):
@@ -744,12 +763,13 @@
         *[apart[k] for k in range(1, pairs)]
     )
     far_other = permute(far_own, "dp", 1)
-    x, a, dy, mix, bias, keep, ex, el = prep(scal, tokens, cotangent, norm_params, talk_in, parts)
+    x, a, dy, mix, bias, keep, ex, el, sel = prep(
+        scal, block_slot, tokens, cotangent, norm_params, talk_in, parts, pairs, ranks * slots
+    )
     far_other, x = lax.optimization_barrier((far_other, x))
-    attn_w, ffn_w = call(
-        select_kernel, "select", 2, 5, [SDS((4, rows, dim), bf16), SDS((9, rows, dim), bf16)],
-        [pltpu.VMEM((2, pairs, slots, rows, dim), bf16)],
-    )(block_slot, scal, conv, mine, far_own, near_other, far_other)
+    sources = (mine, far_own, near_other, far_other)
+    (attn_w,) = call(select_attn_kernel, "select_attn", 0, 5, [SDS((4, rows, dim), bf16)])(sel, *sources)
+    (ffn_w,) = call(select_ffn_kernel, "select_ffn", 0, 6, [SDS((9, rows, dim), bf16)])(sel, conv, *sources)
     attn_2, attn_1 = permute(attn_w, "head", 2), permute(attn_w, "head", 1)
     attn_3 = permute(attn_2, "head", 1)
     attn_w = [attn_w, attn_1, attn_2, attn_3]
@@ -760,25 +780,26 @@
     first = list(ffn_first(mid, dy, norm_params, keep, [ffn_w, ffn_1]))
     first[0], ffn_3 = lax.optimization_barrier((first[0], ffn_3))
     out, dmid, gn2, *ffn_g = ffn_last(mid, dy, norm_params, keep, o, first, [ffn_2, ffn_3])
-    ffn_1, ffn_3 = permute(ffn_g[1], "head", 1), permute(ffn_g[3], "head", 1)
+    ffn_3 = permute(ffn_g[3], "head", 1)
     do, gqa, *sums = scores_back(dmid, mix, keep, ex, el, q, k, v, qw, p, pv, attn_w, 0)
-    do, ffn_1, ffn_3 = lax.optimization_barrier((do, ffn_1, ffn_3))
+    do, ffn_3 = lax.optimization_barrier((do, ffn_3))
     (summed,) = call(half_sum_kernel, "half_sum", 0, 2, [SDS(ffn_3.shape, bf16)])(ffn_g[2], ffn_3)
-    ffn_2 = permute(summed, "head", 2)
+    ffn_g[1], summed = lax.optimization_barrier((ffn_g[1], summed))
+    ffn_2, ffn_1 = permute(summed, "head", 2), permute(ffn_g[1], "head", 1)
     gqb, gk, gv, gt = scores_back(dmid, mix, keep, ex, el, q, k, v, qw, p, pv, [do, *sums], 1)
     both, *attn_g = weights_back(x, a, dmid, norm_params, gn2, gqa, gqb, gk, gv, gt, out, attn_w)
     attn_1, attn_3 = permute(attn_g[1], "head", 1), permute(attn_g[3], "head", 1)
     (summed,) = call(half_sum_kernel, "half_sum", 0, 2, [SDS(attn_3.shape, bf16)])(attn_g[2], attn_3)
+    both, summed = lax.optimization_barrier((both, summed))
     attn_2 = permute(summed, "head", 2)
+    both_2, both_1 = permute(both, "head", 2), permute(both, "head", 1)
+    both_3 = permute(both_2, "head", 1)
     (message,) = call(
         spread_ffn_kernel, "spread_ffn", 2, 3, [SDS((ranks // 2, 2, slots, rows, 256), bf16)]
     )(block_slot, scal, ffn_g[0], ffn_1, ffn_2)
-    both, message = lax.optimization_barrier((both, message))
-    both_2, both_1 = permute(both, "head", 2), permute(both, "head", 1)
-    both_3 = permute(both_2, "head", 1)
     near_own, far_own, near_other, far_other = call(
-        spread_attn_kernel, "spread_attn", 2, 4, [SDS((half,) + message.shape[2:], bf16)] * 4, parts=3,
-    )(block_slot, scal, message, attn_g[0], attn_1, attn_2)
+        spread_attn_kernel, "spread_attn", 0, 5, [SDS((half,) + message.shape[2:], bf16)] * 4, parts=3,
+    )(sel, message, attn_g[0], attn_1, attn_2)
     slot_shape = (slots, rows, 256)
     far_other = permute(far_other, "dp", 1)
     near_other = permute(near_other, "dp", 1)

time: 61.2 us -> 60.6 us (level)
    pallas_call x3 -> x4, Pallas kernels: 2.4 us -> 2.2 us  [the longest x1 1.12 us: prep(): pl.pallas_call(functools.partial(prep_kernel, pairs=pairs), grid_spec=plt...]
  transfers between devices with their start and end apart: 25 -> 25, of which waited for: 13 -> 12; matrix products, arithmetic and copies ran while one was open for 0% -> 0% of each run, Pallas kernels for 20% -> 20%
where the time goes in v10:
time: 60.6 us; the launch traced here: 60.4 us
  starting transfers between devices  22.1 us (36%)
  waiting for transfers between devices  17.7 us (29%)
  Pallas kernels  16.4 us (27%)
  between operations  2.95 us (5%)
  local copies, waits for them, and re-layouts  1.27 us (2%)
    ppermute x25, starting transfers between devices, permute(): lax.ppermute(x, axis, [(i, i ^ k) for i in range(lax.axis_size(axis))])  22.1 us
    ppermute x25, waiting for transfers between devices, permute(): lax.ppermute(x, axis, [(i, i ^ k) for i in range(lax.axis_size(axis))])  17.7 us
    pallas_call x2, Pallas kernels, scores_back(): call(scores_back_kernel, 'scores_back', 0, 11 + len(more), outs, scratch,...  3.35 us
    pallas_call x1, Pallas kernels, ffn_last(): call(ffn_last_kernel, 'ffn_last', 0, 14 + late, [SDS((SIDE * SIDE, dim),...  2.3 us
    pallas_call x1, Pallas kernels, attn_fwd(): call(attn_fwd_kernel, 'attn_fwd', 0, 5 + len(w), [SDS((pad, dim), f32)] +...  2.17 us
    pallas_call x1, Pallas kernels, local(): pl.pallas_call(assemble_kernel, grid=(1,), in_specs=[SM] + [whole(*both.s...  1.99 us
    pallas_call x1, Pallas kernels, ffn_first(): call(ffn_first_kernel, 'ffn_first', 0, 4 + count, [SDS((pad, dim), f32),...  1.57 us
  transfers between devices with their start and end apart: 25, of which 12 were waited for; matrix products, arithmetic and copies ran while one was open for 0% of the time, Pallas kernels for 20%

profile of v10, /device:TPU:0, one launch (start us, length us, event | category | flops | bytes accessed | tf_op | source)
XLA Modules:
  0.0 60.4 jit_solution(7967056983764400532)
XLA Ops:
  0.7 0.9 %copy-done = f32[2,54,216]{2,0,1:T(2,128)S(1)} copy-done((f32[2,54,216]{2,0,1:T(2,128)S(1)}, f32[2,54,216]{2,0,1:T(2,128)}, u32[]{:S(2)}) %copy-start) | copy-done | bytes 93336
  1.5 0.2 cast.1.refs_0_
  1.8 3.0 %collective-permute-start.2 = (bf16[2,54,216]{2,1,0:T(8,128)(2,1)S(1)}, bf16[2,54,216]{2,1,0:T(8,128)(2,1)S(1)}, u32[]{:S(2)}, u32[]{:S(2)}) collective-permute-start(bf16[2,54,216]{2,1,0:T(8,128)(2,1)S(1)} %cast.1.refs_0_), channel_id=1, source_target_pairs={{0,4},{4,0},{8,12},{12,8},{16,20},{20,16},{24,28},{28,24},{1,5},{5... | collective-permute-start | bytes 139976 | tf_op jit(solution)/shard_map/ppermute | solution.py:708
  4.8 1.6 %collective-permute-start.1 = (bf16[2,54,216]{2,1,0:T(8,128)(2,1)S(1)}, bf16[2,54,216]{2,1,0:T(8,128)(2,1)S(1)}, u32[]{:S(2)}, u32[]{:S(2)}) collective-permute-start(bf16[2,54,216]{2,1,0:T(8,128)(2,1)S(1)} %cast.1.refs_0_), channel_id=1, source_target_pairs={{0,8},{4,12},{8,0},{12,4},{16,24},{20,28},{24,16},{28,20},{1,9},{5... | collective-permute-start | bytes 139976 | tf_op jit(solution)/shard_map/ppermute | solution.py:708
  6.4 2.6 %collective-permute-start = (bf16[2,54,216]{2,1,0:T(8,128)(2,1)S(1)}, bf16[2,54,216]{2,1,0:T(8,128)(2,1)S(1)}, u32[]{:S(2)}, u32[]{:S(2)}) collective-permute-start(bf16[2,54,216]{2,1,0:T(8,128)(2,1)S(1)} %cast.1.refs_0_), channel_id=1, source_target_pairs={{0,16},{4,20},{8,24},{12,28},{16,0},{20,4},{24,8},{28,12},{1,17},{... | collective-permute-start | bytes 139976 | tf_op jit(solution)/shard_map/ppermute | solution.py:708
  9.0 0.2 collective-permute-start.3
  9.2 3.1 %collective-permute-done.refs_1_ = bf16[2,54,216]{2,1,0:T(8,128)(2,1)S(1)} collective-permute-done((bf16[2,54,216]{2,1,0:T(8,128)(2,1)S(1)}, bf16[2,54,216]{2,1,0:T(8,128)(2,1)S(1)}, u32[]{:S(2)}, u32[]{:S(2)}) %collective-permute-start) | collective-permute-done | bytes 46688 | tf_op jit(solution)/shard_map/ppermute | solution.py:708
  12.3 2.7 %collective-permute-done.3.refs_2_ = bf16[2,54,216]{2,1,0:T(8,128)(2,1)S(1)} collective-permute-done((bf16[2,54,216]{2,1,0:T(8,128)(2,1)S(1)}, bf16[2,54,216]{2,1,0:T(8,128)(2,1)S(1)}, u32[]{:S(2)}, u32[]{:S(2)}) %collective-permute-start.3) | collective-permute-done | bytes 46688 | tf_op jit(solution)/shard_map/ppermute | solution.py:708
  15.0 0.6 collective-permute-start.4
  17.7 0.2 copy.34.cot_ref
  17.9 1.1 %prep.1 = (f32[224,216]{1,0:T(8,128)S(1)}, bf16[224,216]{1,0:T(8,128)(2,1)S(1)}, f32[224,216]{1,0:T(8,128)S(1)}, f32[2,192,256]{2,1,0:T(8,128)S(1)}, f32[224,128...) custom-call(s32[6]{0:T(128)S(1)} %concatenate.3.scal, ...), custom_call_target="tpu_custom_call" | custom-call | flops 1000000000 | bytes 3000000 | tf_op jit(solution)/shard_map/prep/pallas_call | solution.py:602
  19.0 1.4 %collective-permute-done.4.refs_3_ = bf16[3,2,54,216]{3,2,1,0:T(8,128)(2,1)S(1)} collective-permute-done((bf16[3,2,54,216]{3,2,1,0:T(8,128)(2,1)S(1)}, bf16[3,2,54,216]{3,2,1,0:T(8,128)(2,1)S(1)}, u32[]{:S(2)}, u32[]{:S(2)}) %collective-permute-start.4) | collective-permute-done | bytes 140000 | tf_op jit(solution)/shard_map/ppermute | solution.py:708
  20.5 0.3 select_attn.1.refs_0_
  20.8 1.6 %collective-permute-start.6 = (bf16[4,54,216]{2,1,0:T(8,128)(2,1)S(1)}, bf16[4,54,216]{2,1,0:T(8,128)(2,1)S(1)}, u32[]{:S(2)}, u32[]{:S(2)}) collective-permute-start(bf16[4,54,216]{2,1,0:T(8,128)(2,1)S(1)} %select_attn.1.refs_0_), channel_id=1, source_target_pairs={{0,2},{1,3},{2,0},{3,1},{4,6},{5,7},{6,4},{7,5},{8,10},{9,11},{10,... | collective-permute-start | bytes 279944 | tf_op jit(solution)/shard_map/ppermute | solution.py:708
  22.3 0.5 select_ffn.1.refs_0_
  22.9 0.6 collective-permute-start.8
  23.5 0.5 collective-permute-start.5
  24.0 2.0 %collective-permute-done.6.refs_2_ = bf16[4,54,216]{2,1,0:T(8,128)(2,1)S(1)} collective-permute-done((bf16[4,54,216]{2,1,0:T(8,128)(2,1)S(1)}, bf16[4,54,216]{2,1,0:T(8,128)(2,1)S(1)}, u32[]{:S(2)}, u32[]{:S(2)}) %collective-permute-start.6) | collective-permute-done | bytes 93344 | tf_op jit(solution)/shard_map/ppermute | solution.py:708
  26.0 1.3 %collective-permute-done.7.refs_3_ = bf16[4,54,216]{2,1,0:T(8,128)(2,1)S(1)} collective-permute-done((bf16[4,54,216]{2,1,0:T(8,128)(2,1)S(1)}, bf16[4,54,216]{2,1,0:T(8,128)(2,1)S(1)}, u32[]{:S(2)}, u32[]{:S(2)}) %collective-permute-start.7) | collective-permute-done | bytes 93344 | tf_op jit(solution)/shard_map/ppermute | solution.py:708
  27.3 2.2 %attn_fwd.1 = (f32[224,216]{1,0:T(8,128)S(1)}, bf16[224,256]{1,0:T(8,128)(2,1)S(1)}, bf16[224,256]{1,0:T(8,128)(2,1)S(1)}, bf16[224,256]{1,0:T(8,128)(2,1)S(1)},...) custom-call(f32[224,216]{1,0:T(8,128)S(1)} %get-tuple-element.114.x_, ...), custom_call_target="tpu_custom_call" | custom-call | flops 1000000000 | bytes 3000000 | tf_op jit(solution)/shard_map/attn_fwd/pallas_call | solution.py:632
  29.5 0.2 collective-permute-start.10
  29.7 1.6 %ffn_first.1 = (f32[224,216]{1,0:T(8,128)S(1)}, f32[224,128]{1,0:T(8,128)S(1)}, bf16[224,216]{1,0:T(8,128)(2,1)S(1)}, bf16[224,216]{1,0:T(8,128)(2,1)S(1)}, bf16...) custom-call(f32[224,216]{1,0:T(8,128)S(1)} %get-tuple-element.122.mi, ...), custom_call_target="tpu_custom_call" | custom-call | flops 3000000000 | bytes 9000000 | tf_op jit(solution)/shard_map/ffn_first/pallas_call | solution.py:646
  31.3 2.3 %ffn_last.1 = (bf16[196,216]{1,0:T(8,128)(2,1)S(1)}, f32[224,216]{1,0:T(8,128)S(1)}, f32[8,216]{1,0:T(8,128)S(1)}, bf16[9,54,256]{2,1,0:T(8,128)(2,1)S(1)}, bf16...) custom-call(f32[224,216]{1,0:T(8,128)S(1)} %get-tuple-element.122.mid_ref, ...), custom_call_target="tpu_custom_call" | custom-call | flops 4000000000 | bytes 12000000 | tf_op jit(solution)/shard_map/ffn_last/pallas_call | solution.py:660
  33.6 0.4 collective-permute-start.11
  34.0 1.0 %scores_back.2 = (bf16[224,256]{1,0:T(8,128)(2,1)S(1)}, bf16[64,256]{1,0:T(8,128)(2,1)S(1)}, f32[224,256]{1,0:T(8,128)S(1)}, f32[224,256]{1,0:T(8,128)S(1)}, f32...) custom-call(f32[224,216]{1,0:T(8,128)S(1)} %get-tuple-element.140.dmid_ref, f32[2,192,256]{2,1,0:T(8,128)S(1)} %get-tuple-element.116.mix_ref, ...), custom_call_target="tpu_custom_call" | custom-call | flops 4000000000 | bytes 12000000 | tf_op jit(solution)/shard_map/scores_back/pallas_call | solution.py:690
  35.1 0.1 collective-permute-done.11.b_ref
  35.3 0.4 collective-permute-start.12
  35.7 1.1 %collective-permute-start.13 = (bf16[9,54,256]{2,1,0:T(8,128)(2,1)S(1)}, bf16[9,54,256]{2,1,0:T(8,128)(2,1)S(1)}, u32[]{:S(2)}, u32[]{:S(2)}) collective-permute-start(bf16[9,54,256]{2,1,0:T(8,128)(2,1)S(1)} %half_sum.2), channel_id=1, source_target_pairs={{0,2},{1,3},{2,0},{3,1},{4,6},{5,7},{6,4},{7,5},{8,10},{9,11},{10,... | collective-permute-start | bytes 746504 | tf_op jit(solution)/shard_map/ppermute | solution.py:708
  36.8 2.3 %scores_back.3 = (bf16[160,256]{1,0:T(8,128)(2,1)S(1)}, bf16[224,256]{1,0:T(8,128)(2,1)S(1)}, bf16[224,256]{1,0:T(8,128)(2,1)S(1)}, f32[2,12,12]{2,1,0:T(8,128)S(1)}) custom-call(f32[224,216]{1,0:T(8,128)S(1)} %get-tuple-element.140.dmid_ref, f32[2,192,256]{2,1,0:T(8,128)S(1)} %get-tuple-element.116.mix_ref, f32[6,256]{1,0:T(8,128)S(1)} %get-tuple-element.118.keep_ref, ...), custom_call_target="tpu_custom_call" | custom-call | flops 4000000000 | bytes 12000000 | tf_op jit(solution)/shard_map/scores_back/pallas_call | solution.py:690
  39.2 0.6 weights_back.1
  39.8 0.5 collective-permute-start.14
  40.3 0.8 %collective-permute-done.15.b_ref = bf16[3,54,256]{2,1,0:T(8,128)(2,1)S(1)} collective-permute-done((bf16[3,54,256]{2,1,0:T(8,128)(2,1)S(1)}, bf16[3,54,256]{2,1,0:T(8,128)(2,1)S(1)}, u32[]{:S(2)}, u32[]{:S(2)}) %collective-permute-start.15) | collective-permute-done | bytes 82976 | tf_op jit(solution)/shard_map/ppermute | solution.py:708
  41.1 1.0 %collective-permute-start.16 = (bf16[3,54,256]{2,1,0:T(8,128)(2,1)S(1)}, bf16[3,54,256]{2,1,0:T(8,128)(2,1)S(1)}, u32[]{:S(2)}, u32[]{:S(2)}) collective-permute-start(bf16[3,54,256]{2,1,0:T(8,128)(2,1)S(1)} %half_sum.3), channel_id=1, source_target_pairs={{0,2},{1,3},{2,0},{3,1},{4,6},{5,7},{6,4},{7,5},{8,10},{9,11},{10,... | collective-permute-start | bytes 248840 | tf_op jit(solution)/shard_map/ppermute | solution.py:708
  42.1 1.1 %collective-permute-start.20 = (bf16[2,196,216]{2,1,0:T(8,128)(2,1)S(1)}, bf16[2,196,216]{2,1,0:T(8,128)(2,1)S(1)}, u32[]{:S(2)}, u32[]{:S(2)}) collective-permute-start(bf16[2,196,216]{2,1,0:T(8,128)(2,1)S(1)} %get-tuple-element.175.refs_0_), channel_id=1, source_target_pairs={{0,2},{1,3},{2,0},{3,1},{4,6},{5,7},{6,4},{7,5},{8,10},{9,11},{10,... | collective-permute-start | bytes 508040 | tf_op jit(solution)/shard_map/ppermute | solution.py:708
  43.2 0.7 %collective-permute-done.13.refs_2_ = bf16[9,54,256]{2,1,0:T(8,128)(2,1)S(1)} collective-permute-done((bf16[9,54,256]{2,1,0:T(8,128)(2,1)S(1)}, bf16[9,54,256]{2,1,0:T(8,128)(2,1)S(1)}, u32[]{:S(2)}, u32[]{:S(2)}) %collective-permute-start.13) | collective-permute-done | bytes 248864 | tf_op jit(solution)/shard_map/ppermute | solution.py:708
  44.0 0.7 %spread_ffn.1.old_ref = bf16[4,2,2,54,256]{4,3,2,1,0:T(8,128)(2,1)S(1)} custom-call(s32[12]{0:T(128)S(1)} %copy-done.13, s32[6]{0:T(128)S(1)} %concatenate.3.scal, bf16[9,54,256]{2,1,0:T(8,128)(2,1)S(1)} %get-tuple-element.137.refs_0_, bf16[9,54,256]{2,1,0:T(8,128)(2,1)S(1)} %collective-permute-done.12.refs_1_, ...), custom_call_target="tpu_custom_call" | custom-call | flops 1000000000 | bytes 3000000 | tf_op jit(solution)/shard_map/spread_ffn/pallas_call | solution.py:797
  44.7 1.9 %collective-permute-done.16.refs_2_ = bf16[3,54,256]{2,1,0:T(8,128)(2,1)S(1)} collective-permute-done((bf16[3,54,256]{2,1,0:T(8,128)(2,1)S(1)}, bf16[3,54,256]{2,1,0:T(8,128)(2,1)S(1)}, u32[]{:S(2)}, u32[]{:S(2)}) %collective-permute-start.16) | collective-permute-done | bytes 82976 | tf_op jit(solution)/shard_map/ppermute | solution.py:708
  46.6 0.3 spread_attn.1
  46.9 0.8 %collective-permute-start.17 = (bf16[2,2,54,256]{3,2,1,0:T(8,128)(2,1)S(1)}, bf16[2,2,54,256]{3,2,1,0:T(8,128)(2,1)S(1)}, u32[]{:S(2)}, u32[]{:S(2)}) collective-permute-start(bf16[2,2,54,256]{3,2,1,0:T(8,128)(2,1)S(1)} %get-tuple-element.173), channel_id=1, source_target_pairs={{0,4},{4,0},{8,12},{12,8},{16,20},{20,16},{24,28},{28,24},{1,5},{5... | collective-permute-start | bytes 331784 | tf_op jit(solution)/shard_map/ppermute | solution.py:708
  47.7 1.3 %collective-permute-start.22 = (bf16[2,2,54,256]{3,2,1,0:T(8,128)(2,1)S(1)}, bf16[2,2,54,256]{3,2,1,0:T(8,128)(2,1)S(1)}, u32[]{:S(2)}, u32[]{:S(2)}) collective-permute-start(bf16[2,2,54,256]{3,2,1,0:T(8,128)(2,1)S(1)} %get-tuple-element.181), channel_id=1, source_target_pairs={{0,4},{4,0},{8,12},{12,8},{16,20},{20,16},{24,28},{28,24},{1,5},{5... | collective-permute-start | bytes 331784 | tf_op jit(solution)/shard_map/ppermute | solution.py:708
  49.0 1.2 %collective-permute-done.20.refs_2_ = bf16[2,196,216]{2,1,0:T(8,128)(2,1)S(1)} collective-permute-done((bf16[2,196,216]{2,1,0:T(8,128)(2,1)S(1)}, bf16[2,196,216]{2,1,0:T(8,128)(2,1)S(1)}, u32[]{:S(2)}, u32[]{:S(2)}) %collective-permute-start.20) | collective-permute-done | bytes 169376 | tf_op jit(solution)/shard_map/ppermute | solution.py:708
  50.2 1.6 %collective-permute-done.17.other_ref = bf16[2,2,54,256]{3,2,1,0:T(8,128)(2,1)S(1)} collective-permute-done((bf16[2,2,54,256]{3,2,1,0:T(8,128)(2,1)S(1)}, bf16[2,2,54,256]{3,2,1,0:T(8,128)(2,1)S(1)}, u32[]{:S(2)}, u32[]{:S(2)}) %collective-permute-start.17) | collective-permute-done | bytes 110624 | tf_op jit(solution)/shard_map/ppermute | solution.py:708
  51.8 1.0 %collective-permute-start.18 = (bf16[2,54,256]{2,1,0:T(8,128)(2,1)S(1)}, bf16[2,54,256]{2,1,0:T(8,128)(2,1)S(1)}, u32[]{:S(2)}, u32[]{:S(2)}) collective-permute-start(bf16[2,54,256]{2,1,0:T(8,128)(2,1)S(1)} %get-tuple-element.174), channel_id=1, source_target_pairs={{0,24},{4,28},{8,16},{12,20},{16,8},{20,12},{24,0},{28,4},{1,25},{... | collective-permute-start | bytes 165896 | tf_op jit(solution)/shard_map/ppermute | solution.py:708
  52.8 0.3 collective-permute-start.24
  53.3 3.3 %collective-permute-start.23 = (bf16[2,54,256]{2,1,0:T(8,128)(2,1)S(1)}, bf16[2,54,256]{2,1,0:T(8,128)(2,1)S(1)}, u32[]{:S(2)}, u32[]{:S(2)}) collective-permute-start(bf16[2,54,256]{2,1,0:T(8,128)(2,1)S(1)} %get-tuple-element.183), channel_id=1, source_target_pairs={{0,8},{4,12},{8,0},{12,4},{16,24},{20,28},{24,16},{28,20},{1,9},{5... | collective-permute-start | bytes 165896 | tf_op jit(solution)/shard_map/ppermute | solution.py:708
  56.5 2.0 %assemble.1 = (f32[196,4,216]{2,1,0:T(4,128)}, f32[196,4,216]{2,1,0:T(4,128)}) custom-call(s32[6]{0:T(128)S(1)} %concatenate.3.scal, bf16[2,196,216]{2,1,0:T(8,128)(2,1)S(1)} %get-tuple-element.175.refs_0_, bf16[2,196,216]{2,1,0:T(8,128)(2,1)S(1)} %collective-permute-done.19.refs_1_, bf16[2,196,216]{2,1,0:T(8,128)(2,1)S(1)} %collective-permute-done.20.refs_2_, ...), custom_call_target="tpu_custom_call" | custom-call | flops 1000000000 | bytes 3000000 | tf_op jit(solution)/shard_map/assemble/pallas_call | solution.py:813
  58.5 0.7 %collective-permute-done.24.refs_2_ = bf16[2,54,256]{2,1,0:T(8,128)(2,1)S(1)} collective-permute-done((bf16[2,54,256]{2,1,0:T(8,128)(2,1)S(1)}, bf16[2,54,256]{2,1,0:T(8,128)(2,1)S(1)}, u32[]{:S(2)}, u32[]{:S(2)}) %collective-permute-start.24) | collective-permute-done | bytes 55328 | tf_op jit(solution)/shard_map/ppermute | solution.py:708
  59.3 1.1 %update.1 = (f32[54,2,216]{2,1,0:T(2,128)}, f32[54,2,216]{2,1,0:T(2,128)}, f32[54,2,216]{2,1,0:T(2,128)}, bf16[54,2,216]{2,1,0:T(2,128)(2,1)}, f32[4,216]{1,0:T(...) custom-call(f32[2,54,256]{2,1,0:T(8,128)S(1)} %get-tuple-element.182, ...), custom_call_target="tpu_custom_call" | custom-call | flops 1000000000 | bytes 3000000 | tf_op jit(solution)/shard_map/update/pallas_call | solution.py:720
  (57 shorter events, 0.5 us)
Async XLA Ops:
  0.6 0.9 %copy-start = (f32[2,54,216]{2,0,1:T(2,128)S(1)}, f32[2,54,216]{2,0,1:T(2,128)}, u32[]{:S(2)}) copy-start(f32[2,54,216]{2,0,1:T(2,128)} %param.24) | copy-start | bytes 279940
  1.8 15.9 %copy-start.2 = (f32[2,12,12]{2,0,1:T(2,128)S(1)}, f32[2,12,12]{2,0,1:T(2,128)}, u32[]{:S(2)}) copy-start(f32[2,12,12]{2,0,1:T(2,128)} %param.30) | copy-start | bytes 3460
  1.8 15.9 %copy-start.15 = (bf16[4,196,216]{2,0,1:T(4,128)(2,1)S(1)}, bf16[4,196,216]{2,0,1:T(4,128)(2,1)}, u32[]{:S(2)}) copy-start(bf16[4,196,216]{2,0,1:T(4,128)(2,1)} %param.18) | copy-start | bytes 1016068
  1.8 7.4 %collective-permute-start.2 = (bf16[2,54,216]{2,1,0:T(8,128)(2,1)S(1)}, bf16[2,54,216]{2,1,0:T(8,128)(2,1)S(1)}, u32[]{:S(2)}, u32[]{:S(2)}) collective-permute-start(bf16[2,54,216]{2,1,0:T(8,128)(2,1)S(1)} %cast.1.refs_0_), channel_id=1, source_target_pairs={{0,4},{4,0},{8,12},{12,8},{16,20},{20,16},{24,28},{28,24},{1,5},{5... | collective-permute-start | bytes 139976 | tf_op jit(solution)/shard_map/ppermute | solution.py:708
  4.8 4.4 %collective-permute-start.1 = (bf16[2,54,216]{2,1,0:T(8,128)(2,1)S(1)}, bf16[2,54,216]{2,1,0:T(8,128)(2,1)S(1)}, u32[]{:S(2)}, u32[]{:S(2)}) collective-permute-start(bf16[2,54,216]{2,1,0:T(8,128)(2,1)S(1)} %cast.1.refs_0_), channel_id=1, source_target_pairs={{0,8},{4,12},{8,0},{12,4},{16,24},{20,28},{24,16},{28,20},{1,9},{5... | collective-permute-start | bytes 139976 | tf_op jit(solution)/shard_map/ppermute | solution.py:708
  6.4 5.9 %collective-permute-start = (bf16[2,54,216]{2,1,0:T(8,128)(2,1)S(1)}, bf16[2,54,216]{2,1,0:T(8,128)(2,1)S(1)}, u32[]{:S(2)}, u32[]{:S(2)}) collective-permute-start(bf16[2,54,216]{2,1,0:T(8,128)(2,1)S(1)} %cast.1.refs_0_), channel_id=1, source_target_pairs={{0,16},{4,20},{8,24},{12,28},{16,0},{20,4},{24,8},{28,12},{1,17},{... | collective-permute-start | bytes 139976 | tf_op jit(solution)/shard_map/ppermute | solution.py:708
  9.0 6.0 %collective-permute-start.3 = (bf16[2,54,216]{2,1,0:T(8,128)(2,1)S(1)}, bf16[2,54,216]{2,1,0:T(8,128)(2,1)S(1)}, u32[]{:S(2)}, u32[]{:S(2)}) collective-permute-start(bf16[2,54,216]{2,1,0:T(8,128)(2,1)S(1)} %cast.1.refs_0_), channel_id=1, source_target_pairs={{0,24},{4,28},{8,16},{12,20},{16,8},{20,12},{24,0},{28,4},{1,25},{... | collective-permute-start | bytes 139976 | tf_op jit(solution)/shard_map/ppermute | solution.py:708
  15.0 2.7 %copy-start.14 = (f32[4,196,216]{2,0,1:T(4,128)S(1)}, f32[4,196,216]{2,0,1:T(4,128)}, u32[]{:S(2)}) copy-start(f32[4,196,216]{2,0,1:T(4,128)} %param.19) | copy-start | bytes 2032132
  15.0 2.9 %copy-start.10 = (f32[4,216]{1,0:T(4,128)S(1)}, f32[4,216]{1,0:T(4,128)}, u32[]{:S(2)}) copy-start(f32[4,216]{1,0:T(4,128)} %refs_7_.1) | copy-start | bytes 10372
  15.0 2.9 %copy-start.13 = (s32[12]{0:T(128)S(1)}, s32[12]{0:T(128)}, u32[]{:S(2)}) copy-start(s32[12]{0:T(128)} %slot_ref.3) | copy-start | bytes 148
  15.0 5.5 %collective-permute-start.4 = (bf16[3,2,54,216]{3,2,1,0:T(8,128)(2,1)S(1)}, bf16[3,2,54,216]{3,2,1,0:T(8,128)(2,1)S(1)}, u32[]{:S(2)}, u32[]{:S(2)}) collective-permute-start(bf16[3,2,54,216]{3,2,1,0:T(8,128)(2,1)S(1)} %stack.1.refs_1_), channel_id=1, source_target_pairs={{0,4},{4,0},{8,12},{12,8},{16,20},{20,16},{24,28},{28,24},{1,5},{5... | collective-permute-start | bytes 419912 | tf_op jit(solution)/shard_map/ppermute | solution.py:708
  20.5 1.9 %copy-start.5 = (f32[9,216]{1,0:T(8,128)S(1)}, f32[9,216]{1,0:T(8,128)}, u32[]{:S(2)}) copy-start(f32[9,216]{1,0:T(8,128)} %refs_13_.1) | copy-start | bytes 23332
  20.8 5.2 %collective-permute-start.6 = (bf16[4,54,216]{2,1,0:T(8,128)(2,1)S(1)}, bf16[4,54,216]{2,1,0:T(8,128)(2,1)S(1)}, u32[]{:S(2)}, u32[]{:S(2)}) collective-permute-start(bf16[4,54,216]{2,1,0:T(8,128)(2,1)S(1)} %select_attn.1.refs_0_), channel_id=1, source_target_pairs={{0,2},{1,3},{2,0},{3,1},{4,6},{5,7},{6,4},{7,5},{8,10},{9,11},{10,... | collective-permute-start | bytes 279944 | tf_op jit(solution)/shard_map/ppermute | solution.py:708
  22.9 6.6 %collective-permute-start.8 = (bf16[9,54,216]{2,1,0:T(8,128)(2,1)S(1)}, bf16[9,54,216]{2,1,0:T(8,128)(2,1)S(1)}, u32[]{:S(2)}, u32[]{:S(2)}) collective-permute-start(bf16[9,54,216]{2,1,0:T(8,128)(2,1)S(1)} %select_ffn.1.refs_0_), channel_id=1, source_target_pairs={{0,2},{1,3},{2,0},{3,1},{4,6},{5,7},{6,4},{7,5},{8,10},{9,11},{10,... | collective-permute-start | bytes 629864 | tf_op jit(solution)/shard_map/ppermute | solution.py:708
  23.4 6.3 %collective-permute-start.9 = (bf16[9,54,216]{2,1,0:T(8,128)(2,1)S(1)}, bf16[9,54,216]{2,1,0:T(8,128)(2,1)S(1)}, u32[]{:S(2)}, u32[]{:S(2)}) collective-permute-start(bf16[9,54,216]{2,1,0:T(8,128)(2,1)S(1)} %select_ffn.1.refs_0_), channel_id=1, source_target_pairs={{0,1},{1,0},{2,3},{3,2},{4,5},{5,4},{6,7},{7,6},{8,9},{9,8},{10,11... | collective-permute-start | bytes 629864 | tf_op jit(solution)/shard_map/ppermute | solution.py:708
  23.5 2.6 %collective-permute-start.5 = (bf16[4,54,216]{2,1,0:T(8,128)(2,1)S(1)}, bf16[4,54,216]{2,1,0:T(8,128)(2,1)S(1)}, u32[]{:S(2)}, u32[]{:S(2)}) collective-permute-start(bf16[4,54,216]{2,1,0:T(8,128)(2,1)S(1)} %select_attn.1.refs_0_), channel_id=1, source_target_pairs={{0,1},{1,0},{2,3},{3,2},{4,5},{5,4},{6,7},{7,6},{8,9},{9,8},{10,11... | collective-permute-start | bytes 279944 | tf_op jit(solution)/shard_map/ppermute | solution.py:708
  26.0 1.3 %collective-permute-start.7 = (bf16[4,54,216]{2,1,0:T(8,128)(2,1)S(1)}, bf16[4,54,216]{2,1,0:T(8,128)(2,1)S(1)}, u32[]{:S(2)}, u32[]{:S(2)}) collective-permute-start(bf16[4,54,216]{2,1,0:T(8,128)(2,1)S(1)} %collective-permute-done.6.refs_2_), channel_id=1, source_target_pairs={{0,1},{1,0},{2,3},{3,2},{4,5},{5,4},{6,7},{7,6},{8,9},{9,8},{10,11... | collective-permute-start | bytes 279944 | tf_op jit(solution)/shard_map/ppermute | solution.py:708
  29.5 1.8 %collective-permute-start.10 = (bf16[9,54,216]{2,1,0:T(8,128)(2,1)S(1)}, bf16[9,54,216]{2,1,0:T(8,128)(2,1)S(1)}, u32[]{:S(2)}, u32[]{:S(2)}) collective-permute-start(bf16[9,54,216]{2,1,0:T(8,128)(2,1)S(1)} %collective-permute-done.8.refs_5_), channel_id=1, source_target_pairs={{0,1},{1,0},{2,3},{3,2},{4,5},{5,4},{6,7},{7,6},{8,9},{9,8},{10,11... | collective-permute-start | bytes 629864 | tf_op jit(solution)/shard_map/ppermute | solution.py:708
  33.6 1.6 %collective-permute-start.11 = (bf16[9,54,256]{2,1,0:T(8,128)(2,1)S(1)}, bf16[9,54,256]{2,1,0:T(8,128)(2,1)S(1)}, u32[]{:S(2)}, u32[]{:S(2)}) collective-permute-start(bf16[9,54,256]{2,1,0:T(8,128)(2,1)S(1)} %get-tuple-element.150), channel_id=1, source_target_pairs={{0,1},{1,0},{2,3},{3,2},{4,5},{5,4},{6,7},{7,6},{8,9},{9,8},{10,11... | collective-permute-start | bytes 746504 | tf_op jit(solution)/shard_map/ppermute | solution.py:708
  35.3 8.0 %collective-permute-start.12 = (bf16[9,54,256]{2,1,0:T(8,128)(2,1)S(1)}, bf16[9,54,256]{2,1,0:T(8,128)(2,1)S(1)}, u32[]{:S(2)}, u32[]{:S(2)}) collective-permute-start(bf16[9,54,256]{2,1,0:T(8,128)(2,1)S(1)} %get-tuple-element.152), channel_id=1, source_target_pairs={{0,1},{1,0},{2,3},{3,2},{4,5},{5,4},{6,7},{7,6},{8,9},{9,8},{10,11... | collective-permute-start | bytes 746504 | tf_op jit(solution)/shard_map/ppermute | solution.py:708
  35.7 8.3 %collective-permute-start.13 = (bf16[9,54,256]{2,1,0:T(8,128)(2,1)S(1)}, bf16[9,54,256]{2,1,0:T(8,128)(2,1)S(1)}, u32[]{:S(2)}, u32[]{:S(2)}) collective-permute-start(bf16[9,54,256]{2,1,0:T(8,128)(2,1)S(1)} %half_sum.2), channel_id=1, source_target_pairs={{0,2},{1,3},{2,0},{3,1},{4,6},{5,7},{6,4},{7,5},{8,10},{9,11},{10,... | collective-permute-start | bytes 746504 | tf_op jit(solution)/shard_map/ppermute | solution.py:708
  39.8 1.3 %collective-permute-start.15 = (bf16[3,54,256]{2,1,0:T(8,128)(2,1)S(1)}, bf16[3,54,256]{2,1,0:T(8,128)(2,1)S(1)}, u32[]{:S(2)}, u32[]{:S(2)}) collective-permute-start(bf16[3,54,256]{2,1,0:T(8,128)(2,1)S(1)} %get-tuple-element.170), channel_id=1, source_target_pairs={{0,1},{1,0},{2,3},{3,2},{4,5},{5,4},{6,7},{7,6},{8,9},{9,8},{10,11... | collective-permute-start | bytes 248840 | tf_op jit(solution)/shard_map/ppermute | solution.py:708
  39.8 4.8 %collective-permute-start.14 = (bf16[3,54,256]{2,1,0:T(8,128)(2,1)S(1)}, bf16[3,54,256]{2,1,0:T(8,128)(2,1)S(1)}, u32[]{:S(2)}, u32[]{:S(2)}) collective-permute-start(bf16[3,54,256]{2,1,0:T(8,128)(2,1)S(1)} %get-tuple-element.167), channel_id=1, source_target_pairs={{0,1},{1,0},{2,3},{3,2},{4,5},{5,4},{6,7},{7,6},{8,9},{9,8},{10,11... | collective-permute-start | bytes 248840 | tf_op jit(solution)/shard_map/ppermute | solution.py:708
  41.1 5.4 %collective-permute-start.16 = (bf16[3,54,256]{2,1,0:T(8,128)(2,1)S(1)}, bf16[3,54,256]{2,1,0:T(8,128)(2,1)S(1)}, u32[]{:S(2)}, u32[]{:S(2)}) collective-permute-start(bf16[3,54,256]{2,1,0:T(8,128)(2,1)S(1)} %half_sum.3), channel_id=1, source_target_pairs={{0,2},{1,3},{2,0},{3,1},{4,6},{5,7},{6,4},{7,5},{8,10},{9,11},{10,... | collective-permute-start | bytes 248840 | tf_op jit(solution)/shard_map/ppermute | solution.py:708
  42.1 8.1 %collective-permute-start.20 = (bf16[2,196,216]{2,1,0:T(8,128)(2,1)S(1)}, bf16[2,196,216]{2,1,0:T(8,128)(2,1)S(1)}, u32[]{:S(2)}, u32[]{:S(2)}) collective-permute-start(bf16[2,196,216]{2,1,0:T(8,128)(2,1)S(1)} %get-tuple-element.175.refs_0_), channel_id=1, source_target_pairs={{0,2},{1,3},{2,0},{3,1},{4,6},{5,7},{6,4},{7,5},{8,10},{9,11},{10,... | collective-permute-start | bytes 508040 | tf_op jit(solution)/shard_map/ppermute | solution.py:708
  46.9 4.9 %collective-permute-start.17 = (bf16[2,2,54,256]{3,2,1,0:T(8,128)(2,1)S(1)}, bf16[2,2,54,256]{3,2,1,0:T(8,128)(2,1)S(1)}, u32[]{:S(2)}, u32[]{:S(2)}) collective-permute-start(bf16[2,2,54,256]{3,2,1,0:T(8,128)(2,1)S(1)} %get-tuple-element.173), channel_id=1, source_target_pairs={{0,4},{4,0},{8,12},{12,8},{16,20},{20,16},{24,28},{28,24},{1,5},{5... | collective-permute-start | bytes 331784 | tf_op jit(solution)/shard_map/ppermute | solution.py:708
  47.7 5.5 %collective-permute-start.22 = (bf16[2,2,54,256]{3,2,1,0:T(8,128)(2,1)S(1)}, bf16[2,2,54,256]{3,2,1,0:T(8,128)(2,1)S(1)}, u32[]{:S(2)}, u32[]{:S(2)}) collective-permute-start(bf16[2,2,54,256]{3,2,1,0:T(8,128)(2,1)S(1)} %get-tuple-element.181), channel_id=1, source_target_pairs={{0,4},{4,0},{8,12},{12,8},{16,20},{20,16},{24,28},{28,24},{1,5},{5... | collective-permute-start | bytes 331784 | tf_op jit(solution)/shard_map/ppermute | solution.py:708
  49.0 7.5 %collective-permute-start.19 = (bf16[2,196,216]{2,1,0:T(8,128)(2,1)S(1)}, bf16[2,196,216]{2,1,0:T(8,128)(2,1)S(1)}, u32[]{:S(2)}, u32[]{:S(2)}) collective-permute-start(bf16[2,196,216]{2,1,0:T(8,128)(2,1)S(1)} %get-tuple-element.175.refs_0_), channel_id=1, source_target_pairs={{0,1},{1,0},{2,3},{3,2},{4,5},{5,4},{6,7},{7,6},{8,9},{9,8},{10,11... | collective-permute-start | bytes 508040 | tf_op jit(solution)/shard_map/ppermute | solution.py:708
  50.2 6.3 %collective-permute-start.21 = (bf16[2,196,216]{2,1,0:T(8,128)(2,1)S(1)}, bf16[2,196,216]{2,1,0:T(8,128)(2,1)S(1)}, u32[]{:S(2)}, u32[]{:S(2)}) collective-permute-start(bf16[2,196,216]{2,1,0:T(8,128)(2,1)S(1)} %collective-permute-done.20.refs_2_), channel_id=1, source_target_pairs={{0,1},{1,0},{2,3},{3,2},{4,5},{5,4},{6,7},{7,6},{8,9},{9,8},{10,11... | collective-permute-start | bytes 508040 | tf_op jit(solution)/shard_map/ppermute | solution.py:708
  51.8 6.7 %collective-permute-start.18 = (bf16[2,54,256]{2,1,0:T(8,128)(2,1)S(1)}, bf16[2,54,256]{2,1,0:T(8,128)(2,1)S(1)}, u32[]{:S(2)}, u32[]{:S(2)}) collective-permute-start(bf16[2,54,256]{2,1,0:T(8,128)(2,1)S(1)} %get-tuple-element.174), channel_id=1, source_target_pairs={{0,24},{4,28},{8,16},{12,20},{16,8},{20,12},{24,0},{28,4},{1,25},{... | collective-permute-start | bytes 165896 | tf_op jit(solution)/shard_map/ppermute | solution.py:708
  52.8 6.4 %collective-permute-start.24 = (bf16[2,54,256]{2,1,0:T(8,128)(2,1)S(1)}, bf16[2,54,256]{2,1,0:T(8,128)(2,1)S(1)}, u32[]{:S(2)}, u32[]{:S(2)}) collective-permute-start(bf16[2,54,256]{2,1,0:T(8,128)(2,1)S(1)} %get-tuple-element.184), channel_id=1, source_target_pairs={{0,16},{4,20},{8,24},{12,28},{16,0},{20,4},{24,8},{28,12},{1,17},{... | collective-permute-start | bytes 165896 | tf_op jit(solution)/shard_map/ppermute | solution.py:708
  53.1 6.1 %copy-start.1 = (f32[2,54,216]{2,0,1:T(2,128)S(1)}, f32[2,54,216]{2,0,1:T(2,128)}, u32[]{:S(2)}) copy-start(f32[2,54,216]{2,0,1:T(2,128)} %param.24) | copy-start | bytes 279940
  53.2 6.1 %copy-start.3 = (f32[2,54,216]{2,0,1:T(2,128)S(1)}, f32[2,54,216]{2,0,1:T(2,128)}, u32[]{:S(2)}) copy-start(f32[2,54,216]{2,0,1:T(2,128)} %param.25) | copy-start | bytes 279940
  53.2 6.1 %copy-start.4 = (f32[2,54,216]{2,0,1:T(2,128)S(1)}, f32[2,54,216]{2,0,1:T(2,128)}, u32[]{:S(2)}) copy-start(f32[2,54,216]{2,0,1:T(2,128)} %param.26) | copy-start | bytes 279940
  53.2 6.0 %copy-start.6 = (f32[9,216]{1,0:T(8,128)S(1)}, f32[9,216]{1,0:T(8,128)}, u32[]{:S(2)}) copy-start(f32[9,216]{1,0:T(8,128)} %refs_14_.1) | copy-start | bytes 23332
  53.2 6.0 %copy-start.7 = (f32[9,216]{1,0:T(8,128)S(1)}, f32[9,216]{1,0:T(8,128)}, u32[]{:S(2)}) copy-start(f32[9,216]{1,0:T(8,128)} %refs_15_.1) | copy-start | bytes 23332
  53.2 6.0 %copy-start.8 = (f32[2,12,12]{2,0,1:T(2,128)S(1)}, f32[2,12,12]{2,0,1:T(2,128)}, u32[]{:S(2)}) copy-start(f32[2,12,12]{2,0,1:T(2,128)} %param.31) | copy-start | bytes 3460
  53.2 6.0 %copy-start.9 = (f32[2,12,12]{2,0,1:T(2,128)S(1)}, f32[2,12,12]{2,0,1:T(2,128)}, u32[]{:S(2)}) copy-start(f32[2,12,12]{2,0,1:T(2,128)} %param.32) | copy-start | bytes 3460
  53.2 6.0 %copy-start.11 = (f32[4,216]{1,0:T(4,128)S(1)}, f32[4,216]{1,0:T(4,128)}, u32[]{:S(2)}) copy-start(f32[4,216]{1,0:T(4,128)} %refs_8_.1) | copy-start | bytes 10372
  53.2 6.0 %copy-start.12 = (f32[4,216]{1,0:T(4,128)S(1)}, f32[4,216]{1,0:T(4,128)}, u32[]{:S(2)}) copy-start(f32[4,216]{1,0:T(4,128)} %refs_9_.1) | copy-start | bytes 10372
  53.3 6.0 %collective-permute-start.23 = (bf16[2,54,256]{2,1,0:T(8,128)(2,1)S(1)}, bf16[2,54,256]{2,1,0:T(8,128)(2,1)S(1)}, u32[]{:S(2)}, u32[]{:S(2)}) collective-permute-start(bf16[2,54,256]{2,1,0:T(8,128)(2,1)S(1)} %get-tuple-element.183), channel_id=1, source_target_pairs={{0,8},{4,12},{8,0},{12,4},{16,24},{20,28},{24,16},{28,20},{1,9},{5... | collective-permute-start | bytes 165896 | tf_op jit(solution)/shard_map/ppermute | solution.py:708

commit v11 on v10

--- a/solution.py
+++ b/solution.py
@@ -790,7 +790,7 @@
     both, *attn_g = weights_back(x, a, dmid, norm_params, gn2, gqa, gqb, gk, gv, gt, out, attn_w)
     attn_1, attn_3 = permute(attn_g[1], "head", 1), permute(attn_g[3], "head", 1)
     (summed,) = call(half_sum_kernel, "half_sum", 0, 2, [SDS(attn_3.shape, bf16)])(attn_g[2], attn_3)
-    both, summed = lax.optimization_barrier((both, summed))
+    both, ffn_2 = lax.optimization_barrier((both, ffn_2))
     attn_2 = permute(summed, "head", 2)
     both_2, both_1 = permute(both, "head", 2), permute(both, "head", 1)
     both_3 = permute(both_2, "head", 1)

time: 60.6 us -> 60.6 us (level)
  transfers between devices with their start and end apart: 25 -> 25, of which waited for: 12 -> 11; matrix products, arithmetic and copies ran while one was open for 0% -> 0% of each run, Pallas kernels for 20% -> 20%
where the time goes in v11:
time: 60.6 us; the launch traced here: 60.4 us
  starting transfers between devices  22.3 us (37%)
  waiting for transfers between devices  17.5 us (29%)
  Pallas kernels  16.4 us (27%)
  between operations  2.96 us (5%)
  local copies, waits for them, and re-layouts  1.27 us (2%)
    ppermute x25, starting transfers between devices, permute(): lax.ppermute(x, axis, [(i, i ^ k) for i in range(lax.axis_size(axis))])  22.3 us
    ppermute x25, waiting for transfers between devices, permute(): lax.ppermute(x, axis, [(i, i ^ k) for i in range(lax.axis_size(axis))])  17.5 us
    pallas_call x2, Pallas kernels, scores_back(): call(scores_back_kernel, 'scores_back', 0, 11 + len(more), outs, scratch,...  3.36 us
    pallas_call x1, Pallas kernels, ffn_last(): call(ffn_last_kernel, 'ffn_last', 0, 14 + late, [SDS((SIDE * SIDE, dim),...  2.3 us
    pallas_call x1, Pallas kernels, attn_fwd(): call(attn_fwd_kernel, 'attn_fwd', 0, 5 + len(w), [SDS((pad, dim), f32)] +...  2.17 us
    pallas_call x1, Pallas kernels, local(): pl.pallas_call(assemble_kernel, grid=(1,), in_specs=[SM] + [whole(*both.s...  1.98 us
    pallas_call x1, Pallas kernels, ffn_first(): call(ffn_first_kernel, 'ffn_first', 0, 4 + count, [SDS((pad, dim), f32),...  1.57 us
  transfers between devices with their start and end apart: 25, of which 11 were waited for; matrix products, arithmetic and copies ran while one was open for 0% of the time, Pallas kernels for 20%

profile of v11, /device:TPU:0, one launch (start us, length us, event | category | flops | bytes accessed | tf_op | source)
XLA Modules:
  0.0 60.4 jit_solution(17074405064576886331)
XLA Ops:
  0.7 0.9 %copy-done = f32[2,54,216]{2,0,1:T(2,128)S(1)} copy-done((f32[2,54,216]{2,0,1:T(2,128)S(1)}, f32[2,54,216]{2,0,1:T(2,128)}, u32[]{:S(2)}) %copy-start) | copy-done | bytes 93336
  1.5 0.2 cast.1.refs_0_
  1.8 3.0 %collective-permute-start.2 = (bf16[2,54,216]{2,1,0:T(8,128)(2,1)S(1)}, bf16[2,54,216]{2,1,0:T(8,128)(2,1)S(1)}, u32[]{:S(2)}, u32[]{:S(2)}) collective-permute-start(bf16[2,54,216]{2,1,0:T(8,128)(2,1)S(1)} %cast.1.refs_0_), channel_id=1, source_target_pairs={{0,4},{4,0},{8,12},{12,8},{16,20},{20,16},{24,28},{28,24},{1,5},{5... | collective-permute-start | bytes 139976 | tf_op jit(solution)/shard_map/ppermute | solution.py:708
  4.8 1.6 %collective-permute-start.1 = (bf16[2,54,216]{2,1,0:T(8,128)(2,1)S(1)}, bf16[2,54,216]{2,1,0:T(8,128)(2,1)S(1)}, u32[]{:S(2)}, u32[]{:S(2)}) collective-permute-start(bf16[2,54,216]{2,1,0:T(8,128)(2,1)S(1)} %cast.1.refs_0_), channel_id=1, source_target_pairs={{0,8},{4,12},{8,0},{12,4},{16,24},{20,28},{24,16},{28,20},{1,9},{5... | collective-permute-start | bytes 139976 | tf_op jit(solution)/shard_map/ppermute | solution.py:708
  6.4 2.6 %collective-permute-start = (bf16[2,54,216]{2,1,0:T(8,128)(2,1)S(1)}, bf16[2,54,216]{2,1,0:T(8,128)(2,1)S(1)}, u32[]{:S(2)}, u32[]{:S(2)}) collective-permute-start(bf16[2,54,216]{2,1,0:T(8,128)(2,1)S(1)} %cast.1.refs_0_), channel_id=1, source_target_pairs={{0,16},{4,20},{8,24},{12,28},{16,0},{20,4},{24,8},{28,12},{1,17},{... | collective-permute-start | bytes 139976 | tf_op jit(solution)/shard_map/ppermute | solution.py:708
  9.0 0.2 collective-permute-start.3
  9.2 3.1 %collective-permute-done.refs_1_ = bf16[2,54,216]{2,1,0:T(8,128)(2,1)S(1)} collective-permute-done((bf16[2,54,216]{2,1,0:T(8,128)(2,1)S(1)}, bf16[2,54,216]{2,1,0:T(8,128)(2,1)S(1)}, u32[]{:S(2)}, u32[]{:S(2)}) %collective-permute-start) | collective-permute-done | bytes 46688 | tf_op jit(solution)/shard_map/ppermute | solution.py:708
  12.3 2.7 %collective-permute-done.3.refs_2_ = bf16[2,54,216]{2,1,0:T(8,128)(2,1)S(1)} collective-permute-done((bf16[2,54,216]{2,1,0:T(8,128)(2,1)S(1)}, bf16[2,54,216]{2,1,0:T(8,128)(2,1)S(1)}, u32[]{:S(2)}, u32[]{:S(2)}) %collective-permute-start.3) | collective-permute-done | bytes 46688 | tf_op jit(solution)/shard_map/ppermute | solution.py:708
  15.0 0.6 collective-permute-start.4
  17.6 0.1 concatenate.3.scal
  17.7 0.2 copy.34.cot_ref
  17.9 1.1 %prep.1 = (f32[224,216]{1,0:T(8,128)S(1)}, bf16[224,216]{1,0:T(8,128)(2,1)S(1)}, f32[224,216]{1,0:T(8,128)S(1)}, f32[2,192,256]{2,1,0:T(8,128)S(1)}, f32[224,128...) custom-call(s32[6]{0:T(128)S(1)} %concatenate.3.scal, ...), custom_call_target="tpu_custom_call" | custom-call | flops 1000000000 | bytes 3000000 | tf_op jit(solution)/shard_map/prep/pallas_call | solution.py:602
  19.0 1.4 %collective-permute-done.4.refs_3_ = bf16[3,2,54,216]{3,2,1,0:T(8,128)(2,1)S(1)} collective-permute-done((bf16[3,2,54,216]{3,2,1,0:T(8,128)(2,1)S(1)}, bf16[3,2,54,216]{3,2,1,0:T(8,128)(2,1)S(1)}, u32[]{:S(2)}, u32[]{:S(2)}) %collective-permute-start.4) | collective-permute-done | bytes 140000 | tf_op jit(solution)/shard_map/ppermute | solution.py:708
  20.5 0.3 select_attn.1.refs_0_
  20.8 1.6 %collective-permute-start.6 = (bf16[4,54,216]{2,1,0:T(8,128)(2,1)S(1)}, bf16[4,54,216]{2,1,0:T(8,128)(2,1)S(1)}, u32[]{:S(2)}, u32[]{:S(2)}) collective-permute-start(bf16[4,54,216]{2,1,0:T(8,128)(2,1)S(1)} %select_attn.1.refs_0_), channel_id=1, source_target_pairs={{0,2},{1,3},{2,0},{3,1},{4,6},{5,7},{6,4},{7,5},{8,10},{9,11},{10,... | collective-permute-start | bytes 279944 | tf_op jit(solution)/shard_map/ppermute | solution.py:708
  22.3 0.5 select_ffn.1.refs_0_
  22.9 0.6 collective-permute-start.8
  23.5 0.5 collective-permute-start.5
  24.0 2.0 %collective-permute-done.6.refs_2_ = bf16[4,54,216]{2,1,0:T(8,128)(2,1)S(1)} collective-permute-done((bf16[4,54,216]{2,1,0:T(8,128)(2,1)S(1)}, bf16[4,54,216]{2,1,0:T(8,128)(2,1)S(1)}, u32[]{:S(2)}, u32[]{:S(2)}) %collective-permute-start.6) | collective-permute-done | bytes 93344 | tf_op jit(solution)/shard_map/ppermute | solution.py:708
  26.0 1.3 %collective-permute-done.7.refs_3_ = bf16[4,54,216]{2,1,0:T(8,128)(2,1)S(1)} collective-permute-done((bf16[4,54,216]{2,1,0:T(8,128)(2,1)S(1)}, bf16[4,54,216]{2,1,0:T(8,128)(2,1)S(1)}, u32[]{:S(2)}, u32[]{:S(2)}) %collective-permute-start.7) | collective-permute-done | bytes 93344 | tf_op jit(solution)/shard_map/ppermute | solution.py:708
  27.3 2.2 %attn_fwd.1 = (f32[224,216]{1,0:T(8,128)S(1)}, bf16[224,256]{1,0:T(8,128)(2,1)S(1)}, bf16[224,256]{1,0:T(8,128)(2,1)S(1)}, bf16[224,256]{1,0:T(8,128)(2,1)S(1)},...) custom-call(f32[224,216]{1,0:T(8,128)S(1)} %get-tuple-element.114.x_, ...), custom_call_target="tpu_custom_call" | custom-call | flops 1000000000 | bytes 3000000 | tf_op jit(solution)/shard_map/attn_fwd/pallas_call | solution.py:632
  29.5 0.2 collective-permute-start.10
  29.7 1.6 %ffn_first.1 = (f32[224,216]{1,0:T(8,128)S(1)}, f32[224,128]{1,0:T(8,128)S(1)}, bf16[224,216]{1,0:T(8,128)(2,1)S(1)}, bf16[224,216]{1,0:T(8,128)(2,1)S(1)}, bf16...) custom-call(f32[224,216]{1,0:T(8,128)S(1)} %get-tuple-element.122.mi, ...), custom_call_target="tpu_custom_call" | custom-call | flops 3000000000 | bytes 9000000 | tf_op jit(solution)/shard_map/ffn_first/pallas_call | solution.py:646
  31.3 2.3 %ffn_last.1 = (bf16[196,216]{1,0:T(8,128)(2,1)S(1)}, f32[224,216]{1,0:T(8,128)S(1)}, f32[8,216]{1,0:T(8,128)S(1)}, bf16[9,54,256]{2,1,0:T(8,128)(2,1)S(1)}, bf16...) custom-call(f32[224,216]{1,0:T(8,128)S(1)} %get-tuple-element.122.mid_ref, ...), custom_call_target="tpu_custom_call" | custom-call | flops 4000000000 | bytes 12000000 | tf_op jit(solution)/shard_map/ffn_last/pallas_call | solution.py:660
  33.6 0.4 collective-permute-start.11
  34.0 1.0 %scores_back.2 = (bf16[224,256]{1,0:T(8,128)(2,1)S(1)}, bf16[64,256]{1,0:T(8,128)(2,1)S(1)}, f32[224,256]{1,0:T(8,128)S(1)}, f32[224,256]{1,0:T(8,128)S(1)}, f32...) custom-call(f32[224,216]{1,0:T(8,128)S(1)} %get-tuple-element.140.dmid_ref, f32[2,192,256]{2,1,0:T(8,128)S(1)} %get-tuple-element.116.mix_ref, ...), custom_call_target="tpu_custom_call" | custom-call | flops 4000000000 | bytes 12000000 | tf_op jit(solution)/shard_map/scores_back/pallas_call | solution.py:690
  35.1 0.1 collective-permute-done.11.b_ref
  35.3 0.4 collective-permute-start.12
  35.7 1.1 %collective-permute-start.13 = (bf16[9,54,256]{2,1,0:T(8,128)(2,1)S(1)}, bf16[9,54,256]{2,1,0:T(8,128)(2,1)S(1)}, u32[]{:S(2)}, u32[]{:S(2)}) collective-permute-start(bf16[9,54,256]{2,1,0:T(8,128)(2,1)S(1)} %half_sum.2), channel_id=1, source_target_pairs={{0,2},{1,3},{2,0},{3,1},{4,6},{5,7},{6,4},{7,5},{8,10},{9,11},{10,... | collective-permute-start | bytes 746504 | tf_op jit(solution)/shard_map/ppermute | solution.py:708
  36.8 2.3 %scores_back.3 = (bf16[160,256]{1,0:T(8,128)(2,1)S(1)}, bf16[224,256]{1,0:T(8,128)(2,1)S(1)}, bf16[224,256]{1,0:T(8,128)(2,1)S(1)}, f32[2,12,12]{2,1,0:T(8,128)S(1)}) custom-call(f32[224,216]{1,0:T(8,128)S(1)} %get-tuple-element.140.dmid_ref, f32[2,192,256]{2,1,0:T(8,128)S(1)} %get-tuple-element.116.mix_ref, f32[6,256]{1,0:T(8,128)S(1)} %get-tuple-element.118.keep_ref, ...), custom_call_target="tpu_custom_call" | custom-call | flops 4000000000 | bytes 12000000 | tf_op jit(solution)/shard_map/scores_back/pallas_call | solution.py:690
  39.2 0.6 weights_back.1
  39.8 0.5 collective-permute-start.14
  40.3 0.8 %collective-permute-done.15.b_ref = bf16[3,54,256]{2,1,0:T(8,128)(2,1)S(1)} collective-permute-done((bf16[3,54,256]{2,1,0:T(8,128)(2,1)S(1)}, bf16[3,54,256]{2,1,0:T(8,128)(2,1)S(1)}, u32[]{:S(2)}, u32[]{:S(2)}) %collective-permute-start.15) | collective-permute-done | bytes 82976 | tf_op jit(solution)/shard_map/ppermute | solution.py:708
  41.1 1.0 %collective-permute-start.16 = (bf16[3,54,256]{2,1,0:T(8,128)(2,1)S(1)}, bf16[3,54,256]{2,1,0:T(8,128)(2,1)S(1)}, u32[]{:S(2)}, u32[]{:S(2)}) collective-permute-start(bf16[3,54,256]{2,1,0:T(8,128)(2,1)S(1)} %half_sum.3), channel_id=1, source_target_pairs={{0,2},{1,3},{2,0},{3,1},{4,6},{5,7},{6,4},{7,5},{8,10},{9,11},{10,... | collective-permute-start | bytes 248840 | tf_op jit(solution)/shard_map/ppermute | solution.py:708
  42.1 1.9 %collective-permute-done.13.refs_2_ = bf16[9,54,256]{2,1,0:T(8,128)(2,1)S(1)} collective-permute-done((bf16[9,54,256]{2,1,0:T(8,128)(2,1)S(1)}, bf16[9,54,256]{2,1,0:T(8,128)(2,1)S(1)}, u32[]{:S(2)}, u32[]{:S(2)}) %collective-permute-start.13) | collective-permute-done | bytes 248864 | tf_op jit(solution)/shard_map/ppermute | solution.py:708
  44.0 1.3 %collective-permute-start.20 = (bf16[2,196,216]{2,1,0:T(8,128)(2,1)S(1)}, bf16[2,196,216]{2,1,0:T(8,128)(2,1)S(1)}, u32[]{:S(2)}, u32[]{:S(2)}) collective-permute-start(bf16[2,196,216]{2,1,0:T(8,128)(2,1)S(1)} %get-tuple-element.175.refs_0_), channel_id=1, source_target_pairs={{0,2},{1,3},{2,0},{3,1},{4,6},{5,7},{6,4},{7,5},{8,10},{9,11},{10,... | collective-permute-start | bytes 508040 | tf_op jit(solution)/shard_map/ppermute | solution.py:708
  45.3 0.7 %spread_ffn.1.old_ref = bf16[4,2,2,54,256]{4,3,2,1,0:T(8,128)(2,1)S(1)} custom-call(s32[12]{0:T(128)S(1)} %copy-done.13, s32[6]{0:T(128)S(1)} %concatenate.3.scal, bf16[9,54,256]{2,1,0:T(8,128)(2,1)S(1)} %get-tuple-element.137.refs_0_, bf16[9,54,256]{2,1,0:T(8,128)(2,1)S(1)} %collective-permute-done.12.refs_1_, ...), custom_call_target="tpu_custom_call" | custom-call | flops 1000000000 | bytes 3000000 | tf_op jit(solution)/shard_map/spread_ffn/pallas_call | solution.py:797
  46.0 0.3 spread_attn.1
  46.3 0.8 %collective-permute-start.17 = (bf16[2,2,54,256]{3,2,1,0:T(8,128)(2,1)S(1)}, bf16[2,2,54,256]{3,2,1,0:T(8,128)(2,1)S(1)}, u32[]{:S(2)}, u32[]{:S(2)}) collective-permute-start(bf16[2,2,54,256]{3,2,1,0:T(8,128)(2,1)S(1)} %get-tuple-element.173), channel_id=1, source_target_pairs={{0,4},{4,0},{8,12},{12,8},{16,20},{20,16},{24,28},{28,24},{1,5},{5... | collective-permute-start | bytes 331784 | tf_op jit(solution)/shard_map/ppermute | solution.py:708
  47.1 1.3 %collective-permute-start.22 = (bf16[2,2,54,256]{3,2,1,0:T(8,128)(2,1)S(1)}, bf16[2,2,54,256]{3,2,1,0:T(8,128)(2,1)S(1)}, u32[]{:S(2)}, u32[]{:S(2)}) collective-permute-start(bf16[2,2,54,256]{3,2,1,0:T(8,128)(2,1)S(1)} %get-tuple-element.181), channel_id=1, source_target_pairs={{0,4},{4,0},{8,12},{12,8},{16,20},{20,16},{24,28},{28,24},{1,5},{5... | collective-permute-start | bytes 331784 | tf_op jit(solution)/shard_map/ppermute | solution.py:708
  48.4 1.9 %collective-permute-done.20.refs_2_ = bf16[2,196,216]{2,1,0:T(8,128)(2,1)S(1)} collective-permute-done((bf16[2,196,216]{2,1,0:T(8,128)(2,1)S(1)}, bf16[2,196,216]{2,1,0:T(8,128)(2,1)S(1)}, u32[]{:S(2)}, u32[]{:S(2)}) %collective-permute-start.20) | collective-permute-done | bytes 169376 | tf_op jit(solution)/shard_map/ppermute | solution.py:708
  50.3 1.5 %collective-permute-done.17.other_ref = bf16[2,2,54,256]{3,2,1,0:T(8,128)(2,1)S(1)} collective-permute-done((bf16[2,2,54,256]{3,2,1,0:T(8,128)(2,1)S(1)}, bf16[2,2,54,256]{3,2,1,0:T(8,128)(2,1)S(1)}, u32[]{:S(2)}, u32[]{:S(2)}) %collective-permute-start.17) | collective-permute-done | bytes 110624 | tf_op jit(solution)/shard_map/ppermute | solution.py:708
  51.8 1.0 %collective-permute-start.18 = (bf16[2,54,256]{2,1,0:T(8,128)(2,1)S(1)}, bf16[2,54,256]{2,1,0:T(8,128)(2,1)S(1)}, u32[]{:S(2)}, u32[]{:S(2)}) collective-permute-start(bf16[2,54,256]{2,1,0:T(8,128)(2,1)S(1)} %get-tuple-element.174), channel_id=1, source_target_pairs={{0,24},{4,28},{8,16},{12,20},{16,8},{20,12},{24,0},{28,4},{1,25},{... | collective-permute-start | bytes 165896 | tf_op jit(solution)/shard_map/ppermute | solution.py:708
  52.8 0.3 collective-permute-start.24
  53.2 3.3 %collective-permute-start.23 = (bf16[2,54,256]{2,1,0:T(8,128)(2,1)S(1)}, bf16[2,54,256]{2,1,0:T(8,128)(2,1)S(1)}, u32[]{:S(2)}, u32[]{:S(2)}) collective-permute-start(bf16[2,54,256]{2,1,0:T(8,128)(2,1)S(1)} %get-tuple-element.183), channel_id=1, source_target_pairs={{0,8},{4,12},{8,0},{12,4},{16,24},{20,28},{24,16},{28,20},{1,9},{5... | collective-permute-start | bytes 165896 | tf_op jit(solution)/shard_map/ppermute | solution.py:708
  56.5 2.0 %assemble.1 = (f32[196,4,216]{2,1,0:T(4,128)}, f32[196,4,216]{2,1,0:T(4,128)}) custom-call(s32[6]{0:T(128)S(1)} %concatenate.3.scal, bf16[2,196,216]{2,1,0:T(8,128)(2,1)S(1)} %get-tuple-element.175.refs_0_, bf16[2,196,216]{2,1,0:T(8,128)(2,1)S(1)} %collective-permute-done.19.refs_1_, bf16[2,196,216]{2,1,0:T(8,128)(2,1)S(1)} %collective-permute-done.20.refs_2_, ...), custom_call_target="tpu_custom_call" | custom-call | flops 1000000000 | bytes 3000000 | tf_op jit(solution)/shard_map/assemble/pallas_call | solution.py:813
  58.5 0.7 %collective-permute-done.24.refs_2_ = bf16[2,54,256]{2,1,0:T(8,128)(2,1)S(1)} collective-permute-done((bf16[2,54,256]{2,1,0:T(8,128)(2,1)S(1)}, bf16[2,54,256]{2,1,0:T(8,128)(2,1)S(1)}, u32[]{:S(2)}, u32[]{:S(2)}) %collective-permute-start.24) | collective-permute-done | bytes 55328 | tf_op jit(solution)/shard_map/ppermute | solution.py:708
  59.3 1.1 %update.1 = (f32[54,2,216]{2,1,0:T(2,128)}, f32[54,2,216]{2,1,0:T(2,128)}, f32[54,2,216]{2,1,0:T(2,128)}, bf16[54,2,216]{2,1,0:T(2,128)(2,1)}, f32[4,216]{1,0:T(...) custom-call(f32[2,54,256]{2,1,0:T(8,128)S(1)} %get-tuple-element.182, ...), custom_call_target="tpu_custom_call" | custom-call | flops 1000000000 | bytes 3000000 | tf_op jit(solution)/shard_map/update/pallas_call | solution.py:720
  (57 shorter events, 0.4 us)
Async XLA Ops:
  0.6 0.9 %copy-start = (f32[2,54,216]{2,0,1:T(2,128)S(1)}, f32[2,54,216]{2,0,1:T(2,128)}, u32[]{:S(2)}) copy-start(f32[2,54,216]{2,0,1:T(2,128)} %param.24) | copy-start | bytes 279940
  1.8 15.9 %copy-start.2 = (f32[2,12,12]{2,0,1:T(2,128)S(1)}, f32[2,12,12]{2,0,1:T(2,128)}, u32[]{:S(2)}) copy-start(f32[2,12,12]{2,0,1:T(2,128)} %param.30) | copy-start | bytes 3460
  1.8 15.9 %copy-start.15 = (bf16[4,196,216]{2,0,1:T(4,128)(2,1)S(1)}, bf16[4,196,216]{2,0,1:T(4,128)(2,1)}, u32[]{:S(2)}) copy-start(bf16[4,196,216]{2,0,1:T(4,128)(2,1)} %param.18) | copy-start | bytes 1016068
  1.8 7.4 %collective-permute-start.2 = (bf16[2,54,216]{2,1,0:T(8,128)(2,1)S(1)}, bf16[2,54,216]{2,1,0:T(8,128)(2,1)S(1)}, u32[]{:S(2)}, u32[]{:S(2)}) collective-permute-start(bf16[2,54,216]{2,1,0:T(8,128)(2,1)S(1)} %cast.1.refs_0_), channel_id=1, source_target_pairs={{0,4},{4,0},{8,12},{12,8},{16,20},{20,16},{24,28},{28,24},{1,5},{5... | collective-permute-start | bytes 139976 | tf_op jit(solution)/shard_map/ppermute | solution.py:708
  4.8 4.4 %collective-permute-start.1 = (bf16[2,54,216]{2,1,0:T(8,128)(2,1)S(1)}, bf16[2,54,216]{2,1,0:T(8,128)(2,1)S(1)}, u32[]{:S(2)}, u32[]{:S(2)}) collective-permute-start(bf16[2,54,216]{2,1,0:T(8,128)(2,1)S(1)} %cast.1.refs_0_), channel_id=1, source_target_pairs={{0,8},{4,12},{8,0},{12,4},{16,24},{20,28},{24,16},{28,20},{1,9},{5... | collective-permute-start | bytes 139976 | tf_op jit(solution)/shard_map/ppermute | solution.py:708
  6.4 5.9 %collective-permute-start = (bf16[2,54,216]{2,1,0:T(8,128)(2,1)S(1)}, bf16[2,54,216]{2,1,0:T(8,128)(2,1)S(1)}, u32[]{:S(2)}, u32[]{:S(2)}) collective-permute-start(bf16[2,54,216]{2,1,0:T(8,128)(2,1)S(1)} %cast.1.refs_0_), channel_id=1, source_target_pairs={{0,16},{4,20},{8,24},{12,28},{16,0},{20,4},{24,8},{28,12},{1,17},{... | collective-permute-start | bytes 139976 | tf_op jit(solution)/shard_map/ppermute | solution.py:708
  9.0 6.0 %collective-permute-start.3 = (bf16[2,54,216]{2,1,0:T(8,128)(2,1)S(1)}, bf16[2,54,216]{2,1,0:T(8,128)(2,1)S(1)}, u32[]{:S(2)}, u32[]{:S(2)}) collective-permute-start(bf16[2,54,216]{2,1,0:T(8,128)(2,1)S(1)} %cast.1.refs_0_), channel_id=1, source_target_pairs={{0,24},{4,28},{8,16},{12,20},{16,8},{20,12},{24,0},{28,4},{1,25},{... | collective-permute-start | bytes 139976 | tf_op jit(solution)/shard_map/ppermute | solution.py:708
  15.0 2.7 %copy-start.14 = (f32[4,196,216]{2,0,1:T(4,128)S(1)}, f32[4,196,216]{2,0,1:T(4,128)}, u32[]{:S(2)}) copy-start(f32[4,196,216]{2,0,1:T(4,128)} %param.19) | copy-start | bytes 2032132
  15.0 2.9 %copy-start.10 = (f32[4,216]{1,0:T(4,128)S(1)}, f32[4,216]{1,0:T(4,128)}, u32[]{:S(2)}) copy-start(f32[4,216]{1,0:T(4,128)} %refs_7_.1) | copy-start | bytes 10372
  15.0 2.9 %copy-start.13 = (s32[12]{0:T(128)S(1)}, s32[12]{0:T(128)}, u32[]{:S(2)}) copy-start(s32[12]{0:T(128)} %slot_ref.3) | copy-start | bytes 148
  15.0 5.5 %collective-permute-start.4 = (bf16[3,2,54,216]{3,2,1,0:T(8,128)(2,1)S(1)}, bf16[3,2,54,216]{3,2,1,0:T(8,128)(2,1)S(1)}, u32[]{:S(2)}, u32[]{:S(2)}) collective-permute-start(bf16[3,2,54,216]{3,2,1,0:T(8,128)(2,1)S(1)} %stack.1.refs_1_), channel_id=1, source_target_pairs={{0,4},{4,0},{8,12},{12,8},{16,20},{20,16},{24,28},{28,24},{1,5},{5... | collective-permute-start | bytes 419912 | tf_op jit(solution)/shard_map/ppermute | solution.py:708
  20.5 1.9 %copy-start.5 = (f32[9,216]{1,0:T(8,128)S(1)}, f32[9,216]{1,0:T(8,128)}, u32[]{:S(2)}) copy-start(f32[9,216]{1,0:T(8,128)} %refs_13_.1) | copy-start | bytes 23332
  20.8 5.2 %collective-permute-start.6 = (bf16[4,54,216]{2,1,0:T(8,128)(2,1)S(1)}, bf16[4,54,216]{2,1,0:T(8,128)(2,1)S(1)}, u32[]{:S(2)}, u32[]{:S(2)}) collective-permute-start(bf16[4,54,216]{2,1,0:T(8,128)(2,1)S(1)} %select_attn.1.refs_0_), channel_id=1, source_target_pairs={{0,2},{1,3},{2,0},{3,1},{4,6},{5,7},{6,4},{7,5},{8,10},{9,11},{10,... | collective-permute-start | bytes 279944 | tf_op jit(solution)/shard_map/ppermute | solution.py:708
  22.9 6.6 %collective-permute-start.8 = (bf16[9,54,216]{2,1,0:T(8,128)(2,1)S(1)}, bf16[9,54,216]{2,1,0:T(8,128)(2,1)S(1)}, u32[]{:S(2)}, u32[]{:S(2)}) collective-permute-start(bf16[9,54,216]{2,1,0:T(8,128)(2,1)S(1)} %select_ffn.1.refs_0_), channel_id=1, source_target_pairs={{0,2},{1,3},{2,0},{3,1},{4,6},{5,7},{6,4},{7,5},{8,10},{9,11},{10,... | collective-permute-start | bytes 629864 | tf_op jit(solution)/shard_map/ppermute | solution.py:708
  23.4 6.3 %collective-permute-start.9 = (bf16[9,54,216]{2,1,0:T(8,128)(2,1)S(1)}, bf16[9,54,216]{2,1,0:T(8,128)(2,1)S(1)}, u32[]{:S(2)}, u32[]{:S(2)}) collective-permute-start(bf16[9,54,216]{2,1,0:T(8,128)(2,1)S(1)} %select_ffn.1.refs_0_), channel_id=1, source_target_pairs={{0,1},{1,0},{2,3},{3,2},{4,5},{5,4},{6,7},{7,6},{8,9},{9,8},{10,11... | collective-permute-start | bytes 629864 | tf_op jit(solution)/shard_map/ppermute | solution.py:708
  23.5 2.6 %collective-permute-start.5 = (bf16[4,54,216]{2,1,0:T(8,128)(2,1)S(1)}, bf16[4,54,216]{2,1,0:T(8,128)(2,1)S(1)}, u32[]{:S(2)}, u32[]{:S(2)}) collective-permute-start(bf16[4,54,216]{2,1,0:T(8,128)(2,1)S(1)} %select_attn.1.refs_0_), channel_id=1, source_target_pairs={{0,1},{1,0},{2,3},{3,2},{4,5},{5,4},{6,7},{7,6},{8,9},{9,8},{10,11... | collective-permute-start | bytes 279944 | tf_op jit(solution)/shard_map/ppermute | solution.py:708
  26.0 1.3 %collective-permute-start.7 = (bf16[4,54,216]{2,1,0:T(8,128)(2,1)S(1)}, bf16[4,54,216]{2,1,0:T(8,128)(2,1)S(1)}, u32[]{:S(2)}, u32[]{:S(2)}) collective-permute-start(bf16[4,54,216]{2,1,0:T(8,128)(2,1)S(1)} %collective-permute-done.6.refs_2_), channel_id=1, source_target_pairs={{0,1},{1,0},{2,3},{3,2},{4,5},{5,4},{6,7},{7,6},{8,9},{9,8},{10,11... | collective-permute-start | bytes 279944 | tf_op jit(solution)/shard_map/ppermute | solution.py:708
  29.5 1.8 %collective-permute-start.10 = (bf16[9,54,216]{2,1,0:T(8,128)(2,1)S(1)}, bf16[9,54,216]{2,1,0:T(8,128)(2,1)S(1)}, u32[]{:S(2)}, u32[]{:S(2)}) collective-permute-start(bf16[9,54,216]{2,1,0:T(8,128)(2,1)S(1)} %collective-permute-done.8.refs_5_), channel_id=1, source_target_pairs={{0,1},{1,0},{2,3},{3,2},{4,5},{5,4},{6,7},{7,6},{8,9},{9,8},{10,11... | collective-permute-start | bytes 629864 | tf_op jit(solution)/shard_map/ppermute | solution.py:708
  33.6 1.6 %collective-permute-start.11 = (bf16[9,54,256]{2,1,0:T(8,128)(2,1)S(1)}, bf16[9,54,256]{2,1,0:T(8,128)(2,1)S(1)}, u32[]{:S(2)}, u32[]{:S(2)}) collective-permute-start(bf16[9,54,256]{2,1,0:T(8,128)(2,1)S(1)} %get-tuple-element.150), channel_id=1, source_target_pairs={{0,1},{1,0},{2,3},{3,2},{4,5},{5,4},{6,7},{7,6},{8,9},{9,8},{10,11... | collective-permute-start | bytes 746504 | tf_op jit(solution)/shard_map/ppermute | solution.py:708
  35.3 10.0 %collective-permute-start.12 = (bf16[9,54,256]{2,1,0:T(8,128)(2,1)S(1)}, bf16[9,54,256]{2,1,0:T(8,128)(2,1)S(1)}, u32[]{:S(2)}, u32[]{:S(2)}) collective-permute-start(bf16[9,54,256]{2,1,0:T(8,128)(2,1)S(1)} %get-tuple-element.152), channel_id=1, source_target_pairs={{0,1},{1,0},{2,3},{3,2},{4,5},{5,4},{6,7},{7,6},{8,9},{9,8},{10,11... | collective-permute-start | bytes 746504 | tf_op jit(solution)/shard_map/ppermute | solution.py:708
  35.7 8.3 %collective-permute-start.13 = (bf16[9,54,256]{2,1,0:T(8,128)(2,1)S(1)}, bf16[9,54,256]{2,1,0:T(8,128)(2,1)S(1)}, u32[]{:S(2)}, u32[]{:S(2)}) collective-permute-start(bf16[9,54,256]{2,1,0:T(8,128)(2,1)S(1)} %half_sum.2), channel_id=1, source_target_pairs={{0,2},{1,3},{2,0},{3,1},{4,6},{5,7},{6,4},{7,5},{8,10},{9,11},{10,... | collective-permute-start | bytes 746504 | tf_op jit(solution)/shard_map/ppermute | solution.py:708
  39.8 1.3 %collective-permute-start.15 = (bf16[3,54,256]{2,1,0:T(8,128)(2,1)S(1)}, bf16[3,54,256]{2,1,0:T(8,128)(2,1)S(1)}, u32[]{:S(2)}, u32[]{:S(2)}) collective-permute-start(bf16[3,54,256]{2,1,0:T(8,128)(2,1)S(1)} %get-tuple-element.171), channel_id=1, source_target_pairs={{0,1},{1,0},{2,3},{3,2},{4,5},{5,4},{6,7},{7,6},{8,9},{9,8},{10,11... | collective-permute-start | bytes 248840 | tf_op jit(solution)/shard_map/ppermute | solution.py:708
  39.8 6.1 %collective-permute-start.14 = (bf16[3,54,256]{2,1,0:T(8,128)(2,1)S(1)}, bf16[3,54,256]{2,1,0:T(8,128)(2,1)S(1)}, u32[]{:S(2)}, u32[]{:S(2)}) collective-permute-start(bf16[3,54,256]{2,1,0:T(8,128)(2,1)S(1)} %get-tuple-element.169), channel_id=1, source_target_pairs={{0,1},{1,0},{2,3},{3,2},{4,5},{5,4},{6,7},{7,6},{8,9},{9,8},{10,11... | collective-permute-start | bytes 248840 | tf_op jit(solution)/shard_map/ppermute | solution.py:708
  41.1 4.8 %collective-permute-start.16 = (bf16[3,54,256]{2,1,0:T(8,128)(2,1)S(1)}, bf16[3,54,256]{2,1,0:T(8,128)(2,1)S(1)}, u32[]{:S(2)}, u32[]{:S(2)}) collective-permute-start(bf16[3,54,256]{2,1,0:T(8,128)(2,1)S(1)} %half_sum.3), channel_id=1, source_target_pairs={{0,2},{1,3},{2,0},{3,1},{4,6},{5,7},{6,4},{7,5},{8,10},{9,11},{10,... | collective-permute-start | bytes 248840 | tf_op jit(solution)/shard_map/ppermute | solution.py:708
  44.0 6.3 %collective-permute-start.20 = (bf16[2,196,216]{2,1,0:T(8,128)(2,1)S(1)}, bf16[2,196,216]{2,1,0:T(8,128)(2,1)S(1)}, u32[]{:S(2)}, u32[]{:S(2)}) collective-permute-start(bf16[2,196,216]{2,1,0:T(8,128)(2,1)S(1)} %get-tuple-element.175.refs_0_), channel_id=1, source_target_pairs={{0,2},{1,3},{2,0},{3,1},{4,6},{5,7},{6,4},{7,5},{8,10},{9,11},{10,... | collective-permute-start | bytes 508040 | tf_op jit(solution)/shard_map/ppermute | solution.py:708
  46.3 5.5 %collective-permute-start.17 = (bf16[2,2,54,256]{3,2,1,0:T(8,128)(2,1)S(1)}, bf16[2,2,54,256]{3,2,1,0:T(8,128)(2,1)S(1)}, u32[]{:S(2)}, u32[]{:S(2)}) collective-permute-start(bf16[2,2,54,256]{3,2,1,0:T(8,128)(2,1)S(1)} %get-tuple-element.173), channel_id=1, source_target_pairs={{0,4},{4,0},{8,12},{12,8},{16,20},{20,16},{24,28},{28,24},{1,5},{5... | collective-permute-start | bytes 331784 | tf_op jit(solution)/shard_map/ppermute | solution.py:708
  47.1 6.0 %collective-permute-start.22 = (bf16[2,2,54,256]{3,2,1,0:T(8,128)(2,1)S(1)}, bf16[2,2,54,256]{3,2,1,0:T(8,128)(2,1)S(1)}, u32[]{:S(2)}, u32[]{:S(2)}) collective-permute-start(bf16[2,2,54,256]{3,2,1,0:T(8,128)(2,1)S(1)} %get-tuple-element.181), channel_id=1, source_target_pairs={{0,4},{4,0},{8,12},{12,8},{16,20},{20,16},{24,28},{28,24},{1,5},{5... | collective-permute-start | bytes 331784 | tf_op jit(solution)/shard_map/ppermute | solution.py:708
  48.4 8.1 %collective-permute-start.19 = (bf16[2,196,216]{2,1,0:T(8,128)(2,1)S(1)}, bf16[2,196,216]{2,1,0:T(8,128)(2,1)S(1)}, u32[]{:S(2)}, u32[]{:S(2)}) collective-permute-start(bf16[2,196,216]{2,1,0:T(8,128)(2,1)S(1)} %get-tuple-element.175.refs_0_), channel_id=1, source_target_pairs={{0,1},{1,0},{2,3},{3,2},{4,5},{5,4},{6,7},{7,6},{8,9},{9,8},{10,11... | collective-permute-start | bytes 508040 | tf_op jit(solution)/shard_map/ppermute | solution.py:708
  50.3 6.2 %collective-permute-start.21 = (bf16[2,196,216]{2,1,0:T(8,128)(2,1)S(1)}, bf16[2,196,216]{2,1,0:T(8,128)(2,1)S(1)}, u32[]{:S(2)}, u32[]{:S(2)}) collective-permute-start(bf16[2,196,216]{2,1,0:T(8,128)(2,1)S(1)} %collective-permute-done.20.refs_2_), channel_id=1, source_target_pairs={{0,1},{1,0},{2,3},{3,2},{4,5},{5,4},{6,7},{7,6},{8,9},{9,8},{10,11... | collective-permute-start | bytes 508040 | tf_op jit(solution)/shard_map/ppermute | solution.py:708
  51.8 6.7 %collective-permute-start.18 = (bf16[2,54,256]{2,1,0:T(8,128)(2,1)S(1)}, bf16[2,54,256]{2,1,0:T(8,128)(2,1)S(1)}, u32[]{:S(2)}, u32[]{:S(2)}) collective-permute-start(bf16[2,54,256]{2,1,0:T(8,128)(2,1)S(1)} %get-tuple-element.174), channel_id=1, source_target_pairs={{0,24},{4,28},{8,16},{12,20},{16,8},{20,12},{24,0},{28,4},{1,25},{... | collective-permute-start | bytes 165896 | tf_op jit(solution)/shard_map/ppermute | solution.py:708
  52.8 6.4 %collective-permute-start.24 = (bf16[2,54,256]{2,1,0:T(8,128)(2,1)S(1)}, bf16[2,54,256]{2,1,0:T(8,128)(2,1)S(1)}, u32[]{:S(2)}, u32[]{:S(2)}) collective-permute-start(bf16[2,54,256]{2,1,0:T(8,128)(2,1)S(1)} %get-tuple-element.184), channel_id=1, source_target_pairs={{0,16},{4,20},{8,24},{12,28},{16,0},{20,4},{24,8},{28,12},{1,17},{... | collective-permute-start | bytes 165896 | tf_op jit(solution)/shard_map/ppermute | solution.py:708
  53.1 6.1 %copy-start.1 = (f32[2,54,216]{2,0,1:T(2,128)S(1)}, f32[2,54,216]{2,0,1:T(2,128)}, u32[]{:S(2)}) copy-start(f32[2,54,216]{2,0,1:T(2,128)} %param.24) | copy-start | bytes 279940
  53.1 6.1 %copy-start.3 = (f32[2,54,216]{2,0,1:T(2,128)S(1)}, f32[2,54,216]{2,0,1:T(2,128)}, u32[]{:S(2)}) copy-start(f32[2,54,216]{2,0,1:T(2,128)} %param.25) | copy-start | bytes 279940
  53.2 6.1 %copy-start.4 = (f32[2,54,216]{2,0,1:T(2,128)S(1)}, f32[2,54,216]{2,0,1:T(2,128)}, u32[]{:S(2)}) copy-start(f32[2,54,216]{2,0,1:T(2,128)} %param.26) | copy-start | bytes 279940
  53.2 6.0 %copy-start.6 = (f32[9,216]{1,0:T(8,128)S(1)}, f32[9,216]{1,0:T(8,128)}, u32[]{:S(2)}) copy-start(f32[9,216]{1,0:T(8,128)} %refs_14_.1) | copy-start | bytes 23332
  53.2 6.0 %copy-start.7 = (f32[9,216]{1,0:T(8,128)S(1)}, f32[9,216]{1,0:T(8,128)}, u32[]{:S(2)}) copy-start(f32[9,216]{1,0:T(8,128)} %refs_15_.1) | copy-start | bytes 23332
  53.2 6.0 %copy-start.8 = (f32[2,12,12]{2,0,1:T(2,128)S(1)}, f32[2,12,12]{2,0,1:T(2,128)}, u32[]{:S(2)}) copy-start(f32[2,12,12]{2,0,1:T(2,128)} %param.31) | copy-start | bytes 3460
  53.2 6.0 %copy-start.9 = (f32[2,12,12]{2,0,1:T(2,128)S(1)}, f32[2,12,12]{2,0,1:T(2,128)}, u32[]{:S(2)}) copy-start(f32[2,12,12]{2,0,1:T(2,128)} %param.32) | copy-start | bytes 3460
  53.2 6.0 %copy-start.11 = (f32[4,216]{1,0:T(4,128)S(1)}, f32[4,216]{1,0:T(4,128)}, u32[]{:S(2)}) copy-start(f32[4,216]{1,0:T(4,128)} %refs_8_.1) | copy-start | bytes 10372
  53.2 6.0 %copy-start.12 = (f32[4,216]{1,0:T(4,128)S(1)}, f32[4,216]{1,0:T(4,128)}, u32[]{:S(2)}) copy-start(f32[4,216]{1,0:T(4,128)} %refs_9_.1) | copy-start | bytes 10372
  53.2 6.0 %collective-permute-start.23 = (bf16[2,54,256]{2,1,0:T(8,128)(2,1)S(1)}, bf16[2,54,256]{2,1,0:T(8,128)(2,1)S(1)}, u32[]{:S(2)}, u32[]{:S(2)}) collective-permute-start(bf16[2,54,256]{2,1,0:T(8,128)(2,1)S(1)} %get-tuple-element.183), channel_id=1, source_target_pairs={{0,8},{4,12},{8,0},{12,4},{16,24},{20,28},{24,16},{28,20},{1,9},{5... | collective-permute-start | bytes 165896 | tf_op jit(solution)/shard_map/ppermute | solution.py:708

commit v12 on v10

--- a/solution.py
+++ b/solution.py
@@ -115,6 +115,7 @@
 def load_weight(dst_ref, w_refs, b):
     for k, w_ref in enumerate(w_refs):
         dst_ref[64 * k : 64 * k + 54, :] = w_ref[b]
+        dst_ref[64 * k + 54 : 64 * k + 64, :] = jnp.zeros((10, dst_ref.shape[1]), bf16)
 
 
 def tiled(rows, heads):
@@ -130,7 +131,6 @@
     mid_ref, q_ref, k_ref, v_ref, o_ref, qw_ref, p_ref, pv_ref, ws_ref, t_ref = refs
     heads = mix_ref.shape[1] // PITCH
     a = a_ref[...]
-    ws_ref[...] = jnp.zeros_like(ws_ref)
     for b, dst in enumerate((q_ref, k_ref, v_ref)):
         load_weight(ws_ref.at[b], w_refs, b)
         dst[...] = nt(a, ws_ref[b]).astype(bf16)
@@ -322,7 +322,6 @@
     if part == 0:
         w_refs, refs = refs[:parts], refs[parts:]
         do_ref, gq_ref, gk_ref, gv_ref, g0_ref, g1_ref, wo_ref, dw_ref, dp_ref, dt_ref = refs
-        wo_ref[...] = jnp.zeros_like(wo_ref)
         load_weight(wo_ref, w_refs, 3)
         f = dmid_ref[...].astype(bf16)
         keep = keep_ref[0:1, :]
@@ -386,7 +385,6 @@
     ws_ref, tmp_ref, flat_ref, sm_ref = refs
     heads = gt_ref.shape[1]
     dim = x_ref.shape[1]
-    ws_ref[...] = jnp.zeros_like(ws_ref)
     for b in range(3):
         load_weight(ws_ref.at[b], w_refs, b)
     gq = jnp.concatenate([gqa_ref[...], gqb_ref[...]], axis=0)

time: 60.6 us -> 60.6 us (level)
  no operation moved by 1% of the time
where the time goes in v12:
time: 60.6 us; the launch traced here: 60.4 us
  starting transfers between devices  22.1 us (36%)
  waiting for transfers between devices  17.7 us (29%)
  Pallas kernels  16.3 us (27%)
  between operations  2.95 us (5%)
  local copies, waits for them, and re-layouts  1.27 us (2%)
    ppermute x25, starting transfers between devices, permute(): lax.ppermute(x, axis, [(i, i ^ k) for i in range(lax.axis_size(axis))])  22.1 us
    ppermute x25, waiting for transfers between devices, permute(): lax.ppermute(x, axis, [(i, i ^ k) for i in range(lax.axis_size(axis))])  17.7 us
    pallas_call x2, Pallas kernels, scores_back(): call(scores_back_kernel, 'scores_back', 0, 11 + len(more), outs, scratch,...  3.35 us
    pallas_call x1, Pallas kernels, ffn_last(): call(ffn_last_kernel, 'ffn_last', 0, 14 + late, [SDS((SIDE * SIDE, dim),...  2.3 us
    pallas_call x1, Pallas kernels, attn_fwd(): call(attn_fwd_kernel, 'attn_fwd', 0, 5 + len(w), [SDS((pad, dim), f32)] +...  2.13 us
    pallas_call x1, Pallas kernels, local(): pl.pallas_call(assemble_kernel, grid=(1,), in_specs=[SM] + [whole(*both.s...  1.99 us
    pallas_call x1, Pallas kernels, ffn_first(): call(ffn_first_kernel, 'ffn_first', 0, 4 + count, [SDS((pad, dim), f32),...  1.57 us
  transfers between devices with their start and end apart: 25, of which 12 were waited for; matrix products, arithmetic and copies ran while one was open for 0% of the time, Pallas kernels for 20%

profile of v12, /device:TPU:0, one launch (start us, length us, event | category | flops | bytes accessed | tf_op | source)
XLA Modules:
  0.0 60.4 jit_solution(12638362291009262126)
XLA Ops:
  0.7 0.9 %copy-done = f32[2,54,216]{2,0,1:T(2,128)S(1)} copy-done((f32[2,54,216]{2,0,1:T(2,128)S(1)}, f32[2,54,216]{2,0,1:T(2,128)}, u32[]{:S(2)}) %copy-start) | copy-done | bytes 93336
  1.5 0.2 cast.1.refs_0_
  1.8 3.0 %collective-permute-start.2 = (bf16[2,54,216]{2,1,0:T(8,128)(2,1)S(1)}, bf16[2,54,216]{2,1,0:T(8,128)(2,1)S(1)}, u32[]{:S(2)}, u32[]{:S(2)}) collective-permute-start(bf16[2,54,216]{2,1,0:T(8,128)(2,1)S(1)} %cast.1.refs_0_), channel_id=1, source_target_pairs={{0,4},{4,0},{8,12},{12,8},{16,20},{20,16},{24,28},{28,24},{1,5},{5... | collective-permute-start | bytes 139976 | tf_op jit(solution)/shard_map/ppermute | solution.py:706
  4.8 1.6 %collective-permute-start.1 = (bf16[2,54,216]{2,1,0:T(8,128)(2,1)S(1)}, bf16[2,54,216]{2,1,0:T(8,128)(2,1)S(1)}, u32[]{:S(2)}, u32[]{:S(2)}) collective-permute-start(bf16[2,54,216]{2,1,0:T(8,128)(2,1)S(1)} %cast.1.refs_0_), channel_id=1, source_target_pairs={{0,8},{4,12},{8,0},{12,4},{16,24},{20,28},{24,16},{28,20},{1,9},{5... | collective-permute-start | bytes 139976 | tf_op jit(solution)/shard_map/ppermute | solution.py:706
  6.4 2.6 %collective-permute-start = (bf16[2,54,216]{2,1,0:T(8,128)(2,1)S(1)}, bf16[2,54,216]{2,1,0:T(8,128)(2,1)S(1)}, u32[]{:S(2)}, u32[]{:S(2)}) collective-permute-start(bf16[2,54,216]{2,1,0:T(8,128)(2,1)S(1)} %cast.1.refs_0_), channel_id=1, source_target_pairs={{0,16},{4,20},{8,24},{12,28},{16,0},{20,4},{24,8},{28,12},{1,17},{... | collective-permute-start | bytes 139976 | tf_op jit(solution)/shard_map/ppermute | solution.py:706
  9.0 0.2 collective-permute-start.3
  9.2 3.1 %collective-permute-done.refs_1_ = bf16[2,54,216]{2,1,0:T(8,128)(2,1)S(1)} collective-permute-done((bf16[2,54,216]{2,1,0:T(8,128)(2,1)S(1)}, bf16[2,54,216]{2,1,0:T(8,128)(2,1)S(1)}, u32[]{:S(2)}, u32[]{:S(2)}) %collective-permute-start) | collective-permute-done | bytes 46688 | tf_op jit(solution)/shard_map/ppermute | solution.py:706
  12.3 2.7 %collective-permute-done.3.refs_2_ = bf16[2,54,216]{2,1,0:T(8,128)(2,1)S(1)} collective-permute-done((bf16[2,54,216]{2,1,0:T(8,128)(2,1)S(1)}, bf16[2,54,216]{2,1,0:T(8,128)(2,1)S(1)}, u32[]{:S(2)}, u32[]{:S(2)}) %collective-permute-start.3) | collective-permute-done | bytes 46688 | tf_op jit(solution)/shard_map/ppermute | solution.py:706
  15.0 0.6 collective-permute-start.4
  17.7 0.2 copy.34.cot_ref
  17.9 1.1 %prep.1 = (f32[224,216]{1,0:T(8,128)S(1)}, bf16[224,216]{1,0:T(8,128)(2,1)S(1)}, f32[224,216]{1,0:T(8,128)S(1)}, f32[2,192,256]{2,1,0:T(8,128)S(1)}, f32[224,128...) custom-call(s32[6]{0:T(128)S(1)} %concatenate.3.scal, ...), custom_call_target="tpu_custom_call" | custom-call | flops 1000000000 | bytes 3000000 | tf_op jit(solution)/shard_map/prep/pallas_call | solution.py:600
  19.0 1.4 %collective-permute-done.4.refs_3_ = bf16[3,2,54,216]{3,2,1,0:T(8,128)(2,1)S(1)} collective-permute-done((bf16[3,2,54,216]{3,2,1,0:T(8,128)(2,1)S(1)}, bf16[3,2,54,216]{3,2,1,0:T(8,128)(2,1)S(1)}, u32[]{:S(2)}, u32[]{:S(2)}) %collective-permute-start.4) | collective-permute-done | bytes 140000 | tf_op jit(solution)/shard_map/ppermute | solution.py:706
  20.5 0.3 select_attn.1.refs_0_
  20.8 1.6 %collective-permute-start.6 = (bf16[4,54,216]{2,1,0:T(8,128)(2,1)S(1)}, bf16[4,54,216]{2,1,0:T(8,128)(2,1)S(1)}, u32[]{:S(2)}, u32[]{:S(2)}) collective-permute-start(bf16[4,54,216]{2,1,0:T(8,128)(2,1)S(1)} %select_attn.1.refs_0_), channel_id=1, source_target_pairs={{0,2},{1,3},{2,0},{3,1},{4,6},{5,7},{6,4},{7,5},{8,10},{9,11},{10,... | collective-permute-start | bytes 279944 | tf_op jit(solution)/shard_map/ppermute | solution.py:706
  22.3 0.5 select_ffn.1.refs_0_
  22.9 0.6 collective-permute-start.8
  23.5 0.5 collective-permute-start.5
  24.0 2.0 %collective-permute-done.6.refs_2_ = bf16[4,54,216]{2,1,0:T(8,128)(2,1)S(1)} collective-permute-done((bf16[4,54,216]{2,1,0:T(8,128)(2,1)S(1)}, bf16[4,54,216]{2,1,0:T(8,128)(2,1)S(1)}, u32[]{:S(2)}, u32[]{:S(2)}) %collective-permute-start.6) | collective-permute-done | bytes 93344 | tf_op jit(solution)/shard_map/ppermute | solution.py:706
  26.0 1.3 %collective-permute-done.7.refs_3_ = bf16[4,54,216]{2,1,0:T(8,128)(2,1)S(1)} collective-permute-done((bf16[4,54,216]{2,1,0:T(8,128)(2,1)S(1)}, bf16[4,54,216]{2,1,0:T(8,128)(2,1)S(1)}, u32[]{:S(2)}, u32[]{:S(2)}) %collective-permute-start.7) | collective-permute-done | bytes 93344 | tf_op jit(solution)/shard_map/ppermute | solution.py:706
  27.3 2.1 %attn_fwd.1 = (f32[224,216]{1,0:T(8,128)S(1)}, bf16[224,256]{1,0:T(8,128)(2,1)S(1)}, bf16[224,256]{1,0:T(8,128)(2,1)S(1)}, bf16[224,256]{1,0:T(8,128)(2,1)S(1)},...) custom-call(f32[224,216]{1,0:T(8,128)S(1)} %get-tuple-element.114.x_, ...), custom_call_target="tpu_custom_call" | custom-call | flops 1000000000 | bytes 3000000 | tf_op jit(solution)/shard_map/attn_fwd/pallas_call | solution.py:630
  29.5 0.2 collective-permute-start.10
  29.7 1.6 %ffn_first.1 = (f32[224,216]{1,0:T(8,128)S(1)}, f32[224,128]{1,0:T(8,128)S(1)}, bf16[224,216]{1,0:T(8,128)(2,1)S(1)}, bf16[224,216]{1,0:T(8,128)(2,1)S(1)}, bf16...) custom-call(f32[224,216]{1,0:T(8,128)S(1)} %get-tuple-element.122.mi, ...), custom_call_target="tpu_custom_call" | custom-call | flops 3000000000 | bytes 9000000 | tf_op jit(solution)/shard_map/ffn_first/pallas_call | solution.py:644
  31.3 2.3 %ffn_last.1 = (bf16[196,216]{1,0:T(8,128)(2,1)S(1)}, f32[224,216]{1,0:T(8,128)S(1)}, f32[8,216]{1,0:T(8,128)S(1)}, bf16[9,54,256]{2,1,0:T(8,128)(2,1)S(1)}, bf16...) custom-call(f32[224,216]{1,0:T(8,128)S(1)} %get-tuple-element.122.mid_ref, ...), custom_call_target="tpu_custom_call" | custom-call | flops 4000000000 | bytes 12000000 | tf_op jit(solution)/shard_map/ffn_last/pallas_call | solution.py:658
  33.6 0.4 collective-permute-start.11
  34.0 1.0 %scores_back.2 = (bf16[224,256]{1,0:T(8,128)(2,1)S(1)}, bf16[64,256]{1,0:T(8,128)(2,1)S(1)}, f32[224,256]{1,0:T(8,128)S(1)}, f32[224,256]{1,0:T(8,128)S(1)}, f32...) custom-call(f32[224,216]{1,0:T(8,128)S(1)} %get-tuple-element.140.dmid_ref, f32[2,192,256]{2,1,0:T(8,128)S(1)} %get-tuple-element.116.mix_ref, ...), custom_call_target="tpu_custom_call" | custom-call | flops 4000000000 | bytes 12000000 | tf_op jit(solution)/shard_map/scores_back/pallas_call | solution.py:688
  35.1 0.1 collective-permute-done.11.b_ref
  35.3 0.4 collective-permute-start.12
  35.7 1.1 %collective-permute-start.13 = (bf16[9,54,256]{2,1,0:T(8,128)(2,1)S(1)}, bf16[9,54,256]{2,1,0:T(8,128)(2,1)S(1)}, u32[]{:S(2)}, u32[]{:S(2)}) collective-permute-start(bf16[9,54,256]{2,1,0:T(8,128)(2,1)S(1)} %half_sum.2), channel_id=1, source_target_pairs={{0,2},{1,3},{2,0},{3,1},{4,6},{5,7},{6,4},{7,5},{8,10},{9,11},{10,... | collective-permute-start | bytes 746504 | tf_op jit(solution)/shard_map/ppermute | solution.py:706
  36.8 2.3 %scores_back.3 = (bf16[160,256]{1,0:T(8,128)(2,1)S(1)}, bf16[224,256]{1,0:T(8,128)(2,1)S(1)}, bf16[224,256]{1,0:T(8,128)(2,1)S(1)}, f32[2,12,12]{2,1,0:T(8,128)S(1)}) custom-call(f32[224,216]{1,0:T(8,128)S(1)} %get-tuple-element.140.dmid_ref, f32[2,192,256]{2,1,0:T(8,128)S(1)} %get-tuple-element.116.mix_ref, f32[6,256]{1,0:T(8,128)S(1)} %get-tuple-element.118.keep_ref, ...), custom_call_target="tpu_custom_call" | custom-call | flops 4000000000 | bytes 12000000 | tf_op jit(solution)/shard_map/scores_back/pallas_call | solution.py:688
  39.1 0.6 weights_back.1
  39.8 0.5 collective-permute-start.14
  40.3 0.8 %collective-permute-done.15.b_ref = bf16[3,54,256]{2,1,0:T(8,128)(2,1)S(1)} collective-permute-done((bf16[3,54,256]{2,1,0:T(8,128)(2,1)S(1)}, bf16[3,54,256]{2,1,0:T(8,128)(2,1)S(1)}, u32[]{:S(2)}, u32[]{:S(2)}) %collective-permute-start.15) | collective-permute-done | bytes 82976 | tf_op jit(solution)/shard_map/ppermute | solution.py:706
  41.1 1.0 %collective-permute-start.16 = (bf16[3,54,256]{2,1,0:T(8,128)(2,1)S(1)}, bf16[3,54,256]{2,1,0:T(8,128)(2,1)S(1)}, u32[]{:S(2)}, u32[]{:S(2)}) collective-permute-start(bf16[3,54,256]{2,1,0:T(8,128)(2,1)S(1)} %half_sum.3), channel_id=1, source_target_pairs={{0,2},{1,3},{2,0},{3,1},{4,6},{5,7},{6,4},{7,5},{8,10},{9,11},{10,... | collective-permute-start | bytes 248840 | tf_op jit(solution)/shard_map/ppermute | solution.py:706
  42.1 1.1 %collective-permute-start.20 = (bf16[2,196,216]{2,1,0:T(8,128)(2,1)S(1)}, bf16[2,196,216]{2,1,0:T(8,128)(2,1)S(1)}, u32[]{:S(2)}, u32[]{:S(2)}) collective-permute-start(bf16[2,196,216]{2,1,0:T(8,128)(2,1)S(1)} %get-tuple-element.175.refs_0_), channel_id=1, source_target_pairs={{0,2},{1,3},{2,0},{3,1},{4,6},{5,7},{6,4},{7,5},{8,10},{9,11},{10,... | collective-permute-start | bytes 508040 | tf_op jit(solution)/shard_map/ppermute | solution.py:706
  43.2 0.8 %collective-permute-done.13.refs_2_ = bf16[9,54,256]{2,1,0:T(8,128)(2,1)S(1)} collective-permute-done((bf16[9,54,256]{2,1,0:T(8,128)(2,1)S(1)}, bf16[9,54,256]{2,1,0:T(8,128)(2,1)S(1)}, u32[]{:S(2)}, u32[]{:S(2)}) %collective-permute-start.13) | collective-permute-done | bytes 248864 | tf_op jit(solution)/shard_map/ppermute | solution.py:706
  44.0 0.7 %spread_ffn.1.old_ref = bf16[4,2,2,54,256]{4,3,2,1,0:T(8,128)(2,1)S(1)} custom-call(s32[12]{0:T(128)S(1)} %copy-done.13, s32[6]{0:T(128)S(1)} %concatenate.3.scal, bf16[9,54,256]{2,1,0:T(8,128)(2,1)S(1)} %get-tuple-element.137.refs_0_, bf16[9,54,256]{2,1,0:T(8,128)(2,1)S(1)} %collective-permute-done.12.refs_1_, ...), custom_call_target="tpu_custom_call" | custom-call | flops 1000000000 | bytes 3000000 | tf_op jit(solution)/shard_map/spread_ffn/pallas_call | solution.py:795
  44.6 1.9 %collective-permute-done.16.refs_2_ = bf16[3,54,256]{2,1,0:T(8,128)(2,1)S(1)} collective-permute-done((bf16[3,54,256]{2,1,0:T(8,128)(2,1)S(1)}, bf16[3,54,256]{2,1,0:T(8,128)(2,1)S(1)}, u32[]{:S(2)}, u32[]{:S(2)}) %collective-permute-start.16) | collective-permute-done | bytes 82976 | tf_op jit(solution)/shard_map/ppermute | solution.py:706
  46.5 0.3 spread_attn.1
  46.8 0.8 %collective-permute-start.17 = (bf16[2,2,54,256]{3,2,1,0:T(8,128)(2,1)S(1)}, bf16[2,2,54,256]{3,2,1,0:T(8,128)(2,1)S(1)}, u32[]{:S(2)}, u32[]{:S(2)}) collective-permute-start(bf16[2,2,54,256]{3,2,1,0:T(8,128)(2,1)S(1)} %get-tuple-element.173), channel_id=1, source_target_pairs={{0,4},{4,0},{8,12},{12,8},{16,20},{20,16},{24,28},{28,24},{1,5},{5... | collective-permute-start | bytes 331784 | tf_op jit(solution)/shard_map/ppermute | solution.py:706
  47.6 1.3 %collective-permute-start.22 = (bf16[2,2,54,256]{3,2,1,0:T(8,128)(2,1)S(1)}, bf16[2,2,54,256]{3,2,1,0:T(8,128)(2,1)S(1)}, u32[]{:S(2)}, u32[]{:S(2)}) collective-permute-start(bf16[2,2,54,256]{3,2,1,0:T(8,128)(2,1)S(1)} %get-tuple-element.181), channel_id=1, source_target_pairs={{0,4},{4,0},{8,12},{12,8},{16,20},{20,16},{24,28},{28,24},{1,5},{5... | collective-permute-start | bytes 331784 | tf_op jit(solution)/shard_map/ppermute | solution.py:706
  48.9 1.3 %collective-permute-done.20.refs_2_ = bf16[2,196,216]{2,1,0:T(8,128)(2,1)S(1)} collective-permute-done((bf16[2,196,216]{2,1,0:T(8,128)(2,1)S(1)}, bf16[2,196,216]{2,1,0:T(8,128)(2,1)S(1)}, u32[]{:S(2)}, u32[]{:S(2)}) %collective-permute-start.20) | collective-permute-done | bytes 169376 | tf_op jit(solution)/shard_map/ppermute | solution.py:706
  50.2 1.6 %collective-permute-done.17.other_ref = bf16[2,2,54,256]{3,2,1,0:T(8,128)(2,1)S(1)} collective-permute-done((bf16[2,2,54,256]{3,2,1,0:T(8,128)(2,1)S(1)}, bf16[2,2,54,256]{3,2,1,0:T(8,128)(2,1)S(1)}, u32[]{:S(2)}, u32[]{:S(2)}) %collective-permute-start.17) | collective-permute-done | bytes 110624 | tf_op jit(solution)/shard_map/ppermute | solution.py:706
  51.8 1.0 %collective-permute-start.18 = (bf16[2,54,256]{2,1,0:T(8,128)(2,1)S(1)}, bf16[2,54,256]{2,1,0:T(8,128)(2,1)S(1)}, u32[]{:S(2)}, u32[]{:S(2)}) collective-permute-start(bf16[2,54,256]{2,1,0:T(8,128)(2,1)S(1)} %get-tuple-element.174), channel_id=1, source_target_pairs={{0,24},{4,28},{8,16},{12,20},{16,8},{20,12},{24,0},{28,4},{1,25},{... | collective-permute-start | bytes 165896 | tf_op jit(solution)/shard_map/ppermute | solution.py:706
  52.8 0.3 collective-permute-start.24
  53.2 3.3 %collective-permute-start.23 = (bf16[2,54,256]{2,1,0:T(8,128)(2,1)S(1)}, bf16[2,54,256]{2,1,0:T(8,128)(2,1)S(1)}, u32[]{:S(2)}, u32[]{:S(2)}) collective-permute-start(bf16[2,54,256]{2,1,0:T(8,128)(2,1)S(1)} %get-tuple-element.183), channel_id=1, source_target_pairs={{0,8},{4,12},{8,0},{12,4},{16,24},{20,28},{24,16},{28,20},{1,9},{5... | collective-permute-start | bytes 165896 | tf_op jit(solution)/shard_map/ppermute | solution.py:706
  56.5 2.0 %assemble.1 = (f32[196,4,216]{2,1,0:T(4,128)}, f32[196,4,216]{2,1,0:T(4,128)}) custom-call(s32[6]{0:T(128)S(1)} %concatenate.3.scal, bf16[2,196,216]{2,1,0:T(8,128)(2,1)S(1)} %get-tuple-element.175.refs_0_, bf16[2,196,216]{2,1,0:T(8,128)(2,1)S(1)} %collective-permute-done.19.refs_1_, bf16[2,196,216]{2,1,0:T(8,128)(2,1)S(1)} %collective-permute-done.20.refs_2_, ...), custom_call_target="tpu_custom_call" | custom-call | flops 1000000000 | bytes 3000000 | tf_op jit(solution)/shard_map/assemble/pallas_call | solution.py:811
  58.5 0.7 %collective-permute-done.24.refs_2_ = bf16[2,54,256]{2,1,0:T(8,128)(2,1)S(1)} collective-permute-done((bf16[2,54,256]{2,1,0:T(8,128)(2,1)S(1)}, bf16[2,54,256]{2,1,0:T(8,128)(2,1)S(1)}, u32[]{:S(2)}, u32[]{:S(2)}) %collective-permute-start.24) | collective-permute-done | bytes 55328 | tf_op jit(solution)/shard_map/ppermute | solution.py:706
  59.2 1.1 %update.1 = (f32[54,2,216]{2,1,0:T(2,128)}, f32[54,2,216]{2,1,0:T(2,128)}, f32[54,2,216]{2,1,0:T(2,128)}, bf16[54,2,216]{2,1,0:T(2,128)(2,1)}, f32[4,216]{1,0:T(...) custom-call(f32[2,54,256]{2,1,0:T(8,128)S(1)} %get-tuple-element.182, ...), custom_call_target="tpu_custom_call" | custom-call | flops 1000000000 | bytes 3000000 | tf_op jit(solution)/shard_map/update/pallas_call | solution.py:718
  (57 shorter events, 0.5 us)
Async XLA Ops:
  0.6 0.9 %copy-start = (f32[2,54,216]{2,0,1:T(2,128)S(1)}, f32[2,54,216]{2,0,1:T(2,128)}, u32[]{:S(2)}) copy-start(f32[2,54,216]{2,0,1:T(2,128)} %param.24) | copy-start | bytes 279940
  1.8 15.9 %copy-start.2 = (f32[2,12,12]{2,0,1:T(2,128)S(1)}, f32[2,12,12]{2,0,1:T(2,128)}, u32[]{:S(2)}) copy-start(f32[2,12,12]{2,0,1:T(2,128)} %param.30) | copy-start | bytes 3460
  1.8 15.9 %copy-start.15 = (bf16[4,196,216]{2,0,1:T(4,128)(2,1)S(1)}, bf16[4,196,216]{2,0,1:T(4,128)(2,1)}, u32[]{:S(2)}) copy-start(bf16[4,196,216]{2,0,1:T(4,128)(2,1)} %param.18) | copy-start | bytes 1016068
  1.8 7.4 %collective-permute-start.2 = (bf16[2,54,216]{2,1,0:T(8,128)(2,1)S(1)}, bf16[2,54,216]{2,1,0:T(8,128)(2,1)S(1)}, u32[]{:S(2)}, u32[]{:S(2)}) collective-permute-start(bf16[2,54,216]{2,1,0:T(8,128)(2,1)S(1)} %cast.1.refs_0_), channel_id=1, source_target_pairs={{0,4},{4,0},{8,12},{12,8},{16,20},{20,16},{24,28},{28,24},{1,5},{5... | collective-permute-start | bytes 139976 | tf_op jit(solution)/shard_map/ppermute | solution.py:706
  4.8 4.4 %collective-permute-start.1 = (bf16[2,54,216]{2,1,0:T(8,128)(2,1)S(1)}, bf16[2,54,216]{2,1,0:T(8,128)(2,1)S(1)}, u32[]{:S(2)}, u32[]{:S(2)}) collective-permute-start(bf16[2,54,216]{2,1,0:T(8,128)(2,1)S(1)} %cast.1.refs_0_), channel_id=1, source_target_pairs={{0,8},{4,12},{8,0},{12,4},{16,24},{20,28},{24,16},{28,20},{1,9},{5... | collective-permute-start | bytes 139976 | tf_op jit(solution)/shard_map/ppermute | solution.py:706
  6.4 5.9 %collective-permute-start = (bf16[2,54,216]{2,1,0:T(8,128)(2,1)S(1)}, bf16[2,54,216]{2,1,0:T(8,128)(2,1)S(1)}, u32[]{:S(2)}, u32[]{:S(2)}) collective-permute-start(bf16[2,54,216]{2,1,0:T(8,128)(2,1)S(1)} %cast.1.refs_0_), channel_id=1, source_target_pairs={{0,16},{4,20},{8,24},{12,28},{16,0},{20,4},{24,8},{28,12},{1,17},{... | collective-permute-start | bytes 139976 | tf_op jit(solution)/shard_map/ppermute | solution.py:706
  9.0 6.0 %collective-permute-start.3 = (bf16[2,54,216]{2,1,0:T(8,128)(2,1)S(1)}, bf16[2,54,216]{2,1,0:T(8,128)(2,1)S(1)}, u32[]{:S(2)}, u32[]{:S(2)}) collective-permute-start(bf16[2,54,216]{2,1,0:T(8,128)(2,1)S(1)} %cast.1.refs_0_), channel_id=1, source_target_pairs={{0,24},{4,28},{8,16},{12,20},{16,8},{20,12},{24,0},{28,4},{1,25},{... | collective-permute-start | bytes 139976 | tf_op jit(solution)/shard_map/ppermute | solution.py:706
  15.0 2.7 %copy-start.14 = (f32[4,196,216]{2,0,1:T(4,128)S(1)}, f32[4,196,216]{2,0,1:T(4,128)}, u32[]{:S(2)}) copy-start(f32[4,196,216]{2,0,1:T(4,128)} %param.19) | copy-start | bytes 2032132
  15.0 2.9 %copy-start.10 = (f32[4,216]{1,0:T(4,128)S(1)}, f32[4,216]{1,0:T(4,128)}, u32[]{:S(2)}) copy-start(f32[4,216]{1,0:T(4,128)} %refs_7_.1) | copy-start | bytes 10372
  15.0 2.9 %copy-start.13 = (s32[12]{0:T(128)S(1)}, s32[12]{0:T(128)}, u32[]{:S(2)}) copy-start(s32[12]{0:T(128)} %slot_ref.3) | copy-start | bytes 148
  15.0 5.5 %collective-permute-start.4 = (bf16[3,2,54,216]{3,2,1,0:T(8,128)(2,1)S(1)}, bf16[3,2,54,216]{3,2,1,0:T(8,128)(2,1)S(1)}, u32[]{:S(2)}, u32[]{:S(2)}) collective-permute-start(bf16[3,2,54,216]{3,2,1,0:T(8,128)(2,1)S(1)} %stack.1.refs_1_), channel_id=1, source_target_pairs={{0,4},{4,0},{8,12},{12,8},{16,20},{20,16},{24,28},{28,24},{1,5},{5... | collective-permute-start | bytes 419912 | tf_op jit(solution)/shard_map/ppermute | solution.py:706
  20.5 1.9 %copy-start.5 = (f32[9,216]{1,0:T(8,128)S(1)}, f32[9,216]{1,0:T(8,128)}, u32[]{:S(2)}) copy-start(f32[9,216]{1,0:T(8,128)} %refs_13_.1) | copy-start | bytes 23332
  20.8 5.2 %collective-permute-start.6 = (bf16[4,54,216]{2,1,0:T(8,128)(2,1)S(1)}, bf16[4,54,216]{2,1,0:T(8,128)(2,1)S(1)}, u32[]{:S(2)}, u32[]{:S(2)}) collective-permute-start(bf16[4,54,216]{2,1,0:T(8,128)(2,1)S(1)} %select_attn.1.refs_0_), channel_id=1, source_target_pairs={{0,2},{1,3},{2,0},{3,1},{4,6},{5,7},{6,4},{7,5},{8,10},{9,11},{10,... | collective-permute-start | bytes 279944 | tf_op jit(solution)/shard_map/ppermute | solution.py:706
  22.9 6.6 %collective-permute-start.8 = (bf16[9,54,216]{2,1,0:T(8,128)(2,1)S(1)}, bf16[9,54,216]{2,1,0:T(8,128)(2,1)S(1)}, u32[]{:S(2)}, u32[]{:S(2)}) collective-permute-start(bf16[9,54,216]{2,1,0:T(8,128)(2,1)S(1)} %select_ffn.1.refs_0_), channel_id=1, source_target_pairs={{0,2},{1,3},{2,0},{3,1},{4,6},{5,7},{6,4},{7,5},{8,10},{9,11},{10,... | collective-permute-start | bytes 629864 | tf_op jit(solution)/shard_map/ppermute | solution.py:706
  23.4 6.2 %collective-permute-start.9 = (bf16[9,54,216]{2,1,0:T(8,128)(2,1)S(1)}, bf16[9,54,216]{2,1,0:T(8,128)(2,1)S(1)}, u32[]{:S(2)}, u32[]{:S(2)}) collective-permute-start(bf16[9,54,216]{2,1,0:T(8,128)(2,1)S(1)} %select_ffn.1.refs_0_), channel_id=1, source_target_pairs={{0,1},{1,0},{2,3},{3,2},{4,5},{5,4},{6,7},{7,6},{8,9},{9,8},{10,11... | collective-permute-start | bytes 629864 | tf_op jit(solution)/shard_map/ppermute | solution.py:706
  23.5 2.6 %collective-permute-start.5 = (bf16[4,54,216]{2,1,0:T(8,128)(2,1)S(1)}, bf16[4,54,216]{2,1,0:T(8,128)(2,1)S(1)}, u32[]{:S(2)}, u32[]{:S(2)}) collective-permute-start(bf16[4,54,216]{2,1,0:T(8,128)(2,1)S(1)} %select_attn.1.refs_0_), channel_id=1, source_target_pairs={{0,1},{1,0},{2,3},{3,2},{4,5},{5,4},{6,7},{7,6},{8,9},{9,8},{10,11... | collective-permute-start | bytes 279944 | tf_op jit(solution)/shard_map/ppermute | solution.py:706
  26.0 1.3 %collective-permute-start.7 = (bf16[4,54,216]{2,1,0:T(8,128)(2,1)S(1)}, bf16[4,54,216]{2,1,0:T(8,128)(2,1)S(1)}, u32[]{:S(2)}, u32[]{:S(2)}) collective-permute-start(bf16[4,54,216]{2,1,0:T(8,128)(2,1)S(1)} %collective-permute-done.6.refs_2_), channel_id=1, source_target_pairs={{0,1},{1,0},{2,3},{3,2},{4,5},{5,4},{6,7},{7,6},{8,9},{9,8},{10,11... | collective-permute-start | bytes 279944 | tf_op jit(solution)/shard_map/ppermute | solution.py:706
  29.5 1.8 %collective-permute-start.10 = (bf16[9,54,216]{2,1,0:T(8,128)(2,1)S(1)}, bf16[9,54,216]{2,1,0:T(8,128)(2,1)S(1)}, u32[]{:S(2)}, u32[]{:S(2)}) collective-permute-start(bf16[9,54,216]{2,1,0:T(8,128)(2,1)S(1)} %collective-permute-done.8.refs_5_), channel_id=1, source_target_pairs={{0,1},{1,0},{2,3},{3,2},{4,5},{5,4},{6,7},{7,6},{8,9},{9,8},{10,11... | collective-permute-start | bytes 629864 | tf_op jit(solution)/shard_map/ppermute | solution.py:706
  33.6 1.6 %collective-permute-start.11 = (bf16[9,54,256]{2,1,0:T(8,128)(2,1)S(1)}, bf16[9,54,256]{2,1,0:T(8,128)(2,1)S(1)}, u32[]{:S(2)}, u32[]{:S(2)}) collective-permute-start(bf16[9,54,256]{2,1,0:T(8,128)(2,1)S(1)} %get-tuple-element.150), channel_id=1, source_target_pairs={{0,1},{1,0},{2,3},{3,2},{4,5},{5,4},{6,7},{7,6},{8,9},{9,8},{10,11... | collective-permute-start | bytes 746504 | tf_op jit(solution)/shard_map/ppermute | solution.py:706
  35.3 7.9 %collective-permute-start.12 = (bf16[9,54,256]{2,1,0:T(8,128)(2,1)S(1)}, bf16[9,54,256]{2,1,0:T(8,128)(2,1)S(1)}, u32[]{:S(2)}, u32[]{:S(2)}) collective-permute-start(bf16[9,54,256]{2,1,0:T(8,128)(2,1)S(1)} %get-tuple-element.152), channel_id=1, source_target_pairs={{0,1},{1,0},{2,3},{3,2},{4,5},{5,4},{6,7},{7,6},{8,9},{9,8},{10,11... | collective-permute-start | bytes 746504 | tf_op jit(solution)/shard_map/ppermute | solution.py:706
  35.7 8.3 %collective-permute-start.13 = (bf16[9,54,256]{2,1,0:T(8,128)(2,1)S(1)}, bf16[9,54,256]{2,1,0:T(8,128)(2,1)S(1)}, u32[]{:S(2)}, u32[]{:S(2)}) collective-permute-start(bf16[9,54,256]{2,1,0:T(8,128)(2,1)S(1)} %half_sum.2), channel_id=1, source_target_pairs={{0,2},{1,3},{2,0},{3,1},{4,6},{5,7},{6,4},{7,5},{8,10},{9,11},{10,... | collective-permute-start | bytes 746504 | tf_op jit(solution)/shard_map/ppermute | solution.py:706
  39.7 1.3 %collective-permute-start.15 = (bf16[3,54,256]{2,1,0:T(8,128)(2,1)S(1)}, bf16[3,54,256]{2,1,0:T(8,128)(2,1)S(1)}, u32[]{:S(2)}, u32[]{:S(2)}) collective-permute-start(bf16[3,54,256]{2,1,0:T(8,128)(2,1)S(1)} %get-tuple-element.170), channel_id=1, source_target_pairs={{0,1},{1,0},{2,3},{3,2},{4,5},{5,4},{6,7},{7,6},{8,9},{9,8},{10,11... | collective-permute-start | bytes 248840 | tf_op jit(solution)/shard_map/ppermute | solution.py:706
  39.8 4.8 %collective-permute-start.14 = (bf16[3,54,256]{2,1,0:T(8,128)(2,1)S(1)}, bf16[3,54,256]{2,1,0:T(8,128)(2,1)S(1)}, u32[]{:S(2)}, u32[]{:S(2)}) collective-permute-start(bf16[3,54,256]{2,1,0:T(8,128)(2,1)S(1)} %get-tuple-element.167), channel_id=1, source_target_pairs={{0,1},{1,0},{2,3},{3,2},{4,5},{5,4},{6,7},{7,6},{8,9},{9,8},{10,11... | collective-permute-start | bytes 248840 | tf_op jit(solution)/shard_map/ppermute | solution.py:706
  41.1 5.4 %collective-permute-start.16 = (bf16[3,54,256]{2,1,0:T(8,128)(2,1)S(1)}, bf16[3,54,256]{2,1,0:T(8,128)(2,1)S(1)}, u32[]{:S(2)}, u32[]{:S(2)}) collective-permute-start(bf16[3,54,256]{2,1,0:T(8,128)(2,1)S(1)} %half_sum.3), channel_id=1, source_target_pairs={{0,2},{1,3},{2,0},{3,1},{4,6},{5,7},{6,4},{7,5},{8,10},{9,11},{10,... | collective-permute-start | bytes 248840 | tf_op jit(solution)/shard_map/ppermute | solution.py:706
  42.1 8.1 %collective-permute-start.20 = (bf16[2,196,216]{2,1,0:T(8,128)(2,1)S(1)}, bf16[2,196,216]{2,1,0:T(8,128)(2,1)S(1)}, u32[]{:S(2)}, u32[]{:S(2)}) collective-permute-start(bf16[2,196,216]{2,1,0:T(8,128)(2,1)S(1)} %get-tuple-element.175.refs_0_), channel_id=1, source_target_pairs={{0,2},{1,3},{2,0},{3,1},{4,6},{5,7},{6,4},{7,5},{8,10},{9,11},{10,... | collective-permute-start | bytes 508040 | tf_op jit(solution)/shard_map/ppermute | solution.py:706
  46.8 5.0 %collective-permute-start.17 = (bf16[2,2,54,256]{3,2,1,0:T(8,128)(2,1)S(1)}, bf16[2,2,54,256]{3,2,1,0:T(8,128)(2,1)S(1)}, u32[]{:S(2)}, u32[]{:S(2)}) collective-permute-start(bf16[2,2,54,256]{3,2,1,0:T(8,128)(2,1)S(1)} %get-tuple-element.173), channel_id=1, source_target_pairs={{0,4},{4,0},{8,12},{12,8},{16,20},{20,16},{24,28},{28,24},{1,5},{5... | collective-permute-start | bytes 331784 | tf_op jit(solution)/shard_map/ppermute | solution.py:706
  47.6 5.5 %collective-permute-start.22 = (bf16[2,2,54,256]{3,2,1,0:T(8,128)(2,1)S(1)}, bf16[2,2,54,256]{3,2,1,0:T(8,128)(2,1)S(1)}, u32[]{:S(2)}, u32[]{:S(2)}) collective-permute-start(bf16[2,2,54,256]{3,2,1,0:T(8,128)(2,1)S(1)} %get-tuple-element.181), channel_id=1, source_target_pairs={{0,4},{4,0},{8,12},{12,8},{16,20},{20,16},{24,28},{28,24},{1,5},{5... | collective-permute-start | bytes 331784 | tf_op jit(solution)/shard_map/ppermute | solution.py:706
  48.9 7.6 %collective-permute-start.19 = (bf16[2,196,216]{2,1,0:T(8,128)(2,1)S(1)}, bf16[2,196,216]{2,1,0:T(8,128)(2,1)S(1)}, u32[]{:S(2)}, u32[]{:S(2)}) collective-permute-start(bf16[2,196,216]{2,1,0:T(8,128)(2,1)S(1)} %get-tuple-element.175.refs_0_), channel_id=1, source_target_pairs={{0,1},{1,0},{2,3},{3,2},{4,5},{5,4},{6,7},{7,6},{8,9},{9,8},{10,11... | collective-permute-start | bytes 508040 | tf_op jit(solution)/shard_map/ppermute | solution.py:706
  50.2 6.3 %collective-permute-start.21 = (bf16[2,196,216]{2,1,0:T(8,128)(2,1)S(1)}, bf16[2,196,216]{2,1,0:T(8,128)(2,1)S(1)}, u32[]{:S(2)}, u32[]{:S(2)}) collective-permute-start(bf16[2,196,216]{2,1,0:T(8,128)(2,1)S(1)} %collective-permute-done.20.refs_2_), channel_id=1, source_target_pairs={{0,1},{1,0},{2,3},{3,2},{4,5},{5,4},{6,7},{7,6},{8,9},{9,8},{10,11... | collective-permute-start | bytes 508040 | tf_op jit(solution)/shard_map/ppermute | solution.py:706
  51.8 6.7 %collective-permute-start.18 = (bf16[2,54,256]{2,1,0:T(8,128)(2,1)S(1)}, bf16[2,54,256]{2,1,0:T(8,128)(2,1)S(1)}, u32[]{:S(2)}, u32[]{:S(2)}) collective-permute-start(bf16[2,54,256]{2,1,0:T(8,128)(2,1)S(1)} %get-tuple-element.174), channel_id=1, source_target_pairs={{0,24},{4,28},{8,16},{12,20},{16,8},{20,12},{24,0},{28,4},{1,25},{... | collective-permute-start | bytes 165896 | tf_op jit(solution)/shard_map/ppermute | solution.py:706
  52.8 6.4 %collective-permute-start.24 = (bf16[2,54,256]{2,1,0:T(8,128)(2,1)S(1)}, bf16[2,54,256]{2,1,0:T(8,128)(2,1)S(1)}, u32[]{:S(2)}, u32[]{:S(2)}) collective-permute-start(bf16[2,54,256]{2,1,0:T(8,128)(2,1)S(1)} %get-tuple-element.184), channel_id=1, source_target_pairs={{0,16},{4,20},{8,24},{12,28},{16,0},{20,4},{24,8},{28,12},{1,17},{... | collective-permute-start | bytes 165896 | tf_op jit(solution)/shard_map/ppermute | solution.py:706
  53.1 6.0 %copy-start.1 = (f32[2,54,216]{2,0,1:T(2,128)S(1)}, f32[2,54,216]{2,0,1:T(2,128)}, u32[]{:S(2)}) copy-start(f32[2,54,216]{2,0,1:T(2,128)} %param.24) | copy-start | bytes 279940
  53.1 6.0 %copy-start.3 = (f32[2,54,216]{2,0,1:T(2,128)S(1)}, f32[2,54,216]{2,0,1:T(2,128)}, u32[]{:S(2)}) copy-start(f32[2,54,216]{2,0,1:T(2,128)} %param.25) | copy-start | bytes 279940
  53.1 6.0 %copy-start.4 = (f32[2,54,216]{2,0,1:T(2,128)S(1)}, f32[2,54,216]{2,0,1:T(2,128)}, u32[]{:S(2)}) copy-start(f32[2,54,216]{2,0,1:T(2,128)} %param.26) | copy-start | bytes 279940
  53.2 6.0 %copy-start.6 = (f32[9,216]{1,0:T(8,128)S(1)}, f32[9,216]{1,0:T(8,128)}, u32[]{:S(2)}) copy-start(f32[9,216]{1,0:T(8,128)} %refs_14_.1) | copy-start | bytes 23332
  53.2 6.0 %copy-start.7 = (f32[9,216]{1,0:T(8,128)S(1)}, f32[9,216]{1,0:T(8,128)}, u32[]{:S(2)}) copy-start(f32[9,216]{1,0:T(8,128)} %refs_15_.1) | copy-start | bytes 23332
  53.2 6.0 %copy-start.8 = (f32[2,12,12]{2,0,1:T(2,128)S(1)}, f32[2,12,12]{2,0,1:T(2,128)}, u32[]{:S(2)}) copy-start(f32[2,12,12]{2,0,1:T(2,128)} %param.31) | copy-start | bytes 3460
  53.2 6.0 %copy-start.9 = (f32[2,12,12]{2,0,1:T(2,128)S(1)}, f32[2,12,12]{2,0,1:T(2,128)}, u32[]{:S(2)}) copy-start(f32[2,12,12]{2,0,1:T(2,128)} %param.32) | copy-start | bytes 3460
  53.2 6.0 %copy-start.11 = (f32[4,216]{1,0:T(4,128)S(1)}, f32[4,216]{1,0:T(4,128)}, u32[]{:S(2)}) copy-start(f32[4,216]{1,0:T(4,128)} %refs_8_.1) | copy-start | bytes 10372
  53.2 6.0 %copy-start.12 = (f32[4,216]{1,0:T(4,128)S(1)}, f32[4,216]{1,0:T(4,128)}, u32[]{:S(2)}) copy-start(f32[4,216]{1,0:T(4,128)} %refs_9_.1) | copy-start | bytes 10372
  53.2 5.9 %collective-permute-start.23 = (bf16[2,54,256]{2,1,0:T(8,128)(2,1)S(1)}, bf16[2,54,256]{2,1,0:T(8,128)(2,1)S(1)}, u32[]{:S(2)}, u32[]{:S(2)}) collective-permute-start(bf16[2,54,256]{2,1,0:T(8,128)(2,1)S(1)} %get-tuple-element.183), channel_id=1, source_target_pairs={{0,8},{4,12},{8,0},{12,4},{16,24},{20,28},{24,16},{28,20},{1,9},{5... | collective-permute-start | bytes 165896 | tf_op jit(solution)/shard_map/ppermute | solution.py:706
